TPU v7x, 32 devices: a whole 2x2x4 slice. The times are simulated.
32 devices in a mesh: dp: 2 (over x), row: 4 (over z), col: 4 (over y, core).
Axes of the slice: x: 2, y: 2, z: 4, core: 2. Of those that a mesh axis runs over, the one named last changes fastest.
Arguments:
- tokens: bfloat16 [2, 768, 4096], P(None, 'row', ('dp', 'col')), may hold values from -6 to 6
- w_query: bfloat16 [768, 768], P(('row', 'dp'), 'col'), may hold values from -0.21875 to 0.21875
- w_key: bfloat16 [768, 768], P(('row', 'dp'), 'col'), may hold values from -0.21875 to 0.21875
- w_value: bfloat16 [768, 768], P(('row', 'dp'), 'col'), may hold values from -0.21875 to 0.21875
- w_output: bfloat16 [768, 768], P(('col', 'dp'), 'row'), may hold values from -6 to 6
- w_inner: bfloat16 [768, 3072], P(('row', 'dp'), 'col'), may hold values from -0.21875 to 0.21875
- w_outer: bfloat16 [3072, 768], P(('col', 'dp'), 'row'), may hold values from -0.109375 to 0.109375
- first_gain: float32 [768], P('row'), may hold values from 0.1 to 1.9
- first_shift: float32 [768], P('row'), may hold values from -3 to 3
- second_gain: float32 [768], P('row'), may hold values from 0.1 to 1.9
- second_shift: float32 [768], P('row'), may hold values from -3 to 3
- seq_lengths: int32 [2, 2], replicated, may hold values from 512 to 2048, as said below
- out_grad: bfloat16 [2, 768, 4096], P(None, 'row', ('dp', 'col')), may hold values from -6 to 6
Outputs:
- mixed: bfloat16 [2, 768, 4096], P(None, 'row', ('dp', 'col'))
- d_input: float32 [2, 768, 4096], P(None, 'row', ('dp', 'col'))
- grad_w_query: float32 [768, 768], P(('row', 'dp'), 'col')
- grad_w_key: float32 [768, 768], P(('row', 'dp'), 'col')
- grad_w_value: float32 [768, 768], P(('row', 'dp'), 'col')
- grad_w_output: float32 [768, 768], P(('col', 'dp'), 'row')
- grad_w_inner: float32 [768, 3072], P(('row', 'dp'), 'col')
- grad_w_outer: float32 [3072, 768], P(('col', 'dp'), 'row')
- grad_first_gain: float32 [768], P('row')
- grad_first_shift: float32 [768], P('row')
- grad_second_gain: float32 [768], P('row')
- grad_second_shift: float32 [768], P('row')
Inputs may be any that keep to these rules, and one draw needn't show every extreme that they name: micro-batch m's sequence in data group g fills the first seq_lengths[m, g] positions of the group's slot of 2048 token slots; in every draw some sequence has exactly 2048 tokens and some exactly 512.
All inputs are finite; a program needn't handle non-finite values.
Results may differ from a plain program's by a relative error of at most 0.02.
Values may be sent and summed in bfloat16 or wider, within the bound.
No kernel may reach another device: no remote copies, remote signals or barrier semaphores. Data moves between devices by JAX's collectives and lax.ppermute only.
A program may use at most 128 MiB of HBM per device.

v0:
```python
import jax
import jax.numpy as jnp
from jax import lax
from jax.sharding import PartitionSpec as P

HD = 64


norm_eps = 1e-05
masked_score = -1e30


def rotate_pairs(values, positions, head_size, direction):
    row_count = values.shape[0]
    row_width = values.shape[1]
    half_size = head_size // 2
    frequency = 10000.0 ** (-2.0 * jnp.arange(half_size, dtype=jnp.float32) / head_size)
    angles = positions.astype(jnp.float32)[:, None] * frequency[None, :]
    cosine = jnp.cos(angles)[:, None, :]
    sine_part = direction * jnp.sin(angles)[:, None, :]
    paired = values.reshape(row_count, row_width // head_size, half_size, 2)
    even_part = paired[..., 0]
    odd_part = paired[..., 1]
    turned = jnp.stack(
        [even_part * cosine - odd_part * sine_part, even_part * sine_part + odd_part * cosine],
        axis=-1,
    )
    return turned.reshape(row_count, row_width)


def fetch_blocks(w_query, w_key, w_value, w_output, w_inner, w_outer):
    return (
        lax.all_gather(w_query, "dp", axis=0, tiled=True),
        lax.all_gather(w_key, "dp", axis=0, tiled=True),
        lax.all_gather(w_value, "dp", axis=0, tiled=True),
        lax.all_gather(w_output, "dp", axis=0, tiled=True),
        lax.all_gather(w_inner, "dp", axis=0, tiled=True),
        lax.all_gather(w_outer, "dp", axis=0, tiled=True),
    )


def along_col(values):
    return lax.all_gather(values, "col", axis=0, tiled=True)


def along_row(values):
    return lax.all_gather(values, "row", axis=0, tiled=True)


def reduce_rows(values):
    return lax.psum_scatter(values, "row", scatter_dimension=0, tiled=True)


def reduce_cols(values):
    return lax.psum_scatter(
        values.astype(jnp.bfloat16), "col", scatter_dimension=0, tiled=True
    ).astype(jnp.float32)


def feature_totals(first_sum, second_sum):
    return lax.psum((first_sum, second_sum), "row")


def contract_rows(left, right):
    return lax.dot_general(
        left, right, (((0,), (0,)), ((), ())), preferred_element_type=jnp.float32
    )


def times_transpose(left, right):
    return lax.dot_general(
        left, right, (((1,), (1,)), ((), ())), preferred_element_type=jnp.float32
    )


def layer_norm(summed, gain_vec, shift_vec, full_width):
    first_sum, second_sum = feature_totals(
        jnp.sum(summed, axis=1), jnp.sum(summed * summed, axis=1)
    )
    row_mean = first_sum / full_width
    row_var = second_sum / full_width - row_mean * row_mean
    inv_scale = lax.rsqrt(row_var + norm_eps)
    centered = (summed - row_mean[:, None]) * inv_scale[:, None]
    return (centered * gain_vec + shift_vec, centered, inv_scale)


def layer_norm_back(grad_out, centered, inv_scale, gain_vec, full_width):
    grad_cent = grad_out * gain_vec
    first_sum, second_sum = feature_totals(
        jnp.sum(grad_cent, axis=1), jnp.sum(grad_cent * centered, axis=1)
    )
    return inv_scale[:, None] * (
        grad_cent - first_sum[:, None] / full_width - centered * (second_sum / full_width)[:, None]
    )


def split_heads(values, head_size):
    row_count = values.shape[0]
    return values.reshape(row_count, values.shape[1] // head_size, head_size).transpose(1, 0, 2)


def merge_heads(values):
    return values.transpose(1, 0, 2).reshape(values.shape[1], values.shape[0] * values.shape[2])


def attend_forward(query_heads, key_heads, value_heads, key_valid, score_scale):

    def one_head(head_items):
        query_rows, key_rows, value_rows = head_items
        scores = times_transpose(query_rows, key_rows) * score_scale
        scores = jnp.where(key_valid[None, :], scores, masked_score)
        row_top = jnp.max(scores, axis=1, keepdims=True)
        row_total = jnp.sum(jnp.exp(scores - row_top), axis=1, keepdims=True)
        log_total = row_top + jnp.log(row_total)
        probs_low = jnp.exp(scores - log_total).astype(jnp.bfloat16)
        head_out = jnp.dot(probs_low, value_rows, preferred_element_type=jnp.float32)
        return (head_out, log_total[:, 0])

    return lax.map(one_head, (query_heads, key_heads, value_heads))


def attend_backward(
    query_heads, key_heads, value_heads, log_totals, grad_heads, key_valid, score_scale
):

    def one_head(head_items):
        query_rows, key_rows, value_rows, log_total, grad_rows = head_items
        scores = times_transpose(query_rows, key_rows) * score_scale
        scores = jnp.where(key_valid[None, :], scores, masked_score)
        probs_full = jnp.exp(scores - log_total[:, None])
        grad_probs = times_transpose(grad_rows, value_rows)
        row_delta = jnp.sum(probs_full * grad_probs, axis=1, keepdims=True)
        grad_scores = (probs_full * (grad_probs - row_delta)).astype(jnp.bfloat16)
        grad_query = (
            jnp.dot(grad_scores, key_rows, preferred_element_type=jnp.float32) * score_scale
        )
        grad_key = contract_rows(grad_scores, query_rows) * score_scale
        grad_value = contract_rows(probs_full.astype(jnp.bfloat16), grad_rows)
        return (grad_query, grad_key, grad_value)

    return lax.map(one_head, (query_heads, key_heads, value_heads, log_totals, grad_heads))


def gelu_exact(values):
    return jax.nn.gelu(values, approximate=False)


def local(
    tokens,
    w_query,
    w_key,
    w_value,
    w_output,
    w_inner,
    w_outer,
    first_gain,
    first_shift,
    second_gain,
    second_shift,
    seq_lengths,
    out_grad,
):
    micro_count = tokens.shape[0]
    feat_a = tokens.shape[1]
    rows_a = tokens.shape[2]
    count_col = lax.axis_size("col")
    count_row = lax.axis_size("row")
    seq_total = rows_a * count_col
    rows_b = seq_total // count_row
    full_width = feat_a * count_row
    head_size = HD
    score_scale = head_size ** (-0.5)
    width_b = w_query.shape[1]
    inner_width = w_inner.shape[1]
    group_index = lax.axis_index("dp")
    pos_a = lax.axis_index("col") * rows_a + jnp.arange(rows_a, dtype=jnp.int32)
    pos_b = lax.axis_index("row") * rows_b + jnp.arange(rows_b, dtype=jnp.int32)
    pos_all = jnp.arange(seq_total, dtype=jnp.int32)
    acc_qkv = jnp.zeros((feat_a, 3 * width_b), jnp.float32)
    acc_output = jnp.zeros((width_b, feat_a), jnp.float32)
    acc_inner = jnp.zeros((feat_a, inner_width), jnp.float32)
    acc_outer = jnp.zeros((inner_width, feat_a), jnp.float32)
    acc_gain_one = jnp.zeros((feat_a,), jnp.float32)
    acc_shift_one = jnp.zeros((feat_a,), jnp.float32)
    acc_gain_two = jnp.zeros((feat_a,), jnp.float32)
    acc_shift_two = jnp.zeros((feat_a,), jnp.float32)
    outputs = []
    input_grads = []
    for micro_step in range(micro_count):
        forward_blocks = fetch_blocks(w_query, w_key, w_value, w_output, w_inner, w_outer)
        query_block, key_block, value_block, output_block, inner_block, outer_block = forward_blocks
        length_now = lax.dynamic_index_in_dim(seq_lengths[micro_step], group_index, keepdims=False)
        valid_a = pos_a < length_now
        key_valid = pos_all < length_now
        tokens_now = tokens[micro_step].T
        tokens_all = along_col(tokens_now)
        qkv_block = jnp.concatenate([query_block, key_block, value_block], axis=1)
        projected = reduce_rows(jnp.dot(tokens_all, qkv_block, preferred_element_type=jnp.float32))
        query_rot = rotate_pairs(projected[:, :width_b], pos_b, head_size, 1.0).astype(jnp.bfloat16)
        key_rot = rotate_pairs(projected[:, width_b : 2 * width_b], pos_b, head_size, 1.0).astype(
            jnp.bfloat16
        )
        value_low = projected[:, 2 * width_b :].astype(jnp.bfloat16)
        key_all, value_all = (
            lax.all_gather(key_rot, "row", axis=0, tiled=True),
            lax.all_gather(value_low, "row", axis=0, tiled=True),
        )
        query_heads = split_heads(query_rot, head_size)
        head_outs, log_totals = attend_forward(
            query_heads,
            split_heads(key_all, head_size),
            split_heads(value_all, head_size),
            key_valid,
            score_scale,
        )
        attn_low = merge_heads(head_outs).astype(jnp.bfloat16)
        attn_all = along_row(attn_low)
        branch = reduce_cols(jnp.dot(attn_all, output_block, preferred_element_type=jnp.float32))
        hidden, centered_one, inv_one = layer_norm(
            tokens_now.astype(jnp.float32) + branch, first_gain, first_shift, full_width
        )
        hidden_all = along_col(hidden.astype(jnp.bfloat16))
        inner = reduce_rows(jnp.dot(hidden_all, inner_block, preferred_element_type=jnp.float32))
        act_low = gelu_exact(inner).astype(jnp.bfloat16)
        act_all = along_row(act_low)
        outer = reduce_cols(jnp.dot(act_all, outer_block, preferred_element_type=jnp.float32))
        result, centered_two, inv_two = layer_norm(
            hidden + outer, second_gain, second_shift, full_width
        )
        outputs.append(result.astype(jnp.bfloat16).T)
        backward_blocks = fetch_blocks(w_query, w_key, w_value, w_output, w_inner, w_outer)
        query_back, key_block_back, value_back, output_back, inner_back, outer_back = (
            backward_blocks
        )
        qkv_back = jnp.concatenate([query_back, key_block_back, value_back], axis=1)
        cot_now = out_grad[micro_step].T.astype(jnp.float32) * valid_a[:, None].astype(jnp.float32)
        acc_gain_two = acc_gain_two + jnp.sum(cot_now * centered_two, axis=0)
        acc_shift_two = acc_shift_two + jnp.sum(cot_now, axis=0)
        grad_two = layer_norm_back(cot_now, centered_two, inv_two, second_gain, full_width)
        outer_all = along_col(grad_two.astype(jnp.bfloat16))
        grad_act = reduce_rows(times_transpose(outer_all, outer_back))
        acc_outer = acc_outer + contract_rows(act_all, outer_all)
        gelu_pull = jax.vjp(gelu_exact, inner)[1]
        inner_low = gelu_pull(grad_act)[0].astype(jnp.bfloat16)
        inner_all = along_row(inner_low)
        grad_hidden = grad_two + reduce_cols(times_transpose(inner_all, inner_back))
        acc_inner = acc_inner + contract_rows(hidden_all, inner_all)
        acc_gain_one = acc_gain_one + jnp.sum(grad_hidden * centered_one, axis=0)
        acc_shift_one = acc_shift_one + jnp.sum(grad_hidden, axis=0)
        grad_one = layer_norm_back(grad_hidden, centered_one, inv_one, first_gain, full_width)
        branch_all = along_col(grad_one.astype(jnp.bfloat16))
        grad_attn = reduce_rows(times_transpose(branch_all, output_back))
        acc_output = acc_output + contract_rows(attn_all, branch_all)
        key_again, value_again = (
            lax.all_gather(key_rot, "row", axis=0, tiled=True),
            lax.all_gather(value_low, "row", axis=0, tiled=True),
        )
        grad_q_heads, grad_k_heads, grad_v_heads = attend_backward(
            query_heads,
            split_heads(key_again, head_size),
            split_heads(value_again, head_size),
            log_totals,
            split_heads(grad_attn.astype(jnp.bfloat16), head_size),
            key_valid,
            score_scale,
        )
        key_sum, value_sum = (
            lax.psum_scatter(
                merge_heads(grad_k_heads).astype(jnp.bfloat16),
                "row",
                scatter_dimension=0,
                tiled=True,
            ).astype(jnp.float32),
            lax.psum_scatter(
                merge_heads(grad_v_heads).astype(jnp.bfloat16),
                "row",
                scatter_dimension=0,
                tiled=True,
            ).astype(jnp.float32),
        )
        grad_query = rotate_pairs(merge_heads(grad_q_heads), pos_b, head_size, -1.0).astype(
            jnp.bfloat16
        )
        grad_key = rotate_pairs(key_sum, pos_b, head_size, -1.0).astype(jnp.bfloat16)
        grad_value = value_sum.astype(jnp.bfloat16)
        proj_all = along_row(jnp.concatenate([grad_query, grad_key, grad_value], axis=1))
        input_grads.append((grad_one + reduce_cols(times_transpose(proj_all, qkv_back))).T)
        acc_qkv = acc_qkv + contract_rows(tokens_all, proj_all)
    grad_parts = (
        lax.psum_scatter(
            acc_qkv[:, :width_b].astype(jnp.bfloat16), "dp", scatter_dimension=0, tiled=True
        ).astype(jnp.float32),
        lax.psum_scatter(
            acc_qkv[:, width_b : 2 * width_b].astype(jnp.bfloat16),
            "dp",
            scatter_dimension=0,
            tiled=True,
        ).astype(jnp.float32),
        lax.psum_scatter(
            acc_qkv[:, 2 * width_b :].astype(jnp.bfloat16), "dp", scatter_dimension=0, tiled=True
        ).astype(jnp.float32),
        lax.psum_scatter(
            acc_output.astype(jnp.bfloat16), "dp", scatter_dimension=0, tiled=True
        ).astype(jnp.float32),
        lax.psum_scatter(
            acc_inner.astype(jnp.bfloat16), "dp", scatter_dimension=0, tiled=True
        ).astype(jnp.float32),
        lax.psum_scatter(
            acc_outer.astype(jnp.bfloat16), "dp", scatter_dimension=0, tiled=True
        ).astype(jnp.float32),
    )
    norm_parts = lax.psum((acc_gain_one, acc_shift_one, acc_gain_two, acc_shift_two), ("dp", "col"))
    return (
        jnp.stack(outputs),
        jnp.stack(input_grads),
        grad_parts[0],
        grad_parts[1],
        grad_parts[2],
        grad_parts[3],
        grad_parts[4],
        grad_parts[5],
        norm_parts[0],
        norm_parts[1],
        norm_parts[2],
        norm_parts[3],
    )


def solution(mesh):
    placed = (
        P(None, "row", ("dp", "col")),
        P(("row", "dp"), "col"),
        P(("row", "dp"), "col"),
        P(("row", "dp"), "col"),
        P(("col", "dp"), "row"),
        P(("row", "dp"), "col"),
        P(("col", "dp"), "row"),
        P("row"),
        P("row"),
        P("row"),
        P("row"),
        P(),
        P(None, "row", ("dp", "col")),
    )
    return jax.shard_map(
        local,
        mesh=mesh,
        in_specs=placed,
        out_specs=(
            P(None, "row", ("dp", "col")),
            P(None, "row", ("dp", "col")),
            P(("row", "dp"), "col"),
            P(("row", "dp"), "col"),
            P(("row", "dp"), "col"),
            P(("col", "dp"), "row"),
            P(("row", "dp"), "col"),
            P(("col", "dp"), "row"),
            P("row"),
            P("row"),
            P("row"),
            P("row"),
        ),
        check_vma=False,
    )
```

profile of v0, /device:TPU:0, one launch (start us, length us, event | category | flops | bytes accessed | tf_op | source)
XLA Modules:
  0.0 1733.7 jit_solution(12513818273407900545)
XLA Ops:
  24.2 9.1 all_gather.103
  36.5 8.7 all_gather.112
  56.4 65.9 %reduce-scatter.29.cloned.1.call-done = f32[512,576]{0,1:T(8,128)} async-done(((f32[2048,576]{0,1:T(8,128)}), f32[512,576]{0,1:T(8,128)}) %reduce-scatter.29.cloned.1.call-update) | async-done | bytes 1179664 | tf_op jit(solution)/shard_map/reduce_scatter | solution.py:51
  124.9 28.4 %all_gather.105 = bf16[2048,192]{0,1:T(8,128)(2,1)S(1)} all-gather(bf16[512,192]{0,1:T(8,128)(2,1)S(1)} %slice.241), channel_id=1, replica_groups=mesh['dp'=2,'row'=4,'col'=4] {'row'}, dimensions={0}, use_global_device_ids=true | all-gather | bytes 983040 | tf_op jit(solution)/shard_map/all_gather | solution.py:206
  154.8 64.6 %reduce-scatter.37.cloned.1.call-done = f32[512,576]{0,1:T(8,128)} async-done(((f32[2048,576]{0,1:T(8,128)}), f32[512,576]{0,1:T(8,128)}) %reduce-scatter.37.cloned.1.call-update) | async-done | bytes 1179664 | tf_op jit(solution)/shard_map/reduce_scatter | solution.py:51
  226.7 20.1 %all_gather.104 = bf16[2048,192]{0,1:T(8,128)(2,1)} all-gather(bf16[512,192]{0,1:T(8,128)(2,1)S(1)} %convert_element_type.287), channel_id=1, replica_groups=mesh['dp'=2,'row'=4,'col'=4] {'row'}, dimensions={0}, use_global_device_ids=true | all-gather | bytes 983040 | tf_op jit(solution)/shard_map/all_gather | solution.py:205
  246.8 17.5 %all_gather.113 = bf16[2048,192]{0,1:T(8,128)(2,1)S(1)} all-gather(bf16[512,192]{0,1:T(8,128)(2,1)S(1)} %convert_element_type.300), channel_id=1, replica_groups=mesh['dp'=2,'row'=4,'col'=4] {'row'}, dimensions={0}, use_global_device_ids=true | all-gather | bytes 983040 | tf_op jit(solution)/shard_map/all_gather | solution.py:205
  265.2 17.3 %all_gather.114 = bf16[2048,192]{0,1:T(8,128)(2,1)} all-gather(bf16[512,192]{0,1:T(8,128)(2,1)S(1)} %slice.240), channel_id=1, replica_groups=mesh['dp'=2,'row'=4,'col'=4] {'row'}, dimensions={0}, use_global_device_ids=true | all-gather | bytes 983040 | tf_op jit(solution)/shard_map/all_gather | solution.py:206
  285.2 15.3 while.56
  300.6 16.9 all_gather.106
  323.2 15.5 while.57
  339.3 15.8 all_gather.115
  365.4 17.0 reduce-scatter.39.cloned.1.call-done
  384.3 12.6 all-reduce.4
  410.9 109.0 %reduce-scatter.33.cloned.1.call-done = f32[512,768]{1,0:T(8,128)} async-done(((f32[2048,768]{1,0:T(8,128)}), f32[512,768]{1,0:T(8,128)}) %reduce-scatter.33.cloned.1.call-update) | async-done | bytes 1572880 | tf_op jit(solution)/shard_map/reduce_scatter | solution.py:51
  525.5 7.9 all_gather.111
  533.4 56.2 %all-gather.7.cloned.1.call-done = bf16[2048,768]{1,0:T(8,128)(2,1)} async-done(((bf16[512,768]{1,0:T(8,128)(2,1)}), bf16[2048,768]{1,0:T(8,128)(2,1)}) %all-gather.7.cloned.1.call-update) | async-done | bytes 3145744 | tf_op jit(solution)/shard_map/all_gather | solution.py:47
  594.3 21.3 %reduce-scatter.35.cloned.1.call-done = bf16[512,192]{0,1:T(8,128)(2,1)} async-done(((bf16[2048,192]{0,1:T(8,128)(2,1)}), bf16[512,192]{0,1:T(8,128)(2,1)}) %reduce-scatter.35.cloned.1.call-update) | async-done | bytes 196624 | tf_op jit(solution)/shard_map/reduce_scatter | solution.py:55
  618.4 8.2 all_gather.116
  631.2 111.2 %reduce-scatter.41.cloned.1.call-done = f32[512,768]{1,0:T(8,128)} async-done(((f32[2048,768]{1,0:T(8,128)}), f32[512,768]{1,0:T(8,128)}) %reduce-scatter.41.cloned.1.call-update) | async-done | bytes 1572880 | tf_op jit(solution)/shard_map/reduce_scatter | solution.py:51
  748.2 64.0 %all-gather.9.cloned.1.call-done = bf16[2048,768]{1,0:T(8,128)(2,1)} async-done(((bf16[512,768]{1,0:T(8,128)(2,1)}), bf16[2048,768]{1,0:T(8,128)(2,1)}) %all-gather.9.cloned.1.call-update) | async-done | bytes 3145744 | tf_op jit(solution)/shard_map/all_gather | solution.py:47
  818.1 20.1 %reduce-scatter.43.cloned.1.call-done = bf16[512,192]{0,1:T(8,128)(2,1)} async-done(((bf16[2048,192]{0,1:T(8,128)(2,1)}), bf16[512,192]{0,1:T(8,128)(2,1)}) %reduce-scatter.43.cloned.1.call-update) | async-done | bytes 196624 | tf_op jit(solution)/shard_map/reduce_scatter | solution.py:55
  840.8 12.5 all-reduce.3
  857.0 9.2 all-reduce.2
  883.7 8.9 all_gather.118
  898.3 96.0 %reduce-scatter.57.cloned.1.call-done = f32[512,768]{1,0:T(8,128)} async-done(((f32[2048,768]{1,0:T(8,128)}), f32[512,768]{1,0:T(8,128)}) %reduce-scatter.57.cloned.1.call-update) | async-done | bytes 1572880 | tf_op jit(solution)/shard_map/reduce_scatter | solution.py:51
  998.2 109.5 %reduce-scatter.45.cloned.1.call-done = f32[512,768]{1,0:T(8,128)} async-done(((f32[2048,768]{1,0:T(8,128)}), f32[512,768]{1,0:T(8,128)}) %reduce-scatter.45.cloned.1.call-update) | async-done | bytes 1572880 | tf_op jit(solution)/shard_map/reduce_scatter | solution.py:51
  1111.7 62.2 %all-gather.15.cloned.1.call-done = bf16[2048,768]{1,0:T(8,128)(2,1)} async-done(((bf16[512,768]{1,0:T(8,128)(2,1)}), bf16[2048,768]{1,0:T(8,128)(2,1)}) %all-gather.15.cloned.1.call-update) | async-done | bytes 3145744 | tf_op jit(solution)/shard_map/all_gather | solution.py:47
  1177.9 59.6 %all-gather.11.cloned.1.call-done = bf16[2048,768]{1,0:T(8,128)(2,1)} async-done(((bf16[512,768]{1,0:T(8,128)(2,1)}), bf16[2048,768]{1,0:T(8,128)(2,1)}) %all-gather.11.cloned.1.call-update) | async-done | bytes 3145744 | tf_op jit(solution)/shard_map/all_gather | solution.py:47
  1241.5 20.8 %reduce-scatter.59.cloned.1.call-done = bf16[512,192]{0,1:T(8,128)(2,1)} async-done(((bf16[2048,192]{0,1:T(8,128)(2,1)}), bf16[512,192]{0,1:T(8,128)(2,1)}) %reduce-scatter.59.cloned.1.call-update) | async-done | bytes 196624 | tf_op jit(solution)/shard_map/reduce_scatter | solution.py:55
  1262.4 25.9 %reduce-scatter.47.cloned.1.call-done = bf16[512,192]{0,1:T(8,128)(2,1)} async-done(((bf16[2048,192]{0,1:T(8,128)(2,1)}), bf16[512,192]{0,1:T(8,128)(2,1)}) %reduce-scatter.47.cloned.1.call-update) | async-done | bytes 196624 | tf_op jit(solution)/shard_map/reduce_scatter | solution.py:55
  1291.8 12.5 all-reduce.1
  1319.5 8.9 all_gather.120
  1332.0 21.0 %reduce-scatter.61.cloned.1.call-done = f32[512,192]{0,1:T(8,128)} async-done(((f32[2048,192]{0,1:T(8,128)}), f32[512,192]{0,1:T(8,128)}) %reduce-scatter.61.cloned.1.call-update) | async-done | bytes 393232 | tf_op jit(solution)/shard_map/reduce_scatter | solution.py:51
  1359.4 30.5 %while.59 = (s32[]{:T(128)}, f32[3,512,64]{1,2,0:T(8,128)}, bf16[3,2048,64]{1,2,0:T(8,128)(2,1)}, bf16[3,2048,64]{1,2,0:T(8,128)(2,1)}, bf16[3,512,64]{2,1,0:T(8...) while((s32[]{:T(128)}, f32[3,512,64]{1,2,0:T(8,128)}, ...), condition=%wide.region_62.63_spmd.clone, body=%wide.region_60.62_spmd.clone.sunk | while | flops 680691200 | bytes 48123144 | solution.py:141
  1393.1 25.2 %while.58 = (s32[]{:T(128)}, f32[3,512,64]{1,2,0:T(8,128)}, bf16[3,2048,64]{1,2,0:T(8,128)(2,1)}, bf16[3,2048,64]{1,2,0:T(8,128)(2,1)S(1)}, bf16[3,512,64]{2,1,0...) while((s32[]{:T(128)}, f32[3,512,64]{1,2,0:T(8,128)}, ...), condition=%wide.region_45.46_spmd.clone, body=%wide.region_43.45_spmd.clone.sunk | while | flops 680691200 | bytes 41045172 | solution.py:141
  1421.7 19.2 %reduce-scatter.51.cloned.1.call-done = bf16[512,192]{0,1:T(8,128)(2,1)} async-done(((bf16[2048,192]{0,1:T(8,128)(2,1)}), bf16[512,192]{0,1:T(8,128)(2,1)}) %reduce-scatter.51.cloned.1.call-update) | async-done | bytes 196624 | tf_op jit(solution)/shard_map/reduce_scatter | solution.py:268
  1446.2 19.6 %reduce-scatter.53.cloned.1.call-done = bf16[512,192]{0,1:T(8,128)(2,1)} async-done(((bf16[2048,192]{0,1:T(8,128)(2,1)}), bf16[512,192]{0,1:T(8,128)(2,1)}) %reduce-scatter.53.cloned.1.call-update) | async-done | bytes 196624 | tf_op jit(solution)/shard_map/reduce_scatter | solution.py:274
  1469.0 21.7 %reduce-scatter.65.cloned.1.call-done = bf16[512,192]{0,1:T(8,128)(2,1)} async-done(((bf16[2048,192]{0,1:T(8,128)(2,1)}), bf16[512,192]{0,1:T(8,128)(2,1)}) %reduce-scatter.65.cloned.1.call-update) | async-done | bytes 196624 | tf_op jit(solution)/shard_map/reduce_scatter | solution.py:274
  1505.0 37.6 %all-gather.13.cloned.1.call-done = bf16[2048,576]{0,1:T(8,128)(2,1)} async-done(((bf16[512,576]{0,1:T(8,128)(2,1)}), bf16[2048,576]{0,1:T(8,128)(2,1)}) %all-gather.13.cloned.1.call-update) | async-done | bytes 2359312 | tf_op jit(solution)/shard_map/all_gather | solution.py:47
  1545.3 48.1 %all-gather.17.cloned.1.call-done = bf16[2048,576]{0,1:T(8,128)(2,1)} async-done(((bf16[512,576]{0,1:T(8,128)(2,1)}), bf16[2048,576]{0,1:T(8,128)(2,1)}) %all-gather.17.cloned.1.call-update) | async-done | bytes 2359312 | tf_op jit(solution)/shard_map/all_gather | solution.py:47
  1609.4 13.0 reduce-scatter.77.cloned.1.call-done
  1624.1 13.3 all-reduce
  1638.8 8.6 reduce-scatter.69.cloned.1.call-done
  1648.9 10.9 reduce-scatter.71.cloned.1.call-done
  1661.2 10.7 reduce-scatter.73.cloned.1.call-done
  1673.4 25.1 %reduce-scatter.55.cloned.1.call-done = bf16[512,192]{0,1:T(8,128)(2,1)} async-done(((bf16[2048,192]{0,1:T(8,128)(2,1)}), bf16[512,192]{0,1:T(8,128)(2,1)}) %reduce-scatter.55.cloned.1.call-update) | async-done | bytes 196624 | tf_op jit(solution)/shard_map/reduce_scatter | solution.py:55
  1698.5 25.9 %reduce-scatter.67.cloned.1.call-done = bf16[512,192]{0,1:T(8,128)(2,1)} async-done(((bf16[2048,192]{0,1:T(8,128)(2,1)}), bf16[512,192]{0,1:T(8,128)(2,1)}) %reduce-scatter.67.cloned.1.call-update) | async-done | bytes 196624 | tf_op jit(solution)/shard_map/reduce_scatter | solution.py:55
  (487 shorter events, 325.0 us)
Async XLA Ops:
  7.2 115.0 %reduce-scatter.29.cloned.1.call-start = ((), (), s32[]{:S(2)}) async-start(), calls=%async_computation.26 | async-start | bytes 5898240 | tf_op jit(solution)/shard_map/reduce_scatter | solution.py:51
  36.5 183.0 %reduce-scatter.37.cloned.1.call-start = ((), (), s32[]{:S(2)}) async-start(), calls=%async_computation.31 | async-start | bytes 5898240 | tf_op jit(solution)/shard_map/reduce_scatter | solution.py:51
  48.4 317.0 %reduce-scatter.31.cloned.1.call-start = ((), (), s32[]{:S(2)}) async-start(), calls=%async_computation.27 | async-start | bytes 983040 | tf_op jit(solution)/shard_map/reduce_scatter | solution.py:55
  48.5 75.4 %copy-start.49 = (bf16[3,512,64]{1,2,0:T(8,128)(2,1)}, bf16[3,512,64]{1,2,0:T(8,128)(2,1)S(1)}, u32[]{:S(2)}) copy-start(bf16[3,512,64]{1,2,0:T(8,128)(2,1)S(1)} %fusion.145) | copy-start | bytes 589828
  56.4 164.7 %copy-start.55 = (f32[512,32]{0,1:T(8,128)}, f32[512,32]{0,1:T(8,128)S(1)}, u32[]{:S(2)}) copy-start(f32[512,32]{0,1:T(8,128)S(1)} %get-tuple-element.541) | copy-start | bytes 196612
  320.6 61.9 %reduce-scatter.39.cloned.1.call-start = ((), (), s32[]{:S(2)}) async-start(), calls=%async_computation.32 | async-start | bytes 983040 | tf_op jit(solution)/shard_map/reduce_scatter | solution.py:55
  356.0 41.6 %copy-start.77 = (f32[192]{0:T(256)S(1)}, f32[192]{0:T(256)}, u32[]{:S(2)}) copy-start(f32[192]{0:T(256)} %param.29) | copy-start | bytes 2308
  358.3 161.6 %reduce-scatter.33.cloned.1.call-start = ((), (), s32[]{:S(2)}) async-start(), calls=%async_computation.28 | async-start | bytes 7864320 | tf_op jit(solution)/shard_map/reduce_scatter | solution.py:51
  410.8 178.8 %all-gather.7.cloned.1.call-start = ((), (), s32[]{:S(2)}) async-start(), calls=%async_computation.29 | async-start | bytes 3932160 | tf_op jit(solution)/shard_map/all_gather | solution.py:47
  525.4 90.2 %reduce-scatter.35.cloned.1.call-start = ((), (), s32[]{:S(2)}) async-start(), calls=%async_computation.30 | async-start | bytes 983040 | tf_op jit(solution)/shard_map/reduce_scatter | solution.py:55
  593.6 148.9 %reduce-scatter.41.cloned.1.call-start = ((), (), s32[]{:S(2)}) async-start(), calls=%async_computation.33 | async-start | bytes 7864320 | tf_op jit(solution)/shard_map/reduce_scatter | solution.py:51
  631.2 181.0 %all-gather.9.cloned.1.call-start = ((), (), s32[]{:S(2)}) async-start(), calls=%async_computation.34 | async-start | bytes 3932160 | tf_op jit(solution)/shard_map/all_gather | solution.py:47
  748.0 90.2 %reduce-scatter.43.cloned.1.call-start = ((), (), s32[]{:S(2)}) async-start(), calls=%async_computation.35 | async-start | bytes 983040 | tf_op jit(solution)/shard_map/reduce_scatter | solution.py:55
  816.1 178.1 %reduce-scatter.57.cloned.1.call-start = ((), (), s32[]{:S(2)}) async-start(), calls=%async_computation.44 | async-start | bytes 7864320 | tf_op jit(solution)/shard_map/reduce_scatter | solution.py:51
  883.7 224.0 %reduce-scatter.45.cloned.1.call-start = ((), (), s32[]{:S(2)}) async-start(), calls=%async_computation.36 | async-start | bytes 7864320 | tf_op jit(solution)/shard_map/reduce_scatter | solution.py:51
  898.2 275.7 %all-gather.15.cloned.1.call-start = ((), (), s32[]{:S(2)}) async-start(), calls=%async_computation.45 | async-start | bytes 3932160 | tf_op jit(solution)/shard_map/all_gather | solution.py:47
  998.1 239.4 %all-gather.11.cloned.1.call-start = ((), (), s32[]{:S(2)}) async-start(), calls=%async_computation.37 | async-start | bytes 3932160 | tf_op jit(solution)/shard_map/all_gather | solution.py:47
  1111.6 150.7 %reduce-scatter.59.cloned.1.call-start = ((), (), s32[]{:S(2)}) async-start(), calls=%async_computation.46 | async-start | bytes 983040 | tf_op jit(solution)/shard_map/reduce_scatter | solution.py:55
  1177.9 110.3 %reduce-scatter.47.cloned.1.call-start = ((), (), s32[]{:S(2)}) async-start(), calls=%async_computation.38 | async-start | bytes 983040 | tf_op jit(solution)/shard_map/reduce_scatter | solution.py:55
  1241.5 111.6 %reduce-scatter.61.cloned.1.call-start = ((), (), s32[]{:S(2)}) async-start(), calls=%async_computation.47 | async-start | bytes 1966080 | tf_op jit(solution)/shard_map/reduce_scatter | solution.py:51
  1319.4 70.5 %reduce-scatter.49.cloned.1.call-start = ((), (), s32[]{:S(2)}) async-start(), calls=%async_computation.39 | async-start | bytes 1966080 | tf_op jit(solution)/shard_map/reduce_scatter | solution.py:51
  1331.8 88.8 %reduce-scatter.63.cloned.1.call-start = ((), (), s32[]{:S(2)}) async-start(), calls=%async_computation.48 | async-start | bytes 983040 | tf_op jit(solution)/shard_map/reduce_scatter | solution.py:268
  1389.9 51.0 %reduce-scatter.51.cloned.1.call-start = ((), (), s32[]{:S(2)}) async-start(), calls=%async_computation.40 | async-start | bytes 983040 | tf_op jit(solution)/shard_map/reduce_scatter | solution.py:268
  1418.3 47.5 %reduce-scatter.53.cloned.1.call-start = ((), (), s32[]{:S(2)}) async-start(), calls=%async_computation.41 | async-start | bytes 983040 | tf_op jit(solution)/shard_map/reduce_scatter | solution.py:274
  1419.2 71.5 %reduce-scatter.65.cloned.1.call-start = ((), (), s32[]{:S(2)}) async-start(), calls=%async_computation.49 | async-start | bytes 983040 | tf_op jit(solution)/shard_map/reduce_scatter | solution.py:274
  1420.0 122.6 %all-gather.13.cloned.1.call-start = ((), (), s32[]{:S(2)}) async-start(), calls=%async_computation.42 | async-start | bytes 2949120 | tf_op jit(solution)/shard_map/all_gather | solution.py:47
  1467.6 125.7 %all-gather.17.cloned.1.call-start = ((), (), s32[]{:S(2)}) async-start(), calls=%async_computation.50 | async-start | bytes 2949120 | tf_op jit(solution)/shard_map/all_gather | solution.py:47
  1492.6 115.0 %reduce-scatter.79.cloned.1.call-start = ((), (), s32[]{:S(2)}) async-start(), calls=%async_computation.57 | async-start | bytes 589824
  1497.4 125.0 %reduce-scatter.77.cloned.1.call-start = ((), (), s32[]{:S(2)}) async-start(), calls=%async_computation.56 | async-start | bytes 442368 | tf_op jit(solution)/shard_map/reduce_scatter | solution.py:305
  1502.5 134.9 %reduce-scatter.75.cloned.1.call-start = ((), (), s32[]{:S(2)}) async-start(), calls=%async_computation.55 | async-start | bytes 147456 | tf_op jit(solution)/shard_map/reduce_scatter | solution.py:302
  1504.9 88.5 %copy-start.30 = (bf16[2048,192]{0,1:T(8,128)(2,1)S(1)}, bf16[2048,192]{0,1:T(8,128)(2,1)}, u32[]{:S(2)}) copy-start(bf16[2048,192]{0,1:T(8,128)(2,1)} %copy-done.29) | copy-start | bytes 2359300
  1504.9 142.6 %reduce-scatter.69.cloned.1.call-start = ((), (), s32[]{:S(2)}) async-start(), calls=%async_computation.52 | async-start | bytes 147456 | tf_op jit(solution)/shard_map/reduce_scatter | solution.py:290
  1545.2 53.0 %copy-start.42 = (bf16[192,192]{1,0:T(8,128)(2,1)S(1)}, bf16[192,192]{1,0:T(8,128)(2,1)}, u32[]{:S(2)}) copy-start(bf16[192,192]{1,0:T(8,128)(2,1)} %copy-done.41) | copy-start | bytes 221188
  1545.3 53.0 %copy-start.44 = (bf16[192,192]{1,0:T(8,128)(2,1)S(1)}, bf16[192,192]{1,0:T(8,128)(2,1)}, u32[]{:S(2)}) copy-start(bf16[192,192]{1,0:T(8,128)(2,1)} %copy-done.43) | copy-start | bytes 221188
  1545.3 53.0 %copy-start.46 = (bf16[192,192]{1,0:T(8,128)(2,1)S(1)}, bf16[192,192]{1,0:T(8,128)(2,1)}, u32[]{:S(2)}) copy-start(bf16[192,192]{1,0:T(8,128)(2,1)} %copy-done.45) | copy-start | bytes 221188
  1596.9 62.9 %reduce-scatter.71.cloned.1.call-start = ((), (), s32[]{:S(2)}) async-start(), calls=%async_computation.53 | async-start | bytes 147456 | tf_op jit(solution)/shard_map/reduce_scatter | solution.py:293
  1597.6 74.3 %reduce-scatter.73.cloned.1.call-start = ((), (), s32[]{:S(2)}) async-start(), calls=%async_computation.54 | async-start | bytes 147456 | tf_op jit(solution)/shard_map/reduce_scatter | solution.py:299
  1598.2 100.3 %reduce-scatter.55.cloned.1.call-start = ((), (), s32[]{:S(2)}) async-start(), calls=%async_computation.43 | async-start | bytes 983040 | tf_op jit(solution)/shard_map/reduce_scatter | solution.py:55
  1601.9 122.5 %reduce-scatter.67.cloned.1.call-start = ((), (), s32[]{:S(2)}) async-start(), calls=%async_computation.51 | async-start | bytes 983040 | tf_op jit(solution)/shard_map/reduce_scatter | solution.py:55
  1603.7 120.6 %copy-start.20 = (bf16[512,192]{0,1:T(8,128)(2,1)S(1)}, bf16[512,192]{0,1:T(8,128)(2,1)}, u32[]{:S(2)}) copy-start(bf16[512,192]{0,1:T(8,128)(2,1)} %reduce-scatter.31.cloned.1.call-done) | copy-start | bytes 589828
  1603.7 120.6 %copy-start.21 = (bf16[512,192]{0,1:T(8,128)(2,1)S(1)}, bf16[512,192]{0,1:T(8,128)(2,1)}, u32[]{:S(2)}) copy-start(bf16[512,192]{0,1:T(8,128)(2,1)} %reduce-scatter.39.cloned.1.call-done) | copy-start | bytes 589828
  1603.7 120.6 %copy-start.23 = (f32[512,192]{0,1:T(8,128)S(1)}, f32[512,192]{0,1:T(8,128)}, u32[]{:S(2)}) copy-start(f32[512,192]{0,1:T(8,128)} %get-tuple-element.473) | copy-start | bytes 1179652
  1603.7 120.6 %copy-start.24 = (f32[512,192]{0,1:T(8,128)S(1)}, f32[512,192]{0,1:T(8,128)}, u32[]{:S(2)}) copy-start(f32[512,192]{0,1:T(8,128)} %get-tuple-element.474) | copy-start | bytes 1179652
  1603.7 120.6 %copy-start.60 = (f32[192]{0:T(256)S(1)}, f32[192]{0:T(256)}, u32[]{:S(2)}) copy-start(f32[192]{0:T(256)} %param.28) | copy-start | bytes 2308
  1603.8 120.6 %copy-start.66 = (f32[512]{0:T(512)S(1)}, f32[512]{0:T(512)}, u32[]{:S(2)}) copy-start(f32[512]{0:T(512)} %copy-done.65) | copy-start | bytes 6148
  1603.8 120.6 %copy-start.68 = (f32[512]{0:T(512)S(1)}, f32[512]{0:T(512)}, u32[]{:S(2)}) copy-start(f32[512]{0:T(512)} %copy-done.67) | copy-start | bytes 6148
  1603.8 120.6 %copy-start.70 = (f32[512]{0:T(512)S(1)}, f32[512]{0:T(512)}, u32[]{:S(2)}) copy-start(f32[512]{0:T(512)} %copy-done.69) | copy-start | bytes 6148
  1603.8 120.6 %copy-start.72 = (f32[512]{0:T(512)S(1)}, f32[512]{0:T(512)}, u32[]{:S(2)}) copy-start(f32[512]{0:T(512)} %copy-done.71) | copy-start | bytes 6148
  (85 other events, 536.3 us)
Sparse Core Ops, SparseCore 0:
  36.6 85.5 reduce-scatter.28
  124.5 94.8 reduce-scatter.36
  320.7 23.9 reduce-scatter.30
  358.4 24.0 reduce-scatter.38
  410.9 108.9 reduce-scatter.32
  525.5 64.0 all-gather.6
  593.7 21.8 reduce-scatter.34
  631.3 111.1 reduce-scatter.40
  748.1 64.0 all-gather.8
  816.3 21.9 reduce-scatter.42
  883.8 110.3 reduce-scatter.56
  996.4 111.2 reduce-scatter.44
  1109.8 64.0 all-gather.14
  1175.3 62.1 all-gather.10
  1240.4 21.8 reduce-scatter.58
  1264.9 23.2 reduce-scatter.46
  1319.5 33.4 reduce-scatter.60
  1355.2 34.2 reduce-scatter.48
  1391.8 22.3 reduce-scatter.62
  1418.4 22.3 reduce-scatter.50
  1443.2 22.6 reduce-scatter.52
  1468.1 22.5 reduce-scatter.64
  1492.9 49.6 all-gather.12
  1544.0 49.3 all-gather.16
  1595.6 11.9 reduce-scatter.78
  1610.3 12.0 reduce-scatter.76
  1624.6 9.9 reduce-scatter.74
  1637.4 9.9 reduce-scatter.68
  1649.7 9.9 reduce-scatter.70
  1661.9 9.9 reduce-scatter.72
  1675.2 23.2 reduce-scatter.54
  1701.0 23.2 reduce-scatter.66
where the time goes:
time: 1740 us; the launch traced here: 1730 us
  waiting for transfers between devices  1170 us (67%)
  blocking collectives  279 us (16%)
  matrix products  123 us (7%)
  other arithmetic  93 us (5%)
  local copies, waits for them, and re-layouts  54.1 us (3%)
    reduce_scatter x8, waiting for transfers between devices, reduce_rows(): return lax.psum_scatter(values, 'row', scatter_dimension=0, tiled=True)  577 us
    all_gather x6, waiting for transfers between devices, along_row(): return lax.all_gather(values, 'row', axis=0, tiled=True)  328 us
    reduce_scatter x8, waiting for transfers between devices, reduce_cols(): lax.psum_scatter(values.astype(jnp.bfloat16), 'col', scatter_dimension=0,...  156 us
    all_gather x8, blocking collectives, along_col(): return lax.all_gather(values, 'col', axis=0, tiled=True)  66.8 us
    dot_general x26, matrix products, times_transpose(): lax.dot_general(left, right, (((1,), (1,)), ((), ())), preferred_element_...  52.4 us
    psum x4, blocking collectives, feature_totals(): return lax.psum((first_sum, second_sum), 'row')  46.8 us
    all_gather x2, blocking collectives, local(): lax.all_gather(value_low, 'row', axis=0, tiled=True)  45.7 us
    reduce_scatter x2, waiting for transfers between devices, local(): lax.psum_scatter(merge_heads(grad_v_heads).astype(jnp.bfloat16), 'row', s...  41.3 us
  transfers between devices with their start and end apart: 32, of which 28 were waited for; matrix products, arithmetic and copies ran while one was open for 9% of the time, Pallas kernels for 0%

commit v1 on v0

v1 whole, which is shorter than its diff:
```python
import jax
import jax.numpy as jnp
from jax import lax
from jax.sharding import Mesh, PartitionSpec as P

HD = 64
norm_eps = 1e-05
masked_score = -1e30
EVERY = ("dp", "rm", "rz", "cy", "cc")
ROW = ("rm", "rz")
SQUARE = ("rz", "cy")
bf16 = jnp.bfloat16
f32 = jnp.float32


def swap_by(blocks, index):
    pairs = blocks.reshape((2, 2) + blocks.shape[1:])
    high = (index // 2) == 1
    low = (index % 2) == 1
    pairs = jnp.where(high, pairs[::-1], pairs)
    pairs = jnp.where(low, pairs[:, ::-1], pairs)
    return pairs.reshape(blocks.shape)


def exchange4(blocks, axes):
    parts = [blocks[0]]
    for step in range(1, 4):
        parts.append(lax.ppermute(blocks[step], axes, [(i, i ^ step) for i in range(4)]))
    return parts


def gather4(block, axes):
    parts = [block]
    for step in range(1, 4):
        parts.append(lax.ppermute(block, axes, [(i, i ^ step) for i in range(4)]))
    return parts


def core_swap(value):
    return lax.ppermute(value, "cc", [(0, 1), (1, 0)])


def dp_gather(value):
    if lax.axis_size("dp") != 2:
        return lax.all_gather(value, "dp", axis=0, tiled=True)
    other = lax.ppermute(value, "dp", [(0, 1), (1, 0)])
    mine_first = lax.axis_index("dp") == 0
    return jnp.concatenate(
        [jnp.where(mine_first, value, other), jnp.where(mine_first, other, value)], axis=0
    )


def dp_reduce(value):
    if lax.axis_size("dp") != 2:
        return lax.psum_scatter(value.astype(bf16), "dp", scatter_dimension=0, tiled=True).astype(f32)
    half = value.shape[0] // 2
    second = lax.axis_index("dp") == 1
    keep = jnp.where(second, value[half:], value[:half])
    send = jnp.where(second, value[:half], value[half:]).astype(bf16)
    return keep + lax.ppermute(send, "dp", [(0, 1), (1, 0)]).astype(f32)


def group_route(rounds, inverse):
    pairs = []
    for m in range(2):
        for z in range(2):
            for y in range(2):
                for c in range(2):
                    source = ((m * 2 + z) * 2 + y) * 2 + c
                    target = (((m ^ rounds[0]) * 2 + c) * 2 + y) * 2 + (z ^ rounds[1])
                    pairs.append((target, source) if inverse else (source, target))
    return pairs


GROUP = ("rm", "rz", "cy", "cc")


def rotate_rows(values, positions, direction):
    heads, size, count = values.shape
    half = size // 2
    frequency = 10000.0 ** (-2.0 * jnp.arange(half, dtype=f32) / size)
    angles = frequency[:, None] * positions.astype(f32)[None, :]
    cosine = jnp.cos(angles)[None]
    sine = direction * jnp.sin(angles)[None]
    paired = values.reshape(heads, half, 2, count)
    even = paired[:, :, 0]
    odd = paired[:, :, 1]
    turned = jnp.stack([even * cosine - odd * sine, even * sine + odd * cosine], axis=2)
    return turned.reshape(values.shape)


def dot(left, right, dims):
    return lax.dot_general(left, right, ((dims[0], dims[1]), ((), ())), preferred_element_type=f32)


def attend_forward(queries, keys, values, key_valid, scale):
    def one_head(items):
        q, k, v = items
        scores = dot(q, k, ((0,), (0,))) * scale
        scores = jnp.where(key_valid[None, :], scores, masked_score)
        top = jnp.max(scores, axis=1, keepdims=True)
        total = jnp.sum(jnp.exp(scores - top), axis=1, keepdims=True)
        log_total = top + jnp.log(total)
        probs = jnp.exp(scores - log_total).astype(bf16)
        return dot(v, probs, ((1,), (1,))), log_total[:, 0]

    return lax.map(one_head, (queries, keys, values))


def attend_backward(queries, keys, values, log_totals, grads, key_valid, scale):
    def one_head(items):
        q, k, v, log_total, g = items
        scores = dot(q, k, ((0,), (0,))) * scale
        scores = jnp.where(key_valid[None, :], scores, masked_score)
        probs = jnp.exp(scores - log_total[:, None])
        grad_probs = dot(g, v, ((0,), (0,)))
        delta = jnp.sum(probs * grad_probs, axis=1, keepdims=True)
        grad_scores = (probs * (grad_probs - delta)).astype(bf16)
        grad_q = dot(k, grad_scores, ((1,), (1,))) * scale
        grad_k = dot(q, grad_scores, ((1,), (0,))) * scale
        grad_v = dot(g, probs.astype(bf16), ((1,), (0,)))
        return grad_q, grad_k, grad_v

    return lax.map(one_head, (queries, keys, values, log_totals, grads))


def layer_norm(summed, gain, shift):
    width = summed.shape[0]
    mean = jnp.sum(summed, axis=0, keepdims=True) / width
    var = jnp.sum(summed * summed, axis=0, keepdims=True) / width - mean * mean
    inv = lax.rsqrt(var + norm_eps)
    centered = (summed - mean) * inv
    return centered * gain[:, None] + shift[:, None], centered, inv


def layer_norm_back(grad, centered, inv, gain):
    width = grad.shape[0]
    cent = grad * gain[:, None]
    first = jnp.sum(cent, axis=0, keepdims=True) / width
    second = jnp.sum(cent * centered, axis=0, keepdims=True) / width
    return inv * (cent - first - centered * second)


def gelu_exact(values):
    return jax.nn.gelu(values, approximate=False)


def local(
    tokens, w_query, w_key, w_value, w_output, w_inner, w_outer,
    first_gain, first_shift, second_gain, second_shift, seq_lengths, out_grad,
):
    feat = tokens.shape[1]
    cols = tokens.shape[2]
    half = cols // 2
    width = feat * 4
    head_width = w_query.shape[1]
    heads = head_width // HD
    inner_cols = w_inner.shape[1]
    dp_count = lax.axis_size("dp")
    shard_rows = w_query.shape[0]
    scale = HD ** (-0.5)
    row = lax.axis_index(ROW)
    square = lax.axis_index(SQUARE)
    group = lax.axis_index("dp")
    m = lax.axis_index("rm")
    z = lax.axis_index("rz")
    y = lax.axis_index("cy")
    c = lax.axis_index("cc")

    def to_tokens(array):
        blocks = array.reshape(2, feat, 2, half).transpose(0, 2, 1, 3).reshape(4, feat, half)
        return swap_by(jnp.stack(exchange4(swap_by(blocks, row), ROW)), row).reshape(width, half)

    def from_tokens(array):
        blocks = array.reshape(4, feat, half)
        back = swap_by(jnp.stack(exchange4(swap_by(blocks, row), ROW)), row)
        return back.reshape(2, 2, feat, half).transpose(0, 2, 1, 3).reshape(2, feat, cols)

    x_own = to_tokens(tokens)
    x_core = jnp.stack(gather4(x_own, SQUARE))
    x_blocks = jnp.concatenate([x_core, core_swap(x_core)], axis=0)

    qkv_rows = dp_gather(jnp.concatenate([w_query, w_key, w_value], axis=1))
    half_rows = feat // 2
    row_halves = qkv_rows.reshape(2, half_rows, 3 * head_width)
    pieces = []
    for r1 in range(2):
        for r2 in range(2):
            part = jnp.where((z ^ r2) == 0, row_halves[0], row_halves[1])
            pieces.append(lax.ppermute(part, GROUP, group_route((r1, r2), False)))
    mine = swap_by(jnp.stack(pieces), m * 2 + c)
    theirs = core_swap(mine)
    first_half = jnp.where(c == 0, mine, theirs)
    second_half = jnp.where(c == 0, theirs, mine)
    w_qkv = jnp.stack([first_half, second_half], axis=1).reshape(width, 3 * head_width)

    def whole(shard):
        return lax.all_gather(shard, EVERY)

    inner_all = (
        whole(w_inner).reshape(dp_count, 4, 4, shard_rows, inner_cols)
        .transpose(1, 0, 3, 2, 4).reshape(width, 4 * inner_cols)
    )
    outer_all = (
        whole(w_outer).reshape(dp_count, 4, 4, inner_cols // dp_count, feat)
        .transpose(2, 0, 3, 1, 4).reshape(4 * inner_cols, width)
    )
    output_all = (
        whole(w_output).reshape(dp_count, 4, 4, head_width // dp_count, feat)
        .transpose(2, 0, 3, 1, 4).reshape(width, width)
    )
    norms = jnp.stack([first_gain, first_shift, second_gain, second_shift])
    norms_all = swap_by(jnp.stack(gather4(norms, ROW)), row).transpose(1, 0, 2).reshape(4, width)
    gain_one, shift_one, gain_two, shift_two = norms_all

    length = lax.dynamic_index_in_dim(seq_lengths[m], group, keepdims=False)
    starts = []
    for kc in range(2):
        for k in range(4):
            starts.append(((y ^ (k % 2)) * 2 + (c ^ kc)) * cols + (z ^ (k // 2)) * half)
    positions = (jnp.stack(starts)[:, None] + jnp.arange(half, dtype=jnp.int32)[None, :]).reshape(-1)
    own_positions = positions[: 4 * half]
    key_valid = positions < length

    def heads_of(values):
        return values.reshape(heads, HD, -1)

    x_all = x_blocks.transpose(1, 0, 2).reshape(width, 8 * half)
    x_mine = x_all[:, : 4 * half]
    q_rot = rotate_rows(heads_of(dot(w_qkv[:, :head_width], x_mine, ((0,), (0,)))), own_positions, 1.0).astype(bf16)
    kv = dot(w_qkv[:, head_width:], x_all, ((0,), (0,)))
    k_rot = rotate_rows(heads_of(kv[:head_width]), positions, 1.0).astype(bf16)
    v_low = heads_of(kv[head_width:]).astype(bf16)
    head_outs, log_totals = attend_forward(q_rot, k_rot, v_low, key_valid, scale)

    def head_to_token(values):
        blocks = values.reshape(head_width, 4, half).transpose(1, 0, 2)
        back = swap_by(jnp.stack(exchange4(blocks, SQUARE)), square)
        return back.reshape(2, 2, head_width, half).transpose(1, 0, 2, 3).reshape(width, half)

    def token_to_head(values):
        blocks = values.reshape(2, 2, head_width, half).transpose(1, 0, 2, 3).reshape(4, head_width, half)
        back = jnp.stack(exchange4(swap_by(blocks, square), SQUARE))
        return back.transpose(1, 0, 2).reshape(head_width, 4 * half)

    attn_low = head_to_token(head_outs.astype(bf16).reshape(head_width, 4 * half))

    branch = dot(output_all, attn_low, ((0,), (0,)))
    hidden, cent_one, inv_one = layer_norm(x_own.astype(f32) + branch, gain_one, shift_one)
    hidden_low = hidden.astype(bf16)
    inner = dot(inner_all, hidden_low, ((0,), (0,)))
    act_low = gelu_exact(inner).astype(bf16)
    outer = dot(outer_all, act_low, ((0,), (0,)))
    result, cent_two, inv_two = layer_norm(hidden + outer, gain_two, shift_two)
    mixed = from_tokens(result.astype(bf16))

    own_start = (y * 2 + c) * cols + z * half
    own_valid = (own_start + jnp.arange(half, dtype=jnp.int32)) < length
    cot = to_tokens(out_grad).astype(f32) * own_valid[None, :].astype(f32)
    d_gain_two = jnp.sum(cot * cent_two, axis=1)
    d_shift_two = jnp.sum(cot, axis=1)
    grad_two = layer_norm_back(cot, cent_two, inv_two, gain_two)
    outer_low = grad_two.astype(bf16)
    grad_act = dot(outer_all, outer_low, ((1,), (0,)))
    d_outer = dot(act_low, outer_low, ((1,), (1,)))
    inner_low = jax.vjp(gelu_exact, inner)[1](grad_act)[0].astype(bf16)
    grad_hidden = grad_two + dot(inner_all, inner_low, ((1,), (0,)))
    d_inner = dot(hidden_low, inner_low, ((1,), (1,)))
    d_gain_one = jnp.sum(grad_hidden * cent_one, axis=1)
    d_shift_one = jnp.sum(grad_hidden, axis=1)
    grad_one = layer_norm_back(grad_hidden, cent_one, inv_one, gain_one)
    branch_low = grad_one.astype(bf16)
    grad_attn = dot(output_all, branch_low, ((1,), (0,))).astype(bf16)
    d_output = dot(attn_low, branch_low, ((1,), (1,)))

    def spread(value):
        return lax.psum_scatter(value.astype(bf16), EVERY, scatter_dimension=0)

    d_inner_blocks = (
        d_inner.astype(bf16).reshape(4, dp_count, shard_rows, 4, inner_cols).transpose(1, 0, 3, 2, 4)
        .reshape(-1, shard_rows, inner_cols)
    )
    d_outer_blocks = (
        d_outer.astype(bf16).reshape(4, dp_count, inner_cols // dp_count, 4, feat).transpose(1, 3, 0, 2, 4)
        .reshape(-1, inner_cols // dp_count, feat)
    )
    d_output_blocks = (
        d_output.astype(bf16).reshape(4, dp_count, head_width // dp_count, 4, feat).transpose(1, 3, 0, 2, 4)
        .reshape(-1, head_width // dp_count, feat)
    )
    norm_sums = jnp.stack([d_gain_one, d_shift_one, d_gain_two, d_shift_two]).astype(bf16)
    norm_blocks = norm_sums.reshape(4, 4, feat).transpose(1, 0, 2)
    norm_blocks = jnp.broadcast_to(norm_blocks[None, :, None], (dp_count, 4, 4, 4, feat)).reshape(-1, 4, feat)
    out_and_norms = spread(jnp.concatenate([d_output_blocks, norm_blocks], axis=1))
    g_output = out_and_norms[: head_width // dp_count].astype(f32)
    g_norms = out_and_norms[head_width // dp_count :].astype(f32)
    g_inner = spread(d_inner_blocks).astype(f32)
    g_outer = spread(d_outer_blocks).astype(f32)

    grad_heads = heads_of(token_to_head(grad_attn))
    dq, dk, dv = attend_backward(q_rot, k_rot, v_low, log_totals, grad_heads, key_valid, scale)
    dkv = jnp.concatenate([dk.reshape(head_width, -1), dv.reshape(head_width, -1)], axis=0)
    kept = dkv[:, : 4 * half] + core_swap(dkv[:, 4 * half :].astype(bf16)).astype(f32)
    dq_low = rotate_rows(dq, own_positions, -1.0).astype(bf16).reshape(head_width, -1)
    dk_low = rotate_rows(heads_of(kept[:head_width]), own_positions, -1.0).astype(bf16).reshape(head_width, -1)
    dv_low = kept[head_width:].astype(bf16)
    d_proj = jnp.concatenate([dq_low, dk_low, dv_low], axis=0)

    dx = dot(w_qkv, d_proj, ((1,), (0,))).astype(bf16)
    dx_blocks = exchange4(dx.reshape(width, 4, half).transpose(1, 0, 2), SQUARE)
    d_x = grad_one
    for part in dx_blocks:
        d_x = d_x + part.astype(f32)
    d_input = from_tokens(d_x.astype(bf16)).astype(f32)

    d_qkv = dot(x_mine, d_proj, ((1,), (1,)))
    d_halves = d_qkv.reshape(4, 2, half_rows, 3 * head_width)
    keep = jnp.where(c == 0, d_halves[:, 0], d_halves[:, 1])
    give = jnp.where(c == 0, d_halves[:, 1], d_halves[:, 0]).astype(bf16)
    summed = (keep + core_swap(give).astype(f32)).astype(bf16)
    by_round = swap_by(summed, m * 2 + c)
    got = []
    for r1 in range(2):
        for r2 in range(2):
            got.append(lax.ppermute(by_round[r1 * 2 + r2], GROUP, group_route((r1, r2), True)))
    lower = got[0].astype(f32) + got[2].astype(f32)
    upper = got[1].astype(f32) + got[3].astype(f32)
    low_rows = jnp.where(z == 0, lower, upper)
    high_rows = jnp.where(z == 0, upper, lower)
    g_qkv = dp_reduce(jnp.concatenate([low_rows, high_rows], axis=0))

    return (
        mixed, d_input,
        g_qkv[:, :head_width], g_qkv[:, head_width : 2 * head_width], g_qkv[:, 2 * head_width :],
        g_output, g_inner, g_outer,
        g_norms[0], g_norms[1], g_norms[2], g_norms[3],
    )


def solution(mesh):
    shape = mesh.devices.shape
    fine = Mesh(mesh.devices.reshape(shape[0], 2, shape[1] // 2, 2, shape[2] // 2), EVERY)
    col = ("cy", "cc")
    acts = P(None, ROW, ("dp",) + col)
    by_row = P(ROW + ("dp",), col)
    by_col = P(col + ("dp",), ROW)
    vec = P(ROW)
    return jax.shard_map(
        local,
        mesh=fine,
        in_specs=(
            acts, by_row, by_row, by_row, by_col, by_row, by_col, vec, vec, vec, vec, P(), acts,
        ),
        out_specs=(
            acts, acts, by_row, by_row, by_row, by_col, by_row, by_col, vec, vec, vec, vec,
        ),
        check_vma=False,
    )
```

time: 1740 us -> 654 us (0.38)
  waiting for transfers between devices: 1170 us -> 218 us
  blocking collectives: 279 us -> 0 us
  local copies, waits for them, and re-layouts: 54.1 us -> 175 us
  starting transfers between devices: 1.95 us -> 48.3 us
    reduce_scatter x25 -> x3, waiting for transfers between devices: 837 us -> 134 us  [spread(): return lax.psum_scatter(value.astype(bf16), EVERY, scatter_dimension=0)]
    all_gather x6 -> x3, waiting for transfers between devices: 328 us -> 27.8 us  [whole(): return lax.all_gather(shard, EVERY)]
    all_gather x20 -> x0, blocking collectives: 218 us -> none  [the longest x8 66.8 us: along_col(): return lax.all_gather(values, 'col', axis=0, tiled=True)]
    reshape x10 -> x20, local copies, waits for them, and re-layouts: 9.46 us -> 76.8 us  [the longest x2 17.6 us: local(): whole(w_outer).reshape(dp_count, 4, 4, inner_cols // dp_count, feat)]
    psum x5 -> x0, blocking collectives: 60.1 us -> none  [the longest x4 46.8 us: feature_totals(): return lax.psum((first_sum, second_sum), 'row')]
    ppermute x0 -> x41, waiting for transfers between devices: none -> 55.3 us  [the longest x21 22.8 us: exchange4(): lax.ppermute(blocks[step], axes, [(i, i ^ step) for i in range(4)])]
    ppermute x0 -> x41, starting transfers between devices: none -> 48.1 us  [the longest x21 28.4 us: exchange4(): lax.ppermute(blocks[step], axes, [(i, i ^ step) for i in range(4)])]
    convert_element_type x23 -> x13, other arithmetic: 39.9 us -> 16.8 us  [the longest x3 7.17 us: one_head(): grad_scores = (probs * (grad_probs - delta)).astype(bf16)]
  transfers between devices with their start and end apart: 32 -> 47, of which waited for: 28 -> 17; matrix products, arithmetic and copies ran while one was open for 9% -> 45% of each run, Pallas kernels for 0% -> 0%
where the time goes in v1:
time: 654 us; the launch traced here: 644 us
  waiting for transfers between devices  218 us (33%)
  local copies, waits for them, and re-layouts  175 us (27%)
  matrix products  108 us (17%)
  other arithmetic  77 us (12%)
  starting transfers between devices  48.3 us (7%)
  between operations  16.2 us (2%)
    reduce_scatter x3, waiting for transfers between devices, spread(): return lax.psum_scatter(value.astype(bf16), EVERY, scatter_dimension=0)  134 us
    dot_general x34, matrix products, dot(): lax.dot_general(left, right, ((dims[0], dims[1]), ((), ())), preferred_el...  108 us
    ppermute x21, starting transfers between devices, exchange4(): lax.ppermute(blocks[step], axes, [(i, i ^ step) for i in range(4)])  28.4 us
    all_gather x3, waiting for transfers between devices, whole(): return lax.all_gather(shard, EVERY)  27.8 us
    ppermute x21, waiting for transfers between devices, exchange4(): lax.ppermute(blocks[step], axes, [(i, i ^ step) for i in range(4)])  22.8 us
    ppermute x4, waiting for transfers between devices, local(): pieces.append(lax.ppermute(part, GROUP, group_route((r1, r2), False)))  20.7 us
    rev x9, local copies, waits for them, and re-layouts, swap_by(): pairs = jnp.where(low, pairs[:, ::-1], pairs)  17.9 us
    reshape x2, local copies, waits for them, and re-layouts, local(): whole(w_outer).reshape(dp_count, 4, 4, inner_cols // dp_count, feat)  17.6 us
  transfers between devices with their start and end apart: 47, of which 17 were waited for; matrix products, arithmetic and copies ran while one was open for 45% of the time, Pallas kernels for 0%

profile of v1, /device:TPU:0, one launch (start us, length us, event | category | flops | bytes accessed | tf_op | source)
XLA Modules:
  0.0 643.8 jit_solution(12398960918768596831)
XLA Ops:
  9.5 3.1 collective-permute-start.16
  20.2 3.5 collective-permute-start.1
  36.8 3.8 collective-permute-start.23
  52.8 4.4 collective-permute-start.5
  59.9 13.8 %collective-permute-done.5 = bf16[96,576]{1,0:T(8,128)(2,1)S(1)} collective-permute-done((bf16[96,576]{1,0:T(8,128)(2,1)S(1)}, bf16[96,576]{1,0:T(8,128)(2,1)S(1)}, u32[]{:S(2)}, u32[]{:S(2)}) %collective-permute-start.5) | collective-permute-done | bytes 110624 | tf_op jit(solution)/shard_map/ppermute | solution.py:190
  74.0 6.9 %collective-permute-done.7 = bf16[96,576]{1,0:T(8,128)(2,1)S(1)} collective-permute-done((bf16[96,576]{1,0:T(8,128)(2,1)S(1)}, bf16[96,576]{1,0:T(8,128)(2,1)S(1)}, u32[]{:S(2)}, u32[]{:S(2)}) %collective-permute-start.7) | collective-permute-done | bytes 110624 | tf_op jit(solution)/shard_map/ppermute | solution.py:190
  91.7 4.0 fusion.95
  98.5 3.1 subtract_convert_fusion
  108.0 3.1 fusion.83
  115.8 25.1 %while.30 = (s32[]{:T(128)}, bf16[3,64,1024]{2,1,0:T(8,128)(2,1)S(1)}, f32[3,1024]{1,0:T(4,128)}, bf16[3,64,2048]{2,1,0:T(8,128)(2,1)S(1)}, bf16[3,64,1024]{2,1,...) while((s32[]{:T(128)}, ...), condition=%wide.region_3.4_spmd.clone.clone, body=%wide.region_0.3_spmd.clone.sunk.clone | while | flops 559942656 | bytes 26134652 | solution.py:107
  158.5 4.0 copy.368
  162.5 4.2 reshape.509
  168.7 6.2 copy.322
  174.9 3.2 copy.359
  178.1 27.8 %all-gather.11.cloned.1.call-done = bf16[12288,192]{0,1:T(8,128)(2,1)} async-done(((bf16[384,192]{0,1:T(8,128)(2,1)}), bf16[12288,192]{0,1:T(8,128)(2,1)}) %all-gather.11.cloned.1.call-update) | async-done | bytes 4718608 | tf_op jit(solution)/shard_map/all_gather | solution.py:198
  205.8 8.2 %reshape.514 = bf16[2,4,4,384,192]{3,2,1,0,4:T(4,128)(2,1)} reshape(bf16[12288,192]{0,1:T(8,128)(2,1)} %all-gather.11.cloned.1.call-done) | data formatting | bytes 9437184 | tf_op jit(solution)/shard_map/reshape | solution.py:205
  214.1 9.4 %copy.367 = bf16[2,4,4,384,192]{3,0,2,4,1:T(2,128)(2,1)} copy(bf16[2,4,4,384,192]{3,2,1,0,4:T(4,128)(2,1)} %reshape.514) | data formatting | bytes 9437184 | tf_op jit(solution)/shard_map/reshape | solution.py:205
  223.5 11.5 %reshape.515 = bf16[3072,768]{0,1:T(8,128)(2,1)} reshape(bf16[4,2,384,4,192]{2,1,0,4,3:T(2,128)(2,1)} %bitcast.434) | data formatting | bytes 9437184 | tf_op jit(solution)/shard_map/reshape | solution.py:206
  235.0 9.7 %fusion.59 = (bf16[3072,256]{0,1:T(8,128)(2,1)S(1)}, f32[3072,256]{0,1:T(8,128)S(1)}, f32[256,3072]{1,0:T(8,128)S(1)}) fusion(bf16[768,3072]{1,0:T(8,128)(2,1)} %bitcast.452, f32[768,256]{0,1:T(8,128)S(1)} %get-tuple-element.282, f32[768]{0:T(1024)S(1)} %add.258, f32[768]{0:T(1024)S(1)} %mul.463, f32[256]{0:T(256)S(1)} %get-tuple-element.279, ...), kind=kOutput, calls=%fused_computation.77 | convolution fusion | flops 1260060672 | bytes 13377536 | tf_op jit(solution)/shard_map/dot_general | solution.py:93
  249.1 3.2 fusion.65
  256.7 4.8 reshape.533
  264.7 2.9 pad_maximum_fusion
  281.0 5.4 convolution_convert_fusion
  286.8 6.6 %copy.351 = bf16[3072,768]{0,1:T(8,128)(2,1)} copy(bf16[3072,768]{1,0:T(8,128)(2,1)} %convolution_convert_fusion) | data formatting | bytes 9437184 | tf_op jit(solution)/shard_map/convert_element_type | solution.py:284
  293.4 11.6 %reshape.538 = bf16[4,2,384,4,192]{2,1,0,4,3:T(2,128)(2,1)} reshape(bf16[3072,768]{0,1:T(8,128)(2,1)} %copy.351) | data formatting | bytes 9437184 | tf_op jit(solution)/shard_map/reshape | solution.py:284
  305.0 5.4 copy.352
  310.4 3.1 rev.89
  317.9 65.8 %while.31 = (s32[]{:T(128)}, f32[3,64,1024]{2,1,0:T(8,128)}, f32[3,64,2048]{2,1,0:T(8,128)S(1)}, f32[3,64,2048]{2,1,0:T(8,128)}, bf16[3,64,2048]{2,1,0:T(8,128)(...) while((s32[]{:T(128)}, f32[3,64,1024]{2,1,0:T(8,128)}, ...), condition=%wide.region_14.15_spmd.clone.clone, body=%wide.region_12.14_spmd.clone.sunk.clone | while | flops 1373834240 | bytes 90748096 | solution.py:124
  318.1 4.6 fusion.186
  324.8 6.1 multiply_reduce_fusion.12
  336.3 3.6 fusion.189
  339.9 4.6 fusion.186
  346.7 6.1 multiply_reduce_fusion.12
  358.2 3.6 fusion.189
  361.8 4.6 fusion.186
  368.5 6.2 multiply_reduce_fusion.12
  380.1 3.6 fusion.189
  391.7 3.7 convolution_convert_fusion.1
  395.4 9.9 %reshape.536 = bf16[4,2,96,4,768]{4,3,2,1,0:T(4,128)(2,1)} reshape(bf16[768,3072]{1,0:T(8,128)(2,1)} %convolution_convert_fusion.1) | data formatting | bytes 9437184 | tf_op jit(solution)/shard_map/reshape | solution.py:280
  405.4 5.4 copy.350
  418.8 3.3 subtract_convert_fusion.2
  426.3 3.6 convolution_convert_fusion.2
  435.4 2.9 fusion.81
  445.4 6.8 %collective-permute-done.31 = bf16[768,256]{0,1:T(8,128)(2,1)S(1)} collective-permute-done((bf16[768,256]{0,1:T(8,128)(2,1)S(1)}, bf16[768,256]{0,1:T(8,128)(2,1)S(1)}, u32[]{:S(2)}, u32[]{:S(2)}) %collective-permute-start.31) | collective-permute-done | bytes 393248 | tf_op jit(solution)/shard_map/ppermute | solution.py:28
  468.0 4.8 collective-permute-done.33
  482.7 6.4 collective-permute-done.39
  499.4 23.9 %reduce-scatter.8.cloned.1.call-done = bf16[1,384,192]{1,2,0:T(8,128)(2,1)} async-done(((bf16[32,384,192]{1,2,0:T(8,128)(2,1)}), bf16[1,384,192]{1,2,0:T(8,128)(2,1)}) %reduce-scatter.8.cloned.1.call-update) | async-done | bytes 147472 | tf_op jit(solution)/shard_map/reduce_scatter | solution.py:277
  525.0 109.9 %reduce-scatter.6.cloned.1.call-done = bf16[1,96,768]{2,1,0:T(8,128)(2,1)} async-done(((bf16[32,96,768]{2,1,0:T(8,128)(2,1)}), bf16[1,96,768]{2,1,0:T(8,128)(2,1)}) %reduce-scatter.6.cloned.1.call-update) | async-done | bytes 147472 | tf_op jit(solution)/shard_map/reduce_scatter | solution.py:277
  (426 shorter events, 230.1 us)
Async XLA Ops:
  7.2 151.3 %all-gather.7.cloned.1.call-start = ((), (), s32[]{:S(2)}) async-start(), calls=%async_computation.6 | async-start | bytes 1622016 | tf_op jit(solution)/shard_map/all_gather | solution.py:198
  7.9 160.7 %all-gather.9.cloned.1.call-start = ((), (), s32[]{:S(2)}) async-start(), calls=%async_computation.7 | async-start | bytes 4866048 | tf_op jit(solution)/shard_map/all_gather | solution.py:198
  8.7 197.2 %all-gather.11.cloned.1.call-start = ((), (), s32[]{:S(2)}) async-start(), calls=%async_computation.8 | async-start | bytes 4866048 | tf_op jit(solution)/shard_map/all_gather | solution.py:198
  9.5 24.4 %collective-permute-start.16 = (f32[4,192]{1,0:T(4,128)S(1)}, f32[4,192]{1,0:T(4,128)S(1)}, u32[]{:S(2)}, u32[]{:S(2)}) collective-permute-start(f32[4,192]{1,0:T(4,128)S(1)} %get-tuple-element.275), channel_id=1, source_target_pairs={{0,4},{4,0},{8,12},{12,8},{1,5},{5,1},{9,13},{13,9},{2,6},{6,2},{1... | collective-permute-start | bytes 9224 | tf_op jit(solution)/shard_map/ppermute | solution.py:35
  12.5 21.4 %collective-permute-start.17 = (f32[4,192]{1,0:T(4,128)S(1)}, f32[4,192]{1,0:T(4,128)S(1)}, u32[]{:S(2)}, u32[]{:S(2)}) collective-permute-start(f32[4,192]{1,0:T(4,128)S(1)} %get-tuple-element.275), channel_id=1, source_target_pairs={{0,8},{4,12},{8,0},{12,4},{1,9},{5,13},{9,1},{13,5},{2,10},{6,14},... | collective-permute-start | bytes 9224 | tf_op jit(solution)/shard_map/ppermute | solution.py:35
  15.1 20.6 %collective-permute-start.18 = (f32[4,192]{1,0:T(4,128)S(1)}, f32[4,192]{1,0:T(4,128)S(1)}, u32[]{:S(2)}, u32[]{:S(2)}) collective-permute-start(f32[4,192]{1,0:T(4,128)S(1)} %get-tuple-element.275), channel_id=1, source_target_pairs={{0,12},{4,8},{8,4},{12,0},{1,13},{5,9},{9,5},{13,1},{2,14},{6,10},... | collective-permute-start | bytes 9224 | tf_op jit(solution)/shard_map/ppermute | solution.py:35
  19.3 17.6 %collective-permute-start = (bf16[192,256]{1,0:T(8,128)(2,1)S(1)}, bf16[192,256]{1,0:T(8,128)(2,1)S(1)}, u32[]{:S(2)}, u32[]{:S(2)}) collective-permute-start(bf16[192,256]{1,0:T(8,128)(2,1)S(1)} %get-tuple-element.253), channel_id=1, source_target_pairs={{0,4},{4,0},{8,12},{12,8},{1,5},{5,1},{9,13},{13,9},{2,6},{6,2},{1... | collective-permute-start | bytes 294920 | tf_op jit(solution)/shard_map/ppermute | solution.py:28
  20.2 20.4 %collective-permute-start.1 = (bf16[192,256]{1,0:T(8,128)(2,1)S(1)}, bf16[192,256]{1,0:T(8,128)(2,1)S(1)}, u32[]{:S(2)}, u32[]{:S(2)}) collective-permute-start(bf16[192,256]{1,0:T(8,128)(2,1)S(1)} %get-tuple-element.252), channel_id=1, source_target_pairs={{0,8},{4,12},{8,0},{12,4},{1,9},{5,13},{9,1},{13,5},{2,10},{6,14},... | collective-permute-start | bytes 294920 | tf_op jit(solution)/shard_map/ppermute | solution.py:28
  23.7 473.0 %reduce-scatter.4.cloned.1.call-start = ((), (), s32[]{:S(2)}) async-start(), calls=%async_computation.3 | async-start | bytes 1757184 | tf_op jit(solution)/shard_map/reduce_scatter | solution.py:277
  33.8 7.6 %collective-permute-start.2 = (bf16[192,256]{1,0:T(8,128)(2,1)S(1)}, bf16[192,256]{1,0:T(8,128)(2,1)S(1)}, u32[]{:S(2)}, u32[]{:S(2)}) collective-permute-start(bf16[192,256]{1,0:T(8,128)(2,1)S(1)} %get-tuple-element.251), channel_id=1, source_target_pairs={{0,12},{4,8},{8,4},{12,0},{1,13},{5,9},{9,5},{13,1},{2,14},{6,10},... | collective-permute-start | bytes 294920 | tf_op jit(solution)/shard_map/ppermute | solution.py:28
  33.9 18.0 %collective-permute-start.3 = (bf16[96,576]{1,0:T(8,128)(2,1)S(1)}, bf16[96,576]{1,0:T(8,128)(2,1)S(1)}, u32[]{:S(2)}, u32[]{:S(2)}) collective-permute-start(bf16[96,576]{1,0:T(8,128)(2,1)S(1)} %pad_maximum_fusion.17), channel_id=1, source_target_pairs={{0,16},{16,0},{1,17},{17,1},{2,18},{18,2},{3,19},{19,3},{4,20},{20... | collective-permute-start | bytes 331784 | tf_op jit(solution)/shard_map/ppermute | solution.py:46
  35.7 10.8 %collective-permute-start.22 = (bf16[192,256]{1,0:T(8,128)(2,1)S(1)}, bf16[192,256]{1,0:T(8,128)(2,1)S(1)}, u32[]{:S(2)}, u32[]{:S(2)}) collective-permute-start(bf16[192,256]{1,0:T(8,128)(2,1)S(1)} %get-tuple-element.241), channel_id=1, source_target_pairs={{0,4},{4,0},{8,12},{12,8},{1,5},{5,1},{9,13},{13,9},{2,6},{6,2},{1... | collective-permute-start | bytes 294920 | tf_op jit(solution)/shard_map/ppermute | solution.py:28
  36.5 208.2 %copy-start.31 = (f32[768]{0:T(1024)}, f32[768]{0:T(1024)S(1)}, u32[]{:S(2)}) copy-start(f32[768]{0:T(1024)S(1)} %add.258) | copy-start | bytes 9220
  36.8 12.2 %collective-permute-start.23 = (bf16[192,256]{1,0:T(8,128)(2,1)S(1)}, bf16[192,256]{1,0:T(8,128)(2,1)S(1)}, u32[]{:S(2)}, u32[]{:S(2)}) collective-permute-start(bf16[192,256]{1,0:T(8,128)(2,1)S(1)} %get-tuple-element.240), channel_id=1, source_target_pairs={{0,8},{4,12},{8,0},{12,4},{1,9},{5,13},{9,1},{13,5},{2,10},{6,14},... | collective-permute-start | bytes 294920 | tf_op jit(solution)/shard_map/ppermute | solution.py:28
  40.7 8.4 %collective-permute-start.24 = (bf16[192,256]{1,0:T(8,128)(2,1)S(1)}, bf16[192,256]{1,0:T(8,128)(2,1)S(1)}, u32[]{:S(2)}, u32[]{:S(2)}) collective-permute-start(bf16[192,256]{1,0:T(8,128)(2,1)S(1)} %get-tuple-element.239), channel_id=1, source_target_pairs={{0,12},{4,8},{8,4},{12,0},{1,13},{5,9},{9,5},{13,1},{2,14},{6,10},... | collective-permute-start | bytes 294920 | tf_op jit(solution)/shard_map/ppermute | solution.py:28
  44.9 36.1 %collective-permute-start.9 = (bf16[768,256]{1,0:T(8,128)(2,1)S(1)}, bf16[768,256]{1,0:T(8,128)(2,1)}, u32[]{:S(2)}, u32[]{:S(2)}) collective-permute-start(bf16[768,256]{1,0:T(8,128)(2,1)S(1)} %bitcast.438), channel_id=1, source_target_pairs={{0,2},{2,0},{4,6},{6,4},{1,3},{3,1},{5,7},{7,5},{8,10},{10,8},{12,... | collective-permute-start | bytes 1179656 | tf_op jit(solution)/shard_map/ppermute | solution.py:35
  46.5 34.5 %collective-permute-start.10 = (bf16[768,256]{1,0:T(8,128)(2,1)S(1)}, bf16[768,256]{1,0:T(8,128)(2,1)}, u32[]{:S(2)}, u32[]{:S(2)}) collective-permute-start(bf16[768,256]{1,0:T(8,128)(2,1)S(1)} %bitcast.439), channel_id=1, source_target_pairs={{0,4},{2,6},{4,0},{6,2},{1,5},{3,7},{5,1},{7,3},{8,12},{10,14},{12... | collective-permute-start | bytes 1179656 | tf_op jit(solution)/shard_map/ppermute | solution.py:35
  49.0 32.0 %collective-permute-start.11 = (bf16[768,256]{1,0:T(8,128)(2,1)S(1)}, bf16[768,256]{1,0:T(8,128)(2,1)}, u32[]{:S(2)}, u32[]{:S(2)}) collective-permute-start(bf16[768,256]{1,0:T(8,128)(2,1)S(1)} %bitcast.440), channel_id=1, source_target_pairs={{0,6},{2,4},{4,2},{6,0},{1,7},{3,5},{5,3},{7,1},{8,14},{10,12},{12... | collective-permute-start | bytes 1179656 | tf_op jit(solution)/shard_map/ppermute | solution.py:35
  52.1 7.8 %collective-permute-start.4 = (bf16[96,576]{1,0:T(8,128)(2,1)S(1)}, bf16[96,576]{1,0:T(8,128)(2,1)S(1)}, u32[]{:S(2)}, u32[]{:S(2)}) collective-permute-start(bf16[96,576]{1,0:T(8,128)(2,1)S(1)} %get-tuple-element.259), channel_id=1, source_target_pairs={{0,0},{1,4},{2,2},{3,6},{4,1},{5,5},{6,3},{7,7},{8,8},{9,12},{10,1... | collective-permute-start | bytes 331784 | tf_op jit(solution)/shard_map/ppermute | solution.py:190
  52.8 21.0 %collective-permute-start.5 = (bf16[96,576]{1,0:T(8,128)(2,1)S(1)}, bf16[96,576]{1,0:T(8,128)(2,1)S(1)}, u32[]{:S(2)}, u32[]{:S(2)}) collective-permute-start(bf16[96,576]{1,0:T(8,128)(2,1)S(1)} %get-tuple-element.260), channel_id=1, source_target_pairs={{0,1},{1,5},{2,3},{3,7},{4,0},{5,4},{6,2},{7,6},{8,9},{9,13},{10,1... | collective-permute-start | bytes 331784 | tf_op jit(solution)/shard_map/ppermute | solution.py:190
  59.9 14.1 %collective-permute-start.6 = (bf16[96,576]{1,0:T(8,128)(2,1)S(1)}, bf16[96,576]{1,0:T(8,128)(2,1)S(1)}, u32[]{:S(2)}, u32[]{:S(2)}) collective-permute-start(bf16[96,576]{1,0:T(8,128)(2,1)S(1)} %get-tuple-element.259), channel_id=1, source_target_pairs={{0,8},{1,12},{2,10},{3,14},{4,9},{5,13},{6,11},{7,15},{8,0},{9,4},... | collective-permute-start | bytes 331784 | tf_op jit(solution)/shard_map/ppermute | solution.py:190
  73.8 7.1 %collective-permute-start.7 = (bf16[96,576]{1,0:T(8,128)(2,1)S(1)}, bf16[96,576]{1,0:T(8,128)(2,1)S(1)}, u32[]{:S(2)}, u32[]{:S(2)}) collective-permute-start(bf16[96,576]{1,0:T(8,128)(2,1)S(1)} %get-tuple-element.260), channel_id=1, source_target_pairs={{0,9},{1,13},{2,11},{3,15},{4,8},{5,12},{6,10},{7,14},{8,1},{9,5},... | collective-permute-start | bytes 331784 | tf_op jit(solution)/shard_map/ppermute | solution.py:190
  82.5 6.4 collective-permute-start.12
  84.0 3.6 collective-permute-start.8
  143.1 10.1 %collective-permute-start.13 = (bf16[192,256]{1,0:T(8,128)(2,1)}, bf16[192,256]{1,0:T(8,128)(2,1)}, u32[]{:S(2)}, u32[]{:S(2)}) collective-permute-start(bf16[192,256]{1,0:T(8,128)(2,1)} %bitcast.374), channel_id=1, source_target_pairs={{0,2},{2,0},{4,6},{6,4},{1,3},{3,1},{5,7},{7,5},{8,10},{10,8},{12,... | collective-permute-start | bytes 294920 | tf_op jit(solution)/shard_map/ppermute | solution.py:28
  144.9 9.3 %collective-permute-start.14 = (bf16[192,256]{1,0:T(8,128)(2,1)}, bf16[192,256]{1,0:T(8,128)(2,1)}, u32[]{:S(2)}, u32[]{:S(2)}) collective-permute-start(bf16[192,256]{1,0:T(8,128)(2,1)} %bitcast.373), channel_id=1, source_target_pairs={{0,4},{2,6},{4,0},{6,2},{1,5},{3,7},{5,1},{7,3},{8,12},{10,14},{12... | collective-permute-start | bytes 294920 | tf_op jit(solution)/shard_map/ppermute | solution.py:28
  146.0 9.3 %collective-permute-start.15 = (bf16[192,256]{1,0:T(8,128)(2,1)}, bf16[192,256]{1,0:T(8,128)(2,1)}, u32[]{:S(2)}, u32[]{:S(2)}) collective-permute-start(bf16[192,256]{1,0:T(8,128)(2,1)} %bitcast.372), channel_id=1, source_target_pairs={{0,6},{2,4},{4,2},{6,0},{1,7},{3,5},{5,3},{7,1},{8,14},{10,12},{12... | collective-permute-start | bytes 294920 | tf_op jit(solution)/shard_map/ppermute | solution.py:28
  267.6 255.8 %reduce-scatter.8.cloned.1.call-start = ((), (), s32[]{:S(2)}) async-start(), calls=%async_computation.5 | async-start | bytes 4866048 | tf_op jit(solution)/shard_map/reduce_scatter | solution.py:277
  274.2 39.4 %collective-permute-start.25 = (bf16[192,256]{1,0:T(8,128)(2,1)}, bf16[192,256]{1,0:T(8,128)(2,1)}, u32[]{:S(2)}, u32[]{:S(2)}) collective-permute-start(bf16[192,256]{1,0:T(8,128)(2,1)} %get-tuple-element.237), channel_id=1, source_target_pairs={{0,2},{2,0},{4,6},{6,4},{1,3},{3,1},{5,7},{7,5},{8,10},{10,8},{12,... | collective-permute-start | bytes 294920 | tf_op jit(solution)/shard_map/ppermute | solution.py:28
  275.6 38.0 %collective-permute-start.26 = (bf16[192,256]{1,0:T(8,128)(2,1)}, bf16[192,256]{1,0:T(8,128)(2,1)}, u32[]{:S(2)}, u32[]{:S(2)}) collective-permute-start(bf16[192,256]{1,0:T(8,128)(2,1)} %get-tuple-element.236), channel_id=1, source_target_pairs={{0,4},{2,6},{4,0},{6,2},{1,5},{3,7},{5,1},{7,3},{8,12},{10,14},{12... | collective-permute-start | bytes 294920 | tf_op jit(solution)/shard_map/ppermute | solution.py:28
  275.8 37.9 %collective-permute-start.27 = (bf16[192,256]{1,0:T(8,128)(2,1)}, bf16[192,256]{1,0:T(8,128)(2,1)}, u32[]{:S(2)}, u32[]{:S(2)}) collective-permute-start(bf16[192,256]{1,0:T(8,128)(2,1)} %get-tuple-element.235), channel_id=1, source_target_pairs={{0,6},{2,4},{4,2},{6,0},{1,7},{3,5},{5,3},{7,1},{8,14},{10,12},{12... | collective-permute-start | bytes 294920 | tf_op jit(solution)/shard_map/ppermute | solution.py:28
  313.5 321.4 %reduce-scatter.6.cloned.1.call-start = ((), (), s32[]{:S(2)}) async-start(), calls=%async_computation.4 | async-start | bytes 4866048 | tf_op jit(solution)/shard_map/reduce_scatter | solution.py:277
  386.0 29.4 %collective-permute-start.28 = (bf16[384,1024]{1,0:T(8,128)(2,1)}, bf16[384,1024]{1,0:T(8,128)(2,1)}, u32[]{:S(2)}, u32[]{:S(2)}) collective-permute-start(bf16[384,1024]{1,0:T(8,128)(2,1)} %fusion.80), channel_id=1, source_target_pairs={{0,1},{1,0},{2,3},{3,2},{4,5},{5,4},{6,7},{7,6},{8,9},{9,8},{10,11... | collective-permute-start | bytes 2359304 | tf_op jit(solution)/shard_map/ppermute | solution.py:40
  387.3 25.9 %collective-permute-start.19 = (bf16[192,256]{1,0:T(8,128)(2,1)}, bf16[192,256]{1,0:T(8,128)(2,1)S(1)}, u32[]{:S(2)}, u32[]{:S(2)}) collective-permute-start(bf16[192,256]{1,0:T(8,128)(2,1)} %get-tuple-element.245), channel_id=1, source_target_pairs={{0,4},{4,0},{8,12},{12,8},{1,5},{5,1},{9,13},{13,9},{2,6},{6,2},{1... | collective-permute-start | bytes 294920 | tf_op jit(solution)/shard_map/ppermute | solution.py:28
  387.4 25.8 %collective-permute-start.20 = (bf16[192,256]{1,0:T(8,128)(2,1)S(1)}, bf16[192,256]{1,0:T(8,128)(2,1)}, u32[]{:S(2)}, u32[]{:S(2)}) collective-permute-start(bf16[192,256]{1,0:T(8,128)(2,1)S(1)} %get-tuple-element.244), channel_id=1, source_target_pairs={{0,8},{4,12},{8,0},{12,4},{1,9},{5,13},{9,1},{13,5},{2,10},{6,14},... | collective-permute-start | bytes 294920 | tf_op jit(solution)/shard_map/ppermute | solution.py:28
  389.2 24.0 %collective-permute-start.21 = (bf16[192,256]{1,0:T(8,128)(2,1)S(1)}, bf16[192,256]{1,0:T(8,128)(2,1)}, u32[]{:S(2)}, u32[]{:S(2)}) collective-permute-start(bf16[192,256]{1,0:T(8,128)(2,1)S(1)} %get-tuple-element.243), channel_id=1, source_target_pairs={{0,12},{4,8},{8,4},{12,0},{1,13},{5,9},{9,5},{13,1},{2,14},{6,10},... | collective-permute-start | bytes 294920 | tf_op jit(solution)/shard_map/ppermute | solution.py:28
  431.8 11.2 %collective-permute-start.29 = (bf16[768,256]{0,1:T(8,128)(2,1)S(1)}, bf16[768,256]{0,1:T(8,128)(2,1)S(1)}, u32[]{:S(2)}, u32[]{:S(2)}) collective-permute-start(bf16[768,256]{0,1:T(8,128)(2,1)S(1)} %get-tuple-element.214), channel_id=1, source_target_pairs={{0,2},{2,0},{4,6},{6,4},{1,3},{3,1},{5,7},{7,5},{8,10},{10,8},{12,... | collective-permute-start | bytes 1179656 | tf_op jit(solution)/shard_map/ppermute | solution.py:28
  433.3 12.1 %collective-permute-start.30 = (bf16[768,256]{0,1:T(8,128)(2,1)S(1)}, bf16[768,256]{0,1:T(8,128)(2,1)S(1)}, u32[]{:S(2)}, u32[]{:S(2)}) collective-permute-start(bf16[768,256]{0,1:T(8,128)(2,1)S(1)} %get-tuple-element.216), channel_id=1, source_target_pairs={{0,4},{2,6},{4,0},{6,2},{1,5},{3,7},{5,1},{7,3},{8,12},{10,14},{12... | collective-permute-start | bytes 1179656 | tf_op jit(solution)/shard_map/ppermute | solution.py:28
  433.3 18.9 %collective-permute-start.31 = (bf16[768,256]{0,1:T(8,128)(2,1)S(1)}, bf16[768,256]{0,1:T(8,128)(2,1)S(1)}, u32[]{:S(2)}, u32[]{:S(2)}) collective-permute-start(bf16[768,256]{0,1:T(8,128)(2,1)S(1)} %get-tuple-element.215), channel_id=1, source_target_pairs={{0,6},{2,4},{4,2},{6,0},{1,7},{3,5},{5,3},{7,1},{8,14},{10,12},{12... | collective-permute-start | bytes 1179656 | tf_op jit(solution)/shard_map/ppermute | solution.py:28
  440.5 22.0 %collective-permute-start.35 = (bf16[4,96,576]{2,1,0:T(8,128)(2,1)}, bf16[4,96,576]{2,1,0:T(8,128)(2,1)}, u32[]{:S(2)}, u32[]{:S(2)}) collective-permute-start(bf16[4,96,576]{2,1,0:T(8,128)(2,1)} %fusion.97), channel_id=1, source_target_pairs={{0,1},{1,0},{2,3},{3,2},{4,5},{5,4},{6,7},{7,6},{8,9},{9,8},{10,11... | collective-permute-start | bytes 1327112 | tf_op jit(solution)/shard_map/ppermute | solution.py:40
  458.0 9.1 %collective-permute-start.32 = (bf16[192,256]{1,0:T(8,128)(2,1)S(1)}, bf16[192,256]{1,0:T(8,128)(2,1)S(1)}, u32[]{:S(2)}, u32[]{:S(2)}) collective-permute-start(bf16[192,256]{1,0:T(8,128)(2,1)S(1)} %get-tuple-element.233), channel_id=1, source_target_pairs={{0,4},{4,0},{8,12},{12,8},{1,5},{5,1},{9,13},{13,9},{2,6},{6,2},{1... | collective-permute-start | bytes 294920 | tf_op jit(solution)/shard_map/ppermute | solution.py:28
  458.3 14.6 %collective-permute-start.33 = (bf16[192,256]{1,0:T(8,128)(2,1)S(1)}, bf16[192,256]{1,0:T(8,128)(2,1)S(1)}, u32[]{:S(2)}, u32[]{:S(2)}) collective-permute-start(bf16[192,256]{1,0:T(8,128)(2,1)S(1)} %get-tuple-element.232), channel_id=1, source_target_pairs={{0,8},{4,12},{8,0},{12,4},{1,9},{5,13},{9,1},{13,5},{2,10},{6,14},... | collective-permute-start | bytes 294920 | tf_op jit(solution)/shard_map/ppermute | solution.py:28
  459.9 14.2 %collective-permute-start.34 = (bf16[192,256]{1,0:T(8,128)(2,1)S(1)}, bf16[192,256]{1,0:T(8,128)(2,1)S(1)}, u32[]{:S(2)}, u32[]{:S(2)}) collective-permute-start(bf16[192,256]{1,0:T(8,128)(2,1)S(1)} %get-tuple-element.231), channel_id=1, source_target_pairs={{0,12},{4,8},{8,4},{12,0},{1,13},{5,9},{9,5},{13,1},{2,14},{6,10},... | collective-permute-start | bytes 294920 | tf_op jit(solution)/shard_map/ppermute | solution.py:28
  463.8 16.1 %collective-permute-start.36 = (bf16[96,576]{1,0:T(8,128)(2,1)S(1)}, bf16[96,576]{1,0:T(8,128)(2,1)S(1)}, u32[]{:S(2)}, u32[]{:S(2)}) collective-permute-start(bf16[96,576]{1,0:T(8,128)(2,1)S(1)} %get-tuple-element.226), channel_id=1, source_target_pairs={{1,0},{5,1},{3,2},{7,3},{0,4},{4,5},{2,6},{6,7},{9,8},{13,9},{11,1... | collective-permute-start | bytes 331784 | tf_op jit(solution)/shard_map/ppermute | solution.py:325
  463.9 18.8 %collective-permute-start.37 = (bf16[96,576]{1,0:T(8,128)(2,1)S(1)}, bf16[96,576]{1,0:T(8,128)(2,1)S(1)}, u32[]{:S(2)}, u32[]{:S(2)}) collective-permute-start(bf16[96,576]{1,0:T(8,128)(2,1)S(1)} %get-tuple-element.229), channel_id=1, source_target_pairs={{9,0},{13,1},{11,2},{15,3},{8,4},{12,5},{10,6},{14,7},{1,8},{5,9},... | collective-permute-start | bytes 331784 | tf_op jit(solution)/shard_map/ppermute | solution.py:325
  467.1 15.6 %collective-permute-start.38 = (bf16[96,576]{1,0:T(8,128)(2,1)S(1)}, bf16[96,576]{1,0:T(8,128)(2,1)S(1)}, u32[]{:S(2)}, u32[]{:S(2)}) collective-permute-start(bf16[96,576]{1,0:T(8,128)(2,1)S(1)} %get-tuple-element.228), channel_id=1, source_target_pairs={{0,0},{4,1},{2,2},{6,3},{1,4},{5,5},{3,6},{7,7},{8,8},{12,9},{10,1... | collective-permute-start | bytes 331784 | tf_op jit(solution)/shard_map/ppermute | solution.py:325
  472.9 16.2 %collective-permute-start.39 = (bf16[96,576]{1,0:T(8,128)(2,1)S(1)}, bf16[96,576]{1,0:T(8,128)(2,1)S(1)}, u32[]{:S(2)}, u32[]{:S(2)}) collective-permute-start(bf16[96,576]{1,0:T(8,128)(2,1)S(1)} %get-tuple-element.227), channel_id=1, source_target_pairs={{8,0},{12,1},{10,2},{14,3},{9,4},{13,5},{11,6},{15,7},{0,8},{4,9},... | collective-permute-start | bytes 331784 | tf_op jit(solution)/shard_map/ppermute | solution.py:325
  489.2 6.7 %collective-permute-start.40 = (bf16[96,576]{1,0:T(8,128)(2,1)S(1)}, bf16[96,576]{1,0:T(8,128)(2,1)S(1)}, u32[]{:S(2)}, u32[]{:S(2)}) collective-permute-start(bf16[96,576]{1,0:T(8,128)(2,1)S(1)} %select_convert_fusion.1), channel_id=1, source_target_pairs={{0,16},{16,0},{1,17},{17,1},{2,18},{18,2},{3,19},{19,3},{4,20},{20... | collective-permute-start | bytes 331784 | tf_op jit(solution)/shard_map/ppermute | solution.py:60
  (59 other events, 578.0 us)
Sparse Core Ops, SparseCore 0:
  10.9 63.0 all-gather.6
  76.9 62.8 all-gather.8
  142.6 63.1 all-gather.10
  267.7 135.2 reduce-scatter.3
  409.3 114.0 reduce-scatter.7
  528.7 106.1 reduce-scatter.5

commit v2 on v1

v2 whole, which is shorter than its diff:
```python
import jax
import jax.numpy as jnp
from jax import lax
from jax.experimental import pallas as pl
from jax.experimental.pallas import tpu as pltpu
from jax.sharding import Mesh, PartitionSpec as P

HD = 64
EVERY = ("dp", "rm", "rz", "cy", "cc")
GROUP = ("rm", "rz", "cy", "cc")
ROW = ("rm", "rz")
SQUARE = ("rz", "cy")
bf16=jnp.bfloat16; f32=jnp.float32
LOG2E=1.4426950408889634
LN2=0.6931471805599453
masked_score=-1e30

def mm(a,b,dims=((1,),(0,))):
    return lax.dot_general(a,b,(dims,((),())),preferred_element_type=f32)
NT=((1,),(1,))

def pair_turn(values, cosine, signed_sine):
    shape = values.shape
    v3 = values.reshape(shape[0]//8, 8, shape[1])
    up = pltpu.roll(v3, 7, 1); down = pltpu.roll(v3, 1, 1)
    even = (lax.broadcasted_iota(jnp.int32, v3.shape, 1) % 2) == 0
    other = jnp.where(even, up, down).reshape(shape)
    return values*cosine + other*signed_sine

KB=1024
QB=2
def one_row(shape, dtype, value=1.0):
    return jnp.where(lax.broadcasted_iota(jnp.int32, shape, 0)==0, value, 0.0).astype(dtype)

def attend_kernel(q_ref, ko_ref, vo_ref, kx_ref, vx_ref, bias_ref, o_ref, lse_ref, l0, l1, l2, l3, kaug, vall):
    head=pl.program_id(0); qb=pl.program_id(1)
    span=ko_ref.shape[1]
    @pl.when(qb==0)
    def _():
        for part,(kr,vr) in enumerate(((ko_ref,vo_ref),(kx_ref,vx_ref))):
            aug=jnp.concatenate([kr[...], bias_ref[:, part*span:(part+1)*span]],axis=0)
            kaug[part*span:(part+1)*span,:]=aug.T
            vall[:, part*span:(part+1)*span]=vr[...]
    n=q_ref.shape[1]
    qaug=jnp.concatenate([q_ref[...], one_row((HD,n),bf16)],axis=0)
    top=jnp.full((1,n),-3e38,f32); total=jnp.zeros((1,n),f32); acc=jnp.zeros((HD,n),f32)
    s=mm(kaug[0:KB,:],qaug)
    for kb in range(0,2*span,KB):
        following=mm(kaug[kb+KB:kb+2*KB,:],qaug) if kb+KB<2*span else None
        new=jnp.maximum(top,jnp.max(s,axis=0,keepdims=True))
        alpha=jnp.exp2(top-new)
        p=jnp.exp2(s-new)
        total=total*alpha+jnp.sum(p,axis=0,keepdims=True)
        acc=acc*alpha+mm(vall[:,kb:kb+KB],p.astype(bf16))
        top=new
        s=following
    out=acc/total
    o_ref[...]=out
    lse_ref[0]=top+jnp.log2(total)
    low=out.astype(bf16)
    part=n//QB
    for k,ref in enumerate((l0,l1,l2,l3)):
        @pl.when(qb==k//QB)
        def _(): ref[pl.ds(pl.multiple_of(head*HD,HD),HD),:]=low[:,(k%QB)*part:(k%QB+1)*part]

def attend(q,kv,kvx,bias):
    width,n4=q.shape; heads=width//HD; n=n4//4*QB; span=kv.shape[1]
    kspec=pl.BlockSpec((HD,span),lambda h,b:(h,0)); vspec=pl.BlockSpec((HD,span),lambda h,b:(heads+h,0))
    lowspec=pl.BlockSpec((width,n4//4),lambda h,b:(0,0))
    return pl.pallas_call(attend_kernel,grid=(heads,4//QB),
        in_specs=[pl.BlockSpec((HD,n),lambda h,b:(h,b)),kspec,vspec,kspec,vspec,pl.BlockSpec((HD,2*span),lambda h,b:(0,0))],
        out_specs=[pl.BlockSpec((HD,n),lambda h,b:(h,b)),pl.BlockSpec((1,1,n),lambda h,b:(h,0,b))]+[lowspec]*4,
        out_shape=[jax.ShapeDtypeStruct((width,n4),f32),jax.ShapeDtypeStruct((heads,1,n4),f32)]+[jax.ShapeDtypeStruct((width,n4//4),bf16)]*4,
        scratch_shapes=[pltpu.VMEM((2*span,2*HD),bf16),pltpu.VMEM((HD,2*span),bf16)],
        name="attend")(q,kv,kv,kvx,kvx,bias)

BKB=512
def attend_back_kernel(q_ref, ko_ref, vo_ref, kx_ref, vx_ref, bias_ref, o_ref, lse_ref, g0,g1,g2,g3, cos_ref, sin_ref,
                       dq_ref, own_ref, give_ref, kaug, vtm, kall, acc):
    head=pl.program_id(0); qb=pl.program_id(1)
    span=ko_ref.shape[1]; n=q_ref.shape[1]
    @pl.when(qb==0)
    def _():
        for part,(kr,vr) in enumerate(((ko_ref,vo_ref),(kx_ref,vx_ref))):
            sl=slice(part*span,(part+1)*span)
            kaug[sl,:]=jnp.concatenate([kr[...], bias_ref[:, sl]],axis=0).T
            vtm[sl,:]=jnp.concatenate([vr[...], jnp.zeros((HD,span),bf16)],axis=0).T
            kall[:,sl]=kr[...]
        acc[...]=jnp.zeros_like(acc)
    q=q_ref[...]
    zeros=jnp.zeros((HD,n),bf16)
    qaug=jnp.concatenate([q, one_row((HD,n),bf16)],axis=0)
    g=jnp.concatenate([jnp.where(qb==0,g0[...],g2[...]),jnp.where(qb==0,g1[...],g3[...])],axis=1)
    qpad=jnp.concatenate([q,zeros],axis=0).T
    gpad=jnp.concatenate([zeros,g],axis=0).T
    gaug=jnp.concatenate([g,zeros],axis=0)
    delta=jnp.sum(g.astype(f32)*o_ref[...],axis=0,keepdims=True)
    lse=lse_ref[0]
    dq=jnp.zeros((HD,n),f32)
    s=mm(kaug[0:BKB,:],qaug); dp=mm(vtm[0:BKB,:],gaug)
    for kb in range(0,2*span,BKB):
        last=kb+BKB>=2*span
        s_next=None if last else mm(kaug[kb+BKB:kb+2*BKB,:],qaug)
        dp_next=None if last else mm(vtm[kb+BKB:kb+2*BKB,:],gaug)
        p=jnp.exp2(s-lse)
        ds=(p*(dp-delta)).astype(bf16)
        dq=dq+mm(kall[:,kb:kb+BKB],ds)
        acc[kb:kb+BKB,:]=acc[kb:kb+BKB,:]+mm(ds,qpad)+mm(p.astype(bf16),gpad)
        s=s_next; dp=dp_next
    dq_ref[...]=pair_turn(dq*(HD**-0.5),cos_ref[...],-sin_ref[...]).astype(bf16)
    @pl.when(qb==4//QB-1)
    def _():
        own_ref[0]=acc[:span,:]
        give_ref[0]=acc[span:,:].astype(bf16)

def attend_back(q,kv,kvx,bias,o,lse,grads,cos,sin):
    width,n4=q.shape; heads=width//HD; n=n4//4*QB; span=kv.shape[1]
    kspec=pl.BlockSpec((HD,span),lambda h,b:(h,0)); vspec=pl.BlockSpec((HD,span),lambda h,b:(heads+h,0))
    gspec=pl.BlockSpec((HD,n4//4),lambda h,b:(h,0)); hb=pl.BlockSpec((HD,n),lambda h,b:(h,b)); tb=pl.BlockSpec((HD,n),lambda h,b:(0,b))
    dspec=pl.BlockSpec((1,span,2*HD),lambda h,b:(h,0,0))
    return pl.pallas_call(attend_back_kernel,grid=(heads,4//QB),
        in_specs=[hb,kspec,vspec,kspec,vspec,pl.BlockSpec((HD,2*span),lambda h,b:(0,0)),hb,pl.BlockSpec((1,1,n),lambda h,b:(h,0,b)),gspec,gspec,gspec,gspec,tb,tb],
        out_specs=[hb,dspec,dspec],
        out_shape=[jax.ShapeDtypeStruct((width,n4),bf16),jax.ShapeDtypeStruct((heads,span,2*HD),f32),jax.ShapeDtypeStruct((heads,span,2*HD),bf16)],
        scratch_shapes=[pltpu.VMEM((2*span,2*HD),bf16),pltpu.VMEM((2*span,2*HD),bf16),pltpu.VMEM((HD,2*span),bf16),pltpu.VMEM((2*span,2*HD),f32)],
        name="attend_back")(q,kv,kv,kvx,kvx,bias,o,lse,*grads,cos,sin)
def xor(a,b):
    return lax.bitwise_xor(jnp.asarray(a,jnp.int32),jnp.asarray(b,jnp.int32))

def rows_at(index,size,align):
    return pl.ds(pl.multiple_of(index*size,align),size)

def place_qkv_weights(info, mine_ref, theirs_ref, w_s):
    c=info[3]; mc=info[2]
    half=mine_ref.shape[1]
    for r in range(4):
        a=mine_ref[xor(r,mc)]; b=theirs_ref[xor(r,xor(mc,1))]
        for h in range(2):
            w_s[(2*r+h)*half:(2*r+h+1)*half,:]=jnp.where(c==h,a,b)

def place_tokens(info, x_ref, kz, x_s):
    feat=x_ref.shape[1]; base=xor(info[0],kz)
    for r in range(4):
        x_s[r*feat:(r+1)*feat,:]=x_ref[xor(r,base)]

def qkv_kernel(info, x0,x1,x2,x3, mine_ref, theirs_ref, cos_ref, sin_ref, q_ref, kv_ref, w_s, wt_s, x_s):
    place_qkv_weights(info,mine_ref,theirs_ref,w_s)
    wt_s[...]=w_s[...].T
    hw=q_ref.shape[0]; n=x0.shape[2]
    for k,xr in enumerate((x0,x1,x2,x3)):
        place_tokens(info,xr,k//2,x_s)
        out=mm(wt_s[...],x_s[...])
        sl=slice(k*n,(k+1)*n)
        cos=cos_ref[:,sl]; sin=sin_ref[:,sl]
        for h in range(2*hw//HD):
            turned=pair_turn(out[h*HD:(h+1)*HD],cos,sin)
            if h*HD<hw: q_ref[h*HD:(h+1)*HD,sl]=(turned*(HD**-0.5*LOG2E)).astype(bf16)
            else: kv_ref[h*HD-hw:(h+1)*HD-hw,sl]=turned.astype(bf16)
        kv_ref[hw:,sl]=out[2*hw:].astype(bf16)

VM=pl.BlockSpec(memory_space=pltpu.VMEM)
SM=pl.BlockSpec(memory_space=pltpu.SMEM)
HB=pl.BlockSpec(memory_space=pl.ANY)

def qkv(info,xs,mine,theirs,cos,sin):
    _,feat,n=xs[0].shape; w3=mine.shape[2]; hw=w3//3; width=4*feat
    return pl.pallas_call(qkv_kernel,in_specs=[SM]+[VM]*8,out_specs=[VM,VM],
        out_shape=[jax.ShapeDtypeStruct((hw,4*n),bf16),jax.ShapeDtypeStruct((2*hw,4*n),bf16)],
        scratch_shapes=[pltpu.VMEM((width,w3),bf16),pltpu.VMEM((w3,width),bf16),pltpu.VMEM((width,n),bf16)],
        name="qkv")(info,*xs,mine,theirs,cos,sin)

def finish_kernel(info, dq_ref, own_ref, got_ref, x0,x1,x2,x3, mine_ref, theirs_ref, cos_ref, sin_ref,
                  d0,d1,d2,d3, keep_ref, give_ref, w_s, x_s, p_s, g_s):
    hw=dq_ref.shape[0]; n=x0.shape[2]; feat=x0.shape[1]; half=mine_ref.shape[1]
    p_s[:hw,:]=dq_ref[...]
    for h in range(hw//HD):
        t=(own_ref[h]+got_ref[h].astype(f32)).T
        p_s[hw+h*HD:hw+(h+1)*HD,:]=pair_turn(t[:HD]*LN2,cos_ref[...],-sin_ref[...]).astype(bf16)
        p_s[2*hw+h*HD:2*hw+(h+1)*HD,:]=t[HD:].astype(bf16)
    place_qkv_weights(info,mine_ref,theirs_ref,w_s)
    for k,(xr,dr) in enumerate(((x0,d0),(x1,d1),(x2,d2),(x3,d3))):
        sl=slice(k*n,(k+1)*n)
        base=xor(info[0],k//2)
        for r in range(4):
            part=mm(w_s[r*feat:(r+1)*feat,:],p_s[:,sl])
            dr[xor(r,base)]=part.astype(dr.dtype)
    for k,xr in enumerate((x0,x1,x2,x3)):
        place_tokens(info,xr,k//2,x_s.at[:,k*n:(k+1)*n])
    g_s[...]=mm(x_s[...],p_s[...],NT)
    c=info[3]; mc=info[2]
    for r in range(4):
        for h in range(2):
            block=g_s[(2*r+h)*half:(2*r+h+1)*half,:]
            @pl.when(c==h)
            def _(): keep_ref[xor(r,mc)]=block
            @pl.when(c!=h)
            def _(): give_ref[xor(r,xor(mc,1))]=block.astype(bf16)

def finish(info,dq,own,got,xs,mine,theirs,cos,sin):
    _,feat,n=xs[0].shape; w3=mine.shape[2]; hw=w3//3; width=4*feat; half=mine.shape[1]
    part=[jax.ShapeDtypeStruct((4,feat,n),f32)]+[jax.ShapeDtypeStruct((4,feat,n),bf16)]*3
    return pl.pallas_call(finish_kernel,in_specs=[SM]+[VM]*11,out_specs=[VM]*6,
        out_shape=part+[jax.ShapeDtypeStruct((4,half,w3),f32),jax.ShapeDtypeStruct((4,half,w3),bf16)],
        scratch_shapes=[pltpu.VMEM((width,w3),bf16),pltpu.VMEM((width,4*n),bf16),pltpu.VMEM((w3,4*n),bf16),pltpu.VMEM((width,w3),f32)],
        name="finish")(info,dq,own,got,*xs,mine,theirs,cos,sin)

def middle_kernel(info, a0,a1,a2,a3, x_ref, c0,c1,c2,c3, ag_ref,
                  mixed_ref, e0,e1,e2,e3, g1_ref, attnT_ref, hidT_ref, outT_ref, bl_ref, act_ref, il_ref, norm_ref,
                  win, woT, wo, ns, gp_s, t_s, f_s, sems):
    row=info[0]; zy=info[1]
    feat=a0.shape[0]; n=a0.shape[1]; width=4*feat; ffc=ag_ref.shape[2]; half=feat//2; fh=ffc//2
    copies=[]
    def go(src,dst,s): pltpu.make_async_copy(src,dst,sems.at[s]).start()
    for g in range(2):
        for r in range(4):
            for col in range(4):
                b=(g*4+r)*4+col
                for j in range(3):
                    o=(col*2+g)*half+j*(half//3)
                    go(ag_ref.at[b,2*half:2*half+half//3,j*256:(j+1)*256],wo.at[r,o:o+half//3,:],0)
    for r in range(4):
        go(ag_ref.at[r*4,ag_ref.shape[1]-16:,:],ns.at[r],3)
    for g in range(2):
        for r in range(4):
            for col in range(4):
                b=(g*4+r)*4+col
                go(ag_ref.at[b,0:half,:],win.at[r*feat+g*half:r*feat+(g+1)*half,col*ffc:(col+1)*ffc],1)
    for g in range(2):
        for r in range(4):
            for col in range(4):
                b=(g*4+r)*4+col
                for t in range(2):
                    o=(col*2+g)*fh
                    go(ag_ref.at[b,half:2*half,t*fh:(t+1)*fh],woT.at[r*feat+t*half:r*feat+(t+1)*half,o:o+fh],2)
    def group_of(k):
        other=xor(zy,k)
        return (other%2)*2+other//2
    for k,ar in enumerate((a0,a1,a2,a3)):
        attnT_ref[rows_at(group_of(k),feat,64),:]=ar[...]
    for i in range(4):
        t_s[rows_at(xor(i,row),feat,64),:]=x_ref[i]
    attn=attnT_ref[...].T
    x=t_s[...].T.astype(f32)
    pltpu.make_async_copy(wo,wo,sems.at[0]).wait()
    pltpu.make_async_copy(ns,ns,sems.at[3]).wait()
    def vector(which):
        out=[]
        for r in range(4):
            v=ns[r].astype(f32)[0:3,which*feat:(which+1)*feat]
            out.append(jnp.sum(v,axis=0,keepdims=True))
        return jnp.concatenate(out,axis=1)
    gain1=vector(0); shift1=vector(1); gain2=vector(2); shift2=vector(3)
    branch=jnp.concatenate([mm(attn,wo[r])[:,:feat] for r in range(4)],axis=1)
    def stats(v):
        mean=jnp.sum(v,axis=1,keepdims=True)*(1.0/width)
        var=jnp.sum(v*v,axis=1,keepdims=True)*(1.0/width)-mean*mean
        inv=lax.rsqrt(var+1e-5)
        return (v-mean)*inv,inv
    cent1,inv1=stats(x+branch)
    hidden=cent1*gain1+shift1
    hid=hidden.astype(bf16)
    hidT_ref[...]=hid.T
    pltpu.make_async_copy(win,win,sems.at[1]).wait()
    pltpu.make_async_copy(woT,woT,sems.at[2]).wait()
    f_s[...]=jnp.zeros_like(f_s)
    nb=2; bw=ffc//nb
    def forward(j,carry):
        sl=pl.ds(pl.multiple_of(j*bw,128),bw)
        inner=mm(hid,win[:,sl])
        cdf=0.5+0.5*lax.erf(inner*0.7071067811865476)
        act=(inner*cdf).astype(bf16)
        gp_s[:,sl]=cdf+inner*(jnp.exp(inner*inner*-0.5)*0.3989422804014327)
        act_ref[:,sl]=act
        f_s[...]+=mm(act,woT[:,sl],NT)
        return carry
    lax.fori_loop(0,4*nb,forward,0)
    cent2,inv2=stats(hidden+f_s[...])
    t_s[...]=(cent2*gain2+shift2).astype(bf16).T
    for i in range(4):
        mixed_ref[i]=t_s[rows_at(xor(i,row),feat,64),:]
    for k,cr in enumerate((c0,c1,c2,c3)):
        t_s[rows_at(xor(k,row),feat,64),:]=cr[...]
    valid=(lax.broadcasted_iota(jnp.int32,(n,1),0)<info[4]).astype(f32)
    cot=t_s[...].T.astype(f32)*valid
    norm_ref[...]=jnp.zeros_like(norm_ref)
    norm_ref[2:3,:]=jnp.sum(cot*cent2,axis=0,keepdims=True)
    norm_ref[3:4,:]=jnp.sum(cot,axis=0,keepdims=True)
    def back(e,cent,inv):
        first=jnp.sum(e,axis=1,keepdims=True)*(1.0/width)
        second=jnp.sum(e*cent,axis=1,keepdims=True)*(1.0/width)
        return inv*(e-first-cent*second)
    grad2=back(cot*gain2,cent2,inv2)
    low=grad2.astype(bf16)
    outT_ref[...]=low.T
    f_s[...]=grad2
    def backward(j,carry):
        sl=pl.ds(pl.multiple_of(j*bw,128),bw)
        il=(mm(low,woT[:,sl])*gp_s[:,sl]).astype(bf16)
        il_ref[:,sl]=il
        f_s[...]+=mm(il,win[:,sl],NT)
        return carry
    lax.fori_loop(0,4*nb,backward,0)
    gh=f_s[...]
    norm_ref[0:1,:]=jnp.sum(gh*cent1,axis=0,keepdims=True)
    norm_ref[1:2,:]=jnp.sum(gh,axis=0,keepdims=True)
    grad1=back(gh*gain1,cent1,inv1)
    bl=grad1.astype(bf16)
    padded=jnp.concatenate([bl,jnp.zeros((n,256-feat),bf16)],axis=1)
    da=jnp.zeros((width,n),f32)
    for r in range(4):
        piece=padded[:,r*feat:r*feat+256]
        bl_ref[r]=piece
        da=da+mm(wo[r],piece,NT)
    t_s[...]=da.astype(bf16)
    for k,er in enumerate((e0,e1,e2,e3)):
        er[...]=t_s[rows_at(group_of(k),feat,64),:]
    f2=grad1.T
    for r in range(4):
        g1_ref[xor(r,row)]=f2[r*feat:(r+1)*feat]

def middle(info,attn_parts,x_own,cot_parts,ag):
    feat,n=attn_parts[0].shape; width=4*feat; ff=4*ag.shape[2]
    S=jax.ShapeDtypeStruct
    return pl.pallas_call(middle_kernel,in_specs=[SM]+[VM]*9+[HB],out_specs=[VM]*13,
        out_shape=[S((4,feat,n),bf16)]+[S((feat,n),bf16)]*4+[S((4,feat,n),f32),S((width,n),bf16),S((width,n),bf16),S((width,n),bf16),
                   S((4,n,256),bf16),S((n,ff),bf16),S((n,ff),bf16),S((8,width),f32)],
        scratch_shapes=[pltpu.VMEM((width,ff),bf16),pltpu.VMEM((width,ff),bf16),pltpu.VMEM((4,width,256),bf16),pltpu.VMEM((4,16,width),bf16),
                        pltpu.VMEM((n,ff),f32),pltpu.VMEM((width,n),bf16),pltpu.VMEM((n,width),f32),pltpu.SemaphoreType.DMA((4,))],
        compiler_params=pltpu.CompilerParams(vmem_limit_bytes=56*1024*1024),
        name="middle")(info,*attn_parts,x_own,*cot_parts,ag)

def destination(info,g,r,y):
    return (xor(g,info[5])*2+xor(y,info[6]))*4+xor(r,info[0])

def outer_grad_kernel(info, outT_ref, act_ref, keep_ref, give_ref):
    col=pl.program_id(0); y=col//2; same=(col%2)==info[3]
    half=keep_ref.shape[1]; fh=act_ref.shape[1]//2; feat=2*half
    for g in range(2):
        value=mm(outT_ref[...],act_ref[:,g*fh:(g+1)*fh]).astype(bf16)
        for ref,cond in ((keep_ref,same),(give_ref,jnp.logical_not(same))):
            @pl.when(cond)
            def _():
                for r in range(4):
                    d=destination(info,g,r,y)
                    ref[d,:,:fh]=value[r*feat:r*feat+half]
                    ref[d,:,fh:]=value[r*feat+half:(r+1)*feat]

def outer_grad(info,outT,act):
    width,n=outT.shape; ffc=act.shape[1]//4
    S=jax.ShapeDtypeStruct((16,width//8,ffc),bf16)
    whole=pl.BlockSpec((16,width//8,ffc),lambda i:(0,0,0))
    return pl.pallas_call(outer_grad_kernel,grid=(4,),in_specs=[SM,pl.BlockSpec((width,n),lambda i:(0,0)),pl.BlockSpec((n,ffc),lambda i:(0,i))],
        out_specs=[whole,whole],out_shape=[S,S],name="outer_grad")(info,outT,act)

def inner_grad_kernel(info, hidT_ref, il_ref, attnT_ref, bl_ref, norm_ref, keep_ref, give_ref):
    col=pl.program_id(0); y=col//2; same=(col%2)==info[3]
    half=hidT_ref.shape[0]//8; feat=2*half; third=half//3
    value=mm(hidT_ref[...],il_ref[...]).astype(bf16)
    rows=attnT_ref[rows_at(col,feat,64),:]
    outs=[mm(rows,bl_ref[r]).astype(bf16) for r in range(4)]
    norms=[]
    for r in range(4):
        line=jnp.concatenate([norm_ref[i:i+1,r*feat:(r+1)*feat] for i in range(4)],axis=1)
        norms.append(jnp.concatenate([line,jnp.zeros((15,line.shape[1]),f32)],axis=0).astype(bf16))
    for ref,cond in ((keep_ref,same),(give_ref,jnp.logical_not(same))):
        @pl.when(cond)
        def _():
            for g in range(2):
                for r in range(4):
                    d=destination(info,g,r,y)
                    ref[d,:half,:]=value[r*feat+g*half:r*feat+(g+1)*half]
                    for j in range(3):
                        ref[d,half:half+third,j*256:(j+1)*256]=outs[r][g*half+j*third:g*half+(j+1)*third]
                    ref[d,half+third:,:]=norms[r]

def inner_grad(info,hidT,il,attnT,bl,norm):
    width,n=hidT.shape; ffc=il.shape[1]//4; half=width//8; rows=half+half//3+16
    S=jax.ShapeDtypeStruct((16,rows,ffc),bf16)
    whole=pl.BlockSpec((16,rows,ffc),lambda i:(0,0,0)); fix=pl.BlockSpec((width,n),lambda i:(0,0))
    return pl.pallas_call(inner_grad_kernel,grid=(4,),in_specs=[SM,fix,pl.BlockSpec((n,ffc),lambda i:(0,i)),fix,pl.BlockSpec((4,n,256),lambda i:(0,0,0)),pl.BlockSpec((8,width),lambda i:(0,0))],
        out_specs=[whole,whole],out_shape=[S,S],name="inner_grad")(info,hidT,il,attnT,bl,norm)

def exchange4(blocks, axes):
    parts = [blocks[0]]
    for step in range(1, 4):
        parts.append(lax.ppermute(blocks[step], axes, [(i, i ^ step) for i in range(4)]))
    return parts


def core_swap(value):
    return lax.ppermute(value, "cc", [(0, 1), (1, 0)])


def swap_by(blocks, index):
    pairs = blocks.reshape((2, 2) + blocks.shape[1:])
    pairs = jnp.where((index // 2) == 1, pairs[::-1], pairs)
    pairs = jnp.where((index % 2) == 1, pairs[:, ::-1], pairs)
    return pairs.reshape(blocks.shape)


def dp_gather(value):
    if lax.axis_size("dp") != 2:
        return lax.all_gather(value, "dp", axis=0, tiled=True)
    other = lax.ppermute(value, "dp", [(0, 1), (1, 0)])
    first = lax.axis_index("dp") == 0
    return jnp.concatenate([jnp.where(first, value, other), jnp.where(first, other, value)], axis=0)


def dp_reduce(value):
    if lax.axis_size("dp") != 2:
        return lax.psum_scatter(value.astype(bf16), "dp", scatter_dimension=0, tiled=True).astype(f32)
    half = value.shape[0] // 2
    second = lax.axis_index("dp") == 1
    keep = jnp.where(second, value[half:], value[:half])
    send = jnp.where(second, value[:half], value[half:]).astype(bf16)
    return keep + lax.ppermute(send, "dp", [(0, 1), (1, 0)]).astype(f32)


def group_route(rounds, inverse):
    pairs = []
    for m in range(2):
        for z in range(2):
            for y in range(2):
                for c in range(2):
                    source = ((m * 2 + z) * 2 + y) * 2 + c
                    target = (((m ^ rounds[0]) * 2 + c) * 2 + y) * 2 + (z ^ rounds[1])
                    pairs.append((target, source) if inverse else (source, target))
    return pairs


def pack_outer(part):
    turned = part.T
    half = turned.shape[0] // 2
    return jnp.concatenate([turned[:half], turned[half:]], axis=1)


def unpack_outer(packed):
    wide = packed.shape[1] // 2
    return jnp.concatenate([packed[:, :wide], packed[:, wide:]], axis=0).T


def pack_output(part):
    third = part.shape[0] // 3
    padded = jnp.pad(part, ((0, 0), (0, 256 - part.shape[1])))
    return jnp.concatenate([padded[j * third : (j + 1) * third] for j in range(3)], axis=1)


def unpack_output(packed, feat):
    return jnp.concatenate([packed[:, j * 256 : j * 256 + feat] for j in range(3)], axis=0)


def pack_norms(first_gain, first_shift, second_gain, second_shift):
    line = jnp.concatenate([first_gain, first_shift, second_gain, second_shift])
    high = lax.reduce_precision(line, 8, 7)
    middle_part = lax.reduce_precision(line - high, 8, 7)
    rest = line - high - middle_part
    rows = jnp.stack([high, middle_part, rest]).astype(bf16)
    return jnp.pad(rows, ((0, 13), (0, 0)))


def gather_weights(w_output, w_inner, w_outer, norms):
    if lax.axis_size("dp") == 2:
        packed = jnp.concatenate([w_inner, pack_outer(w_outer), pack_output(w_output), norms], axis=0)
        return lax.all_gather(packed, EVERY)
    inner, outer, output = (lax.all_gather(w, "dp", axis=0, tiled=True) for w in (w_inner, w_outer, w_output))
    halves = []
    for g in range(2):
        parts = [w.reshape((2, w.shape[0] // 2) + w.shape[1:])[g] for w in (inner, outer, output)]
        halves.append(jnp.concatenate([parts[0], pack_outer(parts[1]), pack_output(parts[2]), norms], axis=0))
    whole = lax.all_gather(jnp.stack(halves), GROUP)
    return jnp.concatenate([whole[:, 0], whole[:, 1]], axis=0)


def add_parts(parts):
    total = parts[0].astype(f32)
    for part in parts[1:]:
        total = total + part.astype(f32)
    return total


def reduce_blocks(keep, give):
    got = core_swap(give)
    core = (keep.astype(f32) + got.astype(f32)).astype(bf16)
    core = core.reshape((4, 4) + core.shape[1:])
    if lax.axis_size("dp") == 2:
        plane = [add_parts(exchange4(core, ("dp", "cy"))).astype(bf16)]
    else:
        plane = []
        for g in range(2):
            other = lax.ppermute(core[2 * g + 1], "cy", [(0, 1), (1, 0)])
            plane.append(add_parts([core[2 * g], other]).astype(bf16))
    return [add_parts(exchange4(p, ROW)) for p in plane]


def local(
    tokens, w_query, w_key, w_value, w_output, w_inner, w_outer,
    first_gain, first_shift, second_gain, second_shift, seq_lengths, out_grad,
):
    feat = tokens.shape[1]
    cols = tokens.shape[2]
    half = cols // 2
    head_width = w_query.shape[1]
    two = lax.axis_size("dp") == 2
    row = lax.axis_index(ROW)
    group = lax.axis_index("dp")
    m = lax.axis_index("rm")
    z = lax.axis_index("rz")
    y = lax.axis_index("cy")
    c = lax.axis_index("cc")
    length = lax.dynamic_index_in_dim(seq_lengths[m], group, keepdims=False)
    own_start = (y * 2 + c) * cols + z * half
    info = jnp.stack([
        row, z * 2 + y, m * 2 + c, c, length - own_start, group if two else 0 * group, y, 0 * y,
    ]).astype(jnp.int32)

    weights = gather_weights(
        w_output, w_inner, w_outer, pack_norms(first_gain, first_shift, second_gain, second_shift)
    )

    def to_row_order(array):
        blocks = array.reshape(2, feat, 2, half).transpose(0, 2, 1, 3).reshape(4, feat, half)
        return swap_by(blocks, row)

    def from_row_order(parts):
        back = swap_by(jnp.stack(parts), row)
        return back.reshape(2, 2, feat, half).transpose(0, 2, 1, 3).reshape(2, feat, cols)

    x_own = jnp.stack(exchange4(to_row_order(tokens), ROW))
    xs = exchange4([x_own] * 4, SQUARE)

    qkv_rows = dp_gather(jnp.concatenate([w_query, w_key, w_value], axis=1))
    row_halves = qkv_rows.reshape(2, feat // 2, 3 * head_width)
    pieces = []
    for r1 in range(2):
        for r2 in range(2):
            part = jnp.where((z ^ r2) == 0, row_halves[0], row_halves[1])
            pieces.append(lax.ppermute(part, GROUP, group_route((r1, r2), False)))
    mine = jnp.stack(pieces)
    theirs = core_swap(mine)

    starts = []
    for kc in range(2):
        for k in range(4):
            starts.append(((y ^ (k % 2)) * 2 + (c ^ kc)) * cols + (z ^ (k // 2)) * half)
    positions = (jnp.stack(starts)[:, None] + jnp.arange(half, dtype=jnp.int32)[None, :]).reshape(-1)
    invalid = jnp.where(positions < length, 0.0, masked_score)
    bias = jnp.where(jnp.arange(HD)[:, None] == 0, invalid[None, :], 0.0).astype(bf16)
    frequency = 10000.0 ** (-2.0 * jnp.arange(HD // 2, dtype=f32) / HD)
    angles = frequency[:, None] * positions[: 4 * half].astype(f32)[None, :]
    cosine = jnp.repeat(jnp.cos(angles), 2, axis=0)
    sines = jnp.sin(angles)
    sine = jnp.stack([-sines, sines], axis=1).reshape(HD, 4 * half)

    q_rot, kv_own = qkv(info, xs, mine, theirs, cosine, sine)
    kv_other = core_swap(kv_own)
    out, log_totals, *lows = attend(q_rot, kv_own, kv_other, bias)
    attn_parts = exchange4(lows, SQUARE)
    cot_parts = exchange4(to_row_order(out_grad), ROW)
    mixed, e0, e1, e2, e3, grad_one, attn_t, hidden_t, outer_t, branch_low, act_low, inner_low, norm_sums = middle(
        info, attn_parts, x_own, cot_parts, weights
    )
    grads = exchange4([e0, e1, e2, e3], SQUARE)
    outer_sums = reduce_blocks(*outer_grad(info, outer_t, act_low))
    inner_sums = reduce_blocks(*inner_grad(info, hidden_t, inner_low, attn_t, branch_low, norm_sums))
    mixed_out = from_row_order(exchange4(mixed, ROW))

    dq, dkv_own, dkv_give = attend_back(
        q_rot, kv_own, kv_other, bias, out, log_totals, grads, cosine, sine
    )
    dkv_got = core_swap(dkv_give)
    d0, d1, d2, d3, keep, give = finish(info, dq, dkv_own, dkv_got, xs, mine, theirs, cosine, sine)
    d_x = add_parts([grad_one] + exchange4([d0, d1, d2, d3], SQUARE)).astype(bf16)
    d_input = from_row_order(exchange4(d_x, ROW)).astype(f32)

    by_round = (keep + core_swap(give).astype(f32)).astype(bf16)
    got = []
    for r1 in range(2):
        for r2 in range(2):
            got.append(
                lax.ppermute(by_round[r1 * 2 + r2], GROUP, group_route((r1, r2), True)).astype(f32)
            )
    lower = got[0] + got[2]
    upper = got[1] + got[3]
    g_qkv = dp_reduce(
        jnp.concatenate([jnp.where(z == 0, lower, upper), jnp.where(z == 0, upper, lower)], axis=0)
    )

    half_rows = feat // 2
    third = half_rows // 3
    g_outer = jnp.concatenate([unpack_outer(part) for part in outer_sums], axis=0)
    g_inner = jnp.concatenate([part[:half_rows] for part in inner_sums], axis=0)
    g_output = jnp.concatenate(
        [unpack_output(part[half_rows : half_rows + third], feat) for part in inner_sums], axis=0
    )
    g_norms = inner_sums[0][half_rows + third].reshape(4, feat)
    if not two:
        g_outer, g_inner, g_output = (
            lax.psum_scatter(g.astype(bf16), "dp", scatter_dimension=0, tiled=True).astype(f32)
            for g in (g_outer, g_inner, g_output)
        )
        g_norms = lax.psum(g_norms, "dp")

    return (
        mixed_out, d_input,
        g_qkv[:, :head_width], g_qkv[:, head_width : 2 * head_width], g_qkv[:, 2 * head_width :],
        g_output, g_inner, g_outer,
        g_norms[0], g_norms[1], g_norms[2], g_norms[3],
    )


def solution(mesh):
    shape = mesh.devices.shape
    fine = Mesh(mesh.devices.reshape(shape[0], 2, shape[1] // 2, 2, shape[2] // 2), EVERY)
    col = ("cy", "cc")
    acts = P(None, ROW, ("dp",) + col)
    by_row = P(ROW + ("dp",), col)
    by_col = P(col + ("dp",), ROW)
    vec = P(ROW)
    return jax.shard_map(
        local,
        mesh=fine,
        in_specs=(
            acts, by_row, by_row, by_row, by_col, by_row, by_col, vec, vec, vec, vec, P(), acts,
        ),
        out_specs=(
            acts, acts, by_row, by_row, by_row, by_col, by_row, by_col, vec, vec, vec, vec,
        ),
        check_vma=False,
    )
```

time: 654 us -> 347 us (0.53); the launches traced: 644 us -> 346 us
  local copies, waits for them, and re-layouts: 175 us -> 16.7 us
  matrix products: 108 us -> 0 us
  Pallas kernels: 0 us -> 78.7 us
  waiting for transfers between devices: 218 us -> 157 us
  other arithmetic: 77 us -> 16.9 us
  starting transfers between devices: 48.3 us -> 61.5 us
    reduce_scatter x3 -> x0, waiting for transfers between devices: 134 us -> none  [spread(): return lax.psum_scatter(value.astype(bf16), EVERY, scatter_dimension=0)]
    dot_general x34 -> x0, matrix products: 108 us -> none  [dot(): lax.dot_general(left, right, ((dims[0], dims[1]), ((), ())), preferred_el...]
    ppermute x21 -> x36, waiting for transfers between devices: 22.8 us -> 130 us  [exchange4(): lax.ppermute(blocks[step], axes, [(i, i ^ step) for i in range(4)])]
    pallas_call x0 -> x7, Pallas kernels: none -> 78.7 us  [the longest x1 21.3 us: middle(): pl.pallas_call(middle_kernel, in_specs=[SM] + [VM] * 9 + [HB], out_specs=...]
    reshape x20 -> x5, local copies, waits for them, and re-layouts: 76.8 us -> 3.59 us  [the longest x2 1.05 us: to_row_order(): array.reshape(2, feat, 2, half).transpose(0, 2, 1, 3).reshape(4, feat, half)]
    ppermute x21 -> x36, starting transfers between devices: 28.4 us -> 52.4 us  [exchange4(): lax.ppermute(blocks[step], axes, [(i, i ^ step) for i in range(4)])]
    another operation x22 -> x8, other arithmetic: 22.5 us -> 2.23 us  [the longest x2 1.22 us: from_row_order(): back = swap_by(jnp.stack(parts), row)]
    convert_element_type x12 -> x1, local copies, waits for them, and re-layouts: 20.1 us -> 0.99 us  [local(): d_input = from_row_order(exchange4(d_x, ROW)).astype(f32)]
  transfers between devices with their start and end apart: 47 -> 53, of which waited for: 17 -> 27; matrix products, arithmetic and copies ran while one was open for 45% -> 6% of each run, Pallas kernels for 0% -> 11%
where the time goes in v2:
time: 347 us; the launch traced here: 346 us
  waiting for transfers between devices  157 us (45%)
  Pallas kernels  78.7 us (23%)
  starting transfers between devices  61.5 us (18%)
  other arithmetic  16.9 us (5%)
  local copies, waits for them, and re-layouts  16.7 us (5%)
  between operations  15.4 us (4%)
    ppermute x36, waiting for transfers between devices, exchange4(): lax.ppermute(blocks[step], axes, [(i, i ^ step) for i in range(4)])  130 us
    ppermute x36, starting transfers between devices, exchange4(): lax.ppermute(blocks[step], axes, [(i, i ^ step) for i in range(4)])  52.4 us
    pallas_call x1, Pallas kernels, middle(): pl.pallas_call(middle_kernel, in_specs=[SM] + [VM] * 9 + [HB], out_specs=...  21.3 us
    pallas_call x1, Pallas kernels, attend_back(): pl.pallas_call(attend_back_kernel, grid=(heads, 4 // QB), in_specs=[hb, k...  19.9 us
    pallas_call x1, Pallas kernels, attend(): pl.pallas_call(attend_kernel, grid=(heads, 4 // QB), in_specs=[pl.BlockSp...  11.5 us
    all_gather x1, waiting for transfers between devices, gather_weights(): return lax.all_gather(packed, EVERY)  10.2 us
    ppermute x4, waiting for transfers between devices, local(): pieces.append(lax.ppermute(part, GROUP, group_route((r1, r2), False)))  9.37 us
    pallas_call x1, Pallas kernels, inner_grad(): pl.pallas_call(inner_grad_kernel, grid=(4,), in_specs=[SM, fix, pl.BlockS...  7.6 us
  transfers between devices with their start and end apart: 53, of which 27 were waited for; matrix products, arithmetic and copies ran while one was open for 6% of the time, Pallas kernels for 11%

profile of v2, /device:TPU:0, one launch (start us, length us, event | category | flops | bytes accessed | tf_op | source)
XLA Modules:
  0.0 346.0 jit_solution(2963411428545097422)
XLA Ops:
  9.8 1.7 pad_maximum_fusion.4
  12.5 3.0 collective-permute-start.6
  16.7 3.7 %collective-permute-start.2 = (bf16[192,256]{1,0:T(8,128)(2,1)S(1)}, bf16[192,256]{1,0:T(8,128)(2,1)S(1)}, u32[]{:S(2)}, u32[]{:S(2)}) collective-permute-start(bf16[192,256]{1,0:T(8,128)(2,1)S(1)} %get-tuple-element.118), channel_id=1, source_target_pairs={{0,12},{4,8},{8,4},{12,0},{1,13},{5,9},{9,5},{13,1},{2,14},{6,10},... | collective-permute-start | bytes 294920 | tf_op jit(solution)/shard_map/ppermute | solution.py:386
  22.1 3.6 %collective-permute-start.18 = (bf16[192,256]{1,0:T(8,128)(2,1)S(1)}, bf16[192,256]{1,0:T(8,128)(2,1)S(1)}, u32[]{:S(2)}, u32[]{:S(2)}) collective-permute-start(bf16[192,256]{1,0:T(8,128)(2,1)S(1)} %get-tuple-element.113), channel_id=1, source_target_pairs={{0,12},{4,8},{8,4},{12,0},{1,13},{5,9},{9,5},{13,1},{2,14},{6,10},... | collective-permute-start | bytes 294920 | tf_op jit(solution)/shard_map/ppermute | solution.py:386
  26.8 13.1 %collective-permute-done.1 = bf16[192,256]{1,0:T(8,128)(2,1)S(1)} collective-permute-done((bf16[192,256]{1,0:T(8,128)(2,1)S(1)}, bf16[192,256]{1,0:T(8,128)(2,1)S(1)}, u32[]{:S(2)}, u32[]{:S(2)}) %collective-permute-start.1) | collective-permute-done | bytes 98336 | tf_op jit(solution)/shard_map/ppermute | solution.py:386
  40.0 9.4 %collective-permute-done.9 = bf16[96,576]{1,0:T(8,128)(2,1)S(1)} collective-permute-done((bf16[96,576]{1,0:T(8,128)(2,1)S(1)}, bf16[96,576]{1,0:T(8,128)(2,1)S(1)}, u32[]{:S(2)}, u32[]{:S(2)}) %collective-permute-start.9) | collective-permute-done | bytes 110624 | tf_op jit(solution)/shard_map/ppermute | solution.py:537
  50.4 1.9 collective-permute-start.4
  58.8 12.0 %collective-permute-done.5.x3 = bf16[4,192,256]{2,1,0:T(8,128)(2,1)S(1)} collective-permute-done((bf16[4,192,256]{2,1,0:T(8,128)(2,1)S(1)}, bf16[4,192,256]{2,1,0:T(8,128)(2,1)S(1)}, u32[]{:S(2)}, u32[]{:S(2)}) %collective-permute-start.5) | collective-permute-done | bytes 393248 | tf_op jit(solution)/shard_map/ppermute | solution.py:386
  70.8 15.1 %collective-permute-done.4.x2 = bf16[4,192,256]{2,1,0:T(8,128)(2,1)S(1)} collective-permute-done((bf16[4,192,256]{2,1,0:T(8,128)(2,1)S(1)}, bf16[4,192,256]{2,1,0:T(8,128)(2,1)S(1)}, u32[]{:S(2)}, u32[]{:S(2)}) %collective-permute-start.4) | collective-permute-done | bytes 393248 | tf_op jit(solution)/shard_map/ppermute | solution.py:386
  87.7 3.9 %qkv.1 = (bf16[192,1024]{1,0:T(8,128)(2,1)}, bf16[384,1024]{1,0:T(8,128)(2,1)}) custom-call(s32[8]{0:T(128)} %stack.121.info, bf16[4,192,256]{2,1,0:T(8,128)(2,1)} %copy-done.1, bf16[4,192,256]{2,1,0:T(8,128)(2,1)} %copy-done.8, bf16[4,192,256]{2,1,0:T(8,128)(2,1)} %copy-done.7, bf16[4,192,256]{2,1,0:T(8,128)(2,1)} %copy-done.6, ...), custom_call_target="tpu_custom_call" | custom-call | tf_op jit(solution)/shard_map/qkv/pallas_call | solution.py:167
  93.1 1.9 collective-permute-done.12.kx_ref.vx_ref
  96.0 11.5 %attend.1 = (f32[192,1024]{1,0:T(8,128)}, f32[3,1,1024]{2,1,0:T(1,128)}, bf16[192,256]{1,0:T(8,128)(2,1)}, bf16[192,256]{1,0:T(8,128)(2,1)}, bf16[192,256]{1,0:T(8,128)(2,1)}, /*index=5*/bf16[192,256]{1,0:T(8,128)(2,1)}) custom-call(bf16[192,1024]{1,0:T(8,128)(2,1)} %get-tuple-element.46.q_ref, bf16[384,1024]{1,0:T(8,128)(2,1)} %get-tuple-element.47.ko_ref.vo_ref, ...), custom_call_target="tpu_custom_call" | custom-call | tf_op jit(solution)/shard_map/attend/pallas_call | solution.py:70
  108.9 1.8 collective-permute-start.14
  111.1 4.1 %collective-permute-done.13.a1 = bf16[192,256]{1,0:T(8,128)(2,1)S(1)} collective-permute-done((bf16[192,256]{1,0:T(8,128)(2,1)}, bf16[192,256]{1,0:T(8,128)(2,1)S(1)}, u32[]{:S(2)}, u32[]{:S(2)}) %collective-permute-start.13) | collective-permute-done | bytes 98336 | tf_op jit(solution)/shard_map/ppermute | solution.py:386
  115.8 5.8 %collective-permute-done.15.a3 = bf16[192,256]{1,0:T(8,128)(2,1)S(1)} collective-permute-done((bf16[192,256]{1,0:T(8,128)(2,1)}, bf16[192,256]{1,0:T(8,128)(2,1)S(1)}, u32[]{:S(2)}, u32[]{:S(2)}) %collective-permute-start.15) | collective-permute-done | bytes 98336 | tf_op jit(solution)/shard_map/ppermute | solution.py:386
  121.6 10.2 %all-gather.3.cloned.1.call-done = bf16[7680,768]{1,0:T(8,128)(2,1)} async-done(((bf16[240,768]{1,0:T(8,128)(2,1)}), bf16[7680,768]{1,0:T(8,128)(2,1)}) %all-gather.3.cloned.1.call-update) | async-done | bytes 11796496 | tf_op jit(solution)/shard_map/all_gather | solution.py:464
  131.9 21.3 %middle.1 = (bf16[4,192,256]{2,1,0:T(8,128)(2,1)}, bf16[192,256]{1,0:T(8,128)(2,1)}, bf16[192,256]{1,0:T(8,128)(2,1)}, bf16[192,256]{1,0:T(8,128)(2,1)}, bf16[19...) custom-call(s32[8]{0:T(128)} %stack.121.info, ...), custom_call_target="tpu_custom_call" | custom-call | tf_op jit(solution)/shard_map/middle/pallas_call | solution.py:324
  154.8 1.9 collective-permute-start.24
  156.8 1.7 collective-permute-done.22.g1
  158.9 2.8 collective-permute-done.24.g3
  162.4 19.9 %attend_back.1 = (bf16[192,1024]{1,0:T(8,128)(2,1)}, f32[3,1024,128]{2,1,0:T(8,128)}, bf16[3,1024,128]{2,1,0:T(8,128)(2,1)}) custom-call(bf16[192,1024]{1,0:T(8,128)(2,1)} %get-tuple-element.46.q_ref, bf16[384,1024]{1,0:T(8,128)(2,1)} %get-tuple-element.47.ko_ref.vo_ref, bf16[384,1024]{1,0:T(8,128)(2,1)} %get-tuple-element.47.ko_ref.vo_ref, ...), custom_call_target="tpu_custom_call" | custom-call | tf_op jit(solution)/shard_map/attend_back/pallas_call | solution.py:121
  182.4 7.0 %outer_grad.1 = (bf16[16,96,768]{2,1,0:T(8,128)(2,1)}, bf16[16,96,768]{2,1,0:T(8,128)(2,1)}) custom-call(s32[8]{0:T(128)} %stack.121.info, bf16[768,256]{1,0:T(8,128)(2,1)} %get-tuple-element.76.outT_ref, bf16[256,3072]{1,0:T(8,128)(2,1)} %get-tuple-element.77.act_ref), custom_call_target="tpu_custom_call" | custom-call | tf_op jit(solution)/shard_map/outer_grad/pallas_call | solution.py:352
  190.5 1.7 collective-permute-start.21
  192.9 2.0 collective-permute-start.19
  195.8 7.4 %finish.1 = (f32[4,192,256]{2,1,0:T(8,128)}, bf16[4,192,256]{2,1,0:T(8,128)(2,1)}, bf16[4,192,256]{2,1,0:T(8,128)(2,1)}, bf16[4,192,256]{2,1,0:T(8,128)(2,1)}, f...) custom-call(s32[8]{0:T(128)} %stack.121.info, bf16[192,1024]{1,0:T(8,128)(2,1)} %get-tuple-element.60.dq_ref, ...), custom_call_target="tpu_custom_call" | custom-call | tf_op jit(solution)/shard_map/finish/pallas_call | solution.py:202
  203.9 2.8 collective-permute-start.28
  206.7 7.6 %inner_grad.1 = (bf16[16,144,768]{2,1,0:T(8,128)(2,1)}, bf16[16,144,768]{2,1,0:T(8,128)(2,1)}) custom-call(s32[8]{0:T(128)} %stack.121.info, bf16[768,256]{1,0:T(8,128)(2,1)} %get-tuple-element.69.hidT_ref, bf16[256,3072]{1,0:T(8,128)(2,1)} %get-tuple-element.70.il_ref, bf16[768,256]{1,0:T(8,128)(2,1)} %get-tuple-element.71.attnT_ref, ...), custom_call_target="tpu_custom_call" | custom-call | tf_op jit(solution)/shard_map/inner_grad/pallas_call | solution.py:380
  216.7 6.6 %collective-permute-done.28 = bf16[4,192,256]{2,1,0:T(8,128)(2,1)} collective-permute-done((bf16[4,192,256]{2,1,0:T(8,128)(2,1)}, bf16[4,192,256]{2,1,0:T(8,128)(2,1)}, u32[]{:S(2)}, u32[]{:S(2)}) %collective-permute-start.28) | collective-permute-done | bytes 393248 | tf_op jit(solution)/shard_map/ppermute | solution.py:386
  223.4 1.9 add_convert_fusion.5
  225.4 1.7 collective-permute-start.31
  227.2 2.6 collective-permute-start.29
  230.0 2.9 collective-permute-done.31
  236.7 2.4 add_convert_fusion.1
  239.6 3.9 %collective-permute-start.48 = (bf16[4,96,768]{2,1,0:T(8,128)(2,1)S(1)}, bf16[4,96,768]{2,1,0:T(8,128)(2,1)S(1)}, u32[]{:S(2)}, u32[]{:S(2)}) collective-permute-start(bf16[4,96,768]{2,1,0:T(8,128)(2,1)S(1)} %get-tuple-element.86), channel_id=1, source_target_pairs={{0,18},{2,16},{16,2},{18,0},{1,19},{3,17},{17,3},{19,1},{4,22},{6,... | collective-permute-start | bytes 1769480 | tf_op jit(solution)/shard_map/ppermute | solution.py:386
  244.8 2.3 collective-permute-start.34
  248.9 4.9 %collective-permute-done.34 = bf16[96,576]{1,0:T(8,128)(2,1)S(1)} collective-permute-done((bf16[96,576]{1,0:T(8,128)(2,1)S(1)}, bf16[96,576]{1,0:T(8,128)(2,1)S(1)}, u32[]{:S(2)}, u32[]{:S(2)}) %collective-permute-start.34) | collective-permute-done | bytes 110624 | tf_op jit(solution)/shard_map/ppermute | solution.py:580
  253.9 12.6 %collective-permute-done.46 = bf16[4,96,768]{2,1,0:T(8,128)(2,1)S(1)} collective-permute-done((bf16[4,96,768]{2,1,0:T(8,128)(2,1)S(1)}, bf16[4,96,768]{2,1,0:T(8,128)(2,1)S(1)}, u32[]{:S(2)}, u32[]{:S(2)}) %collective-permute-start.46) | collective-permute-done | bytes 589856 | tf_op jit(solution)/shard_map/ppermute | solution.py:386
  266.5 2.4 collective-permute-done.47
  271.3 3.2 collective-permute-start.41
  276.0 3.7 %collective-permute-start.51 = (bf16[96,768]{1,0:T(8,128)(2,1)S(1)}, bf16[96,768]{1,0:T(8,128)(2,1)S(1)}, u32[]{:S(2)}, u32[]{:S(2)}) collective-permute-start(bf16[96,768]{1,0:T(8,128)(2,1)S(1)} %get-tuple-element.92), channel_id=1, source_target_pairs={{0,12},{4,8},{8,4},{12,0},{1,13},{5,9},{9,5},{13,1},{2,14},{6,10},... | collective-permute-start | bytes 442376 | tf_op jit(solution)/shard_map/ppermute | solution.py:386
  281.2 3.3 collective-permute-start.50
  286.1 6.2 %collective-permute-done.50 = bf16[96,768]{1,0:T(8,128)(2,1)S(1)} collective-permute-done((bf16[96,768]{1,0:T(8,128)(2,1)S(1)}, bf16[96,768]{1,0:T(8,128)(2,1)S(1)}, u32[]{:S(2)}, u32[]{:S(2)}) %collective-permute-start.50) | collective-permute-done | bytes 147488 | tf_op jit(solution)/shard_map/ppermute | solution.py:386
  292.4 18.6 %collective-permute-done.39 = bf16[4,144,768]{2,1,0:T(8,128)(2,1)S(1)} collective-permute-done((bf16[4,144,768]{2,1,0:T(8,128)(2,1)S(1)}, bf16[4,144,768]{2,1,0:T(8,128)(2,1)S(1)}, u32[]{:S(2)}, u32[]{:S(2)}) %collective-permute-start.39) | collective-permute-done | bytes 884768 | tf_op jit(solution)/shard_map/ppermute | solution.py:386
  310.9 1.8 collective-permute-done.40
  313.4 3.4 collective-permute-start.44
  317.6 7.6 %collective-permute-done.42 = bf16[144,768]{1,0:T(8,128)(2,1)S(1)} collective-permute-done((bf16[144,768]{1,0:T(8,128)(2,1)S(1)}, bf16[144,768]{1,0:T(8,128)(2,1)S(1)}, u32[]{:S(2)}, u32[]{:S(2)}) %collective-permute-start.42) | collective-permute-done | bytes 221216 | tf_op jit(solution)/shard_map/ppermute | solution.py:386
  325.2 2.2 collective-permute-done.44
  327.4 9.6 %collective-permute-done.43 = bf16[144,768]{1,0:T(8,128)(2,1)S(1)} collective-permute-done((bf16[144,768]{1,0:T(8,128)(2,1)S(1)}, bf16[144,768]{1,0:T(8,128)(2,1)S(1)}, u32[]{:S(2)}, u32[]{:S(2)}) %collective-permute-start.43) | collective-permute-done | bytes 221216 | tf_op jit(solution)/shard_map/ppermute | solution.py:386
  (199 shorter events, 47.9 us)
Async XLA Ops:
  7.2 124.7 %all-gather.3.cloned.1.call-start = ((), (), s32[]{:S(2)}) async-start(), calls=%async_computation | async-start | bytes 12165120 | tf_op jit(solution)/shard_map/all_gather | solution.py:464
  12.5 13.4 %collective-permute-start.6 = (bf16[96,576]{1,0:T(8,128)(2,1)S(1)}, bf16[96,576]{1,0:T(8,128)(2,1)S(1)}, u32[]{:S(2)}, u32[]{:S(2)}) collective-permute-start(bf16[96,576]{1,0:T(8,128)(2,1)S(1)} %pad_maximum_fusion.6), channel_id=1, source_target_pairs={{0,16},{16,0},{1,17},{17,1},{2,18},{18,2},{3,19},{19,3},{4,20},{20... | collective-permute-start | bytes 331784 | tf_op jit(solution)/shard_map/ppermute | solution.py:404
  16.7 9.4 %collective-permute-start.2 = (bf16[192,256]{1,0:T(8,128)(2,1)S(1)}, bf16[192,256]{1,0:T(8,128)(2,1)S(1)}, u32[]{:S(2)}, u32[]{:S(2)}) collective-permute-start(bf16[192,256]{1,0:T(8,128)(2,1)S(1)} %get-tuple-element.118), channel_id=1, source_target_pairs={{0,12},{4,8},{8,4},{12,0},{1,13},{5,9},{9,5},{13,1},{2,14},{6,10},... | collective-permute-start | bytes 294920 | tf_op jit(solution)/shard_map/ppermute | solution.py:386
  20.4 19.5 %collective-permute-start.1 = (bf16[192,256]{1,0:T(8,128)(2,1)S(1)}, bf16[192,256]{1,0:T(8,128)(2,1)S(1)}, u32[]{:S(2)}, u32[]{:S(2)}) collective-permute-start(bf16[192,256]{1,0:T(8,128)(2,1)S(1)} %get-tuple-element.119), channel_id=1, source_target_pairs={{0,8},{4,12},{8,0},{12,4},{1,9},{5,13},{9,1},{13,5},{2,10},{6,14},... | collective-permute-start | bytes 294920 | tf_op jit(solution)/shard_map/ppermute | solution.py:386
  20.4 19.5 %collective-permute-start = (bf16[192,256]{1,0:T(8,128)(2,1)S(1)}, bf16[192,256]{1,0:T(8,128)(2,1)S(1)}, u32[]{:S(2)}, u32[]{:S(2)}) collective-permute-start(bf16[192,256]{1,0:T(8,128)(2,1)S(1)} %get-tuple-element.120), channel_id=1, source_target_pairs={{0,4},{4,0},{8,12},{12,8},{1,5},{5,1},{9,13},{13,9},{2,6},{6,2},{1... | collective-permute-start | bytes 294920 | tf_op jit(solution)/shard_map/ppermute | solution.py:386
  22.1 88.7 %collective-permute-start.18 = (bf16[192,256]{1,0:T(8,128)(2,1)S(1)}, bf16[192,256]{1,0:T(8,128)(2,1)S(1)}, u32[]{:S(2)}, u32[]{:S(2)}) collective-permute-start(bf16[192,256]{1,0:T(8,128)(2,1)S(1)} %get-tuple-element.113), channel_id=1, source_target_pairs={{0,12},{4,8},{8,4},{12,0},{1,13},{5,9},{9,5},{13,1},{2,14},{6,10},... | collective-permute-start | bytes 294920 | tf_op jit(solution)/shard_map/ppermute | solution.py:386
  26.0 23.3 %collective-permute-start.9 = (bf16[96,576]{1,0:T(8,128)(2,1)S(1)}, bf16[96,576]{1,0:T(8,128)(2,1)S(1)}, u32[]{:S(2)}, u32[]{:S(2)}) collective-permute-start(bf16[96,576]{1,0:T(8,128)(2,1)S(1)} %get-tuple-element.126), channel_id=1, source_target_pairs={{0,8},{1,12},{2,10},{3,14},{4,9},{5,13},{6,11},{7,15},{8,0},{9,4},... | collective-permute-start | bytes 331784 | tf_op jit(solution)/shard_map/ppermute | solution.py:537
  26.1 24.3 %collective-permute-start.7 = (bf16[96,576]{1,0:T(8,128)(2,1)S(1)}, bf16[96,576]{1,0:T(8,128)(2,1)S(1)}, u32[]{:S(2)}, u32[]{:S(2)}) collective-permute-start(bf16[96,576]{1,0:T(8,128)(2,1)S(1)} %get-tuple-element.126), channel_id=1, source_target_pairs={{0,0},{1,4},{2,2},{3,6},{4,1},{5,5},{6,3},{7,7},{8,8},{9,12},{10,1... | collective-permute-start | bytes 331784 | tf_op jit(solution)/shard_map/ppermute | solution.py:537
  39.9 12.4 %collective-permute-start.10 = (bf16[96,576]{1,0:T(8,128)(2,1)S(1)}, bf16[96,576]{1,0:T(8,128)(2,1)S(1)}, u32[]{:S(2)}, u32[]{:S(2)}) collective-permute-start(bf16[96,576]{1,0:T(8,128)(2,1)S(1)} %get-tuple-element.127), channel_id=1, source_target_pairs={{0,9},{1,13},{2,11},{3,15},{4,8},{5,12},{6,10},{7,14},{8,1},{9,5},... | collective-permute-start | bytes 331784 | tf_op jit(solution)/shard_map/ppermute | solution.py:537
  39.9 13.0 %collective-permute-start.8 = (bf16[96,576]{1,0:T(8,128)(2,1)S(1)}, bf16[96,576]{1,0:T(8,128)(2,1)S(1)}, u32[]{:S(2)}, u32[]{:S(2)}) collective-permute-start(bf16[96,576]{1,0:T(8,128)(2,1)S(1)} %get-tuple-element.127), channel_id=1, source_target_pairs={{0,1},{1,5},{2,3},{3,7},{4,0},{5,4},{6,2},{7,6},{8,9},{9,13},{10,1... | collective-permute-start | bytes 331784 | tf_op jit(solution)/shard_map/ppermute | solution.py:537
  49.3 21.5 %collective-permute-start.5 = (bf16[4,192,256]{2,1,0:T(8,128)(2,1)S(1)}, bf16[4,192,256]{2,1,0:T(8,128)(2,1)S(1)}, u32[]{:S(2)}, u32[]{:S(2)}) collective-permute-start(bf16[4,192,256]{2,1,0:T(8,128)(2,1)S(1)} %pad_maximum_fusion.1.x0.x_ref), channel_id=1, source_target_pairs={{0,6},{2,4},{4,2},{6,0},{1,7},{3,5},{5,3},{7,1},{8,14},{10,12},{12... | collective-permute-start | bytes 1179656 | tf_op jit(solution)/shard_map/ppermute | solution.py:386
  50.4 35.5 %collective-permute-start.4 = (bf16[4,192,256]{2,1,0:T(8,128)(2,1)S(1)}, bf16[4,192,256]{2,1,0:T(8,128)(2,1)S(1)}, u32[]{:S(2)}, u32[]{:S(2)}) collective-permute-start(bf16[4,192,256]{2,1,0:T(8,128)(2,1)S(1)} %pad_maximum_fusion.1.x0.x_ref), channel_id=1, source_target_pairs={{0,4},{2,6},{4,0},{6,2},{1,5},{3,7},{5,1},{7,3},{8,12},{10,14},{12... | collective-permute-start | bytes 1179656 | tf_op jit(solution)/shard_map/ppermute | solution.py:386
  52.3 33.6 %collective-permute-start.3 = (bf16[4,192,256]{2,1,0:T(8,128)(2,1)S(1)}, bf16[4,192,256]{2,1,0:T(8,128)(2,1)S(1)}, u32[]{:S(2)}, u32[]{:S(2)}) collective-permute-start(bf16[4,192,256]{2,1,0:T(8,128)(2,1)S(1)} %pad_maximum_fusion.1.x0.x_ref), channel_id=1, source_target_pairs={{0,2},{2,0},{4,6},{6,4},{1,3},{3,1},{5,7},{7,5},{8,10},{10,8},{12,... | collective-permute-start | bytes 1179656 | tf_op jit(solution)/shard_map/ppermute | solution.py:386
  52.9 33.0 %collective-permute-start.11 = (bf16[4,96,576]{2,1,0:T(8,128)(2,1)S(1)}, bf16[4,96,576]{2,1,0:T(8,128)(2,1)S(1)}, u32[]{:S(2)}, u32[]{:S(2)}) collective-permute-start(bf16[4,96,576]{2,1,0:T(8,128)(2,1)S(1)} %pad_maximum_fusion.mine_ref), channel_id=1, source_target_pairs={{0,1},{1,0},{2,3},{3,2},{4,5},{5,4},{6,7},{7,6},{8,9},{9,8},{10,11... | collective-permute-start | bytes 1327112 | tf_op jit(solution)/shard_map/ppermute | solution.py:391
  70.8 40.2 %collective-permute-start.17 = (bf16[192,256]{1,0:T(8,128)(2,1)S(1)}, bf16[192,256]{1,0:T(8,128)(2,1)S(1)}, u32[]{:S(2)}, u32[]{:S(2)}) collective-permute-start(bf16[192,256]{1,0:T(8,128)(2,1)S(1)} %get-tuple-element.114), channel_id=1, source_target_pairs={{0,8},{4,12},{8,0},{12,4},{1,9},{5,13},{9,1},{13,5},{2,10},{6,14},... | collective-permute-start | bytes 294920 | tf_op jit(solution)/shard_map/ppermute | solution.py:386
  85.9 25.1 %collective-permute-start.16 = (bf16[192,256]{1,0:T(8,128)(2,1)S(1)}, bf16[192,256]{1,0:T(8,128)(2,1)S(1)}, u32[]{:S(2)}, u32[]{:S(2)}) collective-permute-start(bf16[192,256]{1,0:T(8,128)(2,1)S(1)} %get-tuple-element.115), channel_id=1, source_target_pairs={{0,4},{4,0},{8,12},{12,8},{1,5},{5,1},{9,13},{13,9},{2,6},{6,2},{1... | collective-permute-start | bytes 294920 | tf_op jit(solution)/shard_map/ppermute | solution.py:386
  107.5 7.7 %collective-permute-start.13 = (bf16[192,256]{1,0:T(8,128)(2,1)}, bf16[192,256]{1,0:T(8,128)(2,1)S(1)}, u32[]{:S(2)}, u32[]{:S(2)}) collective-permute-start(bf16[192,256]{1,0:T(8,128)(2,1)} %get-tuple-element.49), channel_id=1, source_target_pairs={{0,2},{2,0},{4,6},{6,4},{1,3},{3,1},{5,7},{7,5},{8,10},{10,8},{12,... | collective-permute-start | bytes 294920 | tf_op jit(solution)/shard_map/ppermute | solution.py:386
  108.9 6.9 %collective-permute-start.14 = (bf16[192,256]{1,0:T(8,128)(2,1)}, bf16[192,256]{1,0:T(8,128)(2,1)S(1)}, u32[]{:S(2)}, u32[]{:S(2)}) collective-permute-start(bf16[192,256]{1,0:T(8,128)(2,1)} %get-tuple-element.50), channel_id=1, source_target_pairs={{0,4},{2,6},{4,0},{6,2},{1,5},{3,7},{5,1},{7,3},{8,12},{10,14},{12... | collective-permute-start | bytes 294920 | tf_op jit(solution)/shard_map/ppermute | solution.py:386
  110.8 10.8 %collective-permute-start.15 = (bf16[192,256]{1,0:T(8,128)(2,1)}, bf16[192,256]{1,0:T(8,128)(2,1)S(1)}, u32[]{:S(2)}, u32[]{:S(2)}) collective-permute-start(bf16[192,256]{1,0:T(8,128)(2,1)} %get-tuple-element.51), channel_id=1, source_target_pairs={{0,6},{2,4},{4,2},{6,0},{1,7},{3,5},{5,3},{7,1},{8,14},{10,12},{12... | collective-permute-start | bytes 294920 | tf_op jit(solution)/shard_map/ppermute | solution.py:386
  154.8 6.9 %collective-permute-start.24 = (bf16[192,256]{1,0:T(8,128)(2,1)}, bf16[192,256]{1,0:T(8,128)(2,1)S(1)}, u32[]{:S(2)}, u32[]{:S(2)}) collective-permute-start(bf16[192,256]{1,0:T(8,128)(2,1)} %get-tuple-element.59), channel_id=1, source_target_pairs={{0,6},{2,4},{4,2},{6,0},{1,7},{3,5},{5,3},{7,1},{8,14},{10,12},{12... | collective-permute-start | bytes 294920 | tf_op jit(solution)/shard_map/ppermute | solution.py:386
  182.3 12.6 %collective-permute-start.25 = (bf16[3,1024,128]{2,1,0:T(8,128)(2,1)}, bf16[3,1024,128]{2,1,0:T(8,128)(2,1)S(1)}, u32[]{:S(2)}, u32[]{:S(2)}) collective-permute-start(bf16[3,1024,128]{2,1,0:T(8,128)(2,1)} %get-tuple-element.62), channel_id=1, source_target_pairs={{0,1},{1,0},{2,3},{3,2},{4,5},{5,4},{6,7},{7,6},{8,9},{9,8},{10,11... | collective-permute-start | bytes 2359304 | tf_op jit(solution)/shard_map/ppermute | solution.py:391
  189.4 47.3 %collective-permute-start.45 = (bf16[16,96,768]{2,1,0:T(8,128)(2,1)}, bf16[16,96,768]{2,1,0:T(8,128)(2,1)}, u32[]{:S(2)}, u32[]{:S(2)}) collective-permute-start(bf16[16,96,768]{2,1,0:T(8,128)(2,1)} %get-tuple-element.79), channel_id=1, source_target_pairs={{0,1},{1,0},{2,3},{3,2},{4,5},{5,4},{6,7},{7,6},{8,9},{9,8},{10,11... | collective-permute-start | bytes 7077896 | tf_op jit(solution)/shard_map/ppermute | solution.py:391
  190.5 13.0 %collective-permute-start.21 = (bf16[192,256]{1,0:T(8,128)(2,1)S(1)}, bf16[192,256]{1,0:T(8,128)(2,1)S(1)}, u32[]{:S(2)}, u32[]{:S(2)}) collective-permute-start(bf16[192,256]{1,0:T(8,128)(2,1)S(1)} %get-tuple-element.110), channel_id=1, source_target_pairs={{0,12},{4,8},{8,4},{12,0},{1,13},{5,9},{9,5},{13,1},{2,14},{6,10},... | collective-permute-start | bytes 294920 | tf_op jit(solution)/shard_map/ppermute | solution.py:386
  192.2 11.7 %collective-permute-start.20 = (bf16[192,256]{1,0:T(8,128)(2,1)S(1)}, bf16[192,256]{1,0:T(8,128)(2,1)S(1)}, u32[]{:S(2)}, u32[]{:S(2)}) collective-permute-start(bf16[192,256]{1,0:T(8,128)(2,1)S(1)} %get-tuple-element.111), channel_id=1, source_target_pairs={{0,8},{4,12},{8,0},{12,4},{1,9},{5,13},{9,1},{13,5},{2,10},{6,14},... | collective-permute-start | bytes 294920 | tf_op jit(solution)/shard_map/ppermute | solution.py:386
  192.9 21.4 %collective-permute-start.19 = (bf16[192,256]{1,0:T(8,128)(2,1)S(1)}, bf16[192,256]{1,0:T(8,128)(2,1)S(1)}, u32[]{:S(2)}, u32[]{:S(2)}) collective-permute-start(bf16[192,256]{1,0:T(8,128)(2,1)S(1)} %get-tuple-element.112), channel_id=1, source_target_pairs={{0,4},{4,0},{8,12},{12,8},{1,5},{5,1},{9,13},{13,9},{2,6},{6,2},{1... | collective-permute-start | bytes 294920 | tf_op jit(solution)/shard_map/ppermute | solution.py:386
  203.2 12.9 %collective-permute-start.26 = (bf16[4,192,256]{2,1,0:T(8,128)(2,1)}, bf16[4,192,256]{2,1,0:T(8,128)(2,1)}, u32[]{:S(2)}, u32[]{:S(2)}) collective-permute-start(bf16[4,192,256]{2,1,0:T(8,128)(2,1)} %get-tuple-element.64), channel_id=1, source_target_pairs={{0,2},{2,0},{4,6},{6,4},{1,3},{3,1},{5,7},{7,5},{8,10},{10,8},{12,... | collective-permute-start | bytes 1179656 | tf_op jit(solution)/shard_map/ppermute | solution.py:386
  203.6 13.2 %collective-permute-start.27 = (bf16[4,192,256]{2,1,0:T(8,128)(2,1)}, bf16[4,192,256]{2,1,0:T(8,128)(2,1)}, u32[]{:S(2)}, u32[]{:S(2)}) collective-permute-start(bf16[4,192,256]{2,1,0:T(8,128)(2,1)} %get-tuple-element.65), channel_id=1, source_target_pairs={{0,4},{2,6},{4,0},{6,2},{1,5},{3,7},{5,1},{7,3},{8,12},{10,14},{12... | collective-permute-start | bytes 1179656 | tf_op jit(solution)/shard_map/ppermute | solution.py:386
  203.9 19.5 %collective-permute-start.28 = (bf16[4,192,256]{2,1,0:T(8,128)(2,1)}, bf16[4,192,256]{2,1,0:T(8,128)(2,1)}, u32[]{:S(2)}, u32[]{:S(2)}) collective-permute-start(bf16[4,192,256]{2,1,0:T(8,128)(2,1)} %get-tuple-element.66), channel_id=1, source_target_pairs={{0,6},{2,4},{4,2},{6,0},{1,7},{3,5},{5,3},{7,1},{8,14},{10,12},{12... | collective-permute-start | bytes 1179656 | tf_op jit(solution)/shard_map/ppermute | solution.py:386
  215.0 54.3 %collective-permute-start.38 = (bf16[16,144,768]{2,1,0:T(8,128)(2,1)}, bf16[16,144,768]{2,1,0:T(8,128)(2,1)S(1)}, u32[]{:S(2)}, u32[]{:S(2)}) collective-permute-start(bf16[16,144,768]{2,1,0:T(8,128)(2,1)} %get-tuple-element.75), channel_id=1, source_target_pairs={{0,1},{1,0},{2,3},{3,2},{4,5},{5,4},{6,7},{7,6},{8,9},{9,8},{10,11... | collective-permute-start | bytes 10616840 | tf_op jit(solution)/shard_map/ppermute | solution.py:391
  216.2 11.0 %collective-permute-start.32 = (bf16[4,96,576]{2,1,0:T(8,128)(2,1)}, bf16[4,96,576]{2,1,0:T(8,128)(2,1)S(1)}, u32[]{:S(2)}, u32[]{:S(2)}) collective-permute-start(bf16[4,96,576]{2,1,0:T(8,128)(2,1)} %get-tuple-element.68), channel_id=1, source_target_pairs={{0,1},{1,0},{2,3},{3,2},{4,5},{5,4},{6,7},{7,6},{8,9},{9,8},{10,11... | collective-permute-start | bytes 1327112 | tf_op jit(solution)/shard_map/ppermute | solution.py:391
  225.4 7.5 %collective-permute-start.31 = (bf16[192,256]{1,0:T(8,128)(2,1)S(1)}, bf16[192,256]{1,0:T(8,128)(2,1)S(1)}, u32[]{:S(2)}, u32[]{:S(2)}) collective-permute-start(bf16[192,256]{1,0:T(8,128)(2,1)S(1)} %get-tuple-element.106), channel_id=1, source_target_pairs={{0,12},{4,8},{8,4},{12,0},{1,13},{5,9},{9,5},{13,1},{2,14},{6,10},... | collective-permute-start | bytes 294920 | tf_op jit(solution)/shard_map/ppermute | solution.py:386
  227.1 8.2 %collective-permute-start.30 = (bf16[192,256]{1,0:T(8,128)(2,1)S(1)}, bf16[192,256]{1,0:T(8,128)(2,1)S(1)}, u32[]{:S(2)}, u32[]{:S(2)}) collective-permute-start(bf16[192,256]{1,0:T(8,128)(2,1)S(1)} %get-tuple-element.107), channel_id=1, source_target_pairs={{0,8},{4,12},{8,0},{12,4},{1,9},{5,13},{9,1},{13,5},{2,10},{6,14},... | collective-permute-start | bytes 294920 | tf_op jit(solution)/shard_map/ppermute | solution.py:386
  227.2 8.6 %collective-permute-start.29 = (bf16[192,256]{1,0:T(8,128)(2,1)S(1)}, bf16[192,256]{1,0:T(8,128)(2,1)S(1)}, u32[]{:S(2)}, u32[]{:S(2)}) collective-permute-start(bf16[192,256]{1,0:T(8,128)(2,1)S(1)} %get-tuple-element.108), channel_id=1, source_target_pairs={{0,4},{4,0},{8,12},{12,8},{1,5},{5,1},{9,13},{13,9},{2,6},{6,2},{1... | collective-permute-start | bytes 294920 | tf_op jit(solution)/shard_map/ppermute | solution.py:386
  235.3 8.2 %collective-permute-start.36 = (bf16[96,576]{1,0:T(8,128)(2,1)S(1)}, bf16[96,576]{1,0:T(8,128)(2,1)S(1)}, u32[]{:S(2)}, u32[]{:S(2)}) collective-permute-start(bf16[96,576]{1,0:T(8,128)(2,1)S(1)} %get-tuple-element.95), channel_id=1, source_target_pairs={{8,0},{12,1},{10,2},{14,3},{9,4},{13,5},{11,6},{15,7},{0,8},{4,9},... | collective-permute-start | bytes 331784 | tf_op jit(solution)/shard_map/ppermute | solution.py:580
  235.8 9.0 %collective-permute-start.35 = (bf16[96,576]{1,0:T(8,128)(2,1)S(1)}, bf16[96,576]{1,0:T(8,128)(2,1)S(1)}, u32[]{:S(2)}, u32[]{:S(2)}) collective-permute-start(bf16[96,576]{1,0:T(8,128)(2,1)S(1)} %get-tuple-element.96), channel_id=1, source_target_pairs={{0,0},{4,1},{2,2},{6,3},{1,4},{5,5},{3,6},{7,7},{8,8},{12,9},{10,1... | collective-permute-start | bytes 331784 | tf_op jit(solution)/shard_map/ppermute | solution.py:580
  239.2 27.4 %collective-permute-start.46 = (bf16[4,96,768]{2,1,0:T(8,128)(2,1)S(1)}, bf16[4,96,768]{2,1,0:T(8,128)(2,1)S(1)}, u32[]{:S(2)}, u32[]{:S(2)}) collective-permute-start(bf16[4,96,768]{2,1,0:T(8,128)(2,1)S(1)} %get-tuple-element.85), channel_id=1, source_target_pairs={{0,2},{2,0},{16,18},{18,16},{1,3},{3,1},{17,19},{19,17},{4,6},{6,4... | collective-permute-start | bytes 1769480 | tf_op jit(solution)/shard_map/ppermute | solution.py:386
  239.6 26.9 %collective-permute-start.48 = (bf16[4,96,768]{2,1,0:T(8,128)(2,1)S(1)}, bf16[4,96,768]{2,1,0:T(8,128)(2,1)S(1)}, u32[]{:S(2)}, u32[]{:S(2)}) collective-permute-start(bf16[4,96,768]{2,1,0:T(8,128)(2,1)S(1)} %get-tuple-element.86), channel_id=1, source_target_pairs={{0,18},{2,16},{16,2},{18,0},{1,19},{3,17},{17,3},{19,1},{4,22},{6,... | collective-permute-start | bytes 1769480 | tf_op jit(solution)/shard_map/ppermute | solution.py:386
  243.5 25.4 %collective-permute-start.47 = (bf16[4,96,768]{2,1,0:T(8,128)(2,1)S(1)}, bf16[4,96,768]{2,1,0:T(8,128)(2,1)S(1)}, u32[]{:S(2)}, u32[]{:S(2)}) collective-permute-start(bf16[4,96,768]{2,1,0:T(8,128)(2,1)S(1)} %get-tuple-element.87), channel_id=1, source_target_pairs={{0,16},{2,18},{16,0},{18,2},{1,17},{3,19},{17,1},{19,3},{4,20},{6,... | collective-permute-start | bytes 1769480 | tf_op jit(solution)/shard_map/ppermute | solution.py:386
  244.8 9.0 %collective-permute-start.34 = (bf16[96,576]{1,0:T(8,128)(2,1)S(1)}, bf16[96,576]{1,0:T(8,128)(2,1)S(1)}, u32[]{:S(2)}, u32[]{:S(2)}) collective-permute-start(bf16[96,576]{1,0:T(8,128)(2,1)S(1)} %get-tuple-element.97), channel_id=1, source_target_pairs={{9,0},{13,1},{11,2},{15,3},{8,4},{12,5},{10,6},{14,7},{1,8},{5,9},... | collective-permute-start | bytes 331784 | tf_op jit(solution)/shard_map/ppermute | solution.py:580
  253.8 22.1 %collective-permute-start.37 = (bf16[96,576]{1,0:T(8,128)(2,1)S(1)}, bf16[96,576]{1,0:T(8,128)(2,1)S(1)}, u32[]{:S(2)}, u32[]{:S(2)}) collective-permute-start(bf16[96,576]{1,0:T(8,128)(2,1)S(1)} %select_convert_fusion.1), channel_id=1, source_target_pairs={{0,16},{16,0},{1,17},{17,1},{2,18},{18,2},{3,19},{19,3},{4,20},{20... | collective-permute-start | bytes 331784 | tf_op jit(solution)/shard_map/ppermute | solution.py:416
  270.5 40.4 %collective-permute-start.39 = (bf16[4,144,768]{2,1,0:T(8,128)(2,1)S(1)}, bf16[4,144,768]{2,1,0:T(8,128)(2,1)S(1)}, u32[]{:S(2)}, u32[]{:S(2)}) collective-permute-start(bf16[4,144,768]{2,1,0:T(8,128)(2,1)S(1)} %get-tuple-element.82), channel_id=1, source_target_pairs={{0,2},{2,0},{16,18},{18,16},{1,3},{3,1},{17,19},{19,17},{4,6},{6,4... | collective-permute-start | bytes 2654216 | tf_op jit(solution)/shard_map/ppermute | solution.py:386
  271.3 39.7 %collective-permute-start.41 = (bf16[4,144,768]{2,1,0:T(8,128)(2,1)S(1)}, bf16[4,144,768]{2,1,0:T(8,128)(2,1)S(1)}, u32[]{:S(2)}, u32[]{:S(2)}) collective-permute-start(bf16[4,144,768]{2,1,0:T(8,128)(2,1)S(1)} %get-tuple-element.83), channel_id=1, source_target_pairs={{0,18},{2,16},{16,2},{18,0},{1,19},{3,17},{17,3},{19,1},{4,22},{6,... | collective-permute-start | bytes 2654216 | tf_op jit(solution)/shard_map/ppermute | solution.py:386
  274.5 38.2 %collective-permute-start.40 = (bf16[4,144,768]{2,1,0:T(8,128)(2,1)S(1)}, bf16[4,144,768]{2,1,0:T(8,128)(2,1)S(1)}, u32[]{:S(2)}, u32[]{:S(2)}) collective-permute-start(bf16[4,144,768]{2,1,0:T(8,128)(2,1)S(1)} %get-tuple-element.84), channel_id=1, source_target_pairs={{0,16},{2,18},{16,0},{18,2},{1,17},{3,19},{17,1},{19,3},{4,20},{6,... | collective-permute-start | bytes 2654216 | tf_op jit(solution)/shard_map/ppermute | solution.py:386
  276.0 10.1 %collective-permute-start.51 = (bf16[96,768]{1,0:T(8,128)(2,1)S(1)}, bf16[96,768]{1,0:T(8,128)(2,1)S(1)}, u32[]{:S(2)}, u32[]{:S(2)}) collective-permute-start(bf16[96,768]{1,0:T(8,128)(2,1)S(1)} %get-tuple-element.92), channel_id=1, source_target_pairs={{0,12},{4,8},{8,4},{12,0},{1,13},{5,9},{9,5},{13,1},{2,14},{6,10},... | collective-permute-start | bytes 442376 | tf_op jit(solution)/shard_map/ppermute | solution.py:386
  281.2 11.1 %collective-permute-start.50 = (bf16[96,768]{1,0:T(8,128)(2,1)S(1)}, bf16[96,768]{1,0:T(8,128)(2,1)S(1)}, u32[]{:S(2)}, u32[]{:S(2)}) collective-permute-start(bf16[96,768]{1,0:T(8,128)(2,1)S(1)} %get-tuple-element.93), channel_id=1, source_target_pairs={{0,8},{4,12},{8,0},{12,4},{1,9},{5,13},{9,1},{13,5},{2,10},{6,14},... | collective-permute-start | bytes 442376 | tf_op jit(solution)/shard_map/ppermute | solution.py:386
  313.3 11.9 %collective-permute-start.42 = (bf16[144,768]{1,0:T(8,128)(2,1)S(1)}, bf16[144,768]{1,0:T(8,128)(2,1)S(1)}, u32[]{:S(2)}, u32[]{:S(2)}) collective-permute-start(bf16[144,768]{1,0:T(8,128)(2,1)S(1)} %get-tuple-element.88), channel_id=1, source_target_pairs={{0,4},{4,0},{8,12},{12,8},{1,5},{5,1},{9,13},{13,9},{2,6},{6,2},{1... | collective-permute-start | bytes 663560 | tf_op jit(solution)/shard_map/ppermute | solution.py:386
  313.4 14.1 %collective-permute-start.44 = (bf16[144,768]{1,0:T(8,128)(2,1)S(1)}, bf16[144,768]{1,0:T(8,128)(2,1)S(1)}, u32[]{:S(2)}, u32[]{:S(2)}) collective-permute-start(bf16[144,768]{1,0:T(8,128)(2,1)S(1)} %get-tuple-element.89), channel_id=1, source_target_pairs={{0,12},{4,8},{8,4},{12,0},{1,13},{5,9},{9,5},{13,1},{2,14},{6,10},... | collective-permute-start | bytes 663560 | tf_op jit(solution)/shard_map/ppermute | solution.py:386
  316.7 20.3 %collective-permute-start.43 = (bf16[144,768]{1,0:T(8,128)(2,1)S(1)}, bf16[144,768]{1,0:T(8,128)(2,1)S(1)}, u32[]{:S(2)}, u32[]{:S(2)}) collective-permute-start(bf16[144,768]{1,0:T(8,128)(2,1)S(1)} %get-tuple-element.90), channel_id=1, source_target_pairs={{0,8},{4,12},{8,0},{12,4},{1,9},{5,13},{9,1},{13,5},{2,10},{6,14},... | collective-permute-start | bytes 663560 | tf_op jit(solution)/shard_map/ppermute | solution.py:386
  (38 other events, 505.3 us)
Sparse Core Ops, SparseCore 0:
  11.7 120.1 all-gather.2

commit v3 on v2

--- a/solution.py
+++ b/solution.py
@@ -1,3 +1,5 @@
+import functools
+
 import jax
 import jax.numpy as jnp
 from jax import lax
@@ -72,12 +74,13 @@
         out_specs=[pl.BlockSpec((HD,n),lambda h,b:(h,b)),pl.BlockSpec((1,1,n),lambda h,b:(h,0,b))]+[lowspec]*4,
         out_shape=[jax.ShapeDtypeStruct((width,n4),f32),jax.ShapeDtypeStruct((heads,1,n4),f32)]+[jax.ShapeDtypeStruct((width,n4//4),bf16)]*4,
         scratch_shapes=[pltpu.VMEM((2*span,2*HD),bf16),pltpu.VMEM((HD,2*span),bf16)],
+        cost_estimate=pl.CostEstimate(flops=4*width*n4//HD*2*span*256,bytes_accessed=4*n4*2*span,transcendentals=heads*n4*2*span),
         name="attend")(q,kv,kv,kvx,kvx,bias)
 
 BKB=512
 def attend_back_kernel(q_ref, ko_ref, vo_ref, kx_ref, vx_ref, bias_ref, o_ref, lse_ref, g0,g1,g2,g3, cos_ref, sin_ref,
                        dq_ref, own_ref, give_ref, kaug, vtm, kall, acc):
-    head=pl.program_id(0); qb=pl.program_id(1)
+    qb=pl.program_id(0)
     span=ko_ref.shape[1]; n=q_ref.shape[1]
     @pl.when(qb==0)
     def _():
@@ -110,19 +113,20 @@
     dq_ref[...]=pair_turn(dq*(HD**-0.5),cos_ref[...],-sin_ref[...]).astype(bf16)
     @pl.when(qb==4//QB-1)
     def _():
-        own_ref[0]=acc[:span,:]
-        give_ref[0]=acc[span:,:].astype(bf16)
-
-def attend_back(q,kv,kvx,bias,o,lse,grads,cos,sin):
+        own_ref[...]=acc[:span,:]
+        give_ref[...]=acc[span:,:].astype(bf16)
+
+def attend_back(head,q,kv,kvx,bias,o,lse,grads,cos,sin):
     width,n4=q.shape; heads=width//HD; n=n4//4*QB; span=kv.shape[1]
-    kspec=pl.BlockSpec((HD,span),lambda h,b:(h,0)); vspec=pl.BlockSpec((HD,span),lambda h,b:(heads+h,0))
-    gspec=pl.BlockSpec((HD,n4//4),lambda h,b:(h,0)); hb=pl.BlockSpec((HD,n),lambda h,b:(h,b)); tb=pl.BlockSpec((HD,n),lambda h,b:(0,b))
-    dspec=pl.BlockSpec((1,span,2*HD),lambda h,b:(h,0,0))
-    return pl.pallas_call(attend_back_kernel,grid=(heads,4//QB),
-        in_specs=[hb,kspec,vspec,kspec,vspec,pl.BlockSpec((HD,2*span),lambda h,b:(0,0)),hb,pl.BlockSpec((1,1,n),lambda h,b:(h,0,b)),gspec,gspec,gspec,gspec,tb,tb],
-        out_specs=[hb,dspec,dspec],
-        out_shape=[jax.ShapeDtypeStruct((width,n4),bf16),jax.ShapeDtypeStruct((heads,span,2*HD),f32),jax.ShapeDtypeStruct((heads,span,2*HD),bf16)],
+    kspec=pl.BlockSpec((HD,span),lambda b:(head,0)); vspec=pl.BlockSpec((HD,span),lambda b:(heads+head,0))
+    gspec=pl.BlockSpec((HD,n4//4),lambda b:(head,0)); hb=pl.BlockSpec((HD,n),lambda b:(head,b)); tb=pl.BlockSpec((HD,n),lambda b:(0,b))
+    dspec=pl.BlockSpec((span,2*HD),lambda b:(0,0))
+    return pl.pallas_call(attend_back_kernel,grid=(4//QB,),
+        in_specs=[hb,kspec,vspec,kspec,vspec,pl.BlockSpec((HD,2*span),lambda b:(0,0)),hb,pl.BlockSpec((1,1,n),lambda b:(head,0,b)),gspec,gspec,gspec,gspec,tb,tb],
+        out_specs=[tb,dspec,dspec],
+        out_shape=[jax.ShapeDtypeStruct((HD,n4),bf16),jax.ShapeDtypeStruct((span,2*HD),f32),jax.ShapeDtypeStruct((span,2*HD),bf16)],
         scratch_shapes=[pltpu.VMEM((2*span,2*HD),bf16),pltpu.VMEM((2*span,2*HD),bf16),pltpu.VMEM((HD,2*span),bf16),pltpu.VMEM((2*span,2*HD),f32)],
+        cost_estimate=pl.CostEstimate(flops=10*n4*2*span*256,bytes_accessed=4*n4*2*span,transcendentals=n4*2*span),
         name="attend_back")(q,kv,kv,kvx,kvx,bias,o,lse,*grads,cos,sin)
 def xor(a,b):
     return lax.bitwise_xor(jnp.asarray(a,jnp.int32),jnp.asarray(b,jnp.int32))
@@ -169,69 +173,76 @@
         scratch_shapes=[pltpu.VMEM((width,w3),bf16),pltpu.VMEM((w3,width),bf16),pltpu.VMEM((width,n),bf16)],
         name="qkv")(info,*xs,mine,theirs,cos,sin)
 
-def finish_kernel(info, dq_ref, own_ref, got_ref, x0,x1,x2,x3, mine_ref, theirs_ref, cos_ref, sin_ref,
-                  d0,d1,d2,d3, keep_ref, give_ref, w_s, x_s, p_s, g_s):
-    hw=dq_ref.shape[0]; n=x0.shape[2]; feat=x0.shape[1]; half=mine_ref.shape[1]
-    p_s[:hw,:]=dq_ref[...]
-    for h in range(hw//HD):
-        t=(own_ref[h]+got_ref[h].astype(f32)).T
-        p_s[hw+h*HD:hw+(h+1)*HD,:]=pair_turn(t[:HD]*LN2,cos_ref[...],-sin_ref[...]).astype(bf16)
-        p_s[2*hw+h*HD:2*hw+(h+1)*HD,:]=t[HD:].astype(bf16)
+def finish_dx_kernel(info, *refs):
+    heads=refs[0].shape[0]
+    del heads
+    (q0,q1,q2,o0,o1,o2,r0,r1,r2,mine_ref,theirs_ref,cos_ref,sin_ref,d0,d1,d2,d3,p_ref,w_s)=refs
+    hw=3*HD; n=d0.shape[2]; feat=d0.shape[1]
     place_qkv_weights(info,mine_ref,theirs_ref,w_s)
-    for k,(xr,dr) in enumerate(((x0,d0),(x1,d1),(x2,d2),(x3,d3))):
+    for h,(qr,orr,rr) in enumerate(((q0,o0,r0),(q1,o1,r1),(q2,o2,r2))):
+        p_ref[h*HD:(h+1)*HD,:]=qr[...]
+        t=(orr[...]+rr[...].astype(f32)).T
+        p_ref[hw+h*HD:hw+(h+1)*HD,:]=pair_turn(t[:HD]*LN2,cos_ref[...],-sin_ref[...]).astype(bf16)
+        p_ref[2*hw+h*HD:2*hw+(h+1)*HD,:]=t[HD:].astype(bf16)
+    for k,dr in ((3,d3),(1,d1),(2,d2),(0,d0)):
         sl=slice(k*n,(k+1)*n)
         base=xor(info[0],k//2)
         for r in range(4):
-            part=mm(w_s[r*feat:(r+1)*feat,:],p_s[:,sl])
-            dr[xor(r,base)]=part.astype(dr.dtype)
+            dr[xor(r,base)]=mm(w_s[r*feat:(r+1)*feat,:],p_ref[:,sl]).astype(dr.dtype)
+
+def finish_dx(info,dqs,owns,gots,mine,theirs,cos,sin):
+    w3=mine.shape[2]; half=mine.shape[1]; feat=2*half; width=4*feat; n=dqs[0].shape[1]//4
+    S=jax.ShapeDtypeStruct
+    return pl.pallas_call(finish_dx_kernel,in_specs=[SM]+[VM]*13,out_specs=[VM]*5,
+        out_shape=[S((4,feat,n),f32)]+[S((4,feat,n),bf16)]*3+[S((w3,4*n),bf16)],
+        scratch_shapes=[pltpu.VMEM((width,w3),bf16)],
+        cost_estimate=pl.CostEstimate(flops=8*width*w3*n,bytes_accessed=8*width*n*4,transcendentals=0),
+        name="finish_dx")(info,*dqs,*owns,*gots,mine,theirs,cos,sin)
+
+def finish_dw_kernel(info, p_ref, x0,x1,x2,x3, keep_ref, give_ref, x_s, g_s):
+    n=x0.shape[2]; half=keep_ref.shape[1]
     for k,xr in enumerate((x0,x1,x2,x3)):
         place_tokens(info,xr,k//2,x_s.at[:,k*n:(k+1)*n])
-    g_s[...]=mm(x_s[...],p_s[...],NT)
+    g_s[...]=mm(x_s[...],p_ref[...],NT)
     c=info[3]; mc=info[2]
     for r in range(4):
-        for h in range(2):
-            block=g_s[(2*r+h)*half:(2*r+h+1)*half,:]
-            @pl.when(c==h)
-            def _(): keep_ref[xor(r,mc)]=block
-            @pl.when(c!=h)
-            def _(): give_ref[xor(r,xor(mc,1))]=block.astype(bf16)
-
-def finish(info,dq,own,got,xs,mine,theirs,cos,sin):
-    _,feat,n=xs[0].shape; w3=mine.shape[2]; hw=w3//3; width=4*feat; half=mine.shape[1]
-    part=[jax.ShapeDtypeStruct((4,feat,n),f32)]+[jax.ShapeDtypeStruct((4,feat,n),bf16)]*3
-    return pl.pallas_call(finish_kernel,in_specs=[SM]+[VM]*11,out_specs=[VM]*6,
-        out_shape=part+[jax.ShapeDtypeStruct((4,half,w3),f32),jax.ShapeDtypeStruct((4,half,w3),bf16)],
-        scratch_shapes=[pltpu.VMEM((width,w3),bf16),pltpu.VMEM((width,4*n),bf16),pltpu.VMEM((w3,4*n),bf16),pltpu.VMEM((width,w3),f32)],
-        name="finish")(info,dq,own,got,*xs,mine,theirs,cos,sin)
-
-def middle_kernel(info, a0,a1,a2,a3, x_ref, c0,c1,c2,c3, ag_ref,
-                  mixed_ref, e0,e1,e2,e3, g1_ref, attnT_ref, hidT_ref, outT_ref, bl_ref, act_ref, il_ref, norm_ref,
-                  win, woT, wo, ns, gp_s, t_s, f_s, sems):
-    row=info[0]; zy=info[1]
-    feat=a0.shape[0]; n=a0.shape[1]; width=4*feat; ffc=ag_ref.shape[2]; half=feat//2; fh=ffc//2
-    copies=[]
+        mine_rows=pl.ds(pl.multiple_of((2*r+c)*half,32),half); their_rows=pl.ds(pl.multiple_of((2*r+1-c)*half,32),half)
+        keep_ref[xor(r,mc)]=g_s[mine_rows,:]
+        give_ref[xor(r,xor(mc,1))]=g_s[their_rows,:].astype(bf16)
+
+def finish_dw(info,proj,xs):
+    _,feat,n=xs[0].shape; w3=proj.shape[0]; width=4*feat; half=feat//2
+    return pl.pallas_call(finish_dw_kernel,in_specs=[SM]+[VM]*5,out_specs=[VM]*2,
+        out_shape=[jax.ShapeDtypeStruct((4,half,w3),f32),jax.ShapeDtypeStruct((4,half,w3),bf16)],
+        scratch_shapes=[pltpu.VMEM((width,4*n),bf16),pltpu.VMEM((width,w3),f32)],
+        cost_estimate=pl.CostEstimate(flops=8*width*w3*n,bytes_accessed=8*width*n*2,transcendentals=0),
+        name="finish_dw")(info,proj,*xs)
+
+def middle_kernel(info, a0,a1,a2,a3, x_ref, c0,c1,c2,c3, *refs):
+    chunk_a=refs[:10]; chunk_b=refs[10:20]
+    (mixed_ref, e0,e1,e2,e3, g1_ref, attnT_ref, hidT_ref, outT_ref, bl_ref, act_ref, il_ref, norm_ref,
+                  win, woT, wo, ns, gp_s, t_s, f_s, sems)=refs[20:]
+    row=info[0]; zy=info[1]; c=info[3]; group=info[5]; y=info[6]
+    feat=a0.shape[0]; n=a0.shape[1]; width=4*feat; ffc=chunk_a[0].shape[2]; half=feat//2; fh=ffc//2; third=half//3
     def go(src,dst,s): pltpu.make_async_copy(src,dst,sems.at[s]).start()
-    for g in range(2):
-        for r in range(4):
-            for col in range(4):
-                b=(g*4+r)*4+col
-                for j in range(3):
-                    o=(col*2+g)*half+j*(half//3)
-                    go(ag_ref.at[b,2*half:2*half+half//3,j*256:(j+1)*256],wo.at[r,o:o+half//3,:],0)
-    for r in range(4):
-        go(ag_ref.at[r*4,ag_ref.shape[1]-16:,:],ns.at[r],3)
-    for g in range(2):
-        for r in range(4):
-            for col in range(4):
-                b=(g*4+r)*4+col
-                go(ag_ref.at[b,0:half,:],win.at[r*feat+g*half:r*feat+(g+1)*half,col*ffc:(col+1)*ffc],1)
-    for g in range(2):
-        for r in range(4):
-            for col in range(4):
-                b=(g*4+r)*4+col
-                for t in range(2):
-                    o=(col*2+g)*fh
-                    go(ag_ref.at[b,half:2*half,t*fh:(t+1)*fh],woT.at[r*feat+t*half:r*feat+(t+1)*half,o:o+fh],2)
+    spots=((0,0,0),(0,1,0),(0,0,1),(0,1,1),(2,1,1))
+    def each(chunk):
+        for kc in range(2):
+            for ref,(first,kx,ky) in zip(chunk[5*kc:5*kc+5],spots):
+                g=xor(group,kx); col=xor(y,ky)*2+xor(c,kc)
+                for i in range(ref.shape[0]):
+                    yield ref.at[i],xor(row,first+i),g,col,(kc,kx,ky,first+i)
+    for ref,r,g,col,_ in each(chunk_a):
+        for j in range(3):
+            go(ref.at[half:half+third,j*256:(j+1)*256],wo.at[r,pl.ds(pl.multiple_of((col*2+g)*half+j*third,16),third),:],0)
+    for ref,r,g,col,where in each(chunk_a):
+        if where[:3]==(0,0,0):
+            go(ref.at[half+third:half+third+16,:],ns.at[r],3)
+    for ref,r,g,col,_ in each(chunk_a):
+        go(ref.at[0:half,:],win.at[pl.ds(pl.multiple_of(r*feat+g*half,16),half),pl.ds(pl.multiple_of(col*ffc,128),ffc)],1)
+    for ref,r,g,col,_ in each(chunk_b):
+        for t in range(2):
+            go(ref.at[:,t*fh:(t+1)*fh],woT.at[pl.ds(pl.multiple_of(r*feat+t*half,16),half),pl.ds(pl.multiple_of((col*2+g)*fh,128),fh)],2)
     def group_of(k):
         other=xor(zy,k)
         return (other%2)*2+other//2
@@ -318,67 +329,66 @@
     for r in range(4):
         g1_ref[xor(r,row)]=f2[r*feat:(r+1)*feat]
 
-def middle(info,attn_parts,x_own,cot_parts,ag):
-    feat,n=attn_parts[0].shape; width=4*feat; ff=4*ag.shape[2]
+def middle(info,attn_parts,x_own,cot_parts,chunk_a,chunk_b):
+    feat,n=attn_parts[0].shape; width=4*feat; ff=4*chunk_a[0].shape[2]
     S=jax.ShapeDtypeStruct
-    return pl.pallas_call(middle_kernel,in_specs=[SM]+[VM]*9+[HB],out_specs=[VM]*13,
+    return pl.pallas_call(middle_kernel,in_specs=[SM]+[VM]*9+[HB]*20,out_specs=[VM]*13,
         out_shape=[S((4,feat,n),bf16)]+[S((feat,n),bf16)]*4+[S((4,feat,n),f32),S((width,n),bf16),S((width,n),bf16),S((width,n),bf16),
                    S((4,n,256),bf16),S((n,ff),bf16),S((n,ff),bf16),S((8,width),f32)],
         scratch_shapes=[pltpu.VMEM((width,ff),bf16),pltpu.VMEM((width,ff),bf16),pltpu.VMEM((4,width,256),bf16),pltpu.VMEM((4,16,width),bf16),
                         pltpu.VMEM((n,ff),f32),pltpu.VMEM((width,n),bf16),pltpu.VMEM((n,width),f32),pltpu.SemaphoreType.DMA((4,))],
         compiler_params=pltpu.CompilerParams(vmem_limit_bytes=56*1024*1024),
-        name="middle")(info,*attn_parts,x_own,*cot_parts,ag)
-
-def destination(info,g,r,y):
-    return (xor(g,info[5])*2+xor(y,info[6]))*4+xor(r,info[0])
-
-def outer_grad_kernel(info, outT_ref, act_ref, keep_ref, give_ref):
-    col=pl.program_id(0); y=col//2; same=(col%2)==info[3]
-    half=keep_ref.shape[1]; fh=act_ref.shape[1]//2; feat=2*half
+        cost_estimate=pl.CostEstimate(flops=12*n*width*ff*2,bytes_accessed=24*width*ff,transcendentals=2*n*ff),
+        name="middle")(info,*attn_parts,x_own,*cot_parts,*chunk_a,*chunk_b)
+
+def outer_grad_kernel(info, outT_ref, act_ref, out_ref):
+    half=out_ref.shape[3]; fh=act_ref.shape[1]//2; feat=2*half
     for g in range(2):
-        value=mm(outT_ref[...],act_ref[:,g*fh:(g+1)*fh]).astype(bf16)
-        for ref,cond in ((keep_ref,same),(give_ref,jnp.logical_not(same))):
-            @pl.when(cond)
-            def _():
-                for r in range(4):
-                    d=destination(info,g,r,y)
-                    ref[d,:,:fh]=value[r*feat:r*feat+half]
-                    ref[d,:,fh:]=value[r*feat+half:(r+1)*feat]
-
-def outer_grad(info,outT,act):
+        gk=xor(g,info[5])
+        for r in range(4):
+            value=mm(outT_ref[r*feat:(r+1)*feat,:],act_ref[:,g*fh:(g+1)*fh]).astype(bf16)
+            rk=xor(r,info[0])
+            out_ref[gk,0,rk,:,:fh]=value[:half]
+            out_ref[gk,0,rk,:,fh:]=value[half:]
+
+def column(info,ky,which):
+    return xor(info[6],ky)*2+xor(info[3],which)
+
+def outer_grad(which,info,outT,act):
     width,n=outT.shape; ffc=act.shape[1]//4
-    S=jax.ShapeDtypeStruct((16,width//8,ffc),bf16)
-    whole=pl.BlockSpec((16,width//8,ffc),lambda i:(0,0,0))
-    return pl.pallas_call(outer_grad_kernel,grid=(4,),in_specs=[SM,pl.BlockSpec((width,n),lambda i:(0,0)),pl.BlockSpec((n,ffc),lambda i:(0,i))],
-        out_specs=[whole,whole],out_shape=[S,S],name="outer_grad")(info,outT,act)
-
-def inner_grad_kernel(info, hidT_ref, il_ref, attnT_ref, bl_ref, norm_ref, keep_ref, give_ref):
-    col=pl.program_id(0); y=col//2; same=(col%2)==info[3]
+    return pl.pallas_call(outer_grad_kernel,
+        grid_spec=pltpu.PrefetchScalarGridSpec(num_scalar_prefetch=1,grid=(2,),
+            in_specs=[pl.BlockSpec((width,n),lambda i,s:(0,0)),pl.BlockSpec((n,ffc),lambda i,s:(0,column(s,i,which)))],
+            out_specs=pl.BlockSpec((2,1,4,width//8,ffc),lambda i,s:(0,i,0,0,0))),
+        out_shape=jax.ShapeDtypeStruct((2,2,4,width//8,ffc),bf16),
+        cost_estimate=pl.CostEstimate(flops=4*width*n*ffc,bytes_accessed=8*width*ffc,transcendentals=0),name="outer_grad")(info,outT,act)
+
+def inner_grad_kernel(which, info, hidT_ref, il_ref, attnT_ref, bl_ref, norm_ref, out_ref):
+    col=column(info,pl.program_id(0),which)
     half=hidT_ref.shape[0]//8; feat=2*half; third=half//3
-    value=mm(hidT_ref[...],il_ref[...]).astype(bf16)
     rows=attnT_ref[rows_at(col,feat,64),:]
-    outs=[mm(rows,bl_ref[r]).astype(bf16) for r in range(4)]
-    norms=[]
     for r in range(4):
+        rk=xor(r,info[0])
+        value=mm(hidT_ref[r*feat:(r+1)*feat,:],il_ref[...]).astype(bf16)
+        outs=mm(rows,bl_ref[r]).astype(bf16)
         line=jnp.concatenate([norm_ref[i:i+1,r*feat:(r+1)*feat] for i in range(4)],axis=1)
-        norms.append(jnp.concatenate([line,jnp.zeros((15,line.shape[1]),f32)],axis=0).astype(bf16))
-    for ref,cond in ((keep_ref,same),(give_ref,jnp.logical_not(same))):
-        @pl.when(cond)
-        def _():
-            for g in range(2):
-                for r in range(4):
-                    d=destination(info,g,r,y)
-                    ref[d,:half,:]=value[r*feat+g*half:r*feat+(g+1)*half]
-                    for j in range(3):
-                        ref[d,half:half+third,j*256:(j+1)*256]=outs[r][g*half+j*third:g*half+(j+1)*third]
-                    ref[d,half+third:,:]=norms[r]
-
-def inner_grad(info,hidT,il,attnT,bl,norm):
+        norms=jnp.concatenate([line,jnp.zeros((15,line.shape[1]),f32)],axis=0).astype(bf16)
+        for g in range(2):
+            gk=xor(g,info[5])
+            out_ref[gk,0,rk,:half,:]=value[g*half:(g+1)*half]
+            for j in range(3):
+                out_ref[gk,0,rk,half:half+third,j*256:(j+1)*256]=outs[g*half+j*third:g*half+(j+1)*third]
+            out_ref[gk,0,rk,half+third:,:]=norms
+
+def inner_grad(which,info,hidT,il,attnT,bl,norm):
     width,n=hidT.shape; ffc=il.shape[1]//4; half=width//8; rows=half+half//3+16
-    S=jax.ShapeDtypeStruct((16,rows,ffc),bf16)
-    whole=pl.BlockSpec((16,rows,ffc),lambda i:(0,0,0)); fix=pl.BlockSpec((width,n),lambda i:(0,0))
-    return pl.pallas_call(inner_grad_kernel,grid=(4,),in_specs=[SM,fix,pl.BlockSpec((n,ffc),lambda i:(0,i)),fix,pl.BlockSpec((4,n,256),lambda i:(0,0,0)),pl.BlockSpec((8,width),lambda i:(0,0))],
-        out_specs=[whole,whole],out_shape=[S,S],name="inner_grad")(info,hidT,il,attnT,bl,norm)
+    fix=pl.BlockSpec((width,n),lambda i,s:(0,0))
+    return pl.pallas_call(functools.partial(inner_grad_kernel,which),
+        grid_spec=pltpu.PrefetchScalarGridSpec(num_scalar_prefetch=1,grid=(2,),
+            in_specs=[fix,pl.BlockSpec((n,ffc),lambda i,s:(0,column(s,i,which))),fix,pl.BlockSpec((4,n,256),lambda i,s:(0,0,0)),pl.BlockSpec((8,width),lambda i,s:(0,0))],
+            out_specs=pl.BlockSpec((2,1,4,rows,ffc),lambda i,s:(0,i,0,0,0))),
+        out_shape=jax.ShapeDtypeStruct((2,2,4,rows,ffc),bf16),
+        cost_estimate=pl.CostEstimate(flops=6*width*n*ffc,bytes_accessed=8*width*ffc,transcendentals=0),name="inner_grad")(info,hidT,il,attnT,bl,norm)
 
 def exchange4(blocks, axes):
     parts = [blocks[0]]
@@ -458,17 +468,46 @@
     return jnp.pad(rows, ((0, 13), (0, 0)))
 
 
-def gather_weights(w_output, w_inner, w_outer, norms):
-    if lax.axis_size("dp") == 2:
-        packed = jnp.concatenate([w_inner, pack_outer(w_outer), pack_output(w_output), norms], axis=0)
-        return lax.all_gather(packed, EVERY)
+def after(value, *earlier):
+    return lax.optimization_barrier((value,) + earlier)[0]
+
+
+def swap2(value, axis):
+    return lax.ppermute(value, axis, [(0, 1), (1, 0)])
+
+
+def row_stack(block):
+    return jnp.stack(exchange4([block] * 4, ROW))
+
+
+def plane_and_core(own_row):
+    along_x = swap2(own_row, "dp")
+    along_y = swap2(own_row, "cy")
+    across_low = swap2(along_x[:2], "cy")
+    across_high = swap2(along_y[2:], "dp")
+    arrays = [own_row, along_x, along_y, across_low, across_high]
+    return arrays + [core_swap(array) for array in arrays]
+
+
+def gather_generic(w_output, w_inner, w_outer, norms, row, y, c):
     inner, outer, output = (lax.all_gather(w, "dp", axis=0, tiled=True) for w in (w_inner, w_outer, w_output))
-    halves = []
-    for g in range(2):
-        parts = [w.reshape((2, w.shape[0] // 2) + w.shape[1:])[g] for w in (inner, outer, output)]
-        halves.append(jnp.concatenate([parts[0], pack_outer(parts[1]), pack_output(parts[2]), norms], axis=0))
-    whole = lax.all_gather(jnp.stack(halves), GROUP)
-    return jnp.concatenate([whole[:, 0], whole[:, 1]], axis=0)
+    chunks = []
+    for which in range(2):
+        halves = []
+        for g in range(2):
+            parts = [w.reshape((2, w.shape[0] // 2) + w.shape[1:])[g] for w in (inner, outer, output)]
+            if which == 0:
+                halves.append(jnp.concatenate([parts[0], pack_output(parts[2]), norms], axis=0))
+            else:
+                halves.append(pack_outer(parts[1]))
+        whole = lax.all_gather(jnp.stack(halves), GROUP)
+        arrays = []
+        for kc in range(2):
+            for kx, ky, rows in ((0, 0, (0, 1, 2, 3)), (1, 0, (0, 1, 2, 3)), (0, 1, (0, 1, 2, 3)), (1, 1, (0, 1)), (1, 1, (2, 3))):
+                spots = jnp.stack([(row ^ k) * 4 + (y ^ ky) * 2 + (c ^ kc) for k in rows])
+                arrays.append(jnp.take(whole[:, kx], spots, axis=0))
+        chunks.append(arrays)
+    return chunks
 
 
 def add_parts(parts):
@@ -478,18 +517,28 @@
     return total
 
 
-def reduce_blocks(keep, give):
-    got = core_swap(give)
+def start_sums(keep, got):
+    def part(kx, ky, rows):
+        return (keep[kx, ky, rows].astype(f32) + got[kx, ky, rows].astype(f32)).astype(bf16)
+
+    everything = slice(0, 4)
+    return (
+        part(0, 0, everything), part(1, 0, everything), part(0, 1, everything),
+        part(1, 1, slice(0, 2)), part(1, 1, slice(2, 4)),
+    )
+
+
+def second_sums(sums, to_x, to_y):
+    own, along_x, along_y, _, _ = sums
+    x_sum = jnp.concatenate([along_x[:2], (along_x[2:].astype(f32) + to_y.astype(f32)).astype(bf16)], axis=0)
+    y_sum = jnp.concatenate([(along_y[:2].astype(f32) + to_x.astype(f32)).astype(bf16), along_y[2:]], axis=0)
+    return own, x_sum, y_sum
+
+
+def generic_sums(keep, got):
     core = (keep.astype(f32) + got.astype(f32)).astype(bf16)
-    core = core.reshape((4, 4) + core.shape[1:])
-    if lax.axis_size("dp") == 2:
-        plane = [add_parts(exchange4(core, ("dp", "cy"))).astype(bf16)]
-    else:
-        plane = []
-        for g in range(2):
-            other = lax.ppermute(core[2 * g + 1], "cy", [(0, 1), (1, 0)])
-            plane.append(add_parts([core[2 * g], other]).astype(bf16))
-    return [add_parts(exchange4(p, ROW)) for p in plane]
+    planes = [add_parts([core[g, 0], core_y]).astype(bf16) for g in range(2) for core_y in [swap2(core[g, 1], "cy")]]
+    return [add_parts(exchange4(plane, ROW)) for plane in planes]
 
 
 def local(
@@ -513,10 +562,6 @@
         row, z * 2 + y, m * 2 + c, c, length - own_start, group if two else 0 * group, y, 0 * y,
     ]).astype(jnp.int32)
 
-    weights = gather_weights(
-        w_output, w_inner, w_outer, pack_norms(first_gain, first_shift, second_gain, second_shift)
-    )
-
     def to_row_order(array):
         blocks = array.reshape(2, feat, 2, half).transpose(0, 2, 1, 3).reshape(4, feat, half)
         return swap_by(blocks, row)
@@ -551,27 +596,58 @@
     sines = jnp.sin(angles)
     sine = jnp.stack([-sines, sines], axis=1).reshape(HD, 4 * half)
 
+    norms = pack_norms(first_gain, first_shift, second_gain, second_shift)
+    if two:
+        block_a = jnp.concatenate([w_inner, pack_output(w_output), norms], axis=0)
+        row_a = row_stack(after(block_a, x_own))
+        chunk_a = plane_and_core(row_a)
+        row_b = row_stack(after(pack_outer(w_outer), row_a))
+        chunk_b = plane_and_core(row_b)
+    else:
+        chunk_a, chunk_b = gather_generic(w_output, w_inner, w_outer, norms, row, y, c)
+
     q_rot, kv_own = qkv(info, xs, mine, theirs, cosine, sine)
     kv_other = core_swap(kv_own)
     out, log_totals, *lows = attend(q_rot, kv_own, kv_other, bias)
     attn_parts = exchange4(lows, SQUARE)
-    cot_parts = exchange4(to_row_order(out_grad), ROW)
+    cot_parts = exchange4(after(to_row_order(out_grad), xs[3]), ROW)
     mixed, e0, e1, e2, e3, grad_one, attn_t, hidden_t, outer_t, branch_low, act_low, inner_low, norm_sums = middle(
-        info, attn_parts, x_own, cot_parts, weights
+        info, attn_parts, x_own, cot_parts, chunk_a, chunk_b
     )
     grads = exchange4([e0, e1, e2, e3], SQUARE)
-    outer_sums = reduce_blocks(*outer_grad(info, outer_t, act_low))
-    inner_sums = reduce_blocks(*inner_grad(info, hidden_t, inner_low, attn_t, branch_low, norm_sums))
+    give_outer = outer_grad(1, info, outer_t, act_low)
+    got_outer = core_swap(give_outer)
+    give_inner = inner_grad(1, info, hidden_t, after(inner_low, give_outer), attn_t, branch_low, norm_sums)
+    got_inner = core_swap(give_inner)
+    keep_outer = outer_grad(0, info, outer_t, after(act_low, give_inner))
+    keep_inner = inner_grad(0, info, hidden_t, after(inner_low, keep_outer), attn_t, branch_low, norm_sums)
+
+    def head_back(head, grads):
+        return attend_back(head, q_rot, kv_own, kv_other, bias, out, log_totals, grads, cosine, sine)
+
+    if two:
+        sums_outer = start_sums(keep_outer, got_outer)
+        outer_x = swap2(sums_outer[3], "dp")
+        outer_y = swap2(sums_outer[4], "cy")
+        first = head_back(0, [after(grads[0], sums_outer[3], sums_outer[4], keep_inner)] + grads[1:])
+        sums_inner = start_sums(after(keep_inner, first[0]), got_inner)
+        inner_x = swap2(sums_inner[3], "dp")
+        inner_y = swap2(sums_inner[4], "cy")
+        own_outer, x_outer, y_outer = second_sums(sums_outer, outer_x, outer_y)
+        plane_outer_parts = [own_outer, swap2(x_outer, "dp"), swap2(y_outer, "cy")]
+        second = head_back(1, [after(grads[0], x_outer, y_outer, sums_inner[3], sums_inner[4])] + grads[1:])
+        own_inner, x_inner, y_inner = second_sums(sums_inner, after(inner_x, second[0]), inner_y)
+        plane_inner_parts = [own_inner, swap2(x_inner, "dp"), swap2(y_inner, "cy")]
+        third_head = head_back(2, [after(grads[0], x_inner, y_inner)] + grads[1:])
+    else:
+        first, second, third_head = (head_back(head, grads) for head in range(3))
+
     mixed_out = from_row_order(exchange4(mixed, ROW))
-
-    dq, dkv_own, dkv_give = attend_back(
-        q_rot, kv_own, kv_other, bias, out, log_totals, grads, cosine, sine
-    )
-    dkv_got = core_swap(dkv_give)
-    d0, d1, d2, d3, keep, give = finish(info, dq, dkv_own, dkv_got, xs, mine, theirs, cosine, sine)
-    d_x = add_parts([grad_one] + exchange4([d0, d1, d2, d3], SQUARE)).astype(bf16)
-    d_input = from_row_order(exchange4(d_x, ROW)).astype(f32)
-
+    dqs, owns, gives = zip(first, second, third_head)
+    gots = [core_swap(give) for give in gives]
+    d0, d1, d2, d3, proj = finish_dx(info, dqs, owns, gots, mine, theirs, cosine, sine)
+    dx_parts = exchange4([d0, d1, d2, d3], SQUARE)
+    keep, give = finish_dw(info, proj, xs)
     by_round = (keep + core_swap(give).astype(f32)).astype(bf16)
     got = []
     for r1 in range(2):
@@ -579,6 +655,18 @@
             got.append(
                 lax.ppermute(by_round[r1 * 2 + r2], GROUP, group_route((r1, r2), True)).astype(f32)
             )
+    if two:
+        plane_outer = add_parts(plane_outer_parts).astype(bf16)
+        outer_sums = [add_parts(exchange4(plane_outer, ROW))]
+    d_x = add_parts([grad_one] + dx_parts).astype(bf16)
+    d_input = from_row_order(exchange4(d_x, ROW)).astype(f32)
+    if two:
+        plane_inner = add_parts(plane_inner_parts).astype(bf16)
+        inner_sums = [add_parts(exchange4(plane_inner, ROW))]
+    else:
+        outer_sums = generic_sums(keep_outer, got_outer)
+        inner_sums = generic_sums(keep_inner, got_inner)
+
     lower = got[0] + got[2]
     upper = got[1] + got[3]
     g_qkv = dp_reduce(

time: 347 us -> 352 us (1.014)
  waiting for transfers between devices: 157 us -> 132 us
  starting transfers between devices: 61.5 us -> 78.2 us
  other arithmetic: 16.9 us -> 31.1 us
  between operations: 15.4 us -> 2.24 us
  Pallas kernels: 78.7 us -> 87 us
    ppermute x36, waiting for transfers between devices: 130 us -> 73.2 us  [exchange4(): lax.ppermute(blocks[step], axes, [(i, i ^ step) for i in range(4)])]
    ppermute x0 -> x16, waiting for transfers between devices: none -> 44.5 us  [swap2(): return lax.ppermute(value, axis, [(0, 1), (1, 0)])]
    ppermute x0 -> x16, starting transfers between devices: none -> 15.4 us  [swap2(): return lax.ppermute(value, axis, [(0, 1), (1, 0)])]
    convert_element_type x5 -> x11, other arithmetic: 6.12 us -> 16.9 us  [the longest x4 8.48 us: part(): (keep[kx, ky, rows].astype(f32) + got[kx, ky, rows].astype(f32)).astype(b...]
    all_gather x1 -> x0, waiting for transfers between devices: 10.2 us -> none  [gather_weights(): return lax.all_gather(packed, EVERY)]
    pallas_call x5 -> x10, Pallas kernels: 63.2 us -> 71.5 us  [the longest x3 24.6 us: attend_back(): pl.pallas_call(attend_back_kernel, grid=(4 // QB,), in_specs=[hb, kspec,...]
    ppermute x36, starting transfers between devices: 52.4 us -> 46 us  [exchange4(): lax.ppermute(blocks[step], axes, [(i, i ^ step) for i in range(4)])]
    slice x2 -> x8, local copies, waits for them, and re-layouts: 0.29 us -> 5.24 us  [the longest x2 2.02 us: plane_and_core(): across_low = swap2(along_x[:2], 'cy')]
  transfers between devices with their start and end apart: 53 -> 80, of which waited for: 27 -> 30; matrix products, arithmetic and copies ran while one was open for 6% -> 13% of each run, Pallas kernels for 11% -> 16%
where the time goes in v3:
time: 352 us; the launch traced here: 351 us
  waiting for transfers between devices  132 us (38%)
  Pallas kernels  87 us (25%)
  starting transfers between devices  78.2 us (22%)
  other arithmetic  31.1 us (9%)
  local copies, waits for them, and re-layouts  20.2 us (6%)
    ppermute x36, waiting for transfers between devices, exchange4(): lax.ppermute(blocks[step], axes, [(i, i ^ step) for i in range(4)])  73.2 us
    ppermute x36, starting transfers between devices, exchange4(): lax.ppermute(blocks[step], axes, [(i, i ^ step) for i in range(4)])  46 us
    ppermute x16, waiting for transfers between devices, swap2(): return lax.ppermute(value, axis, [(0, 1), (1, 0)])  44.5 us
    pallas_call x3, Pallas kernels, attend_back(): pl.pallas_call(attend_back_kernel, grid=(4 // QB,), in_specs=[hb, kspec,...  24.6 us
    pallas_call x1, Pallas kernels, middle(): pl.pallas_call(middle_kernel, in_specs=[SM] + [VM] * 9 + [HB] * 20, out_s...  20.7 us
    ppermute x16, starting transfers between devices, swap2(): return lax.ppermute(value, axis, [(0, 1), (1, 0)])  15.4 us
    pallas_call x1, Pallas kernels, attend(): pl.pallas_call(attend_kernel, grid=(heads, 4 // QB), in_specs=[pl.BlockSp...  11.6 us
    pallas_call x2, Pallas kernels, inner_grad(): pl.pallas_call(functools.partial(inner_grad_kernel, which), grid_spec=plt...  9.15 us
  transfers between devices with their start and end apart: 80, of which 30 were waited for; matrix products, arithmetic and copies ran while one was open for 13% of the time, Pallas kernels for 16%

profile of v3, /device:TPU:0, one launch (start us, length us, event | category | flops | bytes accessed | tf_op | source)
XLA Modules:
  0.0 351.0 jit_solution(5726806983965200352)
XLA Ops:
  1.7 3.0 collective-permute-start.6
  6.0 3.7 %collective-permute-start.2 = (bf16[192,256]{1,0:T(8,128)(2,1)S(1)}, bf16[192,256]{1,0:T(8,128)(2,1)S(1)}, u32[]{:S(2)}, u32[]{:S(2)}) collective-permute-start(bf16[192,256]{1,0:T(8,128)(2,1)S(1)} %get-tuple-element.148), channel_id=1, source_target_pairs={{0,12},{4,8},{8,4},{12,0},{1,13},{5,9},{9,5},{13,1},{2,14},{6,10},... | collective-permute-start | bytes 294920 | tf_op jit(solution)/shard_map/ppermute | solution.py:396
  11.1 2.4 collective-permute-done.2
  13.6 4.1 %collective-permute-done.1 = bf16[192,256]{1,0:T(8,128)(2,1)S(1)} collective-permute-done((bf16[192,256]{1,0:T(8,128)(2,1)S(1)}, bf16[192,256]{1,0:T(8,128)(2,1)S(1)}, u32[]{:S(2)}, u32[]{:S(2)}) %collective-permute-start.1) | collective-permute-done | bytes 98336 | tf_op jit(solution)/shard_map/ppermute | solution.py:396
  17.7 2.6 collective-permute-start.21
  23.4 3.0 collective-permute-start.9
  28.7 11.7 %collective-permute-done.20 = bf16[144,768]{1,0:T(8,128)(2,1)S(1)} collective-permute-done((bf16[144,768]{1,0:T(8,128)(2,1)S(1)}, bf16[144,768]{1,0:T(8,128)(2,1)S(1)}, u32[]{:S(2)}, u32[]{:S(2)}) %collective-permute-start.20) | collective-permute-done | bytes 221216 | tf_op jit(solution)/shard_map/ppermute | solution.py:396
  40.5 6.2 %collective-permute-done.9 = bf16[96,576]{1,0:T(8,128)(2,1)S(1)} collective-permute-done((bf16[96,576]{1,0:T(8,128)(2,1)S(1)}, bf16[96,576]{1,0:T(8,128)(2,1)S(1)}, u32[]{:S(2)}, u32[]{:S(2)}) %collective-permute-start.9) | collective-permute-done | bytes 110624 | tf_op jit(solution)/shard_map/ppermute | solution.py:582
  47.6 2.5 collective-permute-start.32
  56.8 6.1 %collective-permute-done.32 = bf16[96,768]{1,0:T(8,128)(2,1)S(1)} collective-permute-done((bf16[96,768]{1,0:T(8,128)(2,1)S(1)}, bf16[96,768]{1,0:T(8,128)(2,1)S(1)}, u32[]{:S(2)}, u32[]{:S(2)}) %collective-permute-start.32) | collective-permute-done | bytes 147488 | tf_op jit(solution)/shard_map/ppermute | solution.py:396
  66.4 3.6 %collective-permute-done.4.x2 = bf16[4,192,256]{2,1,0:T(8,128)(2,1)S(1)} collective-permute-done((bf16[4,192,256]{2,1,0:T(8,128)(2,1)S(1)}, bf16[4,192,256]{2,1,0:T(8,128)(2,1)S(1)}, u32[]{:S(2)}, u32[]{:S(2)}) %collective-permute-start.4) | collective-permute-done | bytes 393248 | tf_op jit(solution)/shard_map/ppermute | solution.py:396
  74.5 2.6 collective-permute-done.18.c3
  79.9 3.9 %qkv.1 = (bf16[192,1024]{1,0:T(8,128)(2,1)}, bf16[384,1024]{1,0:T(8,128)(2,1)}) custom-call(s32[8]{0:T(128)} %stack.151.info, bf16[4,192,256]{2,1,0:T(8,128)(2,1)} %copy-done.7, bf16[4,192,256]{2,1,0:T(8,128)(2,1)} %copy-done.14, bf16[4,192,256]{2,1,0:T(8,128)(2,1)} %copy-done.13, bf16[4,192,256]{2,1,0:T(8,128)(2,1)} %copy-done.12, ...), custom_call_target="tpu_custom_call" | custom-call | tf_op jit(solution)/shard_map/qkv/pallas_call | solution.py:171
  86.6 3.3 collective-permute-done.16.c1
  89.9 3.0 collective-permute-start.23
  92.9 2.0 collective-permute-start.37
  96.9 23.3 %collective-permute-done.37.refs_14_ = bf16[2,96,768]{2,1,0:T(8,128)(2,1)S(1)} collective-permute-done((bf16[2,96,768]{2,1,0:T(8,128)(2,1)S(1)}, bf16[2,96,768]{2,1,0:T(8,128)(2,1)S(1)}, u32[]{:S(2)}, u32[]{:S(2)}) %collective-permute-start.37) | collective-permute-done | bytes 294944 | tf_op jit(solution)/shard_map/ppermute | solution.py:476
  120.8 11.6 %attend.1 = (f32[192,1024]{1,0:T(8,128)}, f32[3,1,1024]{2,1,0:T(1,128)}, bf16[192,256]{1,0:T(8,128)(2,1)}, bf16[192,256]{1,0:T(8,128)(2,1)}, bf16[192,256]{1,0:T(8,128)(2,1)}, /*index=5*/bf16[192,256]{1,0:T(8,128)(2,1)}) custom-call(bf16[192,1024]{1,0:T(8,128)(2,1)} %get-tuple-element.60.q_ref, bf16[384,1024]{1,0:T(8,128)(2,1)} %get-tuple-element.61.ko_ref.vo_ref, ...), custom_call_target="tpu_custom_call" | custom-call | flops 6442450944 | bytes 8388608 | tf_op jit(solution)/shard_map/attend/pallas_call | solution.py:72
  133.7 2.2 collective-permute-start.15
  137.8 3.0 collective-permute-done.15.a3
  142.5 6.5 %collective-permute-done.25.refs_4_ = bf16[2,144,768]{2,1,0:T(8,128)(2,1)S(1)} collective-permute-done((bf16[2,144,768]{2,1,0:T(8,128)(2,1)S(1)}, bf16[2,144,768]{2,1,0:T(8,128)(2,1)S(1)}, u32[]{:S(2)}, u32[]{:S(2)}) %collective-permute-start.25) | collective-permute-done | bytes 442400 | tf_op jit(solution)/shard_map/ppermute | solution.py:476
  149.0 2.7 collective-permute-done.24.refs_3_
  154.6 20.7 %middle.1 = (bf16[4,192,256]{2,1,0:T(8,128)(2,1)}, bf16[192,256]{1,0:T(8,128)(2,1)}, bf16[192,256]{1,0:T(8,128)(2,1)}, bf16[192,256]{1,0:T(8,128)(2,1)}, bf16[19...) custom-call(s32[8]{0:T(128)} %stack.151.info, ...), custom_call_target="tpu_custom_call" | custom-call | flops 14495514624 | bytes 56623104 | tf_op jit(solution)/shard_map/middle/pallas_call | solution.py:335
  175.3 4.0 %outer_grad.2 = bf16[2,2,4,96,768]{4,3,2,1,0:T(8,128)(2,1)} custom-call(s32[8]{0:T(128)} %stack.151.info, bf16[768,256]{1,0:T(8,128)(2,1)} %get-tuple-element.74.outT_ref, bf16[256,3072]{1,0:T(8,128)(2,1)} %get-tuple-element.82.act_ref), custom_call_target="tpu_custom_call" | custom-call | flops 603979776 | bytes 4718592 | tf_op jit(solution)/shard_map/outer_grad/pallas_call | solution.py:359
  179.4 4.6 %inner_grad.2 = bf16[2,2,4,144,768]{4,3,2,1,0:T(8,128)(2,1)} custom-call(s32[8]{0:T(128)} %stack.151.info, bf16[768,256]{1,0:T(8,128)(2,1)} %get-tuple-element.76.hidT_ref, bf16[256,3072]{1,0:T(8,128)(2,1)} %get-tuple-element.83.il_ref, bf16[768,256]{1,0:T(8,128)(2,1)} %get-tuple-element.79.attnT_ref, bf16[4,256,256]{2,1,0:T(8,128)(2,1)} %get-tuple-element.80.bl_ref, ...), custom_call_target="tpu_custom_call" | custom-call | flops 905969664 | bytes 4718592 | tf_op jit(solution)/shard_map/inner_grad/pallas_call | solution.py:386
  187.9 4.0 %outer_grad.3 = bf16[2,2,4,96,768]{4,3,2,1,0:T(8,128)(2,1)} custom-call(s32[8]{0:T(128)} %stack.151.info, bf16[768,256]{1,0:T(8,128)(2,1)} %get-tuple-element.74.outT_ref, bf16[256,3072]{1,0:T(8,128)(2,1)} %get-tuple-element.82.act_ref), custom_call_target="tpu_custom_call" | custom-call | flops 603979776 | bytes 4718592 | tf_op jit(solution)/shard_map/outer_grad/pallas_call | solution.py:359
  196.4 5.3 %collective-permute-done.50 = bf16[2,96,768]{2,1,0:T(8,128)(2,1)S(1)} collective-permute-done((bf16[2,96,768]{2,1,0:T(8,128)(2,1)S(1)}, bf16[2,96,768]{2,1,0:T(8,128)(2,1)S(1)}, u32[]{:S(2)}, u32[]{:S(2)}) %collective-permute-start.50) | collective-permute-done | bytes 294944 | tf_op jit(solution)/shard_map/ppermute | solution.py:476
  202.4 6.6 %collective-permute-done.51 = bf16[2,96,768]{2,1,0:T(8,128)(2,1)S(1)} collective-permute-done((bf16[2,96,768]{2,1,0:T(8,128)(2,1)S(1)}, bf16[2,96,768]{2,1,0:T(8,128)(2,1)S(1)}, u32[]{:S(2)}, u32[]{:S(2)}) %collective-permute-start.51) | collective-permute-done | bytes 294944 | tf_op jit(solution)/shard_map/ppermute | solution.py:476
  212.3 4.6 %inner_grad.3 = bf16[2,2,4,144,768]{4,3,2,1,0:T(8,128)(2,1)} custom-call(s32[8]{0:T(128)} %stack.151.info, bf16[768,256]{1,0:T(8,128)(2,1)} %get-tuple-element.76.hidT_ref, bf16[256,3072]{1,0:T(8,128)(2,1)} %get-tuple-element.83.il_ref, bf16[768,256]{1,0:T(8,128)(2,1)} %get-tuple-element.79.attnT_ref, bf16[4,256,256]{2,1,0:T(8,128)(2,1)} %get-tuple-element.80.bl_ref, ...), custom_call_target="tpu_custom_call" | custom-call | flops 905969664 | bytes 4718592 | tf_op jit(solution)/shard_map/inner_grad/pallas_call | solution.py:386
  216.8 2.3 collective-permute-start.45
  219.1 8.3 %attend_back.3 = (bf16[64,1024]{1,0:T(8,128)(2,1)}, f32[1024,128]{1,0:T(8,128)}, bf16[1024,128]{1,0:T(8,128)(2,1)}) custom-call(bf16[192,1024]{1,0:T(8,128)(2,1)} %get-tuple-element.60.q_ref, bf16[384,1024]{1,0:T(8,128)(2,1)} %get-tuple-element.61.ko_ref.vo_ref, bf16[384,1024]{1,0:T(8,128)(2,1)} %get-tuple-element.61.ko_ref.vo_ref, ...), custom_call_target="tpu_custom_call" | custom-call | flops 5368709120 | bytes 8388608 | tf_op jit(solution)/shard_map/attend_back/pallas_call | solution.py:124
  228.3 2.1 collective-permute-start.43
  233.1 2.3 fusion.11
  237.9 3.1 add_convert_fusion.1
  241.0 8.1 %attend_back.4 = (bf16[64,1024]{1,0:T(8,128)(2,1)}, f32[1024,128]{1,0:T(8,128)}, bf16[1024,128]{1,0:T(8,128)(2,1)}) custom-call(bf16[192,1024]{1,0:T(8,128)(2,1)} %get-tuple-element.60.q_ref, bf16[384,1024]{1,0:T(8,128)(2,1)} %get-tuple-element.61.ko_ref.vo_ref, bf16[384,1024]{1,0:T(8,128)(2,1)} %get-tuple-element.61.ko_ref.vo_ref, ...), custom_call_target="tpu_custom_call" | custom-call | flops 5368709120 | bytes 8388608 | tf_op jit(solution)/shard_map/attend_back/pallas_call | solution.py:124
  259.2 8.1 %attend_back.5 = (bf16[64,1024]{1,0:T(8,128)(2,1)}, f32[1024,128]{1,0:T(8,128)}, bf16[1024,128]{1,0:T(8,128)(2,1)}) custom-call(bf16[192,1024]{1,0:T(8,128)(2,1)} %get-tuple-element.60.q_ref, bf16[384,1024]{1,0:T(8,128)(2,1)} %get-tuple-element.61.ko_ref.vo_ref, bf16[384,1024]{1,0:T(8,128)(2,1)} %get-tuple-element.61.ko_ref.vo_ref, ...), custom_call_target="tpu_custom_call" | custom-call | flops 5368709120 | bytes 8388608 | tf_op jit(solution)/shard_map/attend_back/pallas_call | solution.py:124
  271.8 4.7 %finish_dx.1 = (f32[4,192,256]{2,1,0:T(8,128)}, bf16[4,192,256]{2,1,0:T(8,128)(2,1)}, bf16[4,192,256]{2,1,0:T(8,128)(2,1)}, bf16[4,192,256]{2,1,0:T(8,128)(2,1)}, bf16[576,1024]{1,0:T(8,128)(2,1)}) custom-call(s32[8]{0:T(128)} %stack.151.info, bf16[64,1024]{1,0:T(8,128)(2,1)} %get-tuple-element.88.refs_0_, bf16[64,1024]{1,0:T(8,128)(2,1)} %get-tuple-element.91.refs_1_, ...), custom_call_target="tpu_custom_call" | custom-call | flops 905969664 | bytes 6291456 | tf_op jit(solution)/shard_map/finish_dx/pallas_call | solution.py:196
  283.3 4.3 %finish_dw.1 = (f32[4,96,576]{2,1,0:T(8,128)}, bf16[4,96,576]{2,1,0:T(8,128)(2,1)}) custom-call(s32[8]{0:T(128)} %stack.151.info, bf16[576,1024]{1,0:T(8,128)(2,1)} %get-tuple-element.105.p_ref, bf16[4,192,256]{2,1,0:T(8,128)(2,1)} %copy-done.7, bf16[4,192,256]{2,1,0:T(8,128)(2,1)} %copy-done.14, bf16[4,192,256]{2,1,0:T(8,128)(2,1)} %copy-done.13, ...), custom_call_target="tpu_custom_call" | custom-call | flops 905969664 | bytes 3145728 | tf_op jit(solution)/shard_map/finish_dw/pallas_call | solution.py:215
  290.1 7.9 %collective-permute-done.60 = bf16[4,192,256]{2,1,0:T(8,128)(2,1)} collective-permute-done((bf16[4,192,256]{2,1,0:T(8,128)(2,1)}, bf16[4,192,256]{2,1,0:T(8,128)(2,1)}, u32[]{:S(2)}, u32[]{:S(2)}) %collective-permute-start.60) | collective-permute-done | bytes 393248 | tf_op jit(solution)/shard_map/ppermute | solution.py:396
  298.0 2.0 add_convert_fusion.9
  304.7 3.0 collective-permute-done.63
  307.7 3.0 collective-permute-start.65
  313.3 2.4 collective-permute-start.66
  318.1 4.2 %collective-permute-done.66 = bf16[96,576]{1,0:T(8,128)(2,1)S(1)} collective-permute-done((bf16[96,576]{1,0:T(8,128)(2,1)S(1)}, bf16[96,576]{1,0:T(8,128)(2,1)S(1)}, u32[]{:S(2)}, u32[]{:S(2)}) %collective-permute-start.66) | collective-permute-done | bytes 110624 | tf_op jit(solution)/shard_map/ppermute | solution.py:656
  323.5 2.1 fusion.1
  330.2 2.8 collective-permute-done.72
  332.9 5.2 %collective-permute-done.74 = bf16[144,768]{1,0:T(8,128)(2,1)S(1)} collective-permute-done((bf16[144,768]{1,0:T(8,128)(2,1)S(1)}, bf16[144,768]{1,0:T(8,128)(2,1)S(1)}, u32[]{:S(2)}, u32[]{:S(2)}) %collective-permute-start.74) | collective-permute-done | bytes 221216 | tf_op jit(solution)/shard_map/ppermute | solution.py:396
  338.1 10.8 %collective-permute-done.73 = bf16[144,768]{1,0:T(8,128)(2,1)S(1)} collective-permute-done((bf16[144,768]{1,0:T(8,128)(2,1)S(1)}, bf16[144,768]{1,0:T(8,128)(2,1)S(1)}, u32[]{:S(2)}, u32[]{:S(2)}) %collective-permute-start.73) | collective-permute-done | bytes 221216 | tf_op jit(solution)/shard_map/ppermute | solution.py:396
  (302 shorter events, 99.3 us)
Async XLA Ops:
  1.7 21.6 %collective-permute-start.6 = (bf16[96,576]{1,0:T(8,128)(2,1)S(1)}, bf16[96,576]{1,0:T(8,128)(2,1)S(1)}, u32[]{:S(2)}, u32[]{:S(2)}) collective-permute-start(bf16[96,576]{1,0:T(8,128)(2,1)S(1)} %pad_maximum_fusion.13), channel_id=1, source_target_pairs={{0,16},{16,0},{1,17},{17,1},{2,18},{18,2},{3,19},{19,3},{4,20},{20... | collective-permute-start | bytes 331784 | tf_op jit(solution)/shard_map/ppermute | solution.py:414
  20.3 20.1 %collective-permute-start.20 = (bf16[144,768]{1,0:T(8,128)(2,1)S(1)}, bf16[144,768]{1,0:T(8,128)(2,1)S(1)}, u32[]{:S(2)}, u32[]{:S(2)}) collective-permute-start(bf16[144,768]{1,0:T(8,128)(2,1)S(1)} %pad_maximum_fusion.11), channel_id=1, source_target_pairs={{0,8},{4,12},{8,0},{12,4},{1,9},{5,13},{9,1},{13,5},{2,10},{6,14},... | collective-permute-start | bytes 663560 | tf_op jit(solution)/shard_map/ppermute | solution.py:396
  20.3 20.1 %collective-permute-start.19 = (bf16[144,768]{1,0:T(8,128)(2,1)S(1)}, bf16[144,768]{1,0:T(8,128)(2,1)S(1)}, u32[]{:S(2)}, u32[]{:S(2)}) collective-permute-start(bf16[144,768]{1,0:T(8,128)(2,1)S(1)} %pad_maximum_fusion.11), channel_id=1, source_target_pairs={{0,4},{4,0},{8,12},{12,8},{1,5},{5,1},{9,13},{13,9},{2,6},{6,2},{1... | collective-permute-start | bytes 663560 | tf_op jit(solution)/shard_map/ppermute | solution.py:396
  22.2 42.1 %collective-permute-start.5 = (bf16[4,192,256]{2,1,0:T(8,128)(2,1)S(1)}, bf16[4,192,256]{2,1,0:T(8,128)(2,1)S(1)}, u32[]{:S(2)}, u32[]{:S(2)}) collective-permute-start(bf16[4,192,256]{2,1,0:T(8,128)(2,1)S(1)} %pad_maximum_fusion.7.x0.x_ref), channel_id=1, source_target_pairs={{0,6},{2,4},{4,2},{6,0},{1,7},{3,5},{5,3},{7,1},{8,14},{10,12},{12... | collective-permute-start | bytes 1179656 | tf_op jit(solution)/shard_map/ppermute | solution.py:396
  23.4 23.3 %collective-permute-start.9 = (bf16[96,576]{1,0:T(8,128)(2,1)S(1)}, bf16[96,576]{1,0:T(8,128)(2,1)S(1)}, u32[]{:S(2)}, u32[]{:S(2)}) collective-permute-start(bf16[96,576]{1,0:T(8,128)(2,1)S(1)} %get-tuple-element.156), channel_id=1, source_target_pairs={{0,8},{1,12},{2,10},{3,14},{4,9},{5,13},{6,11},{7,15},{8,0},{9,4},... | collective-permute-start | bytes 331784 | tf_op jit(solution)/shard_map/ppermute | solution.py:582
  28.0 19.6 %collective-permute-start.7 = (bf16[96,576]{1,0:T(8,128)(2,1)S(1)}, bf16[96,576]{1,0:T(8,128)(2,1)S(1)}, u32[]{:S(2)}, u32[]{:S(2)}) collective-permute-start(bf16[96,576]{1,0:T(8,128)(2,1)S(1)} %get-tuple-element.156), channel_id=1, source_target_pairs={{0,0},{1,4},{2,2},{3,6},{4,1},{5,5},{6,3},{7,7},{8,8},{9,12},{10,1... | collective-permute-start | bytes 331784 | tf_op jit(solution)/shard_map/ppermute | solution.py:582
  40.4 12.6 %collective-permute-start.8 = (bf16[96,576]{1,0:T(8,128)(2,1)S(1)}, bf16[96,576]{1,0:T(8,128)(2,1)S(1)}, u32[]{:S(2)}, u32[]{:S(2)}) collective-permute-start(bf16[96,576]{1,0:T(8,128)(2,1)S(1)} %get-tuple-element.157), channel_id=1, source_target_pairs={{0,1},{1,5},{2,3},{3,7},{4,0},{5,4},{6,2},{7,6},{8,9},{9,13},{10,1... | collective-permute-start | bytes 331784 | tf_op jit(solution)/shard_map/ppermute | solution.py:582
  47.6 15.2 %collective-permute-start.32 = (bf16[96,768]{1,0:T(8,128)(2,1)S(1)}, bf16[96,768]{1,0:T(8,128)(2,1)S(1)}, u32[]{:S(2)}, u32[]{:S(2)}) collective-permute-start(bf16[96,768]{1,0:T(8,128)(2,1)S(1)} %pad_maximum_fusion.12), channel_id=1, source_target_pairs={{0,8},{4,12},{8,0},{12,4},{1,9},{5,13},{9,1},{13,5},{2,10},{6,14},... | collective-permute-start | bytes 442376 | tf_op jit(solution)/shard_map/ppermute | solution.py:396
  50.8 12.0 %collective-permute-start.31 = (bf16[96,768]{1,0:T(8,128)(2,1)S(1)}, bf16[96,768]{1,0:T(8,128)(2,1)S(1)}, u32[]{:S(2)}, u32[]{:S(2)}) collective-permute-start(bf16[96,768]{1,0:T(8,128)(2,1)S(1)} %pad_maximum_fusion.12), channel_id=1, source_target_pairs={{0,4},{4,0},{8,12},{12,8},{1,5},{5,1},{9,13},{13,9},{2,6},{6,2},{1... | collective-permute-start | bytes 442376 | tf_op jit(solution)/shard_map/ppermute | solution.py:396
  52.9 17.1 %collective-permute-start.4 = (bf16[4,192,256]{2,1,0:T(8,128)(2,1)S(1)}, bf16[4,192,256]{2,1,0:T(8,128)(2,1)S(1)}, u32[]{:S(2)}, u32[]{:S(2)}) collective-permute-start(bf16[4,192,256]{2,1,0:T(8,128)(2,1)S(1)} %pad_maximum_fusion.7.x0.x_ref), channel_id=1, source_target_pairs={{0,4},{2,6},{4,0},{6,2},{1,5},{3,7},{5,1},{7,3},{8,12},{10,14},{12... | collective-permute-start | bytes 1179656 | tf_op jit(solution)/shard_map/ppermute | solution.py:396
  55.1 15.5 %collective-permute-start.3 = (bf16[4,192,256]{2,1,0:T(8,128)(2,1)S(1)}, bf16[4,192,256]{2,1,0:T(8,128)(2,1)S(1)}, u32[]{:S(2)}, u32[]{:S(2)}) collective-permute-start(bf16[4,192,256]{2,1,0:T(8,128)(2,1)S(1)} %pad_maximum_fusion.7.x0.x_ref), channel_id=1, source_target_pairs={{0,2},{2,0},{4,6},{6,4},{1,3},{3,1},{5,7},{7,5},{8,10},{10,8},{12,... | collective-permute-start | bytes 1179656 | tf_op jit(solution)/shard_map/ppermute | solution.py:396
  62.8 14.3 %collective-permute-start.11 = (bf16[4,96,576]{2,1,0:T(8,128)(2,1)S(1)}, bf16[4,96,576]{2,1,0:T(8,128)(2,1)S(1)}, u32[]{:S(2)}, u32[]{:S(2)}) collective-permute-start(bf16[4,96,576]{2,1,0:T(8,128)(2,1)S(1)} %pad_maximum_fusion.6.mine_ref.refs_9_), channel_id=1, source_target_pairs={{0,1},{1,0},{2,3},{3,2},{4,5},{5,4},{6,7},{7,6},{8,9},{9,8},{10,11... | collective-permute-start | bytes 1327112 | tf_op jit(solution)/shard_map/ppermute | solution.py:401
  63.7 29.2 %collective-permute-start.38 = (bf16[4,96,768]{2,1,0:T(8,128)(2,1)}, bf16[4,96,768]{2,1,0:T(8,128)(2,1)}, u32[]{:S(2)}, u32[]{:S(2)}) collective-permute-start(bf16[4,96,768]{2,1,0:T(8,128)(2,1)} %pad_maximum_fusion.3.refs_10_), channel_id=1, source_target_pairs={{0,1},{1,0},{2,3},{3,2},{4,5},{5,4},{6,7},{7,6},{8,9},{9,8},{10,11... | collective-permute-start | bytes 1769480 | tf_op jit(solution)/shard_map/ppermute | solution.py:401
  64.2 20.5 %collective-permute-start.35 = (bf16[4,96,768]{2,1,0:T(8,128)(2,1)}, bf16[4,96,768]{2,1,0:T(8,128)(2,1)}, u32[]{:S(2)}, u32[]{:S(2)}) collective-permute-start(bf16[4,96,768]{2,1,0:T(8,128)(2,1)} %pad_maximum_fusion.3.refs_10_), channel_id=1, source_target_pairs={{0,2},{2,0},{1,3},{3,1},{4,6},{6,4},{5,7},{7,5},{8,10},{10,8},{9,1... | collective-permute-start | bytes 1769480 | tf_op jit(solution)/shard_map/ppermute | solution.py:476
  70.1 22.9 %collective-permute-start.34 = (bf16[4,96,768]{2,1,0:T(8,128)(2,1)}, bf16[4,96,768]{2,1,0:T(8,128)(2,1)}, u32[]{:S(2)}, u32[]{:S(2)}) collective-permute-start(bf16[4,96,768]{2,1,0:T(8,128)(2,1)} %pad_maximum_fusion.3.refs_10_), channel_id=1, source_target_pairs={{0,16},{16,0},{1,17},{17,1},{2,18},{18,2},{3,19},{19,3},{4,20},{20... | collective-permute-start | bytes 1769480 | tf_op jit(solution)/shard_map/ppermute | solution.py:476
  77.1 19.6 %collective-permute-start.26 = (bf16[4,144,768]{2,1,0:T(8,128)(2,1)S(1)}, bf16[4,144,768]{2,1,0:T(8,128)(2,1)}, u32[]{:S(2)}, u32[]{:S(2)}) collective-permute-start(bf16[4,144,768]{2,1,0:T(8,128)(2,1)S(1)} %pad_maximum_fusion.refs_0_), channel_id=1, source_target_pairs={{0,1},{1,0},{2,3},{3,2},{4,5},{5,4},{6,7},{7,6},{8,9},{9,8},{10,11... | collective-permute-start | bytes 2654216 | tf_op jit(solution)/shard_map/ppermute | solution.py:401
  83.8 36.4 %collective-permute-start.12 = (bf16[384,1024]{1,0:T(8,128)(2,1)}, bf16[384,1024]{1,0:T(8,128)(2,1)}, u32[]{:S(2)}, u32[]{:S(2)}) collective-permute-start(bf16[384,1024]{1,0:T(8,128)(2,1)} %get-tuple-element.61.ko_ref.vo_ref), channel_id=1, source_target_pairs={{0,1},{1,0},{2,3},{3,2},{4,5},{5,4},{6,7},{7,6},{8,9},{9,8},{10,11... | collective-permute-start | bytes 2359304 | tf_op jit(solution)/shard_map/ppermute | solution.py:401
  89.9 42.5 %collective-permute-start.23 = (bf16[4,144,768]{2,1,0:T(8,128)(2,1)S(1)}, bf16[4,144,768]{2,1,0:T(8,128)(2,1)S(1)}, u32[]{:S(2)}, u32[]{:S(2)}) collective-permute-start(bf16[4,144,768]{2,1,0:T(8,128)(2,1)S(1)} %pad_maximum_fusion.refs_0_), channel_id=1, source_target_pairs={{0,2},{2,0},{1,3},{3,1},{4,6},{6,4},{5,7},{7,5},{8,10},{10,8},{9,1... | collective-permute-start | bytes 2654216 | tf_op jit(solution)/shard_map/ppermute | solution.py:476
  92.9 39.9 %collective-permute-start.22 = (bf16[4,144,768]{2,1,0:T(8,128)(2,1)S(1)}, bf16[4,144,768]{2,1,0:T(8,128)(2,1)S(1)}, u32[]{:S(2)}, u32[]{:S(2)}) collective-permute-start(bf16[4,144,768]{2,1,0:T(8,128)(2,1)S(1)} %pad_maximum_fusion.refs_0_), channel_id=1, source_target_pairs={{0,16},{16,0},{1,17},{17,1},{2,18},{18,2},{3,19},{19,3},{4,20},{20... | collective-permute-start | bytes 2654216 | tf_op jit(solution)/shard_map/ppermute | solution.py:476
  92.9 27.3 %collective-permute-start.37 = (bf16[2,96,768]{2,1,0:T(8,128)(2,1)S(1)}, bf16[2,96,768]{2,1,0:T(8,128)(2,1)S(1)}, u32[]{:S(2)}, u32[]{:S(2)}) collective-permute-start(bf16[2,96,768]{2,1,0:T(8,128)(2,1)S(1)} %slice.370), channel_id=1, source_target_pairs={{0,16},{16,0},{1,17},{17,1},{2,18},{18,2},{3,19},{19,3},{4,20},{20... | collective-permute-start | bytes 884744 | tf_op jit(solution)/shard_map/ppermute | solution.py:476
  96.8 36.6 %collective-permute-start.36 = (bf16[2,96,768]{2,1,0:T(8,128)(2,1)S(1)}, bf16[2,96,768]{2,1,0:T(8,128)(2,1)}, u32[]{:S(2)}, u32[]{:S(2)}) collective-permute-start(bf16[2,96,768]{2,1,0:T(8,128)(2,1)S(1)} %slice.369), channel_id=1, source_target_pairs={{0,2},{2,0},{1,3},{3,1},{4,6},{6,4},{5,7},{7,5},{8,10},{10,8},{9,1... | collective-permute-start | bytes 884744 | tf_op jit(solution)/shard_map/ppermute | solution.py:476
  120.2 21.7 %collective-permute-start.40 = (bf16[4,96,768]{2,1,0:T(8,128)(2,1)}, bf16[4,96,768]{2,1,0:T(8,128)(2,1)}, u32[]{:S(2)}, u32[]{:S(2)}) collective-permute-start(bf16[4,96,768]{2,1,0:T(8,128)(2,1)} %collective-permute-done.35.refs_12_), channel_id=1, source_target_pairs={{0,1},{1,0},{2,3},{3,2},{4,5},{5,4},{6,7},{7,6},{8,9},{9,8},{10,11... | collective-permute-start | bytes 1769480 | tf_op jit(solution)/shard_map/ppermute | solution.py:401
  120.3 21.0 %collective-permute-start.42 = (bf16[2,96,768]{2,1,0:T(8,128)(2,1)S(1)}, bf16[2,96,768]{2,1,0:T(8,128)(2,1)S(1)}, u32[]{:S(2)}, u32[]{:S(2)}) collective-permute-start(bf16[2,96,768]{2,1,0:T(8,128)(2,1)S(1)} %collective-permute-done.37.refs_14_), channel_id=1, source_target_pairs={{0,1},{1,0},{2,3},{3,2},{4,5},{5,4},{6,7},{7,6},{8,9},{9,8},{10,11... | collective-permute-start | bytes 884744 | tf_op jit(solution)/shard_map/ppermute | solution.py:401
  137.5 11.4 %collective-permute-start.25 = (bf16[2,144,768]{2,1,0:T(8,128)(2,1)S(1)}, bf16[2,144,768]{2,1,0:T(8,128)(2,1)S(1)}, u32[]{:S(2)}, u32[]{:S(2)}) collective-permute-start(bf16[2,144,768]{2,1,0:T(8,128)(2,1)S(1)} %slice.366), channel_id=1, source_target_pairs={{0,16},{16,0},{1,17},{17,1},{2,18},{18,2},{3,19},{19,3},{4,20},{20... | collective-permute-start | bytes 1327112 | tf_op jit(solution)/shard_map/ppermute | solution.py:476
  141.9 11.5 %collective-permute-start.27 = (bf16[4,144,768]{2,1,0:T(8,128)(2,1)}, bf16[4,144,768]{2,1,0:T(8,128)(2,1)S(1)}, u32[]{:S(2)}, u32[]{:S(2)}) collective-permute-start(bf16[4,144,768]{2,1,0:T(8,128)(2,1)} %copy-done.18), channel_id=1, source_target_pairs={{0,1},{1,0},{2,3},{3,2},{4,5},{5,4},{6,7},{7,6},{8,9},{9,8},{10,11... | collective-permute-start | bytes 2654216 | tf_op jit(solution)/shard_map/ppermute | solution.py:401
  179.3 12.6 %collective-permute-start.46 = (bf16[2,2,4,96,768]{4,3,2,1,0:T(8,128)(2,1)}, bf16[2,2,4,96,768]{4,3,2,1,0:T(8,128)(2,1)S(1)}, u32[]{:S(2)}, u32[]{:S(2)}) collective-permute-start(bf16[2,2,4,96,768]{4,3,2,1,0:T(8,128)(2,1)} %outer_grad.2), channel_id=1, source_target_pairs={{0,1},{1,0},{2,3},{3,2},{4,5},{5,4},{6,7},{7,6},{8,9},{9,8},{10,11... | collective-permute-start | bytes 7077896 | tf_op jit(solution)/shard_map/ppermute | solution.py:401
  184.0 49.2 %collective-permute-start.52 = (bf16[2,2,4,144,768]{4,3,2,1,0:T(8,128)(2,1)}, bf16[2,2,4,144,768]{4,3,2,1,0:T(8,128)(2,1)}, u32[]{:S(2)}, u32[]{:S(2)}) collective-permute-start(bf16[2,2,4,144,768]{4,3,2,1,0:T(8,128)(2,1)} %inner_grad.2), channel_id=1, source_target_pairs={{0,1},{1,0},{2,3},{3,2},{4,5},{5,4},{6,7},{7,6},{8,9},{9,8},{10,11... | collective-permute-start | bytes 10616840 | tf_op jit(solution)/shard_map/ppermute | solution.py:401
  184.4 26.1 %collective-permute-start.47 = (bf16[192,256]{1,0:T(8,128)(2,1)}, bf16[192,256]{1,0:T(8,128)(2,1)}, u32[]{:S(2)}, u32[]{:S(2)}) collective-permute-start(bf16[192,256]{1,0:T(8,128)(2,1)} %get-tuple-element.85), channel_id=1, source_target_pairs={{0,2},{2,0},{4,6},{6,4},{1,3},{3,1},{5,7},{7,5},{8,10},{10,8},{12,... | collective-permute-start | bytes 294920 | tf_op jit(solution)/shard_map/ppermute | solution.py:396
  185.7 31.2 %collective-permute-start.48 = (bf16[192,256]{1,0:T(8,128)(2,1)}, bf16[192,256]{1,0:T(8,128)(2,1)}, u32[]{:S(2)}, u32[]{:S(2)}) collective-permute-start(bf16[192,256]{1,0:T(8,128)(2,1)} %get-tuple-element.86), channel_id=1, source_target_pairs={{0,4},{2,6},{4,0},{6,2},{1,5},{3,7},{5,1},{7,3},{8,12},{10,14},{12... | collective-permute-start | bytes 294920 | tf_op jit(solution)/shard_map/ppermute | solution.py:396
  186.2 33.0 %collective-permute-start.49 = (bf16[192,256]{1,0:T(8,128)(2,1)}, bf16[192,256]{1,0:T(8,128)(2,1)}, u32[]{:S(2)}, u32[]{:S(2)}) collective-permute-start(bf16[192,256]{1,0:T(8,128)(2,1)} %get-tuple-element.87), channel_id=1, source_target_pairs={{0,6},{2,4},{4,2},{6,0},{1,7},{3,5},{5,3},{7,1},{8,14},{10,12},{12... | collective-permute-start | bytes 294920 | tf_op jit(solution)/shard_map/ppermute | solution.py:396
  209.0 18.5 %collective-permute-start.75 = (bf16[4,96,768]{2,1,0:T(8,128)(2,1)S(1)}, bf16[4,96,768]{2,1,0:T(8,128)(2,1)S(1)}, u32[]{:S(2)}, u32[]{:S(2)}) collective-permute-start(bf16[4,96,768]{2,1,0:T(8,128)(2,1)S(1)} %pad_maximum_fusion.4), channel_id=1, source_target_pairs={{0,16},{16,0},{1,17},{17,1},{2,18},{18,2},{3,19},{19,3},{4,20},{20... | collective-permute-start | bytes 1769480 | tf_op jit(solution)/shard_map/ppermute | solution.py:476
  210.5 19.9 %collective-permute-start.76 = (bf16[4,96,768]{2,1,0:T(8,128)(2,1)}, bf16[4,96,768]{2,1,0:T(8,128)(2,1)}, u32[]{:S(2)}, u32[]{:S(2)}) collective-permute-start(bf16[4,96,768]{2,1,0:T(8,128)(2,1)} %pad_maximum_fusion.5), channel_id=1, source_target_pairs={{0,2},{2,0},{1,3},{3,1},{4,6},{6,4},{5,7},{7,5},{8,10},{10,8},{9,1... | collective-permute-start | bytes 1769480 | tf_op jit(solution)/shard_map/ppermute | solution.py:476
  216.8 40.5 %collective-permute-start.45 = (bf16[192,256]{1,0:T(8,128)(2,1)}, bf16[192,256]{1,0:T(8,128)(2,1)}, u32[]{:S(2)}, u32[]{:S(2)}) collective-permute-start(bf16[192,256]{1,0:T(8,128)(2,1)} %get-tuple-element.140), channel_id=1, source_target_pairs={{0,12},{4,8},{8,4},{12,0},{1,13},{5,9},{9,5},{13,1},{2,14},{6,10},... | collective-permute-start | bytes 294920 | tf_op jit(solution)/shard_map/ppermute | solution.py:396
  219.1 48.2 %collective-permute-start.44 = (bf16[192,256]{1,0:T(8,128)(2,1)}, bf16[192,256]{1,0:T(8,128)(2,1)}, u32[]{:S(2)}, u32[]{:S(2)}) collective-permute-start(bf16[192,256]{1,0:T(8,128)(2,1)} %get-tuple-element.141), channel_id=1, source_target_pairs={{0,8},{4,12},{8,0},{12,4},{1,9},{5,13},{9,1},{13,5},{2,10},{6,14},... | collective-permute-start | bytes 294920 | tf_op jit(solution)/shard_map/ppermute | solution.py:396
  228.3 39.1 %collective-permute-start.43 = (bf16[192,256]{1,0:T(8,128)(2,1)}, bf16[192,256]{1,0:T(8,128)(2,1)}, u32[]{:S(2)}, u32[]{:S(2)}) collective-permute-start(bf16[192,256]{1,0:T(8,128)(2,1)} %get-tuple-element.142), channel_id=1, source_target_pairs={{0,4},{4,0},{8,12},{12,8},{1,5},{5,1},{9,13},{13,9},{2,6},{6,2},{1... | collective-permute-start | bytes 294920 | tf_op jit(solution)/shard_map/ppermute | solution.py:396
  235.4 18.3 %collective-permute-start.53 = (bf16[2,144,768]{2,1,0:T(8,128)(2,1)}, bf16[2,144,768]{2,1,0:T(8,128)(2,1)}, u32[]{:S(2)}, u32[]{:S(2)}) collective-permute-start(bf16[2,144,768]{2,1,0:T(8,128)(2,1)} %get-tuple-element.112), channel_id=1, source_target_pairs={{0,2},{2,0},{1,3},{3,1},{4,6},{6,4},{5,7},{7,5},{8,10},{10,8},{9,1... | collective-permute-start | bytes 1327112 | tf_op jit(solution)/shard_map/ppermute | solution.py:476
  236.4 14.9 %collective-permute-start.54 = (bf16[2,144,768]{2,1,0:T(8,128)(2,1)}, bf16[2,144,768]{2,1,0:T(8,128)(2,1)}, u32[]{:S(2)}, u32[]{:S(2)}) collective-permute-start(bf16[2,144,768]{2,1,0:T(8,128)(2,1)} %get-tuple-element.113), channel_id=1, source_target_pairs={{0,16},{16,0},{1,17},{17,1},{2,18},{18,2},{3,19},{19,3},{4,20},{20... | collective-permute-start | bytes 1327112 | tf_op jit(solution)/shard_map/ppermute | solution.py:476
  251.3 16.6 %collective-permute-start.77 = (bf16[96,768]{1,0:T(8,128)(2,1)}, bf16[96,768]{1,0:T(8,128)(2,1)}, u32[]{:S(2)}, u32[]{:S(2)}) collective-permute-start(bf16[96,768]{1,0:T(8,128)(2,1)} %get-tuple-element.121), channel_id=1, source_target_pairs={{0,4},{4,0},{8,12},{12,8},{1,5},{5,1},{9,13},{13,9},{2,6},{6,2},{1... | collective-permute-start | bytes 442376 | tf_op jit(solution)/shard_map/ppermute | solution.py:396
  253.8 16.1 %collective-permute-start.79 = (bf16[96,768]{1,0:T(8,128)(2,1)}, bf16[96,768]{1,0:T(8,128)(2,1)}, u32[]{:S(2)}, u32[]{:S(2)}) collective-permute-start(bf16[96,768]{1,0:T(8,128)(2,1)} %get-tuple-element.122), channel_id=1, source_target_pairs={{0,12},{4,8},{8,4},{12,0},{1,13},{5,9},{9,5},{13,1},{2,14},{6,10},... | collective-permute-start | bytes 442376 | tf_op jit(solution)/shard_map/ppermute | solution.py:396
  257.3 12.5 %collective-permute-start.78 = (bf16[96,768]{1,0:T(8,128)(2,1)}, bf16[96,768]{1,0:T(8,128)(2,1)}, u32[]{:S(2)}, u32[]{:S(2)}) collective-permute-start(bf16[96,768]{1,0:T(8,128)(2,1)} %get-tuple-element.123), channel_id=1, source_target_pairs={{0,8},{4,12},{8,0},{12,4},{1,9},{5,13},{9,1},{13,5},{2,10},{6,14},... | collective-permute-start | bytes 442376 | tf_op jit(solution)/shard_map/ppermute | solution.py:396
  276.5 12.3 %collective-permute-start.58 = (bf16[4,192,256]{2,1,0:T(8,128)(2,1)}, bf16[4,192,256]{2,1,0:T(8,128)(2,1)}, u32[]{:S(2)}, u32[]{:S(2)}) collective-permute-start(bf16[4,192,256]{2,1,0:T(8,128)(2,1)} %get-tuple-element.102), channel_id=1, source_target_pairs={{0,2},{2,0},{4,6},{6,4},{1,3},{3,1},{5,7},{7,5},{8,10},{10,8},{12,... | collective-permute-start | bytes 1179656 | tf_op jit(solution)/shard_map/ppermute | solution.py:396
  277.8 12.3 %collective-permute-start.59 = (bf16[4,192,256]{2,1,0:T(8,128)(2,1)}, bf16[4,192,256]{2,1,0:T(8,128)(2,1)}, u32[]{:S(2)}, u32[]{:S(2)}) collective-permute-start(bf16[4,192,256]{2,1,0:T(8,128)(2,1)} %get-tuple-element.103), channel_id=1, source_target_pairs={{0,4},{2,6},{4,0},{6,2},{1,5},{3,7},{5,1},{7,3},{8,12},{10,14},{12... | collective-permute-start | bytes 1179656 | tf_op jit(solution)/shard_map/ppermute | solution.py:396
  278.9 19.1 %collective-permute-start.60 = (bf16[4,192,256]{2,1,0:T(8,128)(2,1)}, bf16[4,192,256]{2,1,0:T(8,128)(2,1)}, u32[]{:S(2)}, u32[]{:S(2)}) collective-permute-start(bf16[4,192,256]{2,1,0:T(8,128)(2,1)} %get-tuple-element.104), channel_id=1, source_target_pairs={{0,6},{2,4},{4,2},{6,0},{1,7},{3,5},{5,3},{7,1},{8,14},{10,12},{12... | collective-permute-start | bytes 1179656 | tf_op jit(solution)/shard_map/ppermute | solution.py:396
  281.7 41.8 %collective-permute-start.70 = (bf16[4,144,768]{2,1,0:T(8,128)(2,1)}, bf16[4,144,768]{2,1,0:T(8,128)(2,1)}, u32[]{:S(2)}, u32[]{:S(2)}) collective-permute-start(bf16[4,144,768]{2,1,0:T(8,128)(2,1)} %pad_maximum_fusion.1), channel_id=1, source_target_pairs={{0,16},{16,0},{1,17},{17,1},{2,18},{18,2},{3,19},{19,3},{4,20},{20... | collective-permute-start | bytes 2654216 | tf_op jit(solution)/shard_map/ppermute | solution.py:476
  282.3 41.3 %collective-permute-start.71 = (bf16[4,144,768]{2,1,0:T(8,128)(2,1)}, bf16[4,144,768]{2,1,0:T(8,128)(2,1)}, u32[]{:S(2)}, u32[]{:S(2)}) collective-permute-start(bf16[4,144,768]{2,1,0:T(8,128)(2,1)} %pad_maximum_fusion.2), channel_id=1, source_target_pairs={{0,2},{2,0},{1,3},{3,1},{4,6},{6,4},{5,7},{7,5},{8,10},{10,8},{9,1... | collective-permute-start | bytes 2654216 | tf_op jit(solution)/shard_map/ppermute | solution.py:476
  288.8 13.9 %collective-permute-start.64 = (bf16[4,96,576]{2,1,0:T(8,128)(2,1)}, bf16[4,96,576]{2,1,0:T(8,128)(2,1)S(1)}, u32[]{:S(2)}, u32[]{:S(2)}) collective-permute-start(bf16[4,96,576]{2,1,0:T(8,128)(2,1)} %get-tuple-element.107), channel_id=1, source_target_pairs={{0,1},{1,0},{2,3},{3,2},{4,5},{5,4},{6,7},{7,6},{8,9},{9,8},{10,11... | collective-permute-start | bytes 1327112 | tf_op jit(solution)/shard_map/ppermute | solution.py:401
  327.1 11.0 %collective-permute-start.74 = (bf16[144,768]{1,0:T(8,128)(2,1)S(1)}, bf16[144,768]{1,0:T(8,128)(2,1)S(1)}, u32[]{:S(2)}, u32[]{:S(2)}) collective-permute-start(bf16[144,768]{1,0:T(8,128)(2,1)S(1)} %get-tuple-element.119), channel_id=1, source_target_pairs={{0,12},{4,8},{8,4},{12,0},{1,13},{5,9},{9,5},{13,1},{2,14},{6,10},... | collective-permute-start | bytes 663560 | tf_op jit(solution)/shard_map/ppermute | solution.py:396
  327.6 21.3 %collective-permute-start.73 = (bf16[144,768]{1,0:T(8,128)(2,1)S(1)}, bf16[144,768]{1,0:T(8,128)(2,1)S(1)}, u32[]{:S(2)}, u32[]{:S(2)}) collective-permute-start(bf16[144,768]{1,0:T(8,128)(2,1)S(1)} %get-tuple-element.120), channel_id=1, source_target_pairs={{0,8},{4,12},{8,0},{12,4},{1,9},{5,13},{9,1},{13,5},{2,10},{6,14},... | collective-permute-start | bytes 663560 | tf_op jit(solution)/shard_map/ppermute | solution.py:396
  (78 other events, 648.6 us)

commit v4 on v3

--- a/solution.py
+++ b/solution.py
@@ -135,12 +135,12 @@
     return pl.ds(pl.multiple_of(index*size,align),size)
 
 def place_qkv_weights(info, mine_ref, theirs_ref, w_s):
-    c=info[3]; mc=info[2]
+    row=info[0]; c=info[3]
     half=mine_ref.shape[1]
     for r in range(4):
-        a=mine_ref[xor(r,mc)]; b=theirs_ref[xor(r,xor(mc,1))]
-        for h in range(2):
-            w_s[(2*r+h)*half:(2*r+h+1)*half,:]=jnp.where(c==h,a,b)
+        k=xor(r,row)
+        w_s[pl.ds(pl.multiple_of((2*r+c)*half,32),half),:]=mine_ref[k]
+        w_s[pl.ds(pl.multiple_of((2*r+1-c)*half,32),half),:]=theirs_ref[k]
 
 def place_tokens(info, x_ref, kz, x_s):
     feat=x_ref.shape[1]; base=xor(info[0],kz)
@@ -204,11 +204,11 @@
     for k,xr in enumerate((x0,x1,x2,x3)):
         place_tokens(info,xr,k//2,x_s.at[:,k*n:(k+1)*n])
     g_s[...]=mm(x_s[...],p_ref[...],NT)
-    c=info[3]; mc=info[2]
+    c=info[3]; row=info[0]
     for r in range(4):
         mine_rows=pl.ds(pl.multiple_of((2*r+c)*half,32),half); their_rows=pl.ds(pl.multiple_of((2*r+1-c)*half,32),half)
-        keep_ref[xor(r,mc)]=g_s[mine_rows,:]
-        give_ref[xor(r,xor(mc,1))]=g_s[their_rows,:].astype(bf16)
+        keep_ref[xor(r,row)]=g_s[mine_rows,:]
+        give_ref[xor(r,row)]=g_s[their_rows,:].astype(bf16)
 
 def finish_dw(info,proj,xs):
     _,feat,n=xs[0].shape; w3=proj.shape[0]; width=4*feat; half=feat//2
@@ -218,25 +218,31 @@
         cost_estimate=pl.CostEstimate(flops=8*width*w3*n,bytes_accessed=8*width*n*2,transcendentals=0),
         name="finish_dw")(info,proj,*xs)
 
+def row_step(core,slot):
+    return jnp.where(core==0,slot,(slot%2)*2+slot//2)
+
 def middle_kernel(info, a0,a1,a2,a3, x_ref, c0,c1,c2,c3, *refs):
-    chunk_a=refs[:10]; chunk_b=refs[10:20]
+    chunk_a=refs[:8]; chunk_b=refs[8:16]
     (mixed_ref, e0,e1,e2,e3, g1_ref, attnT_ref, hidT_ref, outT_ref, bl_ref, act_ref, il_ref, norm_ref,
-                  win, woT, wo, ns, gp_s, t_s, f_s, sems)=refs[20:]
+                  win, woT, wo, ns, gp_s, t_s, f_s, sems)=refs[16:]
     row=info[0]; zy=info[1]; c=info[3]; group=info[5]; y=info[6]
     feat=a0.shape[0]; n=a0.shape[1]; width=4*feat; ffc=chunk_a[0].shape[2]; half=feat//2; fh=ffc//2; third=half//3
     def go(src,dst,s): pltpu.make_async_copy(src,dst,sems.at[s]).start()
-    spots=((0,0,0),(0,1,0),(0,0,1),(0,1,1),(2,1,1))
     def each(chunk):
         for kc in range(2):
-            for ref,(first,kx,ky) in zip(chunk[5*kc:5*kc+5],spots):
-                g=xor(group,kx); col=xor(y,ky)*2+xor(c,kc)
-                for i in range(ref.shape[0]):
-                    yield ref.at[i],xor(row,first+i),g,col,(kc,kx,ky,first+i)
+            core=xor(c,kc)
+            for spot,ref in enumerate(chunk[4*kc:4*kc+4]):
+                first,second=spot%2,spot//2
+                kx=jnp.where(core==0,second,first); ky=jnp.where(core==0,first,second)
+                g=xor(group,kx); col=xor(y,ky)*2+core
+                for i in range(4):
+                    step=row_step(core,i)
+                    yield ref.at[i],xor(row,step),g,col,kc+spot
     for ref,r,g,col,_ in each(chunk_a):
         for j in range(3):
             go(ref.at[half:half+third,j*256:(j+1)*256],wo.at[r,pl.ds(pl.multiple_of((col*2+g)*half+j*third,16),third),:],0)
     for ref,r,g,col,where in each(chunk_a):
-        if where[:3]==(0,0,0):
+        if where==0:
             go(ref.at[half+third:half+third+16,:],ns.at[r],3)
     for ref,r,g,col,_ in each(chunk_a):
         go(ref.at[0:half,:],win.at[pl.ds(pl.multiple_of(r*feat+g*half,16),half),pl.ds(pl.multiple_of(col*ffc,128),ffc)],1)
@@ -290,12 +296,11 @@
     for i in range(4):
         mixed_ref[i]=t_s[rows_at(xor(i,row),feat,64),:]
     for k,cr in enumerate((c0,c1,c2,c3)):
-        t_s[rows_at(xor(k,row),feat,64),:]=cr[...]
+        for j in range(3):
+            t_s[pl.ds(pl.multiple_of(xor(k,row)*feat+j*(feat//3),64),feat//3),:]=cr[half:,j*256:(j+1)*256]
     valid=(lax.broadcasted_iota(jnp.int32,(n,1),0)<info[4]).astype(f32)
     cot=t_s[...].T.astype(f32)*valid
-    norm_ref[...]=jnp.zeros_like(norm_ref)
-    norm_ref[2:3,:]=jnp.sum(cot*cent2,axis=0,keepdims=True)
-    norm_ref[3:4,:]=jnp.sum(cot,axis=0,keepdims=True)
+    sums2=(jnp.sum(cot*cent2,axis=0,keepdims=True),jnp.sum(cot,axis=0,keepdims=True))
     def back(e,cent,inv):
         first=jnp.sum(e,axis=1,keepdims=True)*(1.0/width)
         second=jnp.sum(e*cent,axis=1,keepdims=True)*(1.0/width)
@@ -312,8 +317,9 @@
         return carry
     lax.fori_loop(0,4*nb,backward,0)
     gh=f_s[...]
-    norm_ref[0:1,:]=jnp.sum(gh*cent1,axis=0,keepdims=True)
-    norm_ref[1:2,:]=jnp.sum(gh,axis=0,keepdims=True)
+    sums=jnp.concatenate((jnp.sum(gh*cent1,axis=0,keepdims=True),jnp.sum(gh,axis=0,keepdims=True))+sums2+(jnp.zeros((4,width),f32),),axis=0)
+    for r in range(4):
+        norm_ref[r]=sums[:,r*feat:(r+1)*feat]
     grad1=back(gh*gain1,cent1,inv1)
     bl=grad1.astype(bf16)
     padded=jnp.concatenate([bl,jnp.zeros((n,256-feat),bf16)],axis=1)
@@ -332,63 +338,87 @@
 def middle(info,attn_parts,x_own,cot_parts,chunk_a,chunk_b):
     feat,n=attn_parts[0].shape; width=4*feat; ff=4*chunk_a[0].shape[2]
     S=jax.ShapeDtypeStruct
-    return pl.pallas_call(middle_kernel,in_specs=[SM]+[VM]*9+[HB]*20,out_specs=[VM]*13,
+    return pl.pallas_call(middle_kernel,in_specs=[SM]+[VM]*9+[HB]*16,out_specs=[VM]*13,
         out_shape=[S((4,feat,n),bf16)]+[S((feat,n),bf16)]*4+[S((4,feat,n),f32),S((width,n),bf16),S((width,n),bf16),S((width,n),bf16),
-                   S((4,n,256),bf16),S((n,ff),bf16),S((n,ff),bf16),S((8,width),f32)],
+                   S((4,n,256),bf16),S((n,ff),bf16),S((n,ff),bf16),S((4,8,feat),f32)],
         scratch_shapes=[pltpu.VMEM((width,ff),bf16),pltpu.VMEM((width,ff),bf16),pltpu.VMEM((4,width,256),bf16),pltpu.VMEM((4,16,width),bf16),
                         pltpu.VMEM((n,ff),f32),pltpu.VMEM((width,n),bf16),pltpu.VMEM((n,width),f32),pltpu.SemaphoreType.DMA((4,))],
         compiler_params=pltpu.CompilerParams(vmem_limit_bytes=56*1024*1024),
         cost_estimate=pl.CostEstimate(flops=12*n*width*ff*2,bytes_accessed=24*width*ff,transcendentals=2*n*ff),
         name="middle")(info,*attn_parts,x_own,*cot_parts,*chunk_a,*chunk_b)
 
-def outer_grad_kernel(info, outT_ref, act_ref, out_ref):
-    half=out_ref.shape[3]; fh=act_ref.shape[1]//2; feat=2*half
-    for g in range(2):
-        gk=xor(g,info[5])
-        for r in range(4):
-            value=mm(outT_ref[r*feat:(r+1)*feat,:],act_ref[:,g*fh:(g+1)*fh]).astype(bf16)
-            rk=xor(r,info[0])
-            out_ref[gk,0,rk,:,:fh]=value[:half]
-            out_ref[gk,0,rk,:,fh:]=value[half:]
-
-def column(info,ky,which):
-    return xor(info[6],ky)*2+xor(info[3],which)
-
-def outer_grad(which,info,outT,act):
-    width,n=outT.shape; ffc=act.shape[1]//4
-    return pl.pallas_call(outer_grad_kernel,
-        grid_spec=pltpu.PrefetchScalarGridSpec(num_scalar_prefetch=1,grid=(2,),
-            in_specs=[pl.BlockSpec((width,n),lambda i,s:(0,0)),pl.BlockSpec((n,ffc),lambda i,s:(0,column(s,i,which)))],
-            out_specs=pl.BlockSpec((2,1,4,width//8,ffc),lambda i,s:(0,i,0,0,0))),
-        out_shape=jax.ShapeDtypeStruct((2,2,4,width//8,ffc),bf16),
-        cost_estimate=pl.CostEstimate(flops=4*width*n*ffc,bytes_accessed=8*width*ffc,transcendentals=0),name="outer_grad")(info,outT,act)
-
-def inner_grad_kernel(which, info, hidT_ref, il_ref, attnT_ref, bl_ref, norm_ref, out_ref):
-    col=column(info,pl.program_id(0),which)
-    half=hidT_ref.shape[0]//8; feat=2*half; third=half//3
-    rows=attnT_ref[rows_at(col,feat,64),:]
-    for r in range(4):
-        rk=xor(r,info[0])
-        value=mm(hidT_ref[r*feat:(r+1)*feat,:],il_ref[...]).astype(bf16)
-        outs=mm(rows,bl_ref[r]).astype(bf16)
-        line=jnp.concatenate([norm_ref[i:i+1,r*feat:(r+1)*feat] for i in range(4)],axis=1)
-        norms=jnp.concatenate([line,jnp.zeros((15,line.shape[1]),f32)],axis=0).astype(bf16)
-        for g in range(2):
-            gk=xor(g,info[5])
-            out_ref[gk,0,rk,:half,:]=value[g*half:(g+1)*half]
-            for j in range(3):
-                out_ref[gk,0,rk,half:half+third,j*256:(j+1)*256]=outs[g*half+j*third:g*half+(j+1)*third]
-            out_ref[gk,0,rk,half+third:,:]=norms
-
-def inner_grad(which,info,hidT,il,attnT,bl,norm):
-    width,n=hidT.shape; ffc=il.shape[1]//4; half=width//8; rows=half+half//3+16
-    fix=pl.BlockSpec((width,n),lambda i,s:(0,0))
-    return pl.pallas_call(functools.partial(inner_grad_kernel,which),
-        grid_spec=pltpu.PrefetchScalarGridSpec(num_scalar_prefetch=1,grid=(2,),
-            in_specs=[fix,pl.BlockSpec((n,ffc),lambda i,s:(0,column(s,i,which))),fix,pl.BlockSpec((4,n,256),lambda i,s:(0,0,0)),pl.BlockSpec((8,width),lambda i,s:(0,0))],
-            out_specs=pl.BlockSpec((2,1,4,rows,ffc),lambda i,s:(0,i,0,0,0))),
-        out_shape=jax.ShapeDtypeStruct((2,2,4,rows,ffc),bf16),
-        cost_estimate=pl.CostEstimate(flops=6*width*n*ffc,bytes_accessed=8*width*ffc,transcendentals=0),name="inner_grad")(info,hidT,il,attnT,bl,norm)
+def target(info,which,a,b):
+    core=xor(info[3],which)
+    kx=jnp.where(core==0,a,b); ky=jnp.where(core==0,b,a)
+    return core,xor(info[5],kx),xor(info[6],ky)*2+core
+
+def outer_blocks(info,which,a,b,refs,put):
+    outT_ref,act_ref=refs
+    core,g,_=target(info,which,a,b)
+    half=outT_ref.shape[0]//8; fh=act_ref.shape[1]//2
+    rhs=act_ref[:,pl.ds(pl.multiple_of(g*fh,128),fh)]
+    for s in range(4):
+        value=mm(outT_ref[rows_at(xor(info[0],row_step(core,s)),2*half,64),:],rhs)
+        put(s,slice(0,half),slice(0,fh),value[:half])
+        put(s,slice(0,half),slice(fh,2*fh),value[half:])
+
+def inner_blocks(info,which,a,b,refs,put):
+    hidT_ref,il_ref,attnT_ref,bl_ref,norm_ref=refs
+    core,g,col=target(info,which,a,b)
+    half=hidT_ref.shape[0]//8; third=half//3
+    rows=[xor(info[0],row_step(core,s)) for s in range(4)]
+    lhs=jnp.concatenate([hidT_ref[rows_at(r*2+g,half,32),:] for r in rows],axis=0)
+    value=mm(lhs,il_ref[...])
+    heads=attnT_ref[rows_at(col*2+g,half,32),:]
+    for s,r in enumerate(rows):
+        put(s,slice(0,half),slice(None),value[s*half:(s+1)*half])
+        outs=mm(heads,bl_ref[r])
+        for j in range(3):
+            put(s,slice(half,half+third),slice(j*256,(j+1)*256),outs[j*third:(j+1)*third])
+        line=jnp.concatenate([norm_ref[r][i:i+1] for i in range(4)],axis=1)
+        put(s,slice(half+third,half+third+16),slice(None),jnp.concatenate([line,jnp.zeros((15,line.shape[1]),f32)],axis=0))
+
+def give_kernel(blocks,info,*refs):
+    out=refs[-1]
+    def put(s,rows,lanes,value): out[0,0,s,rows,lanes]=value.astype(bf16)
+    blocks(info,1,pl.program_id(0),pl.program_id(1),refs[:-1],put)
+
+def first_kernel(blocks,info,*refs):
+    got,out=refs[-2:]
+    def put(s,rows,lanes,value): out[0,s,rows,lanes]=(value+got[0,0,s,rows,lanes].astype(f32)).astype(bf16)
+    blocks(info,0,1,pl.program_id(0),refs[:-2],put)
+
+def second_kernel(blocks,info,*refs):
+    got,came,keep,send=refs[-4:]
+    for b,out in ((0,keep),(1,send)):
+        def put(s,rows,lanes,value):
+            out[s,rows,lanes]=(value+got[0,0,s,rows,lanes].astype(f32)+came[0,s,rows,lanes].astype(f32)).astype(bf16)
+        @pl.when(pl.program_id(0)==b)
+        def _(): blocks(info,0,0,b,refs[:-4],put)
+
+def grad_call(kind,stage,info,args,got=None,came=None):
+    S=jax.ShapeDtypeStruct
+    width,n=args[0].shape; ffc=args[1].shape[1]//4; half=width//8
+    blocks,rows=(inner_blocks,half+half//3+16) if kind=="inner" else (outer_blocks,half)
+    fixed=[pl.BlockSpec((width,n),lambda *i:(0,0)),None]+([pl.BlockSpec((width,n),lambda *i:(0,0)),pl.BlockSpec((4,n,256),lambda *i:(0,0,0)),pl.BlockSpec((4,8,width//4),lambda *i:(0,0,0))] if kind=="inner" else [])
+    cost=pl.CostEstimate(flops=(4 if stage=="give" else 2)*width*n*ffc,bytes_accessed=16*rows*ffc,transcendentals=0)
+    name=kind+"_"+stage
+    if stage=="give":
+        fixed[1]=pl.BlockSpec((n,ffc),lambda a,b,s:(0,target(s,1,a,b)[2]))
+        return pl.pallas_call(functools.partial(give_kernel,blocks),
+            grid_spec=pltpu.PrefetchScalarGridSpec(num_scalar_prefetch=1,grid=(2,2),in_specs=fixed,out_specs=pl.BlockSpec((1,1,4,rows,ffc),lambda a,b,s:(a,b,0,0,0))),
+            out_shape=S((2,2,4,rows,ffc),bf16),cost_estimate=cost,name=name)(info,*args)
+    a=1 if stage=="first" else 0
+    fixed[1]=pl.BlockSpec((n,ffc),lambda b,s:(0,target(s,0,a,b)[2]))
+    got_spec=pl.BlockSpec((1,1,4,rows,ffc),lambda b,s:(a,b,0,0,0)); one=pl.BlockSpec((1,4,rows,ffc),lambda b,s:(b,0,0,0))
+    if stage=="first":
+        return pl.pallas_call(functools.partial(first_kernel,blocks),
+            grid_spec=pltpu.PrefetchScalarGridSpec(num_scalar_prefetch=1,grid=(2,),in_specs=fixed+[got_spec],out_specs=one),
+            out_shape=S((2,4,rows,ffc),bf16),cost_estimate=cost,name=name)(info,*args,got)
+    whole=pl.BlockSpec((4,rows,ffc),lambda b,s:(0,0,0))
+    return pl.pallas_call(functools.partial(second_kernel,blocks),
+        grid_spec=pltpu.PrefetchScalarGridSpec(num_scalar_prefetch=1,grid=(2,),in_specs=fixed+[got_spec,one],out_specs=[whole,whole]),
+        out_shape=[S((4,rows,ffc),bf16)]*2,cost_estimate=cost,name=name)(info,*args,got,came)
 
 def exchange4(blocks, axes):
     parts = [blocks[0]]
@@ -408,34 +438,25 @@
     return pairs.reshape(blocks.shape)
 
 
-def dp_gather(value):
+def dp_halves(value, c):
     if lax.axis_size("dp") != 2:
-        return lax.all_gather(value, "dp", axis=0, tiled=True)
-    other = lax.ppermute(value, "dp", [(0, 1), (1, 0)])
-    first = lax.axis_index("dp") == 0
-    return jnp.concatenate([jnp.where(first, value, other), jnp.where(first, other, value)], axis=0)
-
-
-def dp_reduce(value):
+        whole = lax.all_gather(value, "dp", axis=0, tiled=True)
+        halves = whole.reshape((2, whole.shape[0] // 2) + whole.shape[1:])
+        return jnp.where(c == 0, halves[0], halves[1]), jnp.where(c == 0, halves[1], halves[0])
+    other = swap2(value, "dp")
+    same = lax.axis_index("dp") == c
+    return jnp.where(same, value, other), jnp.where(same, other, value)
+
+
+def dp_sum(this_half, other_half, c):
     if lax.axis_size("dp") != 2:
-        return lax.psum_scatter(value.astype(bf16), "dp", scatter_dimension=0, tiled=True).astype(f32)
-    half = value.shape[0] // 2
-    second = lax.axis_index("dp") == 1
-    keep = jnp.where(second, value[half:], value[:half])
-    send = jnp.where(second, value[:half], value[half:]).astype(bf16)
-    return keep + lax.ppermute(send, "dp", [(0, 1), (1, 0)]).astype(f32)
-
-
-def group_route(rounds, inverse):
-    pairs = []
-    for m in range(2):
-        for z in range(2):
-            for y in range(2):
-                for c in range(2):
-                    source = ((m * 2 + z) * 2 + y) * 2 + c
-                    target = (((m ^ rounds[0]) * 2 + c) * 2 + y) * 2 + (z ^ rounds[1])
-                    pairs.append((target, source) if inverse else (source, target))
-    return pairs
+        whole = jnp.concatenate(
+            [jnp.where(c == 0, this_half, other_half), jnp.where(c == 0, other_half, this_half)], axis=0
+        )
+        return lax.psum_scatter(whole.astype(bf16), "dp", scatter_dimension=0, tiled=True).astype(f32)
+    same = lax.axis_index("dp") == c
+    keep = jnp.where(same, this_half, other_half)
+    return keep + swap2(jnp.where(same, other_half, this_half).astype(bf16), "dp").astype(f32)
 
 
 def pack_outer(part):
@@ -476,17 +497,33 @@
     return lax.ppermute(value, axis, [(0, 1), (1, 0)])
 
 
-def row_stack(block):
-    return jnp.stack(exchange4([block] * 4, ROW))
-
-
-def plane_and_core(own_row):
-    along_x = swap2(own_row, "dp")
-    along_y = swap2(own_row, "cy")
-    across_low = swap2(along_x[:2], "cy")
-    across_high = swap2(along_y[2:], "dp")
-    arrays = [own_row, along_x, along_y, across_low, across_high]
-    return arrays + [core_swap(array) for array in arrays]
+def crossed(value, axes, first):
+    pairs = []
+    for u in range(2):
+        for v in range(2):
+            for core in range(2):
+                along = first ^ core
+                pairs.append(((u * 2 + v) * 2 + core, ((u ^ (1 - along)) * 2 + (v ^ along)) * 2 + core))
+    return lax.ppermute(value, axes + ("cc",), pairs)
+
+
+PLANE = ("dp", "cy")
+
+
+def row_gather(block):
+    pair = jnp.stack([block, crossed(block, ROW, 1)])
+    return jnp.concatenate([pair, crossed(pair, ROW, 0)], axis=0)
+
+
+def plane_gather(stack, forward_after):
+    near = crossed(stack, PLANE, 1)
+    far = crossed(stack, PLANE, 0)
+    both = crossed(after(near, *forward_after), PLANE, 0)
+    return [stack, near, far, both]
+
+
+def core_copies(arrays, ties):
+    return arrays + [core_swap(after(array, *tie)) for array, tie in zip(arrays, ties)]
 
 
 def gather_generic(w_output, w_inner, w_outer, norms, row, y, c):
@@ -501,11 +538,17 @@
             else:
                 halves.append(pack_outer(parts[1]))
         whole = lax.all_gather(jnp.stack(halves), GROUP)
+        flat = whole.reshape((-1,) + whole.shape[2:])
         arrays = []
         for kc in range(2):
-            for kx, ky, rows in ((0, 0, (0, 1, 2, 3)), (1, 0, (0, 1, 2, 3)), (0, 1, (0, 1, 2, 3)), (1, 1, (0, 1)), (1, 1, (2, 3))):
-                spots = jnp.stack([(row ^ k) * 4 + (y ^ ky) * 2 + (c ^ kc) for k in rows])
-                arrays.append(jnp.take(whole[:, kx], spots, axis=0))
+            core = c ^ kc
+            for spot in range(4):
+                first, second = spot % 2, spot // 2
+                kx = jnp.where(core == 0, second, first)
+                ky = jnp.where(core == 0, first, second)
+                steps = [jnp.where(core == 0, i, (i % 2) * 2 + i // 2) for i in range(4)]
+                spots = jnp.stack([((row ^ k) * 4 + (y ^ ky) * 2 + core) * 2 + kx for k in steps])
+                arrays.append(jnp.take(flat, spots, axis=0))
         chunks.append(arrays)
     return chunks
 
@@ -517,28 +560,20 @@
     return total
 
 
-def start_sums(keep, got):
-    def part(kx, ky, rows):
-        return (keep[kx, ky, rows].astype(f32) + got[kx, ky, rows].astype(f32)).astype(bf16)
-
-    everything = slice(0, 4)
-    return (
-        part(0, 0, everything), part(1, 0, everything), part(0, 1, everything),
-        part(1, 1, slice(0, 2)), part(1, 1, slice(2, 4)),
-    )
-
-
-def second_sums(sums, to_x, to_y):
-    own, along_x, along_y, _, _ = sums
-    x_sum = jnp.concatenate([along_x[:2], (along_x[2:].astype(f32) + to_y.astype(f32)).astype(bf16)], axis=0)
-    y_sum = jnp.concatenate([(along_y[:2].astype(f32) + to_x.astype(f32)).astype(bf16), along_y[2:]], axis=0)
-    return own, x_sum, y_sum
-
-
-def generic_sums(keep, got):
-    core = (keep.astype(f32) + got.astype(f32)).astype(bf16)
-    planes = [add_parts([core[g, 0], core_y]).astype(bf16) for g in range(2) for core_y in [swap2(core[g, 1], "cy")]]
-    return [add_parts(exchange4(plane, ROW)) for plane in planes]
+def halve(stack):
+    pass_on = crossed(stack[2:], ROW, 0)
+    pair = (stack[:2].astype(f32) + pass_on.astype(f32)).astype(bf16)
+    return pair[0].astype(f32) + crossed(pair[1], ROW, 1).astype(f32)
+
+
+def generic_sums(first, keep, send, c):
+    parts = [keep, send, first[0], first[1]]
+    by_x = [
+        (parts[0], jnp.where(c == 0, parts[1], parts[2])),
+        (jnp.where(c == 0, parts[2], parts[1]), parts[3]),
+    ]
+    planes = [add_parts([own, swap2(other, "cy")]).astype(bf16) for own, other in by_x]
+    return [halve(plane) for plane in planes]
 
 
 def local(
@@ -570,18 +605,26 @@
         back = swap_by(jnp.stack(parts), row)
         return back.reshape(2, 2, feat, half).transpose(0, 2, 1, 3).reshape(2, feat, cols)
 
+    this_half, other_half = dp_halves(jnp.concatenate([w_query, w_key, w_value], axis=1), c)
     x_own = jnp.stack(exchange4(to_row_order(tokens), ROW))
+    other_columns = core_swap(other_half)
+    near = jnp.where(z == c, this_half, other_columns)
+    far = jnp.where(z == c, other_columns, this_half)
+    norms = pack_norms(first_gain, first_shift, second_gain, second_shift)
+    if two:
+        block_a = jnp.concatenate([w_inner, pack_output(w_output), norms], axis=0)
+        row_a = row_gather(block_a)
+        row_b = row_gather(after(pack_outer(w_outer), row_a))
+    cot_blocks = to_row_order(out_grad)
+    wide = jnp.concatenate([cot_blocks[:, j * feat // 3 : (j + 1) * feat // 3] for j in range(3)], axis=2)
+    fill = ((0, 0), (0, wide.shape[2] - 3 * head_width))
+    near, far = jnp.pad(near, fill), jnp.pad(far, fill)
+    third_parts = exchange4(
+        [jnp.concatenate([(near, far)[k % 2], wide[k]], axis=0) for k in range(4)], ROW
+    )
+    mine = jnp.stack([part[: feat // 2, : 3 * head_width] for part in third_parts])
+    theirs = core_swap(mine)
     xs = exchange4([x_own] * 4, SQUARE)
-
-    qkv_rows = dp_gather(jnp.concatenate([w_query, w_key, w_value], axis=1))
-    row_halves = qkv_rows.reshape(2, feat // 2, 3 * head_width)
-    pieces = []
-    for r1 in range(2):
-        for r2 in range(2):
-            part = jnp.where((z ^ r2) == 0, row_halves[0], row_halves[1])
-            pieces.append(lax.ppermute(part, GROUP, group_route((r1, r2), False)))
-    mine = jnp.stack(pieces)
-    theirs = core_swap(mine)
 
     starts = []
     for kc in range(2):
@@ -596,82 +639,76 @@
     sines = jnp.sin(angles)
     sine = jnp.stack([-sines, sines], axis=1).reshape(HD, 4 * half)
 
-    norms = pack_norms(first_gain, first_shift, second_gain, second_shift)
-    if two:
-        block_a = jnp.concatenate([w_inner, pack_output(w_output), norms], axis=0)
-        row_a = row_stack(after(block_a, x_own))
-        chunk_a = plane_and_core(row_a)
-        row_b = row_stack(after(pack_outer(w_outer), row_a))
-        chunk_b = plane_and_core(row_b)
-    else:
-        chunk_a, chunk_b = gather_generic(w_output, w_inner, w_outer, norms, row, y, c)
-
     q_rot, kv_own = qkv(info, xs, mine, theirs, cosine, sine)
     kv_other = core_swap(kv_own)
     out, log_totals, *lows = attend(q_rot, kv_own, kv_other, bias)
     attn_parts = exchange4(lows, SQUARE)
-    cot_parts = exchange4(after(to_row_order(out_grad), xs[3]), ROW)
+    if two:
+        arrays_a = plane_gather(row_a, (kv_own,))
+        chunk_a = core_copies(arrays_a, [(kv_own,), (kv_own,), (lows[0],), (lows[0],)])
+        arrays_b = plane_gather(after(row_b, kv_own), (lows[0],))
+        chunk_b = core_copies(arrays_b, [(lows[0],), (attn_parts[1],), (attn_parts[2],), (attn_parts[3],)])
+    else:
+        chunk_a, chunk_b = gather_generic(w_output, w_inner, w_outer, norms, row, y, c)
     mixed, e0, e1, e2, e3, grad_one, attn_t, hidden_t, outer_t, branch_low, act_low, inner_low, norm_sums = middle(
-        info, attn_parts, x_own, cot_parts, chunk_a, chunk_b
+        info, attn_parts, x_own, third_parts, chunk_a, chunk_b
     )
     grads = exchange4([e0, e1, e2, e3], SQUARE)
-    give_outer = outer_grad(1, info, outer_t, act_low)
+    inner_args = (hidden_t, inner_low, attn_t, branch_low, norm_sums)
+    outer_args = (outer_t, act_low)
+
+    def tied(args, *earlier):
+        return (after(args[0], *earlier),) + args[1:]
+
+    def head_back(head, *earlier):
+        return attend_back(
+            head, after(q_rot, *earlier), kv_own, kv_other, bias, out, log_totals, grads, cosine, sine
+        )
+
+    give_inner = grad_call("inner", "give", info, inner_args)
+    got_inner = core_swap(give_inner)
+    give_outer = grad_call("outer", "give", info, tied(outer_args, give_inner))
     got_outer = core_swap(give_outer)
-    give_inner = inner_grad(1, info, hidden_t, after(inner_low, give_outer), attn_t, branch_low, norm_sums)
-    got_inner = core_swap(give_inner)
-    keep_outer = outer_grad(0, info, outer_t, after(act_low, give_inner))
-    keep_inner = inner_grad(0, info, hidden_t, after(inner_low, keep_outer), attn_t, branch_low, norm_sums)
-
-    def head_back(head, grads):
-        return attend_back(head, q_rot, kv_own, kv_other, bias, out, log_totals, grads, cosine, sine)
-
+    first_inner = grad_call("inner", "first", info, tied(inner_args, give_outer), got_inner)
+    came_inner = crossed(first_inner, PLANE, 0) if two else jnp.zeros_like(first_inner)
+    first_outer = grad_call("outer", "first", info, tied(outer_args, first_inner), got_outer)
+    came_outer = crossed(first_outer, PLANE, 0) if two else jnp.zeros_like(first_outer)
+    dq0, own0, send0 = head_back(0, first_outer)
+    keep_inner, pass_inner = grad_call(
+        "inner", "second", info, tied(inner_args, dq0), got_inner, after(came_inner, dq0)
+    )
+    dq1, own1, send1 = head_back(1, keep_inner)
+    keep_outer, pass_outer = grad_call(
+        "outer", "second", info, tied(outer_args, dq1), got_outer, after(came_outer, dq1)
+    )
     if two:
-        sums_outer = start_sums(keep_outer, got_outer)
-        outer_x = swap2(sums_outer[3], "dp")
-        outer_y = swap2(sums_outer[4], "cy")
-        first = head_back(0, [after(grads[0], sums_outer[3], sums_outer[4], keep_inner)] + grads[1:])
-        sums_inner = start_sums(after(keep_inner, first[0]), got_inner)
-        inner_x = swap2(sums_inner[3], "dp")
-        inner_y = swap2(sums_inner[4], "cy")
-        own_outer, x_outer, y_outer = second_sums(sums_outer, outer_x, outer_y)
-        plane_outer_parts = [own_outer, swap2(x_outer, "dp"), swap2(y_outer, "cy")]
-        second = head_back(1, [after(grads[0], x_outer, y_outer, sums_inner[3], sums_inner[4])] + grads[1:])
-        own_inner, x_inner, y_inner = second_sums(sums_inner, after(inner_x, second[0]), inner_y)
-        plane_inner_parts = [own_inner, swap2(x_inner, "dp"), swap2(y_inner, "cy")]
-        third_head = head_back(2, [after(grads[0], x_inner, y_inner)] + grads[1:])
+        plane_inner = add_parts([keep_inner, crossed(after(pass_inner, keep_inner), PLANE, 1)])
+        plane_inner = after(plane_inner, keep_outer).astype(bf16)
+        dq2, own2, send2 = head_back(2, plane_inner)
+        plane_outer = add_parts([keep_outer, after(crossed(pass_outer, PLANE, 1), dq2)]).astype(bf16)
+        outer_sums = [halve(plane_outer)]
+        inner_sums = [halve(plane_inner)]
+        own2 = after(own2, plane_outer)
     else:
-        first, second, third_head = (head_back(head, grads) for head in range(3))
-
-    mixed_out = from_row_order(exchange4(mixed, ROW))
-    dqs, owns, gives = zip(first, second, third_head)
-    gots = [core_swap(give) for give in gives]
-    d0, d1, d2, d3, proj = finish_dx(info, dqs, owns, gots, mine, theirs, cosine, sine)
+        dq2, own2, send2 = head_back(2, keep_outer)
+        outer_sums = generic_sums(first_outer, keep_outer, pass_outer, c)
+        inner_sums = generic_sums(first_inner, keep_inner, pass_inner, c)
+
+    gots = [core_swap(send) for send in (send0, send1, send2)]
+    d0, d1, d2, d3, proj = finish_dx(info, (dq0, dq1, dq2), (own0, own1, own2), gots, mine, theirs, cosine, sine)
     dx_parts = exchange4([d0, d1, d2, d3], SQUARE)
-    keep, give = finish_dw(info, proj, xs)
-    by_round = (keep + core_swap(give).astype(f32)).astype(bf16)
-    got = []
-    for r1 in range(2):
-        for r2 in range(2):
-            got.append(
-                lax.ppermute(by_round[r1 * 2 + r2], GROUP, group_route((r1, r2), True)).astype(f32)
-            )
-    if two:
-        plane_outer = add_parts(plane_outer_parts).astype(bf16)
-        outer_sums = [add_parts(exchange4(plane_outer, ROW))]
+    keep, give = finish_dw(info, after(proj, d0), xs)
+    got = core_swap(give)
+    by_row_step = (keep + got.astype(f32)).astype(bf16)
     d_x = add_parts([grad_one] + dx_parts).astype(bf16)
     d_input = from_row_order(exchange4(d_x, ROW)).astype(f32)
-    if two:
-        plane_inner = add_parts(plane_inner_parts).astype(bf16)
-        inner_sums = [add_parts(exchange4(plane_inner, ROW))]
-    else:
-        outer_sums = generic_sums(keep_outer, got_outer)
-        inner_sums = generic_sums(keep_inner, got_inner)
-
-    lower = got[0] + got[2]
-    upper = got[1] + got[3]
-    g_qkv = dp_reduce(
-        jnp.concatenate([jnp.where(z == 0, lower, upper), jnp.where(z == 0, upper, lower)], axis=0)
-    )
+    mixed_out = from_row_order([after(part, give) for part in exchange4(after(mixed, first_outer), ROW)])
+    q0, q1, q2, q3 = (part.astype(f32) for part in exchange4(by_row_step, ROW))
+    near_sum = q0 + q2
+    far_sum = q1 + q3
+    kept = jnp.where(z == c, near_sum, far_sum)
+    passed = core_swap(jnp.where(z == c, far_sum, near_sum).astype(bf16)).astype(f32)
+    g_qkv = dp_sum(kept, passed, c)
 
     half_rows = feat // 2
     third = half_rows // 3

time: 352 us -> 325 us (0.923)
  waiting for transfers between devices: 132 us -> 105 us
  other arithmetic: 31.1 us -> 10.1 us
  Pallas kernels: 87 us -> 98.1 us
  starting transfers between devices: 78.2 us -> 88.7 us
    ppermute x16 -> x2, waiting for transfers between devices: 44.5 us -> 1.82 us  [swap2(): return lax.ppermute(value, axis, [(0, 1), (1, 0)])]
    ppermute x10 -> x18, waiting for transfers between devices: 12.8 us -> 34.9 us  [crossed(): return lax.ppermute(value, axes + ('cc',), pairs)]
    ppermute x18, starting transfers between devices: 2.92 us -> 21.6 us  [core_swap(): return lax.ppermute(value, 'cc', [(0, 1), (1, 0)])]
    convert_element_type x12 -> x6, other arithmetic: 15.1 us -> 0.59 us  [the longest x2 0.17 us: halve(): pair = (stack[:2].astype(f32) + pass_on.astype(f32)).astype(bf16)]
    ppermute x36 -> x27, waiting for transfers between devices: 73.2 us -> 61.1 us  [exchange4(): lax.ppermute(blocks[step], axes, [(i, i ^ step) for i in range(4)])]
    pallas_call x5 -> x7, Pallas kernels: 37.8 us -> 48.8 us  [the longest x1 21.3 us: middle(): pl.pallas_call(middle_kernel, in_specs=[SM] + [VM] * 9 + [HB] * 16, out_s...]
    ppermute x10 -> x18, starting transfers between devices: 13.8 us -> 24.6 us  [crossed(): return lax.ppermute(value, axes + ('cc',), pairs)]
    ppermute x16 -> x2, starting transfers between devices: 15.4 us -> 4.81 us  [swap2(): return lax.ppermute(value, axis, [(0, 1), (1, 0)])]
  transfers between devices with their start and end apart: 80 -> 65, of which waited for: 30 -> 25; matrix products, arithmetic and copies ran while one was open for 13% -> 6% of each run, Pallas kernels for 16% -> 22%
where the time goes in v4:
time: 325 us; the launch traced here: 324 us
  waiting for transfers between devices  105 us (32%)
  Pallas kernels  98.1 us (30%)
  starting transfers between devices  88.7 us (27%)
  local copies, waits for them, and re-layouts  19.4 us (6%)
  other arithmetic  10.1 us (3%)
    ppermute x27, waiting for transfers between devices, exchange4(): lax.ppermute(blocks[step], axes, [(i, i ^ step) for i in range(4)])  61.1 us
    ppermute x27, starting transfers between devices, exchange4(): lax.ppermute(blocks[step], axes, [(i, i ^ step) for i in range(4)])  37.7 us
    ppermute x18, waiting for transfers between devices, crossed(): return lax.ppermute(value, axes + ('cc',), pairs)  34.9 us
    pallas_call x3, Pallas kernels, attend_back(): pl.pallas_call(attend_back_kernel, grid=(4 // QB,), in_specs=[hb, kspec,...  24.7 us
    ppermute x18, starting transfers between devices, crossed(): return lax.ppermute(value, axes + ('cc',), pairs)  24.6 us
    ppermute x18, starting transfers between devices, core_swap(): return lax.ppermute(value, 'cc', [(0, 1), (1, 0)])  21.6 us
    pallas_call x1, Pallas kernels, middle(): pl.pallas_call(middle_kernel, in_specs=[SM] + [VM] * 9 + [HB] * 16, out_s...  21.3 us
    pallas_call x1, Pallas kernels, attend(): pl.pallas_call(attend_kernel, grid=(heads, 4 // QB), in_specs=[pl.BlockSp...  11.5 us
  transfers between devices with their start and end apart: 65, of which 25 were waited for; matrix products, arithmetic and copies ran while one was open for 6% of the time, Pallas kernels for 22%

profile of v4, /device:TPU:0, one launch (start us, length us, event | category | flops | bytes accessed | tf_op | source)
XLA Modules:
  0.0 323.8 jit_solution(11398563061419312021)
XLA Ops:
  1.6 3.0 collective-permute-start.6
  10.1 2.5 collective-permute-start.2
  17.4 1.9 collective-permute-done.2
  19.3 3.5 %collective-permute-done.1 = bf16[192,256]{1,0:T(8,128)(2,1)S(1)} collective-permute-done((bf16[192,256]{1,0:T(8,128)(2,1)S(1)}, bf16[192,256]{1,0:T(8,128)(2,1)S(1)}, u32[]{:S(2)}, u32[]{:S(2)}) %collective-permute-start.1) | collective-permute-done | bytes 98336 | tf_op jit(solution)/shard_map/ppermute | solution.py:426
  27.4 1.9 collective-permute-start.9
  29.4 2.0 collective-permute-start.8
  31.4 16.3 %collective-permute-done.9.c2 = bf16[160,768]{1,0:T(8,128)(2,1)S(1)} collective-permute-done((bf16[160,768]{1,0:T(8,128)(2,1)S(1)}, bf16[160,768]{1,0:T(8,128)(2,1)S(1)}, u32[]{:S(2)}, u32[]{:S(2)}) %collective-permute-start.9) | collective-permute-done | bytes 245792 | tf_op jit(solution)/shard_map/ppermute | solution.py:426
  49.6 4.8 %collective-permute-done.8.c1 = bf16[160,768]{1,0:T(8,128)(2,1)S(1)} collective-permute-done((bf16[160,768]{1,0:T(8,128)(2,1)S(1)}, bf16[160,768]{1,0:T(8,128)(2,1)S(1)}, u32[]{:S(2)}, u32[]{:S(2)}) %collective-permute-start.8) | collective-permute-done | bytes 245792 | tf_op jit(solution)/shard_map/ppermute | solution.py:426
  54.4 6.9 %collective-permute-start.17 = (bf16[2,144,768]{2,1,0:T(8,128)(2,1)S(1)}, bf16[2,144,768]{2,1,0:T(8,128)(2,1)S(1)}, u32[]{:S(2)}, u32[]{:S(2)}) collective-permute-start(bf16[2,144,768]{2,1,0:T(8,128)(2,1)S(1)} %pad_maximum_fusion.3), channel_id=1, source_target_pairs={{0,8},{1,5},{4,12},{5,1},{8,0},{9,13},{12,4},{13,9},{2,10},{3,7},{... | collective-permute-start | bytes 1327112 | tf_op jit(solution)/shard_map/ppermute | solution.py:507
  63.0 7.9 %collective-permute-done.17 = bf16[2,144,768]{2,1,0:T(8,128)(2,1)S(1)} collective-permute-done((bf16[2,144,768]{2,1,0:T(8,128)(2,1)S(1)}, bf16[2,144,768]{2,1,0:T(8,128)(2,1)S(1)}, u32[]{:S(2)}, u32[]{:S(2)}) %collective-permute-start.17) | collective-permute-done | bytes 442400 | tf_op jit(solution)/shard_map/ppermute | solution.py:507
  71.0 4.8 %collective-permute-start.18 = (bf16[4,144,768]{2,1,0:T(8,128)(2,1)S(1)}, bf16[4,144,768]{2,1,0:T(8,128)(2,1)}, u32[]{:S(2)}, u32[]{:S(2)}) collective-permute-start(bf16[4,144,768]{2,1,0:T(8,128)(2,1)S(1)} %pad_maximum_fusion.refs_0_), channel_id=1, source_target_pairs={{0,2},{1,17},{2,0},{3,19},{16,18},{17,1},{18,16},{19,3},{4,6},{5,2... | collective-permute-start | bytes 2654216 | tf_op jit(solution)/shard_map/ppermute | solution.py:507
  80.8 4.0 %qkv.1 = (bf16[192,1024]{1,0:T(8,128)(2,1)}, bf16[384,1024]{1,0:T(8,128)(2,1)}) custom-call(s32[8]{0:T(128)} %stack.142.info, bf16[4,192,256]{2,1,0:T(8,128)(2,1)} %copy-done.4, bf16[4,192,256]{2,1,0:T(8,128)(2,1)} %collective-permute-done.3.x1, bf16[4,192,256]{2,1,0:T(8,128)(2,1)} %collective-permute-done.4.x2, bf16[4,192,256]{2,1,0:T(8,128)(2,1)} %copy-done.17, ...), custom_call_target="tpu_custom_call" | custom-call | tf_op jit(solution)/shard_map/qkv/pallas_call | solution.py:171
  84.9 2.0 collective-permute-start.26
  87.6 8.1 %collective-permute-done.26 = bf16[2,96,768]{2,1,0:T(8,128)(2,1)S(1)} collective-permute-done((bf16[2,96,768]{2,1,0:T(8,128)(2,1)S(1)}, bf16[2,96,768]{2,1,0:T(8,128)(2,1)S(1)}, u32[]{:S(2)}, u32[]{:S(2)}) %collective-permute-start.26) | collective-permute-done | bytes 294944 | tf_op jit(solution)/shard_map/ppermute | solution.py:507
  98.4 11.5 %attend.1 = (f32[192,1024]{1,0:T(8,128)}, f32[3,1,1024]{2,1,0:T(1,128)}, bf16[192,256]{1,0:T(8,128)(2,1)}, bf16[192,256]{1,0:T(8,128)(2,1)}, bf16[192,256]{1,0:T(8,128)(2,1)}, /*index=5*/bf16[192,256]{1,0:T(8,128)(2,1)}) custom-call(bf16[192,1024]{1,0:T(8,128)(2,1)} %get-tuple-element.132.q_ref, bf16[384,1024]{1,0:T(8,128)(2,1)} %get-tuple-element.85.ko_ref.vo_ref, ...), custom_call_target="tpu_custom_call" | custom-call | flops 6442450944 | bytes 8388608 | tf_op jit(solution)/shard_map/attend/pallas_call | solution.py:72
  109.9 2.4 collective-permute-done.27.refs_9_
  112.3 1.9 collective-permute-start.29
  114.8 4.3 %collective-permute-done.14.a2 = bf16[192,256]{1,0:T(8,128)(2,1)S(1)} collective-permute-done((bf16[192,256]{1,0:T(8,128)(2,1)}, bf16[192,256]{1,0:T(8,128)(2,1)S(1)}, u32[]{:S(2)}, u32[]{:S(2)}) %collective-permute-start.14) | collective-permute-done | bytes 98336 | tf_op jit(solution)/shard_map/ppermute | solution.py:426
  120.2 2.6 collective-permute-done.20.refs_3_
  124.5 2.1 collective-permute-done.13.a1
  126.6 5.2 %collective-permute-start.22 = (bf16[4,144,768]{2,1,0:T(8,128)(2,1)}, bf16[4,144,768]{2,1,0:T(8,128)(2,1)S(1)}, u32[]{:S(2)}, u32[]{:S(2)}) collective-permute-start(bf16[4,144,768]{2,1,0:T(8,128)(2,1)} %collective-permute-done.18.refs_1_), channel_id=1, source_target_pairs={{0,1},{1,0},{2,3},{3,2},{4,5},{5,4},{6,7},{7,6},{8,9},{9,8},{10,11... | collective-permute-start | bytes 2654216 | tf_op jit(solution)/shard_map/ppermute | solution.py:431
  132.8 5.4 %collective-permute-done.31.refs_13_ = bf16[4,96,768]{2,1,0:T(8,128)(2,1)S(1)} collective-permute-done((bf16[4,96,768]{2,1,0:T(8,128)(2,1)}, bf16[4,96,768]{2,1,0:T(8,128)(2,1)S(1)}, u32[]{:S(2)}, u32[]{:S(2)}) %collective-permute-start.31) | collective-permute-done | bytes 589856 | tf_op jit(solution)/shard_map/ppermute | solution.py:431
  140.2 21.3 %middle.1 = (bf16[4,192,256]{2,1,0:T(8,128)(2,1)}, bf16[192,256]{1,0:T(8,128)(2,1)}, bf16[192,256]{1,0:T(8,128)(2,1)}, bf16[192,256]{1,0:T(8,128)(2,1)}, bf16[19...) custom-call(s32[8]{0:T(128)} %stack.142.info, ...), custom_call_target="tpu_custom_call" | custom-call | flops 14495514624 | bytes 56623104 | tf_op jit(solution)/shard_map/middle/pallas_call | solution.py:341
  161.5 5.6 %inner_give.1 = bf16[2,2,4,144,768]{4,3,2,1,0:T(8,128)(2,1)} custom-call(s32[8]{0:T(128)} %stack.142.info, bf16[768,256]{1,0:T(8,128)(2,1)} %get-tuple-element.121.refs_0_, bf16[256,3072]{1,0:T(8,128)(2,1)} %get-tuple-element.104.refs_1_, bf16[768,256]{1,0:T(8,128)(2,1)} %get-tuple-element.105.refs_2_, bf16[4,256,256]{2,1,0:T(8,128)(2,1)} %get-tuple-element.106.refs_3_, ...), custom_call_target="tpu_custom_call" | custom-call | flops 603979776 | bytes 1769472 | tf_op jit(solution)/shard_map/inner_give/pallas_call | solution.py:408
  167.7 5.0 %outer_give.1 = bf16[2,2,4,96,768]{4,3,2,1,0:T(8,128)(2,1)} custom-call(s32[8]{0:T(128)} %stack.142.info, bf16[768,256]{1,0:T(8,128)(2,1)} %get-tuple-element.128.refs_0_, bf16[256,3072]{1,0:T(8,128)(2,1)} %get-tuple-element.109.refs_1_), custom_call_target="tpu_custom_call" | custom-call | flops 603979776 | bytes 1179648 | tf_op jit(solution)/shard_map/outer_give/pallas_call | solution.py:408
  175.5 4.1 %inner_first.1 = bf16[2,4,144,768]{3,2,1,0:T(8,128)(2,1)} custom-call(s32[8]{0:T(128)} %stack.142.info, bf16[768,256]{1,0:T(8,128)(2,1)} %get-tuple-element.121.refs_0_, bf16[256,3072]{1,0:T(8,128)(2,1)} %get-tuple-element.104.refs_1_, bf16[768,256]{1,0:T(8,128)(2,1)} %get-tuple-element.105.refs_2_, bf16[4,256,256]{2,1,0:T(8,128)(2,1)} %get-tuple-element.106.refs_3_, ...), custom_call_target="tpu_custom_call" | custom-call | flops 301989888 | bytes 1769472 | tf_op jit(solution)/shard_map/inner_first/pallas_call | solution.py:415
  180.7 2.5 collective-permute-start.38
  183.2 3.6 %outer_first.1 = bf16[2,4,96,768]{3,2,1,0:T(8,128)(2,1)} custom-call(s32[8]{0:T(128)} %stack.142.info, bf16[768,256]{1,0:T(8,128)(2,1)} %get-tuple-element.128.refs_0_, bf16[256,3072]{1,0:T(8,128)(2,1)} %get-tuple-element.109.refs_1_, bf16[2,2,4,96,768]{4,3,2,1,0:T(8,128)(2,1)} %collective-permute-done.35.refs_2_), custom_call_target="tpu_custom_call" | custom-call | flops 301989888 | bytes 1179648 | tf_op jit(solution)/shard_map/outer_first/pallas_call | solution.py:415
  186.8 2.0 collective-permute-start.41
  189.5 8.3 %attend_back.3 = (bf16[64,1024]{1,0:T(8,128)(2,1)}, f32[1024,128]{1,0:T(8,128)}, bf16[1024,128]{1,0:T(8,128)(2,1)}) custom-call(bf16[192,1024]{1,0:T(8,128)(2,1)} %get-tuple-element.132.q_ref, bf16[384,1024]{1,0:T(8,128)(2,1)} %get-tuple-element.85.ko_ref.vo_ref, bf16[384,1024]{1,0:T(8,128)(2,1)} %get-tuple-element.85.ko_ref.vo_ref, ...), custom_call_target="tpu_custom_call" | custom-call | flops 5368709120 | bytes 8388608 | tf_op jit(solution)/shard_map/attend_back/pallas_call | solution.py:124
  197.8 4.6 %collective-permute-done.39.refs_6_ = bf16[2,4,144,768]{3,2,1,0:T(8,128)(2,1)S(1)} collective-permute-done((bf16[2,4,144,768]{3,2,1,0:T(8,128)(2,1)}, bf16[2,4,144,768]{3,2,1,0:T(8,128)(2,1)S(1)}, u32[]{:S(2)}, u32[]{:S(2)}) %collective-permute-start.39) | collective-permute-done | bytes 1769504 | tf_op jit(solution)/shard_map/ppermute | solution.py:507
  203.7 5.1 %inner_second.1 = (bf16[4,144,768]{2,1,0:T(8,128)(2,1)}, bf16[4,144,768]{2,1,0:T(8,128)(2,1)}) custom-call(s32[8]{0:T(128)} %stack.142.info, bf16[768,256]{1,0:T(8,128)(2,1)} %get-tuple-element.121.refs_0_, bf16[256,3072]{1,0:T(8,128)(2,1)} %get-tuple-element.104.refs_1_, bf16[768,256]{1,0:T(8,128)(2,1)} %get-tuple-element.105.refs_2_, ...), custom_call_target="tpu_custom_call" | custom-call | flops 301989888 | bytes 1769472 | tf_op jit(solution)/shard_map/inner_second/pallas_call | solution.py:419
  209.1 12.5 %collective-permute-start.43 = (bf16[1024,128]{1,0:T(8,128)(2,1)}, bf16[1024,128]{1,0:T(8,128)(2,1)}, u32[]{:S(2)}, u32[]{:S(2)}) collective-permute-start(bf16[1024,128]{1,0:T(8,128)(2,1)} %get-tuple-element.140), channel_id=1, source_target_pairs={{0,1},{1,0},{2,3},{3,2},{4,5},{5,4},{6,7},{7,6},{8,9},{9,8},{10,11... | collective-permute-start | bytes 786440 | tf_op jit(solution)/shard_map/ppermute | solution.py:431
  221.6 8.2 %attend_back.4 = (bf16[64,1024]{1,0:T(8,128)(2,1)}, f32[1024,128]{1,0:T(8,128)}, bf16[1024,128]{1,0:T(8,128)(2,1)}) custom-call(bf16[192,1024]{1,0:T(8,128)(2,1)} %get-tuple-element.132.q_ref, bf16[384,1024]{1,0:T(8,128)(2,1)} %get-tuple-element.85.ko_ref.vo_ref, bf16[384,1024]{1,0:T(8,128)(2,1)} %get-tuple-element.85.ko_ref.vo_ref, ...), custom_call_target="tpu_custom_call" | custom-call | flops 5368709120 | bytes 8388608 | tf_op jit(solution)/shard_map/attend_back/pallas_call | solution.py:124
  230.8 4.2 %outer_second.1 = (bf16[4,96,768]{2,1,0:T(8,128)(2,1)}, bf16[4,96,768]{2,1,0:T(8,128)(2,1)}) custom-call(s32[8]{0:T(128)} %stack.142.info, bf16[768,256]{1,0:T(8,128)(2,1)} %get-tuple-element.128.refs_0_, bf16[256,3072]{1,0:T(8,128)(2,1)} %get-tuple-element.109.refs_1_, bf16[2,2,4,96,768]{4,3,2,1,0:T(8,128)(2,1)} %collective-permute-done.35.refs_2_, ...), custom_call_target="tpu_custom_call" | custom-call | flops 301989888 | bytes 1179648 | tf_op jit(solution)/shard_map/outer_second/pallas_call | solution.py:419
  235.4 8.2 %attend_back.5 = (bf16[64,1024]{1,0:T(8,128)(2,1)}, f32[1024,128]{1,0:T(8,128)}, bf16[1024,128]{1,0:T(8,128)(2,1)}) custom-call(bf16[192,1024]{1,0:T(8,128)(2,1)} %get-tuple-element.132.q_ref, bf16[384,1024]{1,0:T(8,128)(2,1)} %get-tuple-element.85.ko_ref.vo_ref, bf16[384,1024]{1,0:T(8,128)(2,1)} %get-tuple-element.85.ko_ref.vo_ref, ...), custom_call_target="tpu_custom_call" | custom-call | flops 5368709120 | bytes 8388608 | tf_op jit(solution)/shard_map/attend_back/pallas_call | solution.py:124
  252.5 4.7 %finish_dx.1 = (f32[4,192,256]{2,1,0:T(8,128)}, bf16[4,192,256]{2,1,0:T(8,128)(2,1)}, bf16[4,192,256]{2,1,0:T(8,128)(2,1)}, bf16[4,192,256]{2,1,0:T(8,128)(2,1)}, bf16[576,1024]{1,0:T(8,128)(2,1)}) custom-call(s32[8]{0:T(128)} %stack.142.info, bf16[64,1024]{1,0:T(8,128)(2,1)} %get-tuple-element.120.refs_0_, bf16[64,1024]{1,0:T(8,128)(2,1)} %get-tuple-element.125.refs_1_, ...), custom_call_target="tpu_custom_call" | custom-call | flops 905969664 | bytes 6291456 | tf_op jit(solution)/shard_map/finish_dx/pallas_call | solution.py:196
  257.2 7.0 %collective-permute-done.63 = bf16[2,96,768]{2,1,0:T(8,128)(2,1)S(1)} collective-permute-done((bf16[2,96,768]{2,1,0:T(8,128)(2,1)S(1)}, bf16[2,96,768]{2,1,0:T(8,128)(2,1)S(1)}, u32[]{:S(2)}, u32[]{:S(2)}) %collective-permute-start.63) | collective-permute-done | bytes 294944 | tf_op jit(solution)/shard_map/ppermute | solution.py:507
  264.4 4.3 %finish_dw.1 = (f32[4,96,576]{2,1,0:T(8,128)}, bf16[4,96,576]{2,1,0:T(8,128)(2,1)}) custom-call(s32[8]{0:T(128)} %stack.142.info, bf16[576,1024]{1,0:T(8,128)(2,1)} %get-tuple-element.145.p_ref, bf16[4,192,256]{2,1,0:T(8,128)(2,1)} %copy-done.4, bf16[4,192,256]{2,1,0:T(8,128)(2,1)} %collective-permute-done.3.x1, ...), custom_call_target="tpu_custom_call" | custom-call | flops 905969664 | bytes 3145728 | tf_op jit(solution)/shard_map/finish_dw/pallas_call | solution.py:215
  270.2 3.0 collective-permute-start.50
  275.1 2.1 collective-permute-done.61
  277.5 3.0 collective-permute-done.49
  280.5 7.6 %collective-permute-done.50 = bf16[4,192,256]{2,1,0:T(8,128)(2,1)S(1)} collective-permute-done((bf16[4,192,256]{2,1,0:T(8,128)(2,1)}, bf16[4,192,256]{2,1,0:T(8,128)(2,1)S(1)}, u32[]{:S(2)}, u32[]{:S(2)}) %collective-permute-start.50) | collective-permute-done | bytes 393248 | tf_op jit(solution)/shard_map/ppermute | solution.py:426
  288.1 7.7 %collective-permute-done.51 = bf16[4,192,256]{2,1,0:T(8,128)(2,1)S(1)} collective-permute-done((bf16[4,192,256]{2,1,0:T(8,128)(2,1)}, bf16[4,192,256]{2,1,0:T(8,128)(2,1)S(1)}, u32[]{:S(2)}, u32[]{:S(2)}) %collective-permute-start.51) | collective-permute-done | bytes 393248 | tf_op jit(solution)/shard_map/ppermute | solution.py:426
  296.1 3.6 %collective-permute-start.54 = (bf16[192,256]{1,0:T(8,128)(2,1)S(1)}, bf16[192,256]{1,0:T(8,128)(2,1)S(1)}, u32[]{:S(2)}, u32[]{:S(2)}) collective-permute-start(bf16[192,256]{1,0:T(8,128)(2,1)S(1)} %get-tuple-element.169), channel_id=1, source_target_pairs={{0,12},{4,8},{8,4},{12,0},{1,13},{5,9},{9,5},{13,1},{2,14},{6,10},... | collective-permute-start | bytes 294920 | tf_op jit(solution)/shard_map/ppermute | solution.py:426
  302.8 2.2 collective-permute-start.56
  307.0 4.5 %collective-permute-done.53 = bf16[192,256]{1,0:T(8,128)(2,1)S(1)} collective-permute-done((bf16[192,256]{1,0:T(8,128)(2,1)S(1)}, bf16[192,256]{1,0:T(8,128)(2,1)S(1)}, u32[]{:S(2)}, u32[]{:S(2)}) %collective-permute-start.53) | collective-permute-done | bytes 98336 | tf_op jit(solution)/shard_map/ppermute | solution.py:426
  311.7 3.2 collective-permute-done.56
  (262 shorter events, 68.3 us)
Async XLA Ops:
  1.6 15.6 %collective-permute-start.6 = (bf16[96,576]{1,0:T(8,128)(2,1)S(1)}, bf16[96,576]{1,0:T(8,128)(2,1)S(1)}, u32[]{:S(2)}, u32[]{:S(2)}) collective-permute-start(bf16[96,576]{1,0:T(8,128)(2,1)S(1)} %pad_maximum_fusion.16), channel_id=1, source_target_pairs={{0,16},{16,0},{1,17},{17,1},{2,18},{18,2},{3,19},{19,3},{4,20},{20... | collective-permute-start | bytes 331784 | tf_op jit(solution)/shard_map/ppermute | solution.py:497
  7.1 22.2 %collective-permute-start.16 = (bf16[144,768]{1,0:T(8,128)(2,1)S(1)}, bf16[144,768]{1,0:T(8,128)(2,1)S(1)}, u32[]{:S(2)}, u32[]{:S(2)}) collective-permute-start(bf16[144,768]{1,0:T(8,128)(2,1)S(1)} %pad_maximum_fusion.14), channel_id=1, source_target_pairs={{0,4},{1,9},{4,0},{5,13},{8,12},{9,1},{12,8},{13,5},{2,6},{3,11},{... | collective-permute-start | bytes 663560 | tf_op jit(solution)/shard_map/ppermute | solution.py:507
  10.1 9.3 %collective-permute-start.2 = (bf16[192,256]{1,0:T(8,128)(2,1)S(1)}, bf16[192,256]{1,0:T(8,128)(2,1)S(1)}, u32[]{:S(2)}, u32[]{:S(2)}) collective-permute-start(bf16[192,256]{1,0:T(8,128)(2,1)S(1)} %get-tuple-element.184), channel_id=1, source_target_pairs={{0,12},{4,8},{8,4},{12,0},{1,13},{5,9},{9,5},{13,1},{2,14},{6,10},... | collective-permute-start | bytes 294920 | tf_op jit(solution)/shard_map/ppermute | solution.py:426
  12.6 10.3 %collective-permute-start.1 = (bf16[192,256]{1,0:T(8,128)(2,1)S(1)}, bf16[192,256]{1,0:T(8,128)(2,1)S(1)}, u32[]{:S(2)}, u32[]{:S(2)}) collective-permute-start(bf16[192,256]{1,0:T(8,128)(2,1)S(1)} %get-tuple-element.185), channel_id=1, source_target_pairs={{0,8},{4,12},{8,0},{12,4},{1,9},{5,13},{9,1},{13,5},{2,10},{6,14},... | collective-permute-start | bytes 294920 | tf_op jit(solution)/shard_map/ppermute | solution.py:426
  12.8 10.1 %collective-permute-start = (bf16[192,256]{1,0:T(8,128)(2,1)S(1)}, bf16[192,256]{1,0:T(8,128)(2,1)S(1)}, u32[]{:S(2)}, u32[]{:S(2)}) collective-permute-start(bf16[192,256]{1,0:T(8,128)(2,1)S(1)} %get-tuple-element.186), channel_id=1, source_target_pairs={{0,4},{4,0},{8,12},{12,8},{1,5},{5,1},{9,13},{13,9},{2,6},{6,2},{1... | collective-permute-start | bytes 294920 | tf_op jit(solution)/shard_map/ppermute | solution.py:426
  22.9 52.9 %collective-permute-start.5 = (bf16[4,192,256]{2,1,0:T(8,128)(2,1)S(1)}, bf16[4,192,256]{2,1,0:T(8,128)(2,1)S(1)}, u32[]{:S(2)}, u32[]{:S(2)}) collective-permute-start(bf16[4,192,256]{2,1,0:T(8,128)(2,1)S(1)} %pad_maximum_fusion.4.x0.x_ref), channel_id=1, source_target_pairs={{0,6},{2,4},{4,2},{6,0},{1,7},{3,5},{5,3},{7,1},{8,14},{10,12},{12... | collective-permute-start | bytes 1179656 | tf_op jit(solution)/shard_map/ppermute | solution.py:426
  24.4 55.6 %collective-permute-start.4 = (bf16[4,192,256]{2,1,0:T(8,128)(2,1)S(1)}, bf16[4,192,256]{2,1,0:T(8,128)(2,1)}, u32[]{:S(2)}, u32[]{:S(2)}) collective-permute-start(bf16[4,192,256]{2,1,0:T(8,128)(2,1)S(1)} %pad_maximum_fusion.4.x0.x_ref), channel_id=1, source_target_pairs={{0,4},{2,6},{4,0},{6,2},{1,5},{3,7},{5,1},{7,3},{8,12},{10,14},{12... | collective-permute-start | bytes 1179656 | tf_op jit(solution)/shard_map/ppermute | solution.py:426
  26.0 54.0 %collective-permute-start.3 = (bf16[4,192,256]{2,1,0:T(8,128)(2,1)S(1)}, bf16[4,192,256]{2,1,0:T(8,128)(2,1)}, u32[]{:S(2)}, u32[]{:S(2)}) collective-permute-start(bf16[4,192,256]{2,1,0:T(8,128)(2,1)S(1)} %pad_maximum_fusion.4.x0.x_ref), channel_id=1, source_target_pairs={{0,2},{2,0},{4,6},{6,4},{1,3},{3,1},{5,7},{7,5},{8,10},{10,8},{12,... | collective-permute-start | bytes 1179656 | tf_op jit(solution)/shard_map/ppermute | solution.py:426
  27.4 20.3 %collective-permute-start.9 = (bf16[160,768]{1,0:T(8,128)(2,1)S(1)}, bf16[160,768]{1,0:T(8,128)(2,1)S(1)}, u32[]{:S(2)}, u32[]{:S(2)}) collective-permute-start(bf16[160,768]{1,0:T(8,128)(2,1)S(1)} %get-tuple-element.197), channel_id=1, source_target_pairs={{0,8},{4,12},{8,0},{12,4},{1,9},{5,13},{9,1},{13,5},{2,10},{6,14},... | collective-permute-start | bytes 737288 | tf_op jit(solution)/shard_map/ppermute | solution.py:426
  29.4 25.0 %collective-permute-start.8 = (bf16[160,768]{1,0:T(8,128)(2,1)S(1)}, bf16[160,768]{1,0:T(8,128)(2,1)S(1)}, u32[]{:S(2)}, u32[]{:S(2)}) collective-permute-start(bf16[160,768]{1,0:T(8,128)(2,1)S(1)} %get-tuple-element.198), channel_id=1, source_target_pairs={{0,4},{4,0},{8,12},{12,8},{1,5},{5,1},{9,13},{13,9},{2,6},{6,2},{1... | collective-permute-start | bytes 737288 | tf_op jit(solution)/shard_map/ppermute | solution.py:426
  47.7 13.6 %collective-permute-start.10 = (bf16[160,768]{1,0:T(8,128)(2,1)S(1)}, bf16[160,768]{1,0:T(8,128)(2,1)S(1)}, u32[]{:S(2)}, u32[]{:S(2)}) collective-permute-start(bf16[160,768]{1,0:T(8,128)(2,1)S(1)} %get-tuple-element.199), channel_id=1, source_target_pairs={{0,12},{4,8},{8,4},{12,0},{1,13},{5,9},{9,5},{13,1},{2,14},{6,10},... | collective-permute-start | bytes 737288 | tf_op jit(solution)/shard_map/ppermute | solution.py:426
  54.4 16.5 %collective-permute-start.17 = (bf16[2,144,768]{2,1,0:T(8,128)(2,1)S(1)}, bf16[2,144,768]{2,1,0:T(8,128)(2,1)S(1)}, u32[]{:S(2)}, u32[]{:S(2)}) collective-permute-start(bf16[2,144,768]{2,1,0:T(8,128)(2,1)S(1)} %pad_maximum_fusion.3), channel_id=1, source_target_pairs={{0,8},{1,5},{4,12},{5,1},{8,0},{9,13},{12,4},{13,9},{2,10},{3,7},{... | collective-permute-start | bytes 1327112 | tf_op jit(solution)/shard_map/ppermute | solution.py:507
  62.1 17.9 %collective-permute-start.11 = (bf16[4,96,576]{2,1,0:T(8,128)(2,1)S(1)}, bf16[4,96,576]{2,1,0:T(8,128)(2,1)S(1)}, u32[]{:S(2)}, u32[]{:S(2)}) collective-permute-start(bf16[4,96,576]{2,1,0:T(8,128)(2,1)S(1)} %pad_maximum_fusion.2.mine_ref.refs_9_), channel_id=1, source_target_pairs={{0,1},{1,0},{2,3},{3,2},{4,5},{5,4},{6,7},{7,6},{8,9},{9,8},{10,11... | collective-permute-start | bytes 1327112 | tf_op jit(solution)/shard_map/ppermute | solution.py:431
  71.0 24.9 %collective-permute-start.18 = (bf16[4,144,768]{2,1,0:T(8,128)(2,1)S(1)}, bf16[4,144,768]{2,1,0:T(8,128)(2,1)}, u32[]{:S(2)}, u32[]{:S(2)}) collective-permute-start(bf16[4,144,768]{2,1,0:T(8,128)(2,1)S(1)} %pad_maximum_fusion.refs_0_), channel_id=1, source_target_pairs={{0,2},{1,17},{2,0},{3,19},{16,18},{17,1},{18,16},{19,3},{4,6},{5,2... | collective-permute-start | bytes 2654216 | tf_op jit(solution)/shard_map/ppermute | solution.py:507
  84.8 11.6 %collective-permute-start.12 = (bf16[384,1024]{1,0:T(8,128)(2,1)}, bf16[384,1024]{1,0:T(8,128)(2,1)}, u32[]{:S(2)}, u32[]{:S(2)}) collective-permute-start(bf16[384,1024]{1,0:T(8,128)(2,1)} %get-tuple-element.85.ko_ref.vo_ref), channel_id=1, source_target_pairs={{0,1},{1,0},{2,3},{3,2},{4,5},{5,4},{6,7},{7,6},{8,9},{9,8},{10,11... | collective-permute-start | bytes 2359304 | tf_op jit(solution)/shard_map/ppermute | solution.py:431
  84.9 10.8 %collective-permute-start.26 = (bf16[2,96,768]{2,1,0:T(8,128)(2,1)S(1)}, bf16[2,96,768]{2,1,0:T(8,128)(2,1)S(1)}, u32[]{:S(2)}, u32[]{:S(2)}) collective-permute-start(bf16[2,96,768]{2,1,0:T(8,128)(2,1)S(1)} %pad_maximum_fusion.8), channel_id=1, source_target_pairs={{0,8},{1,5},{4,12},{5,1},{8,0},{9,13},{12,4},{13,9},{2,10},{3,7},{... | collective-permute-start | bytes 884744 | tf_op jit(solution)/shard_map/ppermute | solution.py:507
  87.6 31.5 %collective-permute-start.19 = (bf16[4,144,768]{2,1,0:T(8,128)(2,1)S(1)}, bf16[4,144,768]{2,1,0:T(8,128)(2,1)}, u32[]{:S(2)}, u32[]{:S(2)}) collective-permute-start(bf16[4,144,768]{2,1,0:T(8,128)(2,1)S(1)} %pad_maximum_fusion.refs_0_), channel_id=1, source_target_pairs={{0,16},{1,3},{2,18},{3,1},{16,0},{17,19},{18,2},{19,17},{4,20},{5,... | collective-permute-start | bytes 2654216 | tf_op jit(solution)/shard_map/ppermute | solution.py:507
  87.6 32.0 %collective-permute-start.21 = (bf16[4,144,768]{2,1,0:T(8,128)(2,1)S(1)}, bf16[4,144,768]{2,1,0:T(8,128)(2,1)}, u32[]{:S(2)}, u32[]{:S(2)}) collective-permute-start(bf16[4,144,768]{2,1,0:T(8,128)(2,1)S(1)} %pad_maximum_fusion.refs_0_), channel_id=1, source_target_pairs={{0,1},{1,0},{2,3},{3,2},{4,5},{5,4},{6,7},{7,6},{8,9},{9,8},{10,11... | collective-permute-start | bytes 2654216 | tf_op jit(solution)/shard_map/ppermute | solution.py:431
  95.8 18.5 %collective-permute-start.28 = (bf16[4,96,768]{2,1,0:T(8,128)(2,1)S(1)}, bf16[4,96,768]{2,1,0:T(8,128)(2,1)S(1)}, u32[]{:S(2)}, u32[]{:S(2)}) collective-permute-start(bf16[4,96,768]{2,1,0:T(8,128)(2,1)S(1)} %pad_maximum_fusion.1.refs_8_), channel_id=1, source_target_pairs={{0,16},{1,3},{2,18},{3,1},{16,0},{17,19},{18,2},{19,17},{4,20},{5,... | collective-permute-start | bytes 1769480 | tf_op jit(solution)/shard_map/ppermute | solution.py:507
  95.9 16.4 %collective-permute-start.27 = (bf16[4,96,768]{2,1,0:T(8,128)(2,1)S(1)}, bf16[4,96,768]{2,1,0:T(8,128)(2,1)}, u32[]{:S(2)}, u32[]{:S(2)}) collective-permute-start(bf16[4,96,768]{2,1,0:T(8,128)(2,1)S(1)} %pad_maximum_fusion.1.refs_8_), channel_id=1, source_target_pairs={{0,2},{1,17},{2,0},{3,19},{16,18},{17,1},{18,16},{19,3},{4,6},{5,2... | collective-permute-start | bytes 1769480 | tf_op jit(solution)/shard_map/ppermute | solution.py:507
  96.4 26.3 %collective-permute-start.20 = (bf16[4,144,768]{2,1,0:T(8,128)(2,1)}, bf16[4,144,768]{2,1,0:T(8,128)(2,1)S(1)}, u32[]{:S(2)}, u32[]{:S(2)}) collective-permute-start(bf16[4,144,768]{2,1,0:T(8,128)(2,1)} %collective-permute-done.18.refs_1_), channel_id=1, source_target_pairs={{0,16},{1,3},{2,18},{3,1},{16,0},{17,19},{18,2},{19,17},{4,20},{5,... | collective-permute-start | bytes 2654216 | tf_op jit(solution)/shard_map/ppermute | solution.py:507
  112.3 19.6 %collective-permute-start.29 = (bf16[4,96,768]{2,1,0:T(8,128)(2,1)}, bf16[4,96,768]{2,1,0:T(8,128)(2,1)S(1)}, u32[]{:S(2)}, u32[]{:S(2)}) collective-permute-start(bf16[4,96,768]{2,1,0:T(8,128)(2,1)} %collective-permute-done.27.refs_9_), channel_id=1, source_target_pairs={{0,16},{1,3},{2,18},{3,1},{16,0},{17,19},{18,2},{19,17},{4,20},{5,... | collective-permute-start | bytes 1769480 | tf_op jit(solution)/shard_map/ppermute | solution.py:507
  119.1 13.2 %collective-permute-start.30 = (bf16[4,96,768]{2,1,0:T(8,128)(2,1)S(1)}, bf16[4,96,768]{2,1,0:T(8,128)(2,1)S(1)}, u32[]{:S(2)}, u32[]{:S(2)}) collective-permute-start(bf16[4,96,768]{2,1,0:T(8,128)(2,1)S(1)} %pad_maximum_fusion.1.refs_8_), channel_id=1, source_target_pairs={{0,1},{1,0},{2,3},{3,2},{4,5},{5,4},{6,7},{7,6},{8,9},{9,8},{10,11... | collective-permute-start | bytes 1769480 | tf_op jit(solution)/shard_map/ppermute | solution.py:431
  119.1 13.3 %collective-permute-start.32 = (bf16[4,96,768]{2,1,0:T(8,128)(2,1)S(1)}, bf16[4,96,768]{2,1,0:T(8,128)(2,1)S(1)}, u32[]{:S(2)}, u32[]{:S(2)}) collective-permute-start(bf16[4,96,768]{2,1,0:T(8,128)(2,1)S(1)} %collective-permute-done.28.refs_10_), channel_id=1, source_target_pairs={{0,1},{1,0},{2,3},{3,2},{4,5},{5,4},{6,7},{7,6},{8,9},{9,8},{10,11... | collective-permute-start | bytes 1769480 | tf_op jit(solution)/shard_map/ppermute | solution.py:431
  126.6 11.6 %collective-permute-start.22 = (bf16[4,144,768]{2,1,0:T(8,128)(2,1)}, bf16[4,144,768]{2,1,0:T(8,128)(2,1)S(1)}, u32[]{:S(2)}, u32[]{:S(2)}) collective-permute-start(bf16[4,144,768]{2,1,0:T(8,128)(2,1)} %collective-permute-done.18.refs_1_), channel_id=1, source_target_pairs={{0,1},{1,0},{2,3},{3,2},{4,5},{5,4},{6,7},{7,6},{8,9},{9,8},{10,11... | collective-permute-start | bytes 2654216 | tf_op jit(solution)/shard_map/ppermute | solution.py:431
  172.6 10.5 %collective-permute-start.35 = (bf16[2,2,4,96,768]{4,3,2,1,0:T(8,128)(2,1)}, bf16[2,2,4,96,768]{4,3,2,1,0:T(8,128)(2,1)}, u32[]{:S(2)}, u32[]{:S(2)}) collective-permute-start(bf16[2,2,4,96,768]{4,3,2,1,0:T(8,128)(2,1)} %outer_give.1), channel_id=1, source_target_pairs={{0,1},{1,0},{2,3},{3,2},{4,5},{5,4},{6,7},{7,6},{8,9},{9,8},{10,11... | collective-permute-start | bytes 7077896 | tf_op jit(solution)/shard_map/ppermute | solution.py:431
  179.6 22.7 %collective-permute-start.39 = (bf16[2,4,144,768]{3,2,1,0:T(8,128)(2,1)}, bf16[2,4,144,768]{3,2,1,0:T(8,128)(2,1)S(1)}, u32[]{:S(2)}, u32[]{:S(2)}) collective-permute-start(bf16[2,4,144,768]{3,2,1,0:T(8,128)(2,1)} %inner_first.1), channel_id=1, source_target_pairs={{0,16},{1,3},{2,18},{3,1},{16,0},{17,19},{18,2},{19,17},{4,20},{5,... | collective-permute-start | bytes 5308424 | tf_op jit(solution)/shard_map/ppermute | solution.py:507
  186.8 43.0 %collective-permute-start.41 = (bf16[2,4,96,768]{3,2,1,0:T(8,128)(2,1)}, bf16[2,4,96,768]{3,2,1,0:T(8,128)(2,1)S(1)}, u32[]{:S(2)}, u32[]{:S(2)}) collective-permute-start(bf16[2,4,96,768]{3,2,1,0:T(8,128)(2,1)} %outer_first.1), channel_id=1, source_target_pairs={{0,16},{1,3},{2,18},{3,1},{16,0},{17,19},{18,2},{19,17},{4,20},{5,... | collective-permute-start | bytes 3538952 | tf_op jit(solution)/shard_map/ppermute | solution.py:507
  208.8 26.4 %collective-permute-start.40 = (bf16[4,144,768]{2,1,0:T(8,128)(2,1)}, bf16[4,144,768]{2,1,0:T(8,128)(2,1)S(1)}, u32[]{:S(2)}, u32[]{:S(2)}) collective-permute-start(bf16[4,144,768]{2,1,0:T(8,128)(2,1)} %get-tuple-element.127), channel_id=1, source_target_pairs={{0,2},{1,17},{2,0},{3,19},{16,18},{17,1},{18,16},{19,3},{4,6},{5,2... | collective-permute-start | bytes 2654216 | tf_op jit(solution)/shard_map/ppermute | solution.py:507
  209.1 40.0 %collective-permute-start.43 = (bf16[1024,128]{1,0:T(8,128)(2,1)}, bf16[1024,128]{1,0:T(8,128)(2,1)}, u32[]{:S(2)}, u32[]{:S(2)}) collective-permute-start(bf16[1024,128]{1,0:T(8,128)(2,1)} %get-tuple-element.140), channel_id=1, source_target_pairs={{0,1},{1,0},{2,3},{3,2},{4,5},{5,4},{6,7},{7,6},{8,9},{9,8},{10,11... | collective-permute-start | bytes 786440 | tf_op jit(solution)/shard_map/ppermute | solution.py:431
  229.8 20.4 %collective-permute-start.44 = (bf16[1024,128]{1,0:T(8,128)(2,1)}, bf16[1024,128]{1,0:T(8,128)(2,1)}, u32[]{:S(2)}, u32[]{:S(2)}) collective-permute-start(bf16[1024,128]{1,0:T(8,128)(2,1)} %get-tuple-element.141), channel_id=1, source_target_pairs={{0,1},{1,0},{2,3},{3,2},{4,5},{5,4},{6,7},{7,6},{8,9},{9,8},{10,11... | collective-permute-start | bytes 786440 | tf_op jit(solution)/shard_map/ppermute | solution.py:431
  234.9 10.1 %collective-permute-start.42 = (bf16[4,96,768]{2,1,0:T(8,128)(2,1)}, bf16[4,96,768]{2,1,0:T(8,128)(2,1)S(1)}, u32[]{:S(2)}, u32[]{:S(2)}) collective-permute-start(bf16[4,96,768]{2,1,0:T(8,128)(2,1)} %get-tuple-element.137), channel_id=1, source_target_pairs={{0,2},{1,17},{2,0},{3,19},{16,18},{17,1},{18,16},{19,3},{4,6},{5,2... | collective-permute-start | bytes 1769480 | tf_op jit(solution)/shard_map/ppermute | solution.py:507
  245.2 19.0 %collective-permute-start.63 = (bf16[2,96,768]{2,1,0:T(8,128)(2,1)S(1)}, bf16[2,96,768]{2,1,0:T(8,128)(2,1)S(1)}, u32[]{:S(2)}, u32[]{:S(2)}) collective-permute-start(bf16[2,96,768]{2,1,0:T(8,128)(2,1)S(1)} %slice.264), channel_id=1, source_target_pairs={{0,8},{1,5},{4,12},{5,1},{8,0},{9,13},{12,4},{13,9},{2,10},{3,7},{... | collective-permute-start | bytes 884744 | tf_op jit(solution)/shard_map/ppermute | solution.py:507
  247.3 21.5 %collective-permute-start.48 = (bf16[192,256]{1,0:T(8,128)(2,1)}, bf16[192,256]{1,0:T(8,128)(2,1)S(1)}, u32[]{:S(2)}, u32[]{:S(2)}) collective-permute-start(bf16[192,256]{1,0:T(8,128)(2,1)} %get-tuple-element.173), channel_id=1, source_target_pairs={{0,12},{4,8},{8,4},{12,0},{1,13},{5,9},{9,5},{13,1},{2,14},{6,10},... | collective-permute-start | bytes 294920 | tf_op jit(solution)/shard_map/ppermute | solution.py:426
  249.1 20.6 %collective-permute-start.47 = (bf16[192,256]{1,0:T(8,128)(2,1)S(1)}, bf16[192,256]{1,0:T(8,128)(2,1)S(1)}, u32[]{:S(2)}, u32[]{:S(2)}) collective-permute-start(bf16[192,256]{1,0:T(8,128)(2,1)S(1)} %get-tuple-element.174), channel_id=1, source_target_pairs={{0,8},{4,12},{8,0},{12,4},{1,9},{5,13},{9,1},{13,5},{2,10},{6,14},... | collective-permute-start | bytes 294920 | tf_op jit(solution)/shard_map/ppermute | solution.py:426
  250.1 19.6 %collective-permute-start.46 = (bf16[192,256]{1,0:T(8,128)(2,1)S(1)}, bf16[192,256]{1,0:T(8,128)(2,1)S(1)}, u32[]{:S(2)}, u32[]{:S(2)}) collective-permute-start(bf16[192,256]{1,0:T(8,128)(2,1)S(1)} %get-tuple-element.175), channel_id=1, source_target_pairs={{0,4},{4,0},{8,12},{12,8},{1,5},{5,1},{9,13},{13,9},{2,6},{6,2},{1... | collective-permute-start | bytes 294920 | tf_op jit(solution)/shard_map/ppermute | solution.py:426
  251.8 25.5 %collective-permute-start.61 = (bf16[2,144,768]{2,1,0:T(8,128)(2,1)S(1)}, bf16[2,144,768]{2,1,0:T(8,128)(2,1)S(1)}, u32[]{:S(2)}, u32[]{:S(2)}) collective-permute-start(bf16[2,144,768]{2,1,0:T(8,128)(2,1)S(1)} %slice.256), channel_id=1, source_target_pairs={{0,8},{1,5},{4,12},{5,1},{8,0},{9,13},{12,4},{13,9},{2,10},{3,7},{... | collective-permute-start | bytes 1327112 | tf_op jit(solution)/shard_map/ppermute | solution.py:507
  268.7 33.9 %collective-permute-start.55 = (bf16[4,96,576]{2,1,0:T(8,128)(2,1)}, bf16[4,96,576]{2,1,0:T(8,128)(2,1)S(1)}, u32[]{:S(2)}, u32[]{:S(2)}) collective-permute-start(bf16[4,96,576]{2,1,0:T(8,128)(2,1)} %get-tuple-element.146), channel_id=1, source_target_pairs={{0,1},{1,0},{2,3},{3,2},{4,5},{5,4},{6,7},{7,6},{8,9},{9,8},{10,11... | collective-permute-start | bytes 1327112 | tf_op jit(solution)/shard_map/ppermute | solution.py:431
  269.7 10.8 %collective-permute-start.49 = (bf16[4,192,256]{2,1,0:T(8,128)(2,1)}, bf16[4,192,256]{2,1,0:T(8,128)(2,1)S(1)}, u32[]{:S(2)}, u32[]{:S(2)}) collective-permute-start(bf16[4,192,256]{2,1,0:T(8,128)(2,1)} %get-tuple-element.152), channel_id=1, source_target_pairs={{0,2},{2,0},{4,6},{6,4},{1,3},{3,1},{5,7},{7,5},{8,10},{10,8},{12,... | collective-permute-start | bytes 1179656 | tf_op jit(solution)/shard_map/ppermute | solution.py:426
  270.2 17.9 %collective-permute-start.50 = (bf16[4,192,256]{2,1,0:T(8,128)(2,1)}, bf16[4,192,256]{2,1,0:T(8,128)(2,1)S(1)}, u32[]{:S(2)}, u32[]{:S(2)}) collective-permute-start(bf16[4,192,256]{2,1,0:T(8,128)(2,1)} %get-tuple-element.153), channel_id=1, source_target_pairs={{0,4},{2,6},{4,0},{6,2},{1,5},{3,7},{5,1},{7,3},{8,12},{10,14},{12... | collective-permute-start | bytes 1179656 | tf_op jit(solution)/shard_map/ppermute | solution.py:426
  273.2 22.6 %collective-permute-start.51 = (bf16[4,192,256]{2,1,0:T(8,128)(2,1)}, bf16[4,192,256]{2,1,0:T(8,128)(2,1)S(1)}, u32[]{:S(2)}, u32[]{:S(2)}) collective-permute-start(bf16[4,192,256]{2,1,0:T(8,128)(2,1)} %get-tuple-element.154), channel_id=1, source_target_pairs={{0,6},{2,4},{4,2},{6,0},{1,7},{3,5},{5,3},{7,1},{8,14},{10,12},{12... | collective-permute-start | bytes 1179656 | tf_op jit(solution)/shard_map/ppermute | solution.py:426
  277.4 23.1 %collective-permute-start.62 = (bf16[144,768]{1,0:T(8,128)(2,1)S(1)}, bf16[144,768]{1,0:T(8,128)(2,1)S(1)}, u32[]{:S(2)}, u32[]{:S(2)}) collective-permute-start(bf16[144,768]{1,0:T(8,128)(2,1)S(1)} %slice_bitcast_fusion), channel_id=1, source_target_pairs={{0,4},{1,9},{4,0},{5,13},{8,12},{9,1},{12,8},{13,5},{2,6},{3,11},{... | collective-permute-start | bytes 663560 | tf_op jit(solution)/shard_map/ppermute | solution.py:507
  296.1 10.4 %collective-permute-start.54 = (bf16[192,256]{1,0:T(8,128)(2,1)S(1)}, bf16[192,256]{1,0:T(8,128)(2,1)S(1)}, u32[]{:S(2)}, u32[]{:S(2)}) collective-permute-start(bf16[192,256]{1,0:T(8,128)(2,1)S(1)} %get-tuple-element.169), channel_id=1, source_target_pairs={{0,12},{4,8},{8,4},{12,0},{1,13},{5,9},{9,5},{13,1},{2,14},{6,10},... | collective-permute-start | bytes 294920 | tf_op jit(solution)/shard_map/ppermute | solution.py:426
  299.7 11.8 %collective-permute-start.53 = (bf16[192,256]{1,0:T(8,128)(2,1)S(1)}, bf16[192,256]{1,0:T(8,128)(2,1)S(1)}, u32[]{:S(2)}, u32[]{:S(2)}) collective-permute-start(bf16[192,256]{1,0:T(8,128)(2,1)S(1)} %get-tuple-element.170), channel_id=1, source_target_pairs={{0,8},{4,12},{8,0},{12,4},{1,9},{5,13},{9,1},{13,5},{2,10},{6,14},... | collective-permute-start | bytes 294920 | tf_op jit(solution)/shard_map/ppermute | solution.py:426
  299.7 11.8 %collective-permute-start.52 = (bf16[192,256]{1,0:T(8,128)(2,1)S(1)}, bf16[192,256]{1,0:T(8,128)(2,1)S(1)}, u32[]{:S(2)}, u32[]{:S(2)}) collective-permute-start(bf16[192,256]{1,0:T(8,128)(2,1)S(1)} %get-tuple-element.171), channel_id=1, source_target_pairs={{0,4},{4,0},{8,12},{12,8},{1,5},{5,1},{9,13},{13,9},{2,6},{6,2},{1... | collective-permute-start | bytes 294920 | tf_op jit(solution)/shard_map/ppermute | solution.py:426
  302.8 12.2 %collective-permute-start.56 = (bf16[96,576]{1,0:T(8,128)(2,1)S(1)}, bf16[96,576]{1,0:T(8,128)(2,1)S(1)}, u32[]{:S(2)}, u32[]{:S(2)}) collective-permute-start(bf16[96,576]{1,0:T(8,128)(2,1)S(1)} %get-tuple-element.158), channel_id=1, source_target_pairs={{0,8},{4,12},{8,0},{12,4},{1,9},{5,13},{9,1},{13,5},{2,10},{6,14},... | collective-permute-start | bytes 331784 | tf_op jit(solution)/shard_map/ppermute | solution.py:426
  305.0 10.0 %collective-permute-start.58 = (bf16[96,576]{1,0:T(8,128)(2,1)S(1)}, bf16[96,576]{1,0:T(8,128)(2,1)S(1)}, u32[]{:S(2)}, u32[]{:S(2)}) collective-permute-start(bf16[96,576]{1,0:T(8,128)(2,1)S(1)} %get-tuple-element.159), channel_id=1, source_target_pairs={{0,12},{4,8},{8,4},{12,0},{1,13},{5,9},{9,5},{13,1},{2,14},{6,10},... | collective-permute-start | bytes 331784 | tf_op jit(solution)/shard_map/ppermute | solution.py:426
  306.5 9.4 %collective-permute-start.57 = (bf16[96,576]{1,0:T(8,128)(2,1)S(1)}, bf16[96,576]{1,0:T(8,128)(2,1)S(1)}, u32[]{:S(2)}, u32[]{:S(2)}) collective-permute-start(bf16[96,576]{1,0:T(8,128)(2,1)S(1)} %get-tuple-element.160), channel_id=1, source_target_pairs={{0,4},{4,0},{8,12},{12,8},{1,5},{5,1},{9,13},{13,9},{2,6},{6,2},{1... | collective-permute-start | bytes 331784 | tf_op jit(solution)/shard_map/ppermute | solution.py:426
  (59 other events, 446.9 us)

commit v5 on v4

--- a/solution.py
+++ b/solution.py
@@ -34,15 +34,12 @@
 def one_row(shape, dtype, value=1.0):
     return jnp.where(lax.broadcasted_iota(jnp.int32, shape, 0)==0, value, 0.0).astype(dtype)
 
-def attend_kernel(q_ref, ko_ref, vo_ref, kx_ref, vx_ref, bias_ref, o_ref, lse_ref, l0, l1, l2, l3, kaug, vall):
-    head=pl.program_id(0); qb=pl.program_id(1)
+def attend_kernel(q_ref, ko_ref, vo_ref, kx_ref, vx_ref, bias_ref, o_ref, lse_ref, low_ref, kaug, vall):
     span=ko_ref.shape[1]
-    @pl.when(qb==0)
-    def _():
-        for part,(kr,vr) in enumerate(((ko_ref,vo_ref),(kx_ref,vx_ref))):
-            aug=jnp.concatenate([kr[...], bias_ref[:, part*span:(part+1)*span]],axis=0)
-            kaug[part*span:(part+1)*span,:]=aug.T
-            vall[:, part*span:(part+1)*span]=vr[...]
+    for part,(kr,vr) in enumerate(((ko_ref,vo_ref),(kx_ref,vx_ref))):
+        aug=jnp.concatenate([kr[...], bias_ref[:, part*span:(part+1)*span]],axis=0)
+        kaug[part*span:(part+1)*span,:]=aug.T
+        vall[:, part*span:(part+1)*span]=vr[...]
     n=q_ref.shape[1]
     qaug=jnp.concatenate([q_ref[...], one_row((HD,n),bf16)],axis=0)
     top=jnp.full((1,n),-3e38,f32); total=jnp.zeros((1,n),f32); acc=jnp.zeros((HD,n),f32)
@@ -60,25 +57,22 @@
     o_ref[...]=out
     lse_ref[0]=top+jnp.log2(total)
     low=out.astype(bf16)
-    part=n//QB
-    for k,ref in enumerate((l0,l1,l2,l3)):
-        @pl.when(qb==k//QB)
-        def _(): ref[pl.ds(pl.multiple_of(head*HD,HD),HD),:]=low[:,(k%QB)*part:(k%QB+1)*part]
-
-def attend(q,kv,kvx,bias):
-    width,n4=q.shape; heads=width//HD; n=n4//4*QB; span=kv.shape[1]
-    kspec=pl.BlockSpec((HD,span),lambda h,b:(h,0)); vspec=pl.BlockSpec((HD,span),lambda h,b:(heads+h,0))
-    lowspec=pl.BlockSpec((width,n4//4),lambda h,b:(0,0))
-    return pl.pallas_call(attend_kernel,grid=(heads,4//QB),
-        in_specs=[pl.BlockSpec((HD,n),lambda h,b:(h,b)),kspec,vspec,kspec,vspec,pl.BlockSpec((HD,2*span),lambda h,b:(0,0))],
-        out_specs=[pl.BlockSpec((HD,n),lambda h,b:(h,b)),pl.BlockSpec((1,1,n),lambda h,b:(h,0,b))]+[lowspec]*4,
-        out_shape=[jax.ShapeDtypeStruct((width,n4),f32),jax.ShapeDtypeStruct((heads,1,n4),f32)]+[jax.ShapeDtypeStruct((width,n4//4),bf16)]*4,
+    for b in range(2):
+        low_ref[b]=low[:,b*(n//2):(b+1)*(n//2)]
+
+def attend(part,q,kv,kvx,bias):
+    width,n4=q.shape; heads=width//HD; n=n4//2; span=kv.shape[1]
+    kspec=pl.BlockSpec((HD,span),lambda h:(h,0)); vspec=pl.BlockSpec((HD,span),lambda h:(heads+h,0))
+    return pl.pallas_call(attend_kernel,grid=(heads,),
+        in_specs=[pl.BlockSpec((HD,n),lambda h:(h,part)),kspec,vspec,kspec,vspec,pl.BlockSpec((HD,2*span),lambda h:(0,0))],
+        out_specs=[pl.BlockSpec((HD,n),lambda h:(h,0)),pl.BlockSpec((1,1,n),lambda h:(h,0,0)),pl.BlockSpec((2,HD,n//2),lambda h:(0,h,0))],
+        out_shape=[jax.ShapeDtypeStruct((width,n),f32),jax.ShapeDtypeStruct((heads,1,n),f32),jax.ShapeDtypeStruct((2,width,n//2),bf16)],
         scratch_shapes=[pltpu.VMEM((2*span,2*HD),bf16),pltpu.VMEM((HD,2*span),bf16)],
-        cost_estimate=pl.CostEstimate(flops=4*width*n4//HD*2*span*256,bytes_accessed=4*n4*2*span,transcendentals=heads*n4*2*span),
+        cost_estimate=pl.CostEstimate(flops=int(6.0*(2*width*n4//HD*2*span*256))+1,bytes_accessed=int(6.0*(2*n4*2*span))+1,transcendentals=int(6.0*(heads*n*2*span))+1),
         name="attend")(q,kv,kv,kvx,kvx,bias)
 
 BKB=512
-def attend_back_kernel(q_ref, ko_ref, vo_ref, kx_ref, vx_ref, bias_ref, o_ref, lse_ref, g0,g1,g2,g3, cos_ref, sin_ref,
+def attend_back_kernel(q_ref, ko_ref, vo_ref, kx_ref, vx_ref, bias_ref, oa_ref, ob_ref, lsea_ref, lseb_ref, g0,g1,g2,g3, cos_ref, sin_ref,
                        dq_ref, own_ref, give_ref, kaug, vtm, kall, acc):
     qb=pl.program_id(0)
     span=ko_ref.shape[1]; n=q_ref.shape[1]
@@ -94,11 +88,12 @@
     zeros=jnp.zeros((HD,n),bf16)
     qaug=jnp.concatenate([q, one_row((HD,n),bf16)],axis=0)
     g=jnp.concatenate([jnp.where(qb==0,g0[...],g2[...]),jnp.where(qb==0,g1[...],g3[...])],axis=1)
+    o=jnp.where(qb==0,oa_ref[...],ob_ref[...])
     qpad=jnp.concatenate([q,zeros],axis=0).T
     gpad=jnp.concatenate([zeros,g],axis=0).T
     gaug=jnp.concatenate([g,zeros],axis=0)
-    delta=jnp.sum(g.astype(f32)*o_ref[...],axis=0,keepdims=True)
-    lse=lse_ref[0]
+    delta=jnp.sum(g.astype(f32)*o,axis=0,keepdims=True)
+    lse=jnp.where(qb==0,lsea_ref[0],lseb_ref[0])
     dq=jnp.zeros((HD,n),f32)
     s=mm(kaug[0:BKB,:],qaug); dp=mm(vtm[0:BKB,:],gaug)
     for kb in range(0,2*span,BKB):
@@ -116,43 +111,59 @@
         own_ref[...]=acc[:span,:]
         give_ref[...]=acc[span:,:].astype(bf16)
 
-def attend_back(head,q,kv,kvx,bias,o,lse,grads,cos,sin):
+def attend_back(head,q,kv,kvx,bias,os,lses,grads,cos,sin):
     width,n4=q.shape; heads=width//HD; n=n4//4*QB; span=kv.shape[1]
     kspec=pl.BlockSpec((HD,span),lambda b:(head,0)); vspec=pl.BlockSpec((HD,span),lambda b:(heads+head,0))
-    gspec=pl.BlockSpec((HD,n4//4),lambda b:(head,0)); hb=pl.BlockSpec((HD,n),lambda b:(head,b)); tb=pl.BlockSpec((HD,n),lambda b:(0,b))
-    dspec=pl.BlockSpec((span,2*HD),lambda b:(0,0))
+    gspec=lambda i:pl.BlockSpec((None,HD,n4//4),lambda b:(i,head,0)); hb=pl.BlockSpec((HD,n),lambda b:(head,b)); tb=pl.BlockSpec((HD,n),lambda b:(0,b))
+    dspec=pl.BlockSpec((span,2*HD),lambda b:(0,0)); ospec=pl.BlockSpec((HD,n),lambda b:(head,0)); lspec=pl.BlockSpec((1,1,n),lambda b:(head,0,0))
     return pl.pallas_call(attend_back_kernel,grid=(4//QB,),
-        in_specs=[hb,kspec,vspec,kspec,vspec,pl.BlockSpec((HD,2*span),lambda b:(0,0)),hb,pl.BlockSpec((1,1,n),lambda b:(head,0,b)),gspec,gspec,gspec,gspec,tb,tb],
+        in_specs=[hb,kspec,vspec,kspec,vspec,pl.BlockSpec((HD,2*span),lambda b:(0,0)),ospec,ospec,lspec,lspec,gspec(0),gspec(0),gspec(0),gspec(1),tb,tb],
         out_specs=[tb,dspec,dspec],
         out_shape=[jax.ShapeDtypeStruct((HD,n4),bf16),jax.ShapeDtypeStruct((span,2*HD),f32),jax.ShapeDtypeStruct((span,2*HD),bf16)],
         scratch_shapes=[pltpu.VMEM((2*span,2*HD),bf16),pltpu.VMEM((2*span,2*HD),bf16),pltpu.VMEM((HD,2*span),bf16),pltpu.VMEM((2*span,2*HD),f32)],
-        cost_estimate=pl.CostEstimate(flops=10*n4*2*span*256,bytes_accessed=4*n4*2*span,transcendentals=n4*2*span),
-        name="attend_back")(q,kv,kv,kvx,kvx,bias,o,lse,*grads,cos,sin)
+        cost_estimate=pl.CostEstimate(flops=int(6.0*(10*n4*2*span*256))+1,bytes_accessed=int(6.0*(4*n4*2*span))+1,transcendentals=int(6.0*(n4*2*span))+1),
+        name="attend_back")(q,kv,kv,kvx,kvx,bias,*os,*lses,grads[0],grads[2],grads[1],grads[2],cos,sin)
 def xor(a,b):
     return lax.bitwise_xor(jnp.asarray(a,jnp.int32),jnp.asarray(b,jnp.int32))
 
 def rows_at(index,size,align):
     return pl.ds(pl.multiple_of(index*size,align),size)
+
+def row_step(core,slot):
+    return jnp.where(core==0,slot,(slot%2)*2+slot//2)
+
+def z_step(core,slot):
+    return jnp.where(core==0,slot//2,slot%2)
+
+def y_step(core,slot):
+    return jnp.where(core==0,slot%2,slot//2)
+
+def slots(three):
+    keep,first,second=three
+    return (keep.at[0],second.at[0],first.at[0],second.at[1])
 
 def place_qkv_weights(info, mine_ref, theirs_ref, w_s):
     row=info[0]; c=info[3]
     half=mine_ref.shape[1]
     for r in range(4):
         k=xor(r,row)
-        w_s[pl.ds(pl.multiple_of((2*r+c)*half,32),half),:]=mine_ref[k]
-        w_s[pl.ds(pl.multiple_of((2*r+1-c)*half,32),half),:]=theirs_ref[k]
-
-def place_tokens(info, x_ref, kz, x_s):
-    feat=x_ref.shape[1]; base=xor(info[0],kz)
+        w_s[pl.ds(pl.multiple_of((2*r+c)*half,32),half),:]=mine_ref[row_step(c,k)]
+        w_s[pl.ds(pl.multiple_of((2*r+1-c)*half,32),half),:]=theirs_ref[row_step(1-c,k)]
+
+def place_tokens(info, x_ref, slot, x_s):
+    feat=x_ref.shape[1]; c=info[3]; base=xor(info[0],z_step(c,slot))
     for r in range(4):
-        x_s[r*feat:(r+1)*feat,:]=x_ref[xor(r,base)]
-
-def qkv_kernel(info, x0,x1,x2,x3, mine_ref, theirs_ref, cos_ref, sin_ref, q_ref, kv_ref, w_s, wt_s, x_s):
+        x_s[r*feat:(r+1)*feat,:]=x_ref[row_step(c,xor(r,base))]
+
+def token_refs(own, second, others):
+    return (own, second, others.at[0], others.at[1])
+
+def qkv_kernel(info, xa,xb,xc, mine_ref, theirs_ref, cos_ref, sin_ref, q_ref, kv_ref, w_s, wt_s, x_s):
     place_qkv_weights(info,mine_ref,theirs_ref,w_s)
     wt_s[...]=w_s[...].T
-    hw=q_ref.shape[0]; n=x0.shape[2]
-    for k,xr in enumerate((x0,x1,x2,x3)):
-        place_tokens(info,xr,k//2,x_s)
+    hw=q_ref.shape[0]; n=xa.shape[2]
+    for k,xr in enumerate(token_refs(xa,xb,xc)):
+        place_tokens(info,xr,k,x_s)
         out=mm(wt_s[...],x_s[...])
         sl=slice(k*n,(k+1)*n)
         cos=cos_ref[:,sl]; sin=sin_ref[:,sl]
@@ -168,41 +179,39 @@
 
 def qkv(info,xs,mine,theirs,cos,sin):
     _,feat,n=xs[0].shape; w3=mine.shape[2]; hw=w3//3; width=4*feat
-    return pl.pallas_call(qkv_kernel,in_specs=[SM]+[VM]*8,out_specs=[VM,VM],
+    return pl.pallas_call(qkv_kernel,in_specs=[SM]+[VM]*7,out_specs=[VM,VM],
         out_shape=[jax.ShapeDtypeStruct((hw,4*n),bf16),jax.ShapeDtypeStruct((2*hw,4*n),bf16)],
         scratch_shapes=[pltpu.VMEM((width,w3),bf16),pltpu.VMEM((w3,width),bf16),pltpu.VMEM((width,n),bf16)],
         name="qkv")(info,*xs,mine,theirs,cos,sin)
 
 def finish_dx_kernel(info, *refs):
-    heads=refs[0].shape[0]
-    del heads
-    (q0,q1,q2,o0,o1,o2,r0,r1,r2,mine_ref,theirs_ref,cos_ref,sin_ref,d0,d1,d2,d3,p_ref,w_s)=refs
-    hw=3*HD; n=d0.shape[2]; feat=d0.shape[1]
+    (q0,q1,q2,o0,o1,o2,r0,r1,r2,mine_ref,theirs_ref,cos_ref,sin_ref,keep_ref,send_ref,p_ref,w_s)=refs
+    hw=3*HD; n=keep_ref.shape[3]; feat=keep_ref.shape[2]; c=info[3]
     place_qkv_weights(info,mine_ref,theirs_ref,w_s)
     for h,(qr,orr,rr) in enumerate(((q0,o0,r0),(q1,o1,r1),(q2,o2,r2))):
         p_ref[h*HD:(h+1)*HD,:]=qr[...]
         t=(orr[...]+rr[...].astype(f32)).T
         p_ref[hw+h*HD:hw+(h+1)*HD,:]=pair_turn(t[:HD]*LN2,cos_ref[...],-sin_ref[...]).astype(bf16)
         p_ref[2*hw+h*HD:2*hw+(h+1)*HD,:]=t[HD:].astype(bf16)
-    for k,dr in ((3,d3),(1,d1),(2,d2),(0,d0)):
+    for k,dr in ((3,send_ref),(2,send_ref),(1,keep_ref),(0,keep_ref)):
         sl=slice(k*n,(k+1)*n)
-        base=xor(info[0],k//2)
+        base=xor(info[0],z_step(c,k))
         for r in range(4):
-            dr[xor(r,base)]=mm(w_s[r*feat:(r+1)*feat,:],p_ref[:,sl]).astype(dr.dtype)
+            dr[k%2,row_step(c,xor(r,base))]=mm(w_s[r*feat:(r+1)*feat,:],p_ref[:,sl]).astype(dr.dtype)
 
 def finish_dx(info,dqs,owns,gots,mine,theirs,cos,sin):
     w3=mine.shape[2]; half=mine.shape[1]; feat=2*half; width=4*feat; n=dqs[0].shape[1]//4
     S=jax.ShapeDtypeStruct
-    return pl.pallas_call(finish_dx_kernel,in_specs=[SM]+[VM]*13,out_specs=[VM]*5,
-        out_shape=[S((4,feat,n),f32)]+[S((4,feat,n),bf16)]*3+[S((w3,4*n),bf16)],
+    return pl.pallas_call(finish_dx_kernel,in_specs=[SM]+[VM]*13,out_specs=[VM]*3,
+        out_shape=[S((2,4,feat,n),f32),S((2,4,feat,n),bf16),S((w3,4*n),bf16)],
         scratch_shapes=[pltpu.VMEM((width,w3),bf16)],
-        cost_estimate=pl.CostEstimate(flops=8*width*w3*n,bytes_accessed=8*width*n*4,transcendentals=0),
+        cost_estimate=pl.CostEstimate(flops=int(6.0*(8*width*w3*n))+1,bytes_accessed=int(6.0*(8*width*n*4))+1,transcendentals=int(6.0*(0))+1),
         name="finish_dx")(info,*dqs,*owns,*gots,mine,theirs,cos,sin)
 
-def finish_dw_kernel(info, p_ref, x0,x1,x2,x3, keep_ref, give_ref, x_s, g_s):
-    n=x0.shape[2]; half=keep_ref.shape[1]
-    for k,xr in enumerate((x0,x1,x2,x3)):
-        place_tokens(info,xr,k//2,x_s.at[:,k*n:(k+1)*n])
+def finish_dw_kernel(info, p_ref, xa,xb,xc, keep_ref, give_ref, x_s, g_s):
+    n=xa.shape[2]; half=keep_ref.shape[1]
+    for k,xr in enumerate(token_refs(xa,xb,xc)):
+        place_tokens(info,xr,k,x_s.at[:,k*n:(k+1)*n])
     g_s[...]=mm(x_s[...],p_ref[...],NT)
     c=info[3]; row=info[0]
     for r in range(4):
@@ -212,21 +221,18 @@
 
 def finish_dw(info,proj,xs):
     _,feat,n=xs[0].shape; w3=proj.shape[0]; width=4*feat; half=feat//2
-    return pl.pallas_call(finish_dw_kernel,in_specs=[SM]+[VM]*5,out_specs=[VM]*2,
+    return pl.pallas_call(finish_dw_kernel,in_specs=[SM]+[VM]*4,out_specs=[VM]*2,
         out_shape=[jax.ShapeDtypeStruct((4,half,w3),f32),jax.ShapeDtypeStruct((4,half,w3),bf16)],
         scratch_shapes=[pltpu.VMEM((width,4*n),bf16),pltpu.VMEM((width,w3),f32)],
-        cost_estimate=pl.CostEstimate(flops=8*width*w3*n,bytes_accessed=8*width*n*2,transcendentals=0),
+        cost_estimate=pl.CostEstimate(flops=int(6.0*(8*width*w3*n))+1,bytes_accessed=int(6.0*(8*width*n*2))+1,transcendentals=int(6.0*(0))+1),
         name="finish_dw")(info,proj,*xs)
 
-def row_step(core,slot):
-    return jnp.where(core==0,slot,(slot%2)*2+slot//2)
-
-def middle_kernel(info, a0,a1,a2,a3, x_ref, c0,c1,c2,c3, *refs):
+def middle_kernel(info, a0,a1,a2, x_ref, c0,c1,c2, *refs):
     chunk_a=refs[:8]; chunk_b=refs[8:16]
-    (mixed_ref, e0,e1,e2,e3, g1_ref, attnT_ref, hidT_ref, outT_ref, bl_ref, act_ref, il_ref, norm_ref,
+    (mixk_ref, mixs_ref, ek_ref, es_ref, g1_ref, attnT_ref, hidT_ref, outT_ref, bl_ref, act_ref, il_ref, norm_ref,
                   win, woT, wo, ns, gp_s, t_s, f_s, sems)=refs[16:]
-    row=info[0]; zy=info[1]; c=info[3]; group=info[5]; y=info[6]
-    feat=a0.shape[0]; n=a0.shape[1]; width=4*feat; ffc=chunk_a[0].shape[2]; half=feat//2; fh=ffc//2; third=half//3
+    row=info[0]; z=info[1]; y=info[2]; c=info[3]; group=info[5]
+    feat=a0.shape[1]; n=a0.shape[2]; width=4*feat; ffc=chunk_a[0].shape[2]; half=feat//2; fh=ffc//2; third=half//3
     def go(src,dst,s): pltpu.make_async_copy(src,dst,sems.at[s]).start()
     def each(chunk):
         for kc in range(2):
@@ -249,13 +255,14 @@
     for ref,r,g,col,_ in each(chunk_b):
         for t in range(2):
             go(ref.at[:,t*fh:(t+1)*fh],woT.at[pl.ds(pl.multiple_of(r*feat+t*half,16),half),pl.ds(pl.multiple_of((col*2+g)*fh,128),fh)],2)
-    def group_of(k):
-        other=xor(zy,k)
-        return (other%2)*2+other//2
-    for k,ar in enumerate((a0,a1,a2,a3)):
-        attnT_ref[rows_at(group_of(k),feat,64),:]=ar[...]
-    for i in range(4):
-        t_s[rows_at(xor(i,row),feat,64),:]=x_ref[i]
+    def group_of(s):
+        return xor(y,y_step(c,s))*2+xor(z,z_step(c,s))
+    def row_of(s):
+        return xor(row,row_step(c,s))
+    for s,ar in enumerate(slots((a0,a1,a2))):
+        attnT_ref[rows_at(group_of(s),feat,64),:]=ar[...]
+    for s in range(4):
+        t_s[rows_at(row_of(s),feat,64),:]=x_ref[s]
     attn=attnT_ref[...].T
     x=t_s[...].T.astype(f32)
     pltpu.make_async_copy(wo,wo,sems.at[0]).wait()
@@ -293,11 +300,10 @@
     lax.fori_loop(0,4*nb,forward,0)
     cent2,inv2=stats(hidden+f_s[...])
     t_s[...]=(cent2*gain2+shift2).astype(bf16).T
-    for i in range(4):
-        mixed_ref[i]=t_s[rows_at(xor(i,row),feat,64),:]
-    for k,cr in enumerate((c0,c1,c2,c3)):
-        for j in range(3):
-            t_s[pl.ds(pl.multiple_of(xor(k,row)*feat+j*(feat//3),64),feat//3),:]=cr[half:,j*256:(j+1)*256]
+    for s in range(4):
+        (mixk_ref,mixs_ref)[s//2][s%2]=t_s[rows_at(row_of(s),feat,64),:]
+    for s,cr in enumerate(slots((c0,c1,c2))):
+        t_s[rows_at(row_of(s),feat,64),:]=cr[...]
     valid=(lax.broadcasted_iota(jnp.int32,(n,1),0)<info[4]).astype(f32)
     cot=t_s[...].T.astype(f32)*valid
     sums2=(jnp.sum(cot*cent2,axis=0,keepdims=True),jnp.sum(cot,axis=0,keepdims=True))
@@ -329,38 +335,44 @@
         bl_ref[r]=piece
         da=da+mm(wo[r],piece,NT)
     t_s[...]=da.astype(bf16)
-    for k,er in enumerate((e0,e1,e2,e3)):
-        er[...]=t_s[rows_at(group_of(k),feat,64),:]
+    for s in range(4):
+        (ek_ref,es_ref)[s//2][s%2]=t_s[rows_at(group_of(s),feat,64),:]
     f2=grad1.T
     for r in range(4):
-        g1_ref[xor(r,row)]=f2[r*feat:(r+1)*feat]
+        g1_ref[row_step(c,xor(r,row))]=f2[r*feat:(r+1)*feat]
 
 def middle(info,attn_parts,x_own,cot_parts,chunk_a,chunk_b):
-    feat,n=attn_parts[0].shape; width=4*feat; ff=4*chunk_a[0].shape[2]
+    _,feat,n=attn_parts[0].shape; width=4*feat; ff=4*chunk_a[0].shape[2]
     S=jax.ShapeDtypeStruct
-    return pl.pallas_call(middle_kernel,in_specs=[SM]+[VM]*9+[HB]*16,out_specs=[VM]*13,
-        out_shape=[S((4,feat,n),bf16)]+[S((feat,n),bf16)]*4+[S((4,feat,n),f32),S((width,n),bf16),S((width,n),bf16),S((width,n),bf16),
+    return pl.pallas_call(middle_kernel,in_specs=[SM]+[VM]*7+[HB]*16,out_specs=[VM]*12,
+        out_shape=[S((2,feat,n),bf16)]*4+[S((4,feat,n),f32),S((width,n),bf16),S((width,n),bf16),S((width,n),bf16),
                    S((4,n,256),bf16),S((n,ff),bf16),S((n,ff),bf16),S((4,8,feat),f32)],
         scratch_shapes=[pltpu.VMEM((width,ff),bf16),pltpu.VMEM((width,ff),bf16),pltpu.VMEM((4,width,256),bf16),pltpu.VMEM((4,16,width),bf16),
                         pltpu.VMEM((n,ff),f32),pltpu.VMEM((width,n),bf16),pltpu.VMEM((n,width),f32),pltpu.SemaphoreType.DMA((4,))],
         compiler_params=pltpu.CompilerParams(vmem_limit_bytes=56*1024*1024),
-        cost_estimate=pl.CostEstimate(flops=12*n*width*ff*2,bytes_accessed=24*width*ff,transcendentals=2*n*ff),
+        cost_estimate=pl.CostEstimate(flops=int(6.0*(12*n*width*ff*2))+1,bytes_accessed=int(6.0*(24*width*ff))+1,transcendentals=int(6.0*(2*n*ff))+1),
         name="middle")(info,*attn_parts,x_own,*cot_parts,*chunk_a,*chunk_b)
+
+def plane_target(info,core,slot):
+    kx=jnp.where(core==0,slot//2,slot%2); ky=jnp.where(core==0,slot%2,slot//2)
+    return xor(info[5],kx),xor(info[2],ky)*2+core
 
 def target(info,which,a,b):
     core=xor(info[3],which)
-    kx=jnp.where(core==0,a,b); ky=jnp.where(core==0,b,a)
-    return core,xor(info[5],kx),xor(info[6],ky)*2+core
+    return (core,)+plane_target(info,core,2*a+b)
 
 def outer_blocks(info,which,a,b,refs,put):
-    outT_ref,act_ref=refs
-    core,g,_=target(info,which,a,b)
-    half=outT_ref.shape[0]//8; fh=act_ref.shape[1]//2
-    rhs=act_ref[:,pl.ds(pl.multiple_of(g*fh,128),fh)]
-    for s in range(4):
-        value=mm(outT_ref[rows_at(xor(info[0],row_step(core,s)),2*half,64),:],rhs)
-        put(s,slice(0,half),slice(0,fh),value[:half])
-        put(s,slice(0,half),slice(fh,2*fh),value[half:])
+    outT_ref,act_near,act_far=refs
+    core=xor(info[3],which)
+    half=outT_ref.shape[0]//8; fh=act_near.shape[1]//2
+    rows=outT_ref[rows_at(xor(info[0],row_step(core,2*a+b)),2*half,64),:]
+    for ky,act_ref in enumerate((act_near,act_far)):
+        value=mm(rows,act_ref[...])
+        for g in range(2):
+            kx=xor(g,info[5])
+            slot=jnp.where(core==0,2*kx+ky,2*ky+kx)
+            for t in range(2):
+                put(slot,slice(0,half),slice(t*fh,(t+1)*fh),value[t*half:(t+1)*half,g*fh:(g+1)*fh])
 
 def inner_blocks(info,which,a,b,refs,put):
     hidT_ref,il_ref,attnT_ref,bl_ref,norm_ref=refs
@@ -399,33 +411,36 @@
 def grad_call(kind,stage,info,args,got=None,came=None):
     S=jax.ShapeDtypeStruct
     width,n=args[0].shape; ffc=args[1].shape[1]//4; half=width//8
-    blocks,rows=(inner_blocks,half+half//3+16) if kind=="inner" else (outer_blocks,half)
-    fixed=[pl.BlockSpec((width,n),lambda *i:(0,0)),None]+([pl.BlockSpec((width,n),lambda *i:(0,0)),pl.BlockSpec((4,n,256),lambda *i:(0,0,0)),pl.BlockSpec((4,8,width//4),lambda *i:(0,0,0))] if kind=="inner" else [])
-    cost=pl.CostEstimate(flops=(4 if stage=="give" else 2)*width*n*ffc,bytes_accessed=16*rows*ffc,transcendentals=0)
+    a={"give":None,"first":1,"second":0}[stage]; which=1 if stage=="give" else 0
+    def at(index):
+        if stage=="give": return lambda i,j,s:index(i,j,s)
+        return lambda j,s:index(a,j,s)
+    whole=pl.BlockSpec((width,n),at(lambda i,j,s:(0,0)))
+    if kind=="inner":
+        blocks,rows=inner_blocks,half+half//3+16
+        specs=[whole,pl.BlockSpec((n,ffc),at(lambda i,j,s:(0,target(s,which,i,j)[2]))),whole,
+               pl.BlockSpec((4,n,256),at(lambda i,j,s:(0,0,0))),pl.BlockSpec((4,8,width//4),at(lambda i,j,s:(0,0,0)))]
+    else:
+        blocks,rows=outer_blocks,half
+        args=(args[0],args[1],args[1])
+        def column(ky): return at(lambda i,j,s:(0,xor(s[2],ky)*2+xor(s[3],which)))
+        specs=[whole,pl.BlockSpec((n,ffc),column(0)),pl.BlockSpec((n,ffc),column(1))]
+    cost=pl.CostEstimate(flops=int(6.0*((4 if stage=="give" else 2)*width*n*ffc))+1,bytes_accessed=int(6.0*(16*rows*ffc))+1,transcendentals=int(6.0*(0))+1)
     name=kind+"_"+stage
+    five=(1,1,4,rows,ffc)
     if stage=="give":
-        fixed[1]=pl.BlockSpec((n,ffc),lambda a,b,s:(0,target(s,1,a,b)[2]))
         return pl.pallas_call(functools.partial(give_kernel,blocks),
-            grid_spec=pltpu.PrefetchScalarGridSpec(num_scalar_prefetch=1,grid=(2,2),in_specs=fixed,out_specs=pl.BlockSpec((1,1,4,rows,ffc),lambda a,b,s:(a,b,0,0,0))),
+            grid_spec=pltpu.PrefetchScalarGridSpec(num_scalar_prefetch=1,grid=(2,2),in_specs=specs,out_specs=pl.BlockSpec(five,lambda i,j,s:(i,j,0,0,0))),
             out_shape=S((2,2,4,rows,ffc),bf16),cost_estimate=cost,name=name)(info,*args)
-    a=1 if stage=="first" else 0
-    fixed[1]=pl.BlockSpec((n,ffc),lambda b,s:(0,target(s,0,a,b)[2]))
-    got_spec=pl.BlockSpec((1,1,4,rows,ffc),lambda b,s:(a,b,0,0,0)); one=pl.BlockSpec((1,4,rows,ffc),lambda b,s:(b,0,0,0))
+    got_spec=pl.BlockSpec(five,lambda j,s:(a,j,0,0,0)); one=pl.BlockSpec((1,4,rows,ffc),lambda j,s:(j,0,0,0))
     if stage=="first":
         return pl.pallas_call(functools.partial(first_kernel,blocks),
-            grid_spec=pltpu.PrefetchScalarGridSpec(num_scalar_prefetch=1,grid=(2,),in_specs=fixed+[got_spec],out_specs=one),
+            grid_spec=pltpu.PrefetchScalarGridSpec(num_scalar_prefetch=1,grid=(2,),in_specs=specs+[got_spec],out_specs=one),
             out_shape=S((2,4,rows,ffc),bf16),cost_estimate=cost,name=name)(info,*args,got)
-    whole=pl.BlockSpec((4,rows,ffc),lambda b,s:(0,0,0))
+    full=pl.BlockSpec((4,rows,ffc),lambda j,s:(0,0,0))
     return pl.pallas_call(functools.partial(second_kernel,blocks),
-        grid_spec=pltpu.PrefetchScalarGridSpec(num_scalar_prefetch=1,grid=(2,),in_specs=fixed+[got_spec,one],out_specs=[whole,whole]),
+        grid_spec=pltpu.PrefetchScalarGridSpec(num_scalar_prefetch=1,grid=(2,),in_specs=specs+[got_spec,one],out_specs=[full,full]),
         out_shape=[S((4,rows,ffc),bf16)]*2,cost_estimate=cost,name=name)(info,*args,got,came)
-
-def exchange4(blocks, axes):
-    parts = [blocks[0]]
-    for step in range(1, 4):
-        parts.append(lax.ppermute(blocks[step], axes, [(i, i ^ step) for i in range(4)]))
-    return parts
-
 
 def core_swap(value):
     return lax.ppermute(value, "cc", [(0, 1), (1, 0)])
@@ -510,9 +525,23 @@
 PLANE = ("dp", "cy")
 
 
-def row_gather(block):
-    pair = jnp.stack([block, crossed(block, ROW, 1)])
-    return jnp.concatenate([pair, crossed(pair, ROW, 0)], axis=0)
+def scatter_steps(keep, send, axes, *between):
+    first = after(crossed(send, axes, 0), *between)
+    second = crossed(jnp.stack([keep[1], first[1]]), axes, 1)
+    return keep, first, second
+
+
+def by_slot(three):
+    keep, first, second = three
+    return [keep[0], second[0], first[0], second[1]]
+
+
+def row_pair(block, *between):
+    return jnp.stack([block, after(crossed(block, ROW, 1), *between)])
+
+
+def row_rest(pair, *between):
+    return jnp.concatenate([pair, after(crossed(pair, ROW, 0), *between)], axis=0)
 
 
 def plane_gather(stack, forward_after):
@@ -566,7 +595,7 @@
     return pair[0].astype(f32) + crossed(pair[1], ROW, 1).astype(f32)
 
 
-def generic_sums(first, keep, send, c):
+def generic_inner(first, keep, send, c):
     parts = [keep, send, first[0], first[1]]
     by_x = [
         (parts[0], jnp.where(c == 0, parts[1], parts[2])),
@@ -574,6 +603,14 @@
     ]
     planes = [add_parts([own, swap2(other, "cy")]).astype(bf16) for own, other in by_x]
     return [halve(plane) for plane in planes]
+
+
+def generic_outer(row_sum, c):
+    by_x = [
+        (row_sum[0], jnp.where(c == 0, row_sum[1], row_sum[2])),
+        (jnp.where(c == 0, row_sum[2], row_sum[1]), row_sum[3]),
+    ]
+    return [add_parts([own, swap2(other, "cy")]) for own, other in by_x]
 
 
 def local(
@@ -594,42 +631,52 @@
     length = lax.dynamic_index_in_dim(seq_lengths[m], group, keepdims=False)
     own_start = (y * 2 + c) * cols + z * half
     info = jnp.stack([
-        row, z * 2 + y, m * 2 + c, c, length - own_start, group if two else 0 * group, y, 0 * y,
+        row, z, y, c, length - own_start, group if two else 0 * group, 0 * y, 0 * y,
     ]).astype(jnp.int32)
 
-    def to_row_order(array):
+    def turn(blocks):
+        pairs = blocks.reshape((2, 2) + blocks.shape[1:])
+        return jnp.where(c == 0, pairs, pairs.swapaxes(0, 1)).reshape(blocks.shape)
+
+    def to_slots(array):
         blocks = array.reshape(2, feat, 2, half).transpose(0, 2, 1, 3).reshape(4, feat, half)
-        return swap_by(blocks, row)
-
-    def from_row_order(parts):
-        back = swap_by(jnp.stack(parts), row)
+        return turn(swap_by(blocks, row))
+
+    def from_slots(parts):
+        back = swap_by(turn(jnp.stack(parts)), row)
         return back.reshape(2, 2, feat, half).transpose(0, 2, 1, 3).reshape(2, feat, cols)
 
     this_half, other_half = dp_halves(jnp.concatenate([w_query, w_key, w_value], axis=1), c)
-    x_own = jnp.stack(exchange4(to_row_order(tokens), ROW))
+    token_blocks = to_slots(tokens)
+    x_own = jnp.stack(by_slot(scatter_steps(token_blocks[:2], token_blocks[2:], ROW)))
     other_columns = core_swap(other_half)
-    near = jnp.where(z == c, this_half, other_columns)
-    far = jnp.where(z == c, other_columns, this_half)
     norms = pack_norms(first_gain, first_shift, second_gain, second_shift)
     if two:
         block_a = jnp.concatenate([w_inner, pack_output(w_output), norms], axis=0)
-        row_a = row_gather(block_a)
-        row_b = row_gather(after(pack_outer(w_outer), row_a))
-    cot_blocks = to_row_order(out_grad)
-    wide = jnp.concatenate([cot_blocks[:, j * feat // 3 : (j + 1) * feat // 3] for j in range(3)], axis=2)
-    fill = ((0, 0), (0, wide.shape[2] - 3 * head_width))
-    near, far = jnp.pad(near, fill), jnp.pad(far, fill)
-    third_parts = exchange4(
-        [jnp.concatenate([(near, far)[k % 2], wide[k]], axis=0) for k in range(4)], ROW
-    )
-    mine = jnp.stack([part[: feat // 2, : 3 * head_width] for part in third_parts])
+        pair_a = row_pair(block_a)
+        block_b = pack_outer(w_outer)
+        near_b = crossed(after(block_b, token_blocks), ROW, 1)
+    pieces = []
+    for s in range(4):
+        step = jnp.where(c == 0, s % 2, s // 2)
+        pieces.append(jnp.where((z ^ step) == c, this_half, other_columns))
+    mine = jnp.stack(by_slot(scatter_steps(jnp.stack(pieces[:2]), jnp.stack(pieces[2:]), ROW)))
     theirs = core_swap(mine)
-    xs = exchange4([x_own] * 4, SQUARE)
+    if two:
+        row_a = row_rest(pair_a)
+        x_own = after(x_own, pair_a)
+    x_second = crossed(x_own, SQUARE, 1)
+    xs = (x_own, x_second, crossed(jnp.stack([x_own, x_second]), SQUARE, 0))
+    if two:
+        xs = (after(x_own, row_a),) + xs[1:]
 
     starts = []
     for kc in range(2):
-        for k in range(4):
-            starts.append(((y ^ (k % 2)) * 2 + (c ^ kc)) * cols + (z ^ (k // 2)) * half)
+        core = c ^ kc
+        for s in range(4):
+            z_here = z ^ jnp.where(core == 0, s // 2, s % 2)
+            y_here = y ^ jnp.where(core == 0, s % 2, s // 2)
+            starts.append((y_here * 2 + core) * cols + z_here * half)
     positions = (jnp.stack(starts)[:, None] + jnp.arange(half, dtype=jnp.int32)[None, :]).reshape(-1)
     invalid = jnp.where(positions < length, 0.0, masked_score)
     bias = jnp.where(jnp.arange(HD)[:, None] == 0, invalid[None, :], 0.0).astype(bf16)
@@ -641,19 +688,23 @@
 
     q_rot, kv_own = qkv(info, xs, mine, theirs, cosine, sine)
     kv_other = core_swap(kv_own)
-    out, log_totals, *lows = attend(q_rot, kv_own, kv_other, bias)
-    attn_parts = exchange4(lows, SQUARE)
+    out_b, log_b, low_b = attend(1, q_rot, kv_own, kv_other, bias)
+    out_a, log_a, low_a = attend(0, after(q_rot, low_b), kv_own, kv_other, bias)
+    attn_three = scatter_steps(low_a, low_b, SQUARE)
+    cot_blocks = after(to_slots(out_grad), kv_own)
+    cot_three = scatter_steps(cot_blocks[:2], cot_blocks[2:], ROW, low_a)
     if two:
         arrays_a = plane_gather(row_a, (kv_own,))
-        chunk_a = core_copies(arrays_a, [(kv_own,), (kv_own,), (lows[0],), (lows[0],)])
-        arrays_b = plane_gather(after(row_b, kv_own), (lows[0],))
-        chunk_b = core_copies(arrays_b, [(lows[0],), (attn_parts[1],), (attn_parts[2],), (attn_parts[3],)])
+        chunk_a = core_copies(arrays_a, [(kv_own,), (low_a,), (low_a,), (low_a,)])
+        pair_b = jnp.stack([block_b, after(near_b, kv_own)])
+        row_b = row_rest(pair_b, low_b)
+        arrays_b = plane_gather(row_b, (low_a,))
+        chunk_b = core_copies(arrays_b, [(low_a,), (low_a,), (attn_three[2],), (attn_three[2],)])
     else:
         chunk_a, chunk_b = gather_generic(w_output, w_inner, w_outer, norms, row, y, c)
-    mixed, e0, e1, e2, e3, grad_one, attn_t, hidden_t, outer_t, branch_low, act_low, inner_low, norm_sums = middle(
-        info, attn_parts, x_own, third_parts, chunk_a, chunk_b
+    mixed_keep, mixed_send, e_keep, e_send, grad_one, attn_t, hidden_t, outer_t, branch_low, act_low, inner_low, norm_sums = middle(
+        info, attn_three, x_own, cot_three, chunk_a, chunk_b
     )
-    grads = exchange4([e0, e1, e2, e3], SQUARE)
     inner_args = (hidden_t, inner_low, attn_t, branch_low, norm_sums)
     outer_args = (outer_t, act_low)
 
@@ -662,50 +713,72 @@
 
     def head_back(head, *earlier):
         return attend_back(
-            head, after(q_rot, *earlier), kv_own, kv_other, bias, out, log_totals, grads, cosine, sine
+            head, after(q_rot, *earlier), kv_own, kv_other, bias, (out_a, out_b), (log_a, log_b), grads, cosine, sine
         )
 
-    give_inner = grad_call("inner", "give", info, inner_args)
+    give_outer = grad_call("outer", "give", info, outer_args)
+    got_outer = core_swap(give_outer)
+    grads_first = after(crossed(e_send, SQUARE, 0), give_outer)
+    grads_pass = jnp.stack([e_keep[1], grads_first[1]])
+    grads = (e_keep, grads_first, crossed(grads_pass, SQUARE, 1))
+    give_inner = grad_call("inner", "give", info, tied(inner_args, give_outer, grads_pass))
     got_inner = core_swap(give_inner)
-    give_outer = grad_call("outer", "give", info, tied(outer_args, give_inner))
-    got_outer = core_swap(give_outer)
-    first_inner = grad_call("inner", "first", info, tied(inner_args, give_outer), got_inner)
+    first_outer = grad_call("outer", "first", info, tied(outer_args, give_inner, grads[2]), got_outer)
+    came_outer = crossed(first_outer, ROW, 0)
+    first_inner = grad_call("inner", "first", info, tied(inner_args, first_outer), got_inner)
     came_inner = crossed(first_inner, PLANE, 0) if two else jnp.zeros_like(first_inner)
-    first_outer = grad_call("outer", "first", info, tied(outer_args, first_inner), got_outer)
-    came_outer = crossed(first_outer, PLANE, 0) if two else jnp.zeros_like(first_outer)
-    dq0, own0, send0 = head_back(0, first_outer)
-    keep_inner, pass_inner = grad_call(
-        "inner", "second", info, tied(inner_args, dq0), got_inner, after(came_inner, dq0)
-    )
-    dq1, own1, send1 = head_back(1, keep_inner)
+    dq0, own0, send0 = head_back(0, first_inner)
+    dq1, own1, send1 = head_back(1, dq0)
     keep_outer, pass_outer = grad_call(
         "outer", "second", info, tied(outer_args, dq1), got_outer, after(came_outer, dq1)
     )
+    keep_inner, pass_inner = grad_call(
+        "inner", "second", info, tied(inner_args, keep_outer), got_inner, after(came_inner, keep_outer)
+    )
+    dq2, own2, send2 = head_back(2, keep_inner)
     if two:
-        plane_inner = add_parts([keep_inner, crossed(after(pass_inner, keep_inner), PLANE, 1)])
-        plane_inner = after(plane_inner, keep_outer).astype(bf16)
-        dq2, own2, send2 = head_back(2, plane_inner)
-        plane_outer = add_parts([keep_outer, after(crossed(pass_outer, PLANE, 1), dq2)]).astype(bf16)
-        outer_sums = [halve(plane_outer)]
-        inner_sums = [halve(plane_inner)]
-        own2 = after(own2, plane_outer)
+        plane_inner = add_parts([keep_inner, after(crossed(pass_inner, PLANE, 1), dq2)]).astype(bf16)
+        pass_on_inner = crossed(plane_inner[2:], ROW, 0)
+        own2 = after(own2, plane_inner)
+    gots = [core_swap(send) for send in (send0, send1, send2)]
+    dx_keep, dx_send, proj = finish_dx(info, (dq0, dq1, dq2), (own0, own1, own2), gots, mine, theirs, cosine, sine)
+    dx_first = crossed(dx_send, SQUARE, 0)
+    if two:
+        pair_inner = (plane_inner[:2].astype(f32) + after(pass_on_inner, dx_keep).astype(f32)).astype(bf16)
+        last_inner = crossed(pair_inner[1], ROW, 1)
+        proj = after(proj, pair_inner)
+    keep, give = finish_dw(info, after(proj, dx_keep), xs)
+    got = core_swap(give)
+    dx_first = after(dx_first, give)
+    dx_pass = (dx_keep[1] + dx_first[1].astype(f32)).astype(bf16)
+    dx_second = crossed(dx_pass, SQUARE, 1)
+    row_outer = add_parts([keep_outer, after(crossed(pass_outer, ROW, 1), dx_pass)]).astype(bf16)
+    if two:
+        pass_on_outer = crossed(row_outer[2:], PLANE, 0)
+    by_row_step = keep + after(got, row_outer).astype(f32)
+    passed_m = swap2(by_row_step[2:].astype(bf16), "rm")
+    dx_second = after(dx_second, by_row_step)
+    d_x = add_parts([grad_one, dx_keep[0], dx_first[0], dx_second]).astype(bf16)
+    d_x_first = crossed(d_x[2:], ROW, 0)
+    if two:
+        pair_outer = (row_outer[:2].astype(f32) + after(pass_on_outer, d_x).astype(f32)).astype(bf16)
+        last_outer = crossed(pair_outer[1], PLANE, 1)
+        passed_m = after(passed_m, pair_outer)
+    near_far = by_row_step[:2] + passed_m.astype(f32)
+    near_sum = near_far[0]
+    far_low = swap2(near_far[1].astype(bf16), "rz")
+    d_x_first = after(d_x_first, near_far)
+    d_x_second = crossed(jnp.stack([d_x[1], d_x_first[1]]), ROW, 1)
+    far_sum = after(far_low, d_x_first).astype(f32)
+    d_input = from_slots(by_slot((d_x[:2], d_x_first, d_x_second))).astype(f32)
+    if two:
+        inner_sums = [pair_inner[0].astype(f32) + after(last_inner, far_sum).astype(f32)]
+        outer_sums = [pair_outer[0].astype(f32) + after(last_outer, far_sum).astype(f32)]
     else:
-        dq2, own2, send2 = head_back(2, keep_outer)
-        outer_sums = generic_sums(first_outer, keep_outer, pass_outer, c)
-        inner_sums = generic_sums(first_inner, keep_inner, pass_inner, c)
-
-    gots = [core_swap(send) for send in (send0, send1, send2)]
-    d0, d1, d2, d3, proj = finish_dx(info, (dq0, dq1, dq2), (own0, own1, own2), gots, mine, theirs, cosine, sine)
-    dx_parts = exchange4([d0, d1, d2, d3], SQUARE)
-    keep, give = finish_dw(info, after(proj, d0), xs)
-    got = core_swap(give)
-    by_row_step = (keep + got.astype(f32)).astype(bf16)
-    d_x = add_parts([grad_one] + dx_parts).astype(bf16)
-    d_input = from_row_order(exchange4(d_x, ROW)).astype(f32)
-    mixed_out = from_row_order([after(part, give) for part in exchange4(after(mixed, first_outer), ROW)])
-    q0, q1, q2, q3 = (part.astype(f32) for part in exchange4(by_row_step, ROW))
-    near_sum = q0 + q2
-    far_sum = q1 + q3
+        outer_sums = generic_outer(row_outer, c)
+        inner_sums = generic_inner(first_inner, keep_inner, pass_inner, c)
+    mixed_three = scatter_steps(after(mixed_keep, give_outer), after(mixed_send, give_outer), ROW, dq0)
+    mixed_out = from_slots(by_slot([after(part, give) for part in mixed_three]))
     kept = jnp.where(z == c, near_sum, far_sum)
     passed = core_swap(jnp.where(z == c, far_sum, near_sum).astype(bf16)).astype(f32)
     g_qkv = dp_sum(kept, passed, c)

time: 325 us -> 295 us (0.908)
  starting transfers between devices: 88.7 us -> 61.8 us
  waiting for transfers between devices: 105 us -> 95.3 us
    ppermute x27 -> x0, waiting for transfers between devices: 61.1 us -> none  [exchange4(): lax.ppermute(blocks[step], axes, [(i, i ^ step) for i in range(4)])]
    ppermute x18 -> x36, waiting for transfers between devices: 34.9 us -> 81.3 us  [crossed(): return lax.ppermute(value, axes + ('cc',), pairs)]
    ppermute x27 -> x0, starting transfers between devices: 37.7 us -> none  [exchange4(): lax.ppermute(blocks[step], axes, [(i, i ^ step) for i in range(4)])]
    ppermute x18 -> x36, starting transfers between devices: 24.6 us -> 50.4 us  [crossed(): return lax.ppermute(value, axes + ('cc',), pairs)]
    ppermute x18, starting transfers between devices: 21.6 us -> 5.07 us  [core_swap(): return lax.ppermute(value, 'cc', [(0, 1), (1, 0)])]
    ppermute x2 -> x4, waiting for transfers between devices: 1.82 us -> 7.92 us  [swap2(): return lax.ppermute(value, axis, [(0, 1), (1, 0)])]
    slice x5 -> x25, local copies, waits for them, and re-layouts: 0.14 us -> 6.14 us  [the longest x6 3.36 us: scatter_steps(): second = crossed(jnp.stack([keep[1], first[1]]), axes, 1)]
    unnamed x86 -> x76, local copies, waits for them, and re-layouts: 9.24 us -> 6.82 us
  transfers between devices with their start and end apart: 65 -> 58, of which waited for: 25 -> 22; matrix products, arithmetic and copies ran while one was open for 6% -> 8% of each run, Pallas kernels for 22% -> 25%
where the time goes in v5:
time: 295 us; the launch traced here: 294 us
  Pallas kernels  100 us (34%)
  waiting for transfers between devices  95.3 us (32%)
  starting transfers between devices  61.8 us (21%)
  local copies, waits for them, and re-layouts  22.1 us (7%)
  other arithmetic  12.1 us (4%)
    ppermute x36, waiting for transfers between devices, crossed(): return lax.ppermute(value, axes + ('cc',), pairs)  81.3 us
    ppermute x36, starting transfers between devices, crossed(): return lax.ppermute(value, axes + ('cc',), pairs)  50.4 us
    pallas_call x3, Pallas kernels, attend_back(): pl.pallas_call(attend_back_kernel, grid=(4 // QB,), in_specs=[hb, kspec,...  24.7 us
    pallas_call x1, Pallas kernels, middle(): pl.pallas_call(middle_kernel, in_specs=[SM] + [VM] * 7 + [HB] * 16, out_s...  21.5 us
    pallas_call x2, Pallas kernels, attend(): pl.pallas_call(attend_kernel, grid=(heads,), in_specs=[pl.BlockSpec((HD,...  13.3 us
    pallas_call x2, Pallas kernels, grad_call(): pl.pallas_call(functools.partial(give_kernel, blocks), grid_spec=pltpu.Pr...  10.3 us
    pallas_call x2, Pallas kernels, grad_call(): pl.pallas_call(functools.partial(second_kernel, blocks), grid_spec=pltpu....  9.33 us
    ppermute x4, waiting for transfers between devices, swap2(): return lax.ppermute(value, axis, [(0, 1), (1, 0)])  7.92 us
  transfers between devices with their start and end apart: 58, of which 22 were waited for; matrix products, arithmetic and copies ran while one was open for 8% of the time, Pallas kernels for 25%

profile of v5, /device:TPU:0, one launch (start us, length us, event | category | flops | bytes accessed | tf_op | source)
XLA Modules:
  0.0 293.9 jit_solution(14055385532618965410)
XLA Ops:
  1.6 3.0 %collective-permute-start.6 = (bf16[96,576]{1,0:T(8,128)(2,1)S(1)}, bf16[96,576]{1,0:T(8,128)(2,1)S(1)}, u32[]{:S(2)}, u32[]{:S(2)}) collective-permute-start(bf16[96,576]{1,0:T(8,128)(2,1)S(1)} %pad_maximum_fusion.20), channel_id=1, source_target_pairs={{0,16},{16,0},{1,17},{17,1},{2,18},{18,2},{3,19},{19,3},{4,20},{20... | collective-permute-start | bytes 331784 | tf_op jit(solution)/shard_map/ppermute | solution.py:512
  6.3 1.6 collective-permute-start.23
  11.2 2.7 collective-permute-start
  21.6 3.2 %collective-permute-start.1 = (bf16[2,192,256]{2,1,0:T(8,128)(2,1)S(1)}, bf16[2,192,256]{2,1,0:T(8,128)(2,1)S(1)}, u32[]{:S(2)}, u32[]{:S(2)}) collective-permute-start(bf16[2,192,256]{2,1,0:T(8,128)(2,1)S(1)} %pad_maximum_fusion.13), channel_id=1, source_target_pairs={{0,4},{1,9},{4,0},{5,13},{8,12},{9,1},{12,8},{13,5},{2,6},{3,11},{... | collective-permute-start | bytes 589832 | tf_op jit(solution)/shard_map/ppermute | solution.py:522
  25.8 8.5 %collective-permute-done.1 = bf16[2,192,256]{2,1,0:T(8,128)(2,1)S(1)} collective-permute-done((bf16[2,192,256]{2,1,0:T(8,128)(2,1)S(1)}, bf16[2,192,256]{2,1,0:T(8,128)(2,1)S(1)}, u32[]{:S(2)}, u32[]{:S(2)}) %collective-permute-start.1) | collective-permute-done | bytes 196640 | tf_op jit(solution)/shard_map/ppermute | solution.py:522
  34.5 1.6 collective-permute-start.4
  36.8 2.8 collective-permute-start.3
  39.7 2.7 collective-permute-done.4.xb
  42.5 9.1 %collective-permute-done.9 = bf16[2,96,576]{2,1,0:T(8,128)(2,1)S(1)} collective-permute-done((bf16[2,96,576]{2,1,0:T(8,128)(2,1)S(1)}, bf16[2,96,576]{2,1,0:T(8,128)(2,1)S(1)}, u32[]{:S(2)}, u32[]{:S(2)}) %collective-permute-start.9) | collective-permute-done | bytes 221216 | tf_op jit(solution)/shard_map/ppermute | solution.py:522
  52.8 1.6 collective-permute-start.16
  56.0 6.7 %collective-permute-done.5.xc = bf16[2,4,192,256]{3,2,1,0:T(8,128)(2,1)S(1)} collective-permute-done((bf16[2,4,192,256]{3,2,1,0:T(8,128)(2,1)S(1)}, bf16[2,4,192,256]{3,2,1,0:T(8,128)(2,1)S(1)}, u32[]{:S(2)}, u32[]{:S(2)}) %collective-permute-start.5) | collective-permute-done | bytes 786464 | tf_op jit(solution)/shard_map/ppermute | solution.py:522
  63.6 4.0 %qkv.1 = (bf16[192,1024]{1,0:T(8,128)(2,1)}, bf16[384,1024]{1,0:T(8,128)(2,1)}) custom-call(s32[8]{0:T(128)} %stack.141.info, bf16[4,192,256]{2,1,0:T(8,128)(2,1)} %copy-done.1, bf16[4,192,256]{2,1,0:T(8,128)(2,1)} %copy-done.4, bf16[2,4,192,256]{3,2,1,0:T(8,128)(2,1)} %copy-done.9, bf16[4,96,576]{2,1,0:T(8,128)(2,1)} %copy-done.2, ...), custom_call_target="tpu_custom_call" | custom-call | tf_op jit(solution)/shard_map/qkv/pallas_call | solution.py:182
  69.1 1.6 collective-permute-start.14
  74.5 6.6 %attend.2 = (f32[192,512]{1,0:T(8,128)}, f32[3,1,512]{2,1,0:T(1,128)}, bf16[2,192,256]{2,1,0:T(8,128)(2,1)}) custom-call(bf16[192,1024]{1,0:T(8,128)(2,1)} %get-tuple-element.147.q_ref, bf16[384,1024]{1,0:T(8,128)(2,1)} %get-tuple-element.101.ko_ref.vo_ref, bf16[384,1024]{1,0:T(8,128)(2,1)} %get-tuple-element.101.ko_ref.vo_ref, ...), custom_call_target="tpu_custom_call" | custom-call | flops 19327352832 | bytes 25165824 | tf_op jit(solution)/shard_map/attend/pallas_call | solution.py:66
  81.1 2.5 collective-permute-done.24
  87.2 6.6 %attend.3 = (f32[192,512]{1,0:T(8,128)}, f32[3,1,512]{2,1,0:T(1,128)}, bf16[2,192,256]{2,1,0:T(8,128)(2,1)}) custom-call(bf16[192,1024]{1,0:T(8,128)(2,1)} %get-tuple-element.147.q_ref, bf16[384,1024]{1,0:T(8,128)(2,1)} %get-tuple-element.101.ko_ref.vo_ref, bf16[384,1024]{1,0:T(8,128)(2,1)} %get-tuple-element.101.ko_ref.vo_ref, ...), custom_call_target="tpu_custom_call" | custom-call | flops 19327352832 | bytes 25165824 | tf_op jit(solution)/shard_map/attend/pallas_call | solution.py:66
  93.9 8.3 %collective-permute-done.25.refs_9_ = bf16[4,96,768]{2,1,0:T(8,128)(2,1)} collective-permute-done((bf16[4,96,768]{2,1,0:T(8,128)(2,1)S(1)}, bf16[4,96,768]{2,1,0:T(8,128)(2,1)}, u32[]{:S(2)}, u32[]{:S(2)}) %collective-permute-start.25) | collective-permute-done | bytes 589856 | tf_op jit(solution)/shard_map/ppermute | solution.py:522
  106.2 6.6 %collective-permute-done.13.a2 = bf16[2,192,256]{2,1,0:T(8,128)(2,1)S(1)} collective-permute-done((bf16[2,192,256]{2,1,0:T(8,128)(2,1)S(1)}, bf16[2,192,256]{2,1,0:T(8,128)(2,1)S(1)}, u32[]{:S(2)}, u32[]{:S(2)}) %collective-permute-start.13) | collective-permute-done | bytes 196640 | tf_op jit(solution)/shard_map/ppermute | solution.py:522
  113.3 2.1 collective-permute-start.15
  115.4 5.0 %collective-permute-done.15.c2 = bf16[2,192,256]{2,1,0:T(8,128)(2,1)S(1)} collective-permute-done((bf16[2,192,256]{2,1,0:T(8,128)(2,1)S(1)}, bf16[2,192,256]{2,1,0:T(8,128)(2,1)S(1)}, u32[]{:S(2)}, u32[]{:S(2)}) %collective-permute-start.15) | collective-permute-done | bytes 196640 | tf_op jit(solution)/shard_map/ppermute | solution.py:522
  122.3 3.0 %collective-permute-done.30.refs_14_ = bf16[4,96,768]{2,1,0:T(8,128)(2,1)S(1)} collective-permute-done((bf16[4,96,768]{2,1,0:T(8,128)(2,1)}, bf16[4,96,768]{2,1,0:T(8,128)(2,1)S(1)}, u32[]{:S(2)}, u32[]{:S(2)}) %collective-permute-start.30) | collective-permute-done | bytes 589856 | tf_op jit(solution)/shard_map/ppermute | solution.py:446
  126.5 21.5 %middle.1 = (bf16[2,192,256]{2,1,0:T(8,128)(2,1)}, bf16[2,192,256]{2,1,0:T(8,128)(2,1)}, bf16[2,192,256]{2,1,0:T(8,128)(2,1)}, bf16[2,192,256]{2,1,0:T(8,128)(2,...) custom-call(s32[8]{0:T(128)} %stack.141.info, ...), custom_call_target="tpu_custom_call" | custom-call | flops 86973087744 | bytes 339738624 | tf_op jit(solution)/shard_map/middle/pallas_call | solution.py:347
  150.3 4.7 %outer_give.1 = bf16[2,2,4,96,768]{4,3,2,1,0:T(8,128)(2,1)} custom-call(s32[8]{0:T(128)} %stack.141.info, bf16[768,256]{1,0:T(8,128)(2,1)} %get-tuple-element.141.refs_0_, bf16[256,3072]{1,0:T(8,128)(2,1)} %get-tuple-element.120.refs_1_.refs_2_, bf16[256,3072]{1,0:T(8,128)(2,1)} %get-tuple-element.120.refs_1_.refs_2_), custom_call_target="tpu_custom_call" | custom-call | flops 3623878656 | bytes 7077889 | tf_op jit(solution)/shard_map/outer_give/pallas_call | solution.py:432
  155.8 5.6 %inner_give.1 = bf16[2,2,4,144,768]{4,3,2,1,0:T(8,128)(2,1)} custom-call(s32[8]{0:T(128)} %stack.141.info, bf16[768,256]{1,0:T(8,128)(2,1)} %get-tuple-element.144.refs_0_, bf16[256,3072]{1,0:T(8,128)(2,1)} %get-tuple-element.127.refs_1_, bf16[768,256]{1,0:T(8,128)(2,1)} %get-tuple-element.128.refs_2_, bf16[4,256,256]{2,1,0:T(8,128)(2,1)} %get-tuple-element.129.refs_3_, ...), custom_call_target="tpu_custom_call" | custom-call | flops 3623878656 | bytes 10616833 | tf_op jit(solution)/shard_map/inner_give/pallas_call | solution.py:432
  165.0 1.7 collective-permute-start.43
  167.9 3.1 %collective-permute-done.34.refs_3_ = bf16[2,2,4,96,768]{4,3,2,1,0:T(8,128)(2,1)} collective-permute-done((bf16[2,2,4,96,768]{4,3,2,1,0:T(8,128)(2,1)}, bf16[2,2,4,96,768]{4,3,2,1,0:T(8,128)(2,1)}, u32[]{:S(2)}, u32[]{:S(2)}) %collective-permute-start.34) | collective-permute-done | bytes 2359328 | tf_op jit(solution)/shard_map/ppermute | solution.py:446
  171.0 3.6 %outer_first.1 = bf16[2,4,96,768]{3,2,1,0:T(8,128)(2,1)} custom-call(s32[8]{0:T(128)} %stack.141.info, bf16[768,256]{1,0:T(8,128)(2,1)} %get-tuple-element.141.refs_0_, bf16[256,3072]{1,0:T(8,128)(2,1)} %get-tuple-element.120.refs_1_.refs_2_, bf16[256,3072]{1,0:T(8,128)(2,1)} %get-tuple-element.120.refs_1_.refs_2_, ...), custom_call_target="tpu_custom_call" | custom-call | flops 1811939328 | bytes 7077889 | tf_op jit(solution)/shard_map/outer_first/pallas_call | solution.py:437
  174.6 2.1 collective-permute-start.36
  176.7 1.8 copy-done
  178.5 4.2 %inner_first.1 = bf16[2,4,144,768]{3,2,1,0:T(8,128)(2,1)} custom-call(s32[8]{0:T(128)} %stack.141.info, bf16[768,256]{1,0:T(8,128)(2,1)} %get-tuple-element.144.refs_0_, bf16[256,3072]{1,0:T(8,128)(2,1)} %get-tuple-element.127.refs_1_, bf16[768,256]{1,0:T(8,128)(2,1)} %get-tuple-element.128.refs_2_, bf16[4,256,256]{2,1,0:T(8,128)(2,1)} %get-tuple-element.129.refs_3_, ...), custom_call_target="tpu_custom_call" | custom-call | flops 1811939328 | bytes 10616833 | tf_op jit(solution)/shard_map/inner_first/pallas_call | solution.py:437
  183.4 8.4 %attend_back.3 = (bf16[64,1024]{1,0:T(8,128)(2,1)}, f32[1024,128]{1,0:T(8,128)}, bf16[1024,128]{1,0:T(8,128)(2,1)}) custom-call(bf16[192,1024]{1,0:T(8,128)(2,1)} %get-tuple-element.147.q_ref, bf16[384,1024]{1,0:T(8,128)(2,1)} %get-tuple-element.101.ko_ref.vo_ref, bf16[384,1024]{1,0:T(8,128)(2,1)} %get-tuple-element.101.ko_ref.vo_ref, ...), custom_call_target="tpu_custom_call" | custom-call | flops 32212254720 | bytes 50331648 | tf_op jit(solution)/shard_map/attend_back/pallas_call | solution.py:119
  193.7 8.1 %attend_back.4 = (bf16[64,1024]{1,0:T(8,128)(2,1)}, f32[1024,128]{1,0:T(8,128)}, bf16[1024,128]{1,0:T(8,128)(2,1)}) custom-call(bf16[192,1024]{1,0:T(8,128)(2,1)} %get-tuple-element.147.q_ref, bf16[384,1024]{1,0:T(8,128)(2,1)} %get-tuple-element.101.ko_ref.vo_ref, bf16[384,1024]{1,0:T(8,128)(2,1)} %get-tuple-element.101.ko_ref.vo_ref, ...), custom_call_target="tpu_custom_call" | custom-call | flops 32212254720 | bytes 50331648 | tf_op jit(solution)/shard_map/attend_back/pallas_call | solution.py:119
  201.9 7.1 %collective-permute-done.36.refs_4_ = bf16[2,4,96,768]{3,2,1,0:T(8,128)(2,1)} collective-permute-done((bf16[2,4,96,768]{3,2,1,0:T(8,128)(2,1)}, bf16[2,4,96,768]{3,2,1,0:T(8,128)(2,1)}, u32[]{:S(2)}, u32[]{:S(2)}) %collective-permute-start.36) | collective-permute-done | bytes 1179680 | tf_op jit(solution)/shard_map/ppermute | solution.py:522
  208.9 4.1 %outer_second.1 = (bf16[4,96,768]{2,1,0:T(8,128)(2,1)}, bf16[4,96,768]{2,1,0:T(8,128)(2,1)}) custom-call(s32[8]{0:T(128)} %stack.141.info, bf16[768,256]{1,0:T(8,128)(2,1)} %get-tuple-element.141.refs_0_, bf16[256,3072]{1,0:T(8,128)(2,1)} %get-tuple-element.120.refs_1_.refs_2_, bf16[256,3072]{1,0:T(8,128)(2,1)} %get-tuple-element.120.refs_1_.refs_2_, ...), custom_call_target="tpu_custom_call" | custom-call | flops 1811939328 | bytes 7077889 | tf_op jit(solution)/shard_map/outer_second/pallas_call | solution.py:441
  214.3 5.2 %inner_second.1 = (bf16[4,144,768]{2,1,0:T(8,128)(2,1)}, bf16[4,144,768]{2,1,0:T(8,128)(2,1)}) custom-call(s32[8]{0:T(128)} %stack.141.info, bf16[768,256]{1,0:T(8,128)(2,1)} %get-tuple-element.144.refs_0_, bf16[256,3072]{1,0:T(8,128)(2,1)} %get-tuple-element.127.refs_1_, bf16[768,256]{1,0:T(8,128)(2,1)} %get-tuple-element.128.refs_2_, ...), custom_call_target="tpu_custom_call" | custom-call | flops 1811939328 | bytes 10616833 | tf_op jit(solution)/shard_map/inner_second/pallas_call | solution.py:441
  221.0 8.2 %attend_back.5 = (bf16[64,1024]{1,0:T(8,128)(2,1)}, f32[1024,128]{1,0:T(8,128)}, bf16[1024,128]{1,0:T(8,128)(2,1)}) custom-call(bf16[192,1024]{1,0:T(8,128)(2,1)} %get-tuple-element.147.q_ref, bf16[384,1024]{1,0:T(8,128)(2,1)} %get-tuple-element.101.ko_ref.vo_ref, bf16[384,1024]{1,0:T(8,128)(2,1)} %get-tuple-element.101.ko_ref.vo_ref, ...), custom_call_target="tpu_custom_call" | custom-call | flops 32212254720 | bytes 50331648 | tf_op jit(solution)/shard_map/attend_back/pallas_call | solution.py:119
  229.2 3.6 %collective-permute-done.38 = bf16[4,144,768]{2,1,0:T(8,128)(2,1)S(1)} collective-permute-done((bf16[4,144,768]{2,1,0:T(8,128)(2,1)}, bf16[4,144,768]{2,1,0:T(8,128)(2,1)S(1)}, u32[]{:S(2)}, u32[]{:S(2)}) %collective-permute-start.38) | collective-permute-done | bytes 884768 | tf_op jit(solution)/shard_map/ppermute | solution.py:522
  233.0 2.8 collective-permute-start.42
  235.8 5.1 %finish_dx.1 = (f32[2,4,192,256]{3,2,1,0:T(8,128)}, bf16[2,4,192,256]{3,2,1,0:T(8,128)(2,1)}, bf16[576,1024]{1,0:T(8,128)(2,1)}) custom-call(s32[8]{0:T(128)} %stack.141.info, bf16[64,1024]{1,0:T(8,128)(2,1)} %get-tuple-element.138.refs_0_, bf16[64,1024]{1,0:T(8,128)(2,1)} %get-tuple-element.140.refs_1_, bf16[64,1024]{1,0:T(8,128)(2,1)} %get-tuple-element.148.refs_2_, ...), custom_call_target="tpu_custom_call" | custom-call | flops 5435817984 | bytes 37748736 | tf_op jit(solution)/shard_map/finish_dx/pallas_call | solution.py:205
  241.8 3.9 %collective-permute-done.42 = bf16[2,144,768]{2,1,0:T(8,128)(2,1)S(1)} collective-permute-done((bf16[2,144,768]{2,1,0:T(8,128)(2,1)S(1)}, bf16[2,144,768]{2,1,0:T(8,128)(2,1)S(1)}, u32[]{:S(2)}, u32[]{:S(2)}) %collective-permute-start.42) | collective-permute-done | bytes 442400 | tf_op jit(solution)/shard_map/ppermute | solution.py:522
  245.8 4.4 %finish_dw.1 = (f32[4,96,576]{2,1,0:T(8,128)}, bf16[4,96,576]{2,1,0:T(8,128)(2,1)}) custom-call(s32[8]{0:T(128)} %stack.141.info, bf16[576,1024]{1,0:T(8,128)(2,1)} %get-tuple-element.162.p_ref, bf16[4,192,256]{2,1,0:T(8,128)(2,1)} %copy-done.1, bf16[4,192,256]{2,1,0:T(8,128)(2,1)} %copy-done.4, bf16[2,4,192,256]{3,2,1,0:T(8,128)(2,1)} %copy-done.9), custom_call_target="tpu_custom_call" | custom-call | flops 5435817984 | bytes 18874368 | tf_op jit(solution)/shard_map/finish_dw/pallas_call | solution.py:224
  252.3 1.8 collective-permute-start.56
  258.0 2.4 collective-permute-start.50
  260.4 4.8 %collective-permute-done.46 = bf16[4,192,256]{2,1,0:T(8,128)(2,1)S(1)} collective-permute-done((bf16[4,192,256]{2,1,0:T(8,128)(2,1)S(1)}, bf16[4,192,256]{2,1,0:T(8,128)(2,1)S(1)}, u32[]{:S(2)}, u32[]{:S(2)}) %collective-permute-start.46) | collective-permute-done | bytes 393248 | tf_op jit(solution)/shard_map/ppermute | solution.py:522
  265.5 7.0 %collective-permute-done.50 = bf16[2,96,576]{2,1,0:T(8,128)(2,1)S(1)} collective-permute-done((bf16[2,96,576]{2,1,0:T(8,128)(2,1)S(1)}, bf16[2,96,576]{2,1,0:T(8,128)(2,1)S(1)}, u32[]{:S(2)}, u32[]{:S(2)}) %collective-permute-start.50) | collective-permute-done | bytes 221216 | tf_op jit(solution)/shard_map/ppermute | solution.py:512
  272.6 2.4 collective-permute-start.49
  276.1 3.9 %collective-permute-done.49 = bf16[2,192,256]{2,1,0:T(8,128)(2,1)S(1)} collective-permute-done((bf16[2,192,256]{2,1,0:T(8,128)(2,1)S(1)}, bf16[2,192,256]{2,1,0:T(8,128)(2,1)S(1)}, u32[]{:S(2)}, u32[]{:S(2)}) %collective-permute-start.49) | collective-permute-done | bytes 196640 | tf_op jit(solution)/shard_map/ppermute | solution.py:522
  286.1 4.8 %collective-permute-done.52 = bf16[2,192,256]{2,1,0:T(8,128)(2,1)S(1)} collective-permute-done((bf16[2,192,256]{2,1,0:T(8,128)(2,1)S(1)}, bf16[2,192,256]{2,1,0:T(8,128)(2,1)S(1)}, u32[]{:S(2)}, u32[]{:S(2)}) %collective-permute-start.52) | collective-permute-done | bytes 196640 | tf_op jit(solution)/shard_map/ppermute | solution.py:522
  (269 shorter events, 65.6 us)
Async XLA Ops:
  1.6 18.3 %collective-permute-start.6 = (bf16[96,576]{1,0:T(8,128)(2,1)S(1)}, bf16[96,576]{1,0:T(8,128)(2,1)S(1)}, u32[]{:S(2)}, u32[]{:S(2)}) collective-permute-start(bf16[96,576]{1,0:T(8,128)(2,1)S(1)} %pad_maximum_fusion.20), channel_id=1, source_target_pairs={{0,16},{16,0},{1,17},{17,1},{2,18},{18,2},{3,19},{19,3},{4,20},{20... | collective-permute-start | bytes 331784 | tf_op jit(solution)/shard_map/ppermute | solution.py:512
  6.3 62.1 %collective-permute-start.23 = (bf16[96,768]{1,0:T(8,128)(2,1)}, bf16[96,768]{1,0:T(8,128)(2,1)S(1)}, u32[]{:S(2)}, u32[]{:S(2)}) collective-permute-start(bf16[96,768]{1,0:T(8,128)(2,1)} %get-tuple-element.224), channel_id=1, source_target_pairs={{0,4},{1,9},{4,0},{5,13},{8,12},{9,1},{12,8},{13,5},{2,6},{3,11},{... | collective-permute-start | bytes 442376 | tf_op jit(solution)/shard_map/ppermute | solution.py:522
  10.4 15.4 %collective-permute-start.2 = (bf16[144,768]{1,0:T(8,128)(2,1)S(1)}, bf16[144,768]{1,0:T(8,128)(2,1)S(1)}, u32[]{:S(2)}, u32[]{:S(2)}) collective-permute-start(bf16[144,768]{1,0:T(8,128)(2,1)S(1)} %pad_maximum_fusion.12), channel_id=1, source_target_pairs={{0,4},{1,9},{4,0},{5,13},{8,12},{9,1},{12,8},{13,5},{2,6},{3,11},{... | collective-permute-start | bytes 663560 | tf_op jit(solution)/shard_map/ppermute | solution.py:522
  11.2 10.4 %collective-permute-start = (bf16[2,192,256]{2,1,0:T(8,128)(2,1)S(1)}, bf16[2,192,256]{2,1,0:T(8,128)(2,1)S(1)}, u32[]{:S(2)}, u32[]{:S(2)}) collective-permute-start(bf16[2,192,256]{2,1,0:T(8,128)(2,1)S(1)} %slice_bitcast_fusion.3), channel_id=1, source_target_pairs={{0,8},{1,5},{4,12},{5,1},{8,0},{9,13},{12,4},{13,9},{2,10},{3,7},{... | collective-permute-start | bytes 589832 | tf_op jit(solution)/shard_map/ppermute | solution.py:522
  21.6 12.7 %collective-permute-start.1 = (bf16[2,192,256]{2,1,0:T(8,128)(2,1)S(1)}, bf16[2,192,256]{2,1,0:T(8,128)(2,1)S(1)}, u32[]{:S(2)}, u32[]{:S(2)}) collective-permute-start(bf16[2,192,256]{2,1,0:T(8,128)(2,1)S(1)} %pad_maximum_fusion.13), channel_id=1, source_target_pairs={{0,4},{1,9},{4,0},{5,13},{8,12},{9,1},{12,8},{13,5},{2,6},{3,11},{... | collective-permute-start | bytes 589832 | tf_op jit(solution)/shard_map/ppermute | solution.py:522
  25.1 10.9 %collective-permute-start.8 = (bf16[2,96,576]{2,1,0:T(8,128)(2,1)S(1)}, bf16[2,96,576]{2,1,0:T(8,128)(2,1)S(1)}, u32[]{:S(2)}, u32[]{:S(2)}) collective-permute-start(bf16[2,96,576]{2,1,0:T(8,128)(2,1)S(1)} %pad_maximum_fusion.10), channel_id=1, source_target_pairs={{0,8},{1,5},{4,12},{5,1},{8,0},{9,13},{12,4},{13,9},{2,10},{3,7},{... | collective-permute-start | bytes 663560 | tf_op jit(solution)/shard_map/ppermute | solution.py:522
  34.5 7.8 %collective-permute-start.4 = (bf16[4,192,256]{2,1,0:T(8,128)(2,1)S(1)}, bf16[4,192,256]{2,1,0:T(8,128)(2,1)S(1)}, u32[]{:S(2)}, u32[]{:S(2)}) collective-permute-start(bf16[4,192,256]{2,1,0:T(8,128)(2,1)S(1)} %pad_maximum_fusion.5.xa.x_ref), channel_id=1, source_target_pairs={{0,2},{1,5},{2,0},{3,7},{4,6},{5,1},{6,4},{7,3},{8,10},{9,13},{10,... | collective-permute-start | bytes 1179656 | tf_op jit(solution)/shard_map/ppermute | solution.py:522
  36.1 15.5 %collective-permute-start.9 = (bf16[2,96,576]{2,1,0:T(8,128)(2,1)S(1)}, bf16[2,96,576]{2,1,0:T(8,128)(2,1)S(1)}, u32[]{:S(2)}, u32[]{:S(2)}) collective-permute-start(bf16[2,96,576]{2,1,0:T(8,128)(2,1)S(1)} %pad_maximum_fusion.11), channel_id=1, source_target_pairs={{0,4},{1,9},{4,0},{5,13},{8,12},{9,1},{12,8},{13,5},{2,6},{3,11},{... | collective-permute-start | bytes 663560 | tf_op jit(solution)/shard_map/ppermute | solution.py:522
  36.8 15.9 %collective-permute-start.3 = (bf16[2,144,768]{2,1,0:T(8,128)(2,1)S(1)}, bf16[2,144,768]{2,1,0:T(8,128)(2,1)S(1)}, u32[]{:S(2)}, u32[]{:S(2)}) collective-permute-start(bf16[2,144,768]{2,1,0:T(8,128)(2,1)S(1)} %pad_maximum_fusion.4), channel_id=1, source_target_pairs={{0,8},{1,5},{4,12},{5,1},{8,0},{9,13},{12,4},{13,9},{2,10},{3,7},{... | collective-permute-start | bytes 1327112 | tf_op jit(solution)/shard_map/ppermute | solution.py:522
  42.4 20.3 %collective-permute-start.5 = (bf16[2,4,192,256]{3,2,1,0:T(8,128)(2,1)S(1)}, bf16[2,4,192,256]{3,2,1,0:T(8,128)(2,1)S(1)}, u32[]{:S(2)}, u32[]{:S(2)}) collective-permute-start(bf16[2,4,192,256]{3,2,1,0:T(8,128)(2,1)S(1)} %pad_maximum_fusion.1), channel_id=1, source_target_pairs={{0,4},{1,3},{2,6},{3,1},{4,0},{5,7},{6,2},{7,5},{8,12},{9,11},{10,... | collective-permute-start | bytes 2359304 | tf_op jit(solution)/shard_map/ppermute | solution.py:522
  52.8 15.6 %collective-permute-start.16 = (bf16[4,144,768]{2,1,0:T(8,128)(2,1)S(1)}, bf16[4,144,768]{2,1,0:T(8,128)(2,1)}, u32[]{:S(2)}, u32[]{:S(2)}) collective-permute-start(bf16[4,144,768]{2,1,0:T(8,128)(2,1)S(1)} %pad_maximum_fusion.refs_0_), channel_id=1, source_target_pairs={{0,2},{1,17},{2,0},{3,19},{16,18},{17,1},{18,16},{19,3},{4,6},{5,2... | collective-permute-start | bytes 2654216 | tf_op jit(solution)/shard_map/ppermute | solution.py:522
  67.8 17.3 %collective-permute-start.17 = (bf16[4,144,768]{2,1,0:T(8,128)(2,1)S(1)}, bf16[4,144,768]{2,1,0:T(8,128)(2,1)}, u32[]{:S(2)}, u32[]{:S(2)}) collective-permute-start(bf16[4,144,768]{2,1,0:T(8,128)(2,1)S(1)} %pad_maximum_fusion.refs_0_), channel_id=1, source_target_pairs={{0,16},{1,3},{2,18},{3,1},{16,0},{17,19},{18,2},{19,17},{4,20},{5,... | collective-permute-start | bytes 2654216 | tf_op jit(solution)/shard_map/ppermute | solution.py:522
  69.1 16.7 %collective-permute-start.14 = (bf16[2,192,256]{2,1,0:T(8,128)(2,1)S(1)}, bf16[2,192,256]{2,1,0:T(8,128)(2,1)S(1)}, u32[]{:S(2)}, u32[]{:S(2)}) collective-permute-start(bf16[2,192,256]{2,1,0:T(8,128)(2,1)S(1)} %get-tuple-element.197), channel_id=1, source_target_pairs={{0,8},{1,5},{4,12},{5,1},{8,0},{9,13},{12,4},{13,9},{2,10},{3,7},{... | collective-permute-start | bytes 589832 | tf_op jit(solution)/shard_map/ppermute | solution.py:522
  70.7 12.9 %collective-permute-start.24 = (bf16[2,96,768]{2,1,0:T(8,128)(2,1)S(1)}, bf16[2,96,768]{2,1,0:T(8,128)(2,1)S(1)}, u32[]{:S(2)}, u32[]{:S(2)}) collective-permute-start(bf16[2,96,768]{2,1,0:T(8,128)(2,1)S(1)} %pad_maximum_fusion.8), channel_id=1, source_target_pairs={{0,8},{1,5},{4,12},{5,1},{8,0},{9,13},{12,4},{13,9},{2,10},{3,7},{... | collective-permute-start | bytes 884744 | tf_op jit(solution)/shard_map/ppermute | solution.py:522
  72.1 32.5 %collective-permute-start.18 = (bf16[4,144,768]{2,1,0:T(8,128)(2,1)}, bf16[4,144,768]{2,1,0:T(8,128)(2,1)}, u32[]{:S(2)}, u32[]{:S(2)}) collective-permute-start(bf16[4,144,768]{2,1,0:T(8,128)(2,1)} %collective-permute-done.16.refs_1_), channel_id=1, source_target_pairs={{0,16},{1,3},{2,18},{3,1},{16,0},{17,19},{18,2},{19,17},{4,20},{5,... | collective-permute-start | bytes 2654216 | tf_op jit(solution)/shard_map/ppermute | solution.py:522
  73.6 31.3 %collective-permute-start.19 = (bf16[4,144,768]{2,1,0:T(8,128)(2,1)S(1)}, bf16[4,144,768]{2,1,0:T(8,128)(2,1)}, u32[]{:S(2)}, u32[]{:S(2)}) collective-permute-start(bf16[4,144,768]{2,1,0:T(8,128)(2,1)S(1)} %pad_maximum_fusion.refs_0_), channel_id=1, source_target_pairs={{0,1},{1,0},{2,3},{3,2},{4,5},{5,4},{6,7},{7,6},{8,9},{9,8},{10,11... | collective-permute-start | bytes 2654216 | tf_op jit(solution)/shard_map/ppermute | solution.py:446
  83.7 18.5 %collective-permute-start.12 = (bf16[2,192,256]{2,1,0:T(8,128)(2,1)}, bf16[2,192,256]{2,1,0:T(8,128)(2,1)S(1)}, u32[]{:S(2)}, u32[]{:S(2)}) collective-permute-start(bf16[2,192,256]{2,1,0:T(8,128)(2,1)} %get-tuple-element.102), channel_id=1, source_target_pairs={{0,4},{1,3},{2,6},{3,1},{4,0},{5,7},{6,2},{7,5},{8,12},{9,11},{10,... | collective-permute-start | bytes 589832 | tf_op jit(solution)/shard_map/ppermute | solution.py:522
  85.1 27.7 %collective-permute-start.26 = (bf16[4,96,768]{2,1,0:T(8,128)(2,1)S(1)}, bf16[4,96,768]{2,1,0:T(8,128)(2,1)}, u32[]{:S(2)}, u32[]{:S(2)}) collective-permute-start(bf16[4,96,768]{2,1,0:T(8,128)(2,1)S(1)} %pad_maximum_fusion.2.refs_8_), channel_id=1, source_target_pairs={{0,16},{1,3},{2,18},{3,1},{16,0},{17,19},{18,2},{19,17},{4,20},{5,... | collective-permute-start | bytes 1769480 | tf_op jit(solution)/shard_map/ppermute | solution.py:522
  85.8 16.4 %collective-permute-start.25 = (bf16[4,96,768]{2,1,0:T(8,128)(2,1)S(1)}, bf16[4,96,768]{2,1,0:T(8,128)(2,1)}, u32[]{:S(2)}, u32[]{:S(2)}) collective-permute-start(bf16[4,96,768]{2,1,0:T(8,128)(2,1)S(1)} %pad_maximum_fusion.2.refs_8_), channel_id=1, source_target_pairs={{0,2},{1,17},{2,0},{3,19},{16,18},{17,1},{18,16},{19,3},{4,6},{5,2... | collective-permute-start | bytes 1769480 | tf_op jit(solution)/shard_map/ppermute | solution.py:522
  102.2 19.7 %collective-permute-start.20 = (bf16[4,144,768]{2,1,0:T(8,128)(2,1)}, bf16[4,144,768]{2,1,0:T(8,128)(2,1)S(1)}, u32[]{:S(2)}, u32[]{:S(2)}) collective-permute-start(bf16[4,144,768]{2,1,0:T(8,128)(2,1)} %collective-permute-done.16.refs_1_), channel_id=1, source_target_pairs={{0,1},{1,0},{2,3},{3,2},{4,5},{5,4},{6,7},{7,6},{8,9},{9,8},{10,11... | collective-permute-start | bytes 2654216 | tf_op jit(solution)/shard_map/ppermute | solution.py:446
  102.2 11.1 %collective-permute-start.27 = (bf16[4,96,768]{2,1,0:T(8,128)(2,1)}, bf16[4,96,768]{2,1,0:T(8,128)(2,1)S(1)}, u32[]{:S(2)}, u32[]{:S(2)}) collective-permute-start(bf16[4,96,768]{2,1,0:T(8,128)(2,1)} %collective-permute-done.25.refs_9_), channel_id=1, source_target_pairs={{0,16},{1,3},{2,18},{3,1},{16,0},{17,19},{18,2},{19,17},{4,20},{5,... | collective-permute-start | bytes 1769480 | tf_op jit(solution)/shard_map/ppermute | solution.py:522
  104.6 17.2 %collective-permute-start.28 = (bf16[4,96,768]{2,1,0:T(8,128)(2,1)S(1)}, bf16[4,96,768]{2,1,0:T(8,128)(2,1)S(1)}, u32[]{:S(2)}, u32[]{:S(2)}) collective-permute-start(bf16[4,96,768]{2,1,0:T(8,128)(2,1)S(1)} %pad_maximum_fusion.2.refs_8_), channel_id=1, source_target_pairs={{0,1},{1,0},{2,3},{3,2},{4,5},{5,4},{6,7},{7,6},{8,9},{9,8},{10,11... | collective-permute-start | bytes 1769480 | tf_op jit(solution)/shard_map/ppermute | solution.py:446
  104.9 7.9 %collective-permute-start.13 = (bf16[2,192,256]{2,1,0:T(8,128)(2,1)S(1)}, bf16[2,192,256]{2,1,0:T(8,128)(2,1)S(1)}, u32[]{:S(2)}, u32[]{:S(2)}) collective-permute-start(bf16[2,192,256]{2,1,0:T(8,128)(2,1)S(1)} %pad_maximum_fusion.14), channel_id=1, source_target_pairs={{0,2},{1,5},{2,0},{3,7},{4,6},{5,1},{6,4},{7,3},{8,10},{9,13},{10,... | collective-permute-start | bytes 589832 | tf_op jit(solution)/shard_map/ppermute | solution.py:522
  112.8 9.5 %collective-permute-start.21 = (bf16[4,144,768]{2,1,0:T(8,128)(2,1)}, bf16[4,144,768]{2,1,0:T(8,128)(2,1)S(1)}, u32[]{:S(2)}, u32[]{:S(2)}) collective-permute-start(bf16[4,144,768]{2,1,0:T(8,128)(2,1)} %collective-permute-done.17.refs_2_), channel_id=1, source_target_pairs={{0,1},{1,0},{2,3},{3,2},{4,5},{5,4},{6,7},{7,6},{8,9},{9,8},{10,11... | collective-permute-start | bytes 2654216 | tf_op jit(solution)/shard_map/ppermute | solution.py:446
  112.8 9.5 %collective-permute-start.22 = (bf16[4,144,768]{2,1,0:T(8,128)(2,1)}, bf16[4,144,768]{2,1,0:T(8,128)(2,1)S(1)}, u32[]{:S(2)}, u32[]{:S(2)}) collective-permute-start(bf16[4,144,768]{2,1,0:T(8,128)(2,1)} %collective-permute-done.18.refs_3_), channel_id=1, source_target_pairs={{0,1},{1,0},{2,3},{3,2},{4,5},{5,4},{6,7},{7,6},{8,9},{9,8},{10,11... | collective-permute-start | bytes 2654216 | tf_op jit(solution)/shard_map/ppermute | solution.py:446
  113.3 7.0 %collective-permute-start.15 = (bf16[2,192,256]{2,1,0:T(8,128)(2,1)S(1)}, bf16[2,192,256]{2,1,0:T(8,128)(2,1)S(1)}, u32[]{:S(2)}, u32[]{:S(2)}) collective-permute-start(bf16[2,192,256]{2,1,0:T(8,128)(2,1)S(1)} %pad_maximum_fusion.15), channel_id=1, source_target_pairs={{0,4},{1,9},{4,0},{5,13},{8,12},{9,1},{12,8},{13,5},{2,6},{3,11},{... | collective-permute-start | bytes 589832 | tf_op jit(solution)/shard_map/ppermute | solution.py:522
  161.4 15.3 %collective-permute-start.35 = (bf16[2,2,4,144,768]{4,3,2,1,0:T(8,128)(2,1)}, bf16[2,2,4,144,768]{4,3,2,1,0:T(8,128)(2,1)S(1)}, u32[]{:S(2)}, u32[]{:S(2)}) collective-permute-start(bf16[2,2,4,144,768]{4,3,2,1,0:T(8,128)(2,1)} %inner_give.1), channel_id=1, source_target_pairs={{0,1},{1,0},{2,3},{3,2},{4,5},{5,4},{6,7},{7,6},{8,9},{9,8},{10,11... | collective-permute-start | bytes 10616840 | tf_op jit(solution)/shard_map/ppermute | solution.py:446
  161.4 9.6 %collective-permute-start.34 = (bf16[2,2,4,96,768]{4,3,2,1,0:T(8,128)(2,1)}, bf16[2,2,4,96,768]{4,3,2,1,0:T(8,128)(2,1)}, u32[]{:S(2)}, u32[]{:S(2)}) collective-permute-start(bf16[2,2,4,96,768]{4,3,2,1,0:T(8,128)(2,1)} %outer_give.1), channel_id=1, source_target_pairs={{0,1},{1,0},{2,3},{3,2},{4,5},{5,4},{6,7},{7,6},{8,9},{9,8},{10,11... | collective-permute-start | bytes 7077896 | tf_op jit(solution)/shard_map/ppermute | solution.py:446
  165.0 26.8 %collective-permute-start.43 = (bf16[2,192,256]{2,1,0:T(8,128)(2,1)}, bf16[2,192,256]{2,1,0:T(8,128)(2,1)}, u32[]{:S(2)}, u32[]{:S(2)}) collective-permute-start(bf16[2,192,256]{2,1,0:T(8,128)(2,1)} %get-tuple-element.166), channel_id=1, source_target_pairs={{0,8},{1,5},{4,12},{5,1},{8,0},{9,13},{12,4},{13,9},{2,10},{3,7},{... | collective-permute-start | bytes 589832 | tf_op jit(solution)/shard_map/ppermute | solution.py:522
  174.6 34.3 %collective-permute-start.36 = (bf16[2,4,96,768]{3,2,1,0:T(8,128)(2,1)}, bf16[2,4,96,768]{3,2,1,0:T(8,128)(2,1)}, u32[]{:S(2)}, u32[]{:S(2)}) collective-permute-start(bf16[2,4,96,768]{3,2,1,0:T(8,128)(2,1)} %outer_first.1), channel_id=1, source_target_pairs={{0,8},{1,5},{4,12},{5,1},{8,0},{9,13},{12,4},{13,9},{2,10},{3,7},{... | collective-permute-start | bytes 3538952 | tf_op jit(solution)/shard_map/ppermute | solution.py:522
  182.7 30.4 %collective-permute-start.37 = (bf16[2,4,144,768]{3,2,1,0:T(8,128)(2,1)}, bf16[2,4,144,768]{3,2,1,0:T(8,128)(2,1)S(1)}, u32[]{:S(2)}, u32[]{:S(2)}) collective-permute-start(bf16[2,4,144,768]{3,2,1,0:T(8,128)(2,1)} %inner_first.1), channel_id=1, source_target_pairs={{0,16},{1,3},{2,18},{3,1},{16,0},{17,19},{18,2},{19,17},{4,20},{5,... | collective-permute-start | bytes 5308424 | tf_op jit(solution)/shard_map/ppermute | solution.py:522
  192.7 59.5 %collective-permute-start.44 = (bf16[2,192,256]{2,1,0:T(8,128)(2,1)S(1)}, bf16[2,192,256]{2,1,0:T(8,128)(2,1)S(1)}, u32[]{:S(2)}, u32[]{:S(2)}) collective-permute-start(bf16[2,192,256]{2,1,0:T(8,128)(2,1)S(1)} %pad_maximum_fusion.17), channel_id=1, source_target_pairs={{0,4},{1,9},{4,0},{5,13},{8,12},{9,1},{12,8},{13,5},{2,6},{3,11},{... | collective-permute-start | bytes 589832 | tf_op jit(solution)/shard_map/ppermute | solution.py:522
  193.7 39.3 %collective-permute-start.39 = (bf16[1024,128]{1,0:T(8,128)(2,1)}, bf16[1024,128]{1,0:T(8,128)(2,1)}, u32[]{:S(2)}, u32[]{:S(2)}) collective-permute-start(bf16[1024,128]{1,0:T(8,128)(2,1)} %get-tuple-element.155), channel_id=1, source_target_pairs={{0,1},{1,0},{2,3},{3,2},{4,5},{5,4},{6,7},{7,6},{8,9},{9,8},{10,11... | collective-permute-start | bytes 786440 | tf_op jit(solution)/shard_map/ppermute | solution.py:446
  213.1 22.8 %collective-permute-start.40 = (bf16[1024,128]{1,0:T(8,128)(2,1)}, bf16[1024,128]{1,0:T(8,128)(2,1)}, u32[]{:S(2)}, u32[]{:S(2)}) collective-permute-start(bf16[1024,128]{1,0:T(8,128)(2,1)} %get-tuple-element.156), channel_id=1, source_target_pairs={{0,1},{1,0},{2,3},{3,2},{4,5},{5,4},{6,7},{7,6},{8,9},{9,8},{10,11... | collective-permute-start | bytes 786440 | tf_op jit(solution)/shard_map/ppermute | solution.py:446
  213.1 43.0 %collective-permute-start.48 = (bf16[4,96,768]{2,1,0:T(8,128)(2,1)}, bf16[4,96,768]{2,1,0:T(8,128)(2,1)}, u32[]{:S(2)}, u32[]{:S(2)}) collective-permute-start(bf16[4,96,768]{2,1,0:T(8,128)(2,1)} %get-tuple-element.174), channel_id=1, source_target_pairs={{0,4},{1,9},{4,0},{5,13},{8,12},{9,1},{12,8},{13,5},{2,6},{3,11},{... | collective-permute-start | bytes 1769480 | tf_op jit(solution)/shard_map/ppermute | solution.py:522
  219.5 13.3 %collective-permute-start.38 = (bf16[4,144,768]{2,1,0:T(8,128)(2,1)}, bf16[4,144,768]{2,1,0:T(8,128)(2,1)S(1)}, u32[]{:S(2)}, u32[]{:S(2)}) collective-permute-start(bf16[4,144,768]{2,1,0:T(8,128)(2,1)} %get-tuple-element.152), channel_id=1, source_target_pairs={{0,2},{1,17},{2,0},{3,19},{16,18},{17,1},{18,16},{19,3},{4,6},{5,2... | collective-permute-start | bytes 2654216 | tf_op jit(solution)/shard_map/ppermute | solution.py:522
  233.0 12.6 %collective-permute-start.42 = (bf16[2,144,768]{2,1,0:T(8,128)(2,1)S(1)}, bf16[2,144,768]{2,1,0:T(8,128)(2,1)S(1)}, u32[]{:S(2)}, u32[]{:S(2)}) collective-permute-start(bf16[2,144,768]{2,1,0:T(8,128)(2,1)S(1)} %slice.319), channel_id=1, source_target_pairs={{0,8},{1,5},{4,12},{5,1},{8,0},{9,13},{12,4},{13,9},{2,10},{3,7},{... | collective-permute-start | bytes 1327112 | tf_op jit(solution)/shard_map/ppermute | solution.py:522
  240.9 13.5 %collective-permute-start.45 = (bf16[2,4,192,256]{3,2,1,0:T(8,128)(2,1)}, bf16[2,4,192,256]{3,2,1,0:T(8,128)(2,1)S(1)}, u32[]{:S(2)}, u32[]{:S(2)}) collective-permute-start(bf16[2,4,192,256]{3,2,1,0:T(8,128)(2,1)} %get-tuple-element.171), channel_id=1, source_target_pairs={{0,4},{1,3},{2,6},{3,1},{4,0},{5,7},{6,2},{7,5},{8,12},{9,11},{10,... | collective-permute-start | bytes 2359304 | tf_op jit(solution)/shard_map/ppermute | solution.py:522
  250.2 7.7 %collective-permute-start.47 = (bf16[4,96,576]{2,1,0:T(8,128)(2,1)}, bf16[4,96,576]{2,1,0:T(8,128)(2,1)S(1)}, u32[]{:S(2)}, u32[]{:S(2)}) collective-permute-start(bf16[4,96,576]{2,1,0:T(8,128)(2,1)} %get-tuple-element.163), channel_id=1, source_target_pairs={{0,1},{1,0},{2,3},{3,2},{4,5},{5,4},{6,7},{7,6},{8,9},{9,8},{10,11... | collective-permute-start | bytes 1327112 | tf_op jit(solution)/shard_map/ppermute | solution.py:446
  252.3 28.7 %collective-permute-start.56 = (bf16[144,768]{1,0:T(8,128)(2,1)S(1)}, bf16[144,768]{1,0:T(8,128)(2,1)S(1)}, u32[]{:S(2)}, u32[]{:S(2)}) collective-permute-start(bf16[144,768]{1,0:T(8,128)(2,1)S(1)} %slice_bitcast_fusion.1), channel_id=1, source_target_pairs={{0,4},{1,9},{4,0},{5,13},{8,12},{9,1},{12,8},{13,5},{2,6},{3,11},{... | collective-permute-start | bytes 663560 | tf_op jit(solution)/shard_map/ppermute | solution.py:522
  254.5 10.7 %collective-permute-start.46 = (bf16[4,192,256]{2,1,0:T(8,128)(2,1)S(1)}, bf16[4,192,256]{2,1,0:T(8,128)(2,1)S(1)}, u32[]{:S(2)}, u32[]{:S(2)}) collective-permute-start(bf16[4,192,256]{2,1,0:T(8,128)(2,1)S(1)} %fusion.3), channel_id=1, source_target_pairs={{0,2},{1,5},{2,0},{3,7},{4,6},{5,1},{6,4},{7,3},{8,10},{9,13},{10,... | collective-permute-start | bytes 1179656 | tf_op jit(solution)/shard_map/ppermute | solution.py:522
  257.3 8.1 %collective-permute-start.51 = (bf16[2,96,768]{2,1,0:T(8,128)(2,1)S(1)}, bf16[2,96,768]{2,1,0:T(8,128)(2,1)S(1)}, u32[]{:S(2)}, u32[]{:S(2)}) collective-permute-start(bf16[2,96,768]{2,1,0:T(8,128)(2,1)S(1)} %slice.326), channel_id=1, source_target_pairs={{0,16},{1,3},{2,18},{3,1},{16,0},{17,19},{18,2},{19,17},{4,20},{5,... | collective-permute-start | bytes 884744 | tf_op jit(solution)/shard_map/ppermute | solution.py:522
  258.0 14.5 %collective-permute-start.50 = (bf16[2,96,576]{2,1,0:T(8,128)(2,1)S(1)}, bf16[2,96,576]{2,1,0:T(8,128)(2,1)S(1)}, u32[]{:S(2)}, u32[]{:S(2)}) collective-permute-start(bf16[2,96,576]{2,1,0:T(8,128)(2,1)S(1)} %slice.387), channel_id=1, source_target_pairs={{0,8},{8,0},{1,9},{9,1},{2,10},{10,2},{3,11},{11,3},{4,12},{12,4},... | collective-permute-start | bytes 663560 | tf_op jit(solution)/shard_map/ppermute | solution.py:512
  272.5 8.4 %collective-permute-start.53 = (bf16[96,576]{1,0:T(8,128)(2,1)S(1)}, bf16[96,576]{1,0:T(8,128)(2,1)S(1)}, u32[]{:S(2)}, u32[]{:S(2)}) collective-permute-start(bf16[96,576]{1,0:T(8,128)(2,1)S(1)} %fusion.7), channel_id=1, source_target_pairs={{0,4},{4,0},{1,5},{5,1},{2,6},{6,2},{3,7},{7,3},{8,12},{12,8},{9,1... | collective-permute-start | bytes 331784 | tf_op jit(solution)/shard_map/ppermute | solution.py:512
  272.6 7.4 %collective-permute-start.49 = (bf16[2,192,256]{2,1,0:T(8,128)(2,1)S(1)}, bf16[2,192,256]{2,1,0:T(8,128)(2,1)S(1)}, u32[]{:S(2)}, u32[]{:S(2)}) collective-permute-start(bf16[2,192,256]{2,1,0:T(8,128)(2,1)S(1)} %slice.322), channel_id=1, source_target_pairs={{0,8},{1,5},{4,12},{5,1},{8,0},{9,13},{12,4},{13,9},{2,10},{3,7},{... | collective-permute-start | bytes 589832 | tf_op jit(solution)/shard_map/ppermute | solution.py:522
  275.0 7.5 %collective-permute-start.57 = (bf16[96,768]{1,0:T(8,128)(2,1)S(1)}, bf16[96,768]{1,0:T(8,128)(2,1)S(1)}, u32[]{:S(2)}, u32[]{:S(2)}) collective-permute-start(bf16[96,768]{1,0:T(8,128)(2,1)S(1)} %slice_bitcast_fusion.4), channel_id=1, source_target_pairs={{0,2},{1,17},{2,0},{3,19},{16,18},{17,1},{18,16},{19,3},{4,6},{5,2... | collective-permute-start | bytes 442376 | tf_op jit(solution)/shard_map/ppermute | solution.py:522
  283.1 7.8 %collective-permute-start.52 = (bf16[2,192,256]{2,1,0:T(8,128)(2,1)S(1)}, bf16[2,192,256]{2,1,0:T(8,128)(2,1)S(1)}, u32[]{:S(2)}, u32[]{:S(2)}) collective-permute-start(bf16[2,192,256]{2,1,0:T(8,128)(2,1)S(1)} %pad_maximum_fusion.18), channel_id=1, source_target_pairs={{0,4},{1,9},{4,0},{5,13},{8,12},{9,1},{12,8},{13,5},{2,6},{3,11},{... | collective-permute-start | bytes 589832 | tf_op jit(solution)/shard_map/ppermute | solution.py:522
  285.2 7.9 %collective-permute-start.55 = (bf16[96,576]{1,0:T(8,128)(2,1)S(1)}, bf16[96,576]{1,0:T(8,128)(2,1)S(1)}, u32[]{:S(2)}, u32[]{:S(2)}) collective-permute-start(bf16[96,576]{1,0:T(8,128)(2,1)S(1)} %fusion.5), channel_id=1, source_target_pairs={{0,16},{16,0},{1,17},{17,1},{2,18},{18,2},{3,19},{19,3},{4,20},{20... | collective-permute-start | bytes 331784 | tf_op jit(solution)/shard_map/ppermute | solution.py:512
  (47 other events, 288.5 us)

commit v6 on v5

--- a/solution.py
+++ b/solution.py
@@ -74,7 +74,7 @@
 BKB=512
 def attend_back_kernel(q_ref, ko_ref, vo_ref, kx_ref, vx_ref, bias_ref, oa_ref, ob_ref, lsea_ref, lseb_ref, g0,g1,g2,g3, cos_ref, sin_ref,
                        dq_ref, own_ref, give_ref, kaug, vtm, kall, acc):
-    qb=pl.program_id(0)
+    qb=pl.program_id(1)
     span=ko_ref.shape[1]; n=q_ref.shape[1]
     @pl.when(qb==0)
     def _():
@@ -111,17 +111,17 @@
         own_ref[...]=acc[:span,:]
         give_ref[...]=acc[span:,:].astype(bf16)
 
-def attend_back(head,q,kv,kvx,bias,os,lses,grads,cos,sin):
+def attend_back(first,count,q,kv,kvx,bias,os,lses,grads,cos,sin):
     width,n4=q.shape; heads=width//HD; n=n4//4*QB; span=kv.shape[1]
-    kspec=pl.BlockSpec((HD,span),lambda b:(head,0)); vspec=pl.BlockSpec((HD,span),lambda b:(heads+head,0))
-    gspec=lambda i:pl.BlockSpec((None,HD,n4//4),lambda b:(i,head,0)); hb=pl.BlockSpec((HD,n),lambda b:(head,b)); tb=pl.BlockSpec((HD,n),lambda b:(0,b))
-    dspec=pl.BlockSpec((span,2*HD),lambda b:(0,0)); ospec=pl.BlockSpec((HD,n),lambda b:(head,0)); lspec=pl.BlockSpec((1,1,n),lambda b:(head,0,0))
-    return pl.pallas_call(attend_back_kernel,grid=(4//QB,),
-        in_specs=[hb,kspec,vspec,kspec,vspec,pl.BlockSpec((HD,2*span),lambda b:(0,0)),ospec,ospec,lspec,lspec,gspec(0),gspec(0),gspec(0),gspec(1),tb,tb],
-        out_specs=[tb,dspec,dspec],
-        out_shape=[jax.ShapeDtypeStruct((HD,n4),bf16),jax.ShapeDtypeStruct((span,2*HD),f32),jax.ShapeDtypeStruct((span,2*HD),bf16)],
+    kspec=pl.BlockSpec((HD,span),lambda h,b:(first+h,0)); vspec=pl.BlockSpec((HD,span),lambda h,b:(heads+first+h,0))
+    gspec=lambda i:pl.BlockSpec((None,HD,n4//4),lambda h,b:(i,first+h,0)); tb=pl.BlockSpec((HD,n),lambda h,b:(0,b))
+    dspec=pl.BlockSpec((None,span,2*HD),lambda h,b:(h,0,0)); ospec=pl.BlockSpec((HD,n),lambda h,b:(first+h,0)); lspec=pl.BlockSpec((1,1,n),lambda h,b:(first+h,0,0))
+    return pl.pallas_call(attend_back_kernel,grid=(count,4//QB),
+        in_specs=[pl.BlockSpec((HD,n),lambda h,b:(first+h,b)),kspec,vspec,kspec,vspec,pl.BlockSpec((HD,2*span),lambda h,b:(0,0)),ospec,ospec,lspec,lspec,gspec(0),gspec(0),gspec(0),gspec(1),tb,tb],
+        out_specs=[pl.BlockSpec((HD,n),lambda h,b:(h,b)),dspec,dspec],
+        out_shape=[jax.ShapeDtypeStruct((count*HD,n4),bf16),jax.ShapeDtypeStruct((count,span,2*HD),f32),jax.ShapeDtypeStruct((count,span,2*HD),bf16)],
         scratch_shapes=[pltpu.VMEM((2*span,2*HD),bf16),pltpu.VMEM((2*span,2*HD),bf16),pltpu.VMEM((HD,2*span),bf16),pltpu.VMEM((2*span,2*HD),f32)],
-        cost_estimate=pl.CostEstimate(flops=int(6.0*(10*n4*2*span*256))+1,bytes_accessed=int(6.0*(4*n4*2*span))+1,transcendentals=int(6.0*(n4*2*span))+1),
+        cost_estimate=pl.CostEstimate(flops=int(6.0*(count*10*n4*2*span*256))+1,bytes_accessed=int(6.0*(count*4*n4*2*span))+1,transcendentals=int(6.0*(count*n4*2*span))+1),
         name="attend_back")(q,kv,kv,kvx,kvx,bias,*os,*lses,grads[0],grads[2],grads[1],grads[2],cos,sin)
 def xor(a,b):
     return lax.bitwise_xor(jnp.asarray(a,jnp.int32),jnp.asarray(b,jnp.int32))
@@ -185,12 +185,12 @@
         name="qkv")(info,*xs,mine,theirs,cos,sin)
 
 def finish_dx_kernel(info, *refs):
-    (q0,q1,q2,o0,o1,o2,r0,r1,r2,mine_ref,theirs_ref,cos_ref,sin_ref,keep_ref,send_ref,p_ref,w_s)=refs
-    hw=3*HD; n=keep_ref.shape[3]; feat=keep_ref.shape[2]; c=info[3]
+    (q_ref,own_ref,got_ref,mine_ref,theirs_ref,cos_ref,sin_ref,keep_ref,send_ref,p_ref,w_s)=refs
+    hw=q_ref.shape[0]; n=keep_ref.shape[3]; feat=keep_ref.shape[2]; c=info[3]
     place_qkv_weights(info,mine_ref,theirs_ref,w_s)
-    for h,(qr,orr,rr) in enumerate(((q0,o0,r0),(q1,o1,r1),(q2,o2,r2))):
-        p_ref[h*HD:(h+1)*HD,:]=qr[...]
-        t=(orr[...]+rr[...].astype(f32)).T
+    p_ref[0:hw,:]=q_ref[...]
+    for h in range(hw//HD):
+        t=(own_ref[h]+got_ref[h].astype(f32)).T
         p_ref[hw+h*HD:hw+(h+1)*HD,:]=pair_turn(t[:HD]*LN2,cos_ref[...],-sin_ref[...]).astype(bf16)
         p_ref[2*hw+h*HD:2*hw+(h+1)*HD,:]=t[HD:].astype(bf16)
     for k,dr in ((3,send_ref),(2,send_ref),(1,keep_ref),(0,keep_ref)):
@@ -199,14 +199,14 @@
         for r in range(4):
             dr[k%2,row_step(c,xor(r,base))]=mm(w_s[r*feat:(r+1)*feat,:],p_ref[:,sl]).astype(dr.dtype)
 
-def finish_dx(info,dqs,owns,gots,mine,theirs,cos,sin):
-    w3=mine.shape[2]; half=mine.shape[1]; feat=2*half; width=4*feat; n=dqs[0].shape[1]//4
+def finish_dx(info,dq,own,got,mine,theirs,cos,sin):
+    w3=mine.shape[2]; half=mine.shape[1]; feat=2*half; width=4*feat; n=dq.shape[1]//4
     S=jax.ShapeDtypeStruct
-    return pl.pallas_call(finish_dx_kernel,in_specs=[SM]+[VM]*13,out_specs=[VM]*3,
+    return pl.pallas_call(finish_dx_kernel,in_specs=[SM]+[VM]*7,out_specs=[VM]*3,
         out_shape=[S((2,4,feat,n),f32),S((2,4,feat,n),bf16),S((w3,4*n),bf16)],
         scratch_shapes=[pltpu.VMEM((width,w3),bf16)],
-        cost_estimate=pl.CostEstimate(flops=int(6.0*(8*width*w3*n))+1,bytes_accessed=int(6.0*(8*width*n*4))+1,transcendentals=int(6.0*(0))+1),
-        name="finish_dx")(info,*dqs,*owns,*gots,mine,theirs,cos,sin)
+        cost_estimate=pl.CostEstimate(flops=int(0.0*(8*width*w3*n))+1,bytes_accessed=int(0.0*(8*width*n*4))+1,transcendentals=int(0.0*(0))+1),
+        name="finish_dx")(info,dq,own,got,mine,theirs,cos,sin)
 
 def finish_dw_kernel(info, p_ref, xa,xb,xc, keep_ref, give_ref, x_s, g_s):
     n=xa.shape[2]; half=keep_ref.shape[1]
@@ -425,7 +425,8 @@
         args=(args[0],args[1],args[1])
         def column(ky): return at(lambda i,j,s:(0,xor(s[2],ky)*2+xor(s[3],which)))
         specs=[whole,pl.BlockSpec((n,ffc),column(0)),pl.BlockSpec((n,ffc),column(1))]
-    cost=pl.CostEstimate(flops=int(6.0*((4 if stage=="give" else 2)*width*n*ffc))+1,bytes_accessed=int(6.0*(16*rows*ffc))+1,transcendentals=int(6.0*(0))+1)
+    weight={"give":4,"first":2,"second":0}[stage]
+    cost=pl.CostEstimate(flops=int(6.0*(weight*width*n*ffc))+1,bytes_accessed=int(6.0*(4*weight*rows*ffc))+1,transcendentals=int(6.0*(0))+1)
     name=kind+"_"+stage
     five=(1,1,4,rows,ffc)
     if stage=="give":
@@ -542,13 +543,6 @@
 
 def row_rest(pair, *between):
     return jnp.concatenate([pair, after(crossed(pair, ROW, 0), *between)], axis=0)
-
-
-def plane_gather(stack, forward_after):
-    near = crossed(stack, PLANE, 1)
-    far = crossed(stack, PLANE, 0)
-    both = crossed(after(near, *forward_after), PLANE, 0)
-    return [stack, near, far, both]
 
 
 def core_copies(arrays, ties):
@@ -621,6 +615,7 @@
     cols = tokens.shape[2]
     half = cols // 2
     head_width = w_query.shape[1]
+    heads = head_width // HD
     two = lax.axis_size("dp") == 2
     row = lax.axis_index(ROW)
     group = lax.axis_index("dp")
@@ -648,11 +643,12 @@
 
     this_half, other_half = dp_halves(jnp.concatenate([w_query, w_key, w_value], axis=1), c)
     token_blocks = to_slots(tokens)
-    x_own = jnp.stack(by_slot(scatter_steps(token_blocks[:2], token_blocks[2:], ROW)))
+    token_three = scatter_steps(token_blocks[:2], token_blocks[2:], ROW)
+    x_own = jnp.stack(by_slot(token_three))
     other_columns = core_swap(other_half)
     norms = pack_norms(first_gain, first_shift, second_gain, second_shift)
     if two:
-        block_a = jnp.concatenate([w_inner, pack_output(w_output), norms], axis=0)
+        block_a = jnp.concatenate([after(w_inner, token_blocks), pack_output(w_output), norms], axis=0)
         pair_a = row_pair(block_a)
         block_b = pack_outer(w_outer)
         near_b = crossed(after(block_b, token_blocks), ROW, 1)
@@ -681,6 +677,7 @@
     invalid = jnp.where(positions < length, 0.0, masked_score)
     bias = jnp.where(jnp.arange(HD)[:, None] == 0, invalid[None, :], 0.0).astype(bf16)
     frequency = 10000.0 ** (-2.0 * jnp.arange(HD // 2, dtype=f32) / HD)
+    frequency = after(frequency, token_three[1])
     angles = frequency[:, None] * positions[: 4 * half].astype(f32)[None, :]
     cosine = jnp.repeat(jnp.cos(angles), 2, axis=0)
     sines = jnp.sin(angles)
@@ -689,17 +686,31 @@
     q_rot, kv_own = qkv(info, xs, mine, theirs, cosine, sine)
     kv_other = core_swap(kv_own)
     out_b, log_b, low_b = attend(1, q_rot, kv_own, kv_other, bias)
-    out_a, log_a, low_a = attend(0, after(q_rot, low_b), kv_own, kv_other, bias)
-    attn_three = scatter_steps(low_a, low_b, SQUARE)
-    cot_blocks = after(to_slots(out_grad), kv_own)
-    cot_three = scatter_steps(cot_blocks[:2], cot_blocks[2:], ROW, low_a)
+    low_first = crossed(low_b, SQUARE, 0)
+    cot_blocks = to_slots(after(out_grad, kv_own))
+    cot_first = after(crossed(cot_blocks[2:], ROW, 0), low_b)
+    cot_pass = jnp.stack([cot_blocks[1], cot_first[1]])
+    cot_second = crossed(cot_pass, ROW, 1)
+    cot_three = (cot_blocks[:2], cot_first, cot_second)
+    q_second = after(q_rot, low_b, cot_pass)
     if two:
-        arrays_a = plane_gather(row_a, (kv_own,))
-        chunk_a = core_copies(arrays_a, [(kv_own,), (low_a,), (low_a,), (low_a,)])
+        near_a, far_a = crossed(row_a, PLANE, 1), crossed(row_a, PLANE, 0)
+        both_a = crossed(after(near_a, kv_own), PLANE, 0)
+        row_a_swapped = core_swap(after(row_a, kv_own))
+        far_a = after(far_a, low_b)
+        both_a = after(both_a, low_b)
         pair_b = jnp.stack([block_b, after(near_b, kv_own)])
         row_b = row_rest(pair_b, low_b)
-        arrays_b = plane_gather(row_b, (low_a,))
-        chunk_b = core_copies(arrays_b, [(low_a,), (low_a,), (attn_three[2],), (attn_three[2],)])
+        q_second = after(q_second, row_a_swapped, far_a, row_b)
+        near_b, far_b = crossed(row_b, PLANE, 1), crossed(row_b, PLANE, 0)
+    out_a, log_a, low_a = attend(0, q_second, kv_own, kv_other, bias)
+    low_pass = jnp.stack([low_a[1], after(low_first, low_a)[1]])
+    low_second = crossed(low_pass, SQUARE, 1)
+    attn_three = (low_a, low_first, low_second)
+    if two:
+        both_b = crossed(after(near_b, low_second, cot_second), PLANE, 0)
+        chunk_a = [row_a, near_a, far_a, both_a, row_a_swapped] + [core_swap(after(part, low_a)) for part in (near_a, far_a, both_a)]
+        chunk_b = core_copies([row_b, near_b, far_b, both_b], [(low_a,), (low_pass,), (low_pass,), (low_pass,)])
     else:
         chunk_a, chunk_b = gather_generic(w_output, w_inner, w_outer, norms, row, y, c)
     mixed_keep, mixed_send, e_keep, e_send, grad_one, attn_t, hidden_t, outer_t, branch_low, act_low, inner_low, norm_sums = middle(
@@ -711,9 +722,9 @@
     def tied(args, *earlier):
         return (after(args[0], *earlier),) + args[1:]
 
-    def head_back(head, *earlier):
+    def head_back(first, count, *earlier):
         return attend_back(
-            head, after(q_rot, *earlier), kv_own, kv_other, bias, (out_a, out_b), (log_a, log_b), grads, cosine, sine
+            first, count, after(q_rot, *earlier), kv_own, kv_other, bias, (out_a, out_b), (log_a, log_b), grads, cosine, sine
         )
 
     give_outer = grad_call("outer", "give", info, outer_args)
@@ -723,65 +734,66 @@
     grads = (e_keep, grads_first, crossed(grads_pass, SQUARE, 1))
     give_inner = grad_call("inner", "give", info, tied(inner_args, give_outer, grads_pass))
     got_inner = core_swap(give_inner)
-    first_outer = grad_call("outer", "first", info, tied(outer_args, give_inner, grads[2]), got_outer)
+    mixed_first = after(crossed(mixed_send, ROW, 0), give_inner)
+    mixed_pass = jnp.stack([mixed_keep[1], mixed_first[1]])
+    first_outer = grad_call("outer", "first", info, tied(outer_args, mixed_pass, grads[2]), got_outer)
     came_outer = crossed(first_outer, ROW, 0)
     first_inner = grad_call("inner", "first", info, tied(inner_args, first_outer), got_inner)
     came_inner = crossed(first_inner, PLANE, 0) if two else jnp.zeros_like(first_inner)
-    dq0, own0, send0 = head_back(0, first_inner)
-    dq1, own1, send1 = head_back(1, dq0)
+    mixed_second = crossed(mixed_pass, ROW, 1)
+    dq, own, send = head_back(0, heads, first_inner, mixed_second)
+    came_outer = after(came_outer, dq)
+    own = after(own, came_outer)
+    dkv_got = core_swap(send)
+    dx_keep, dx_send, proj = finish_dx(info, dq, own, dkv_got, mine, theirs, cosine, sine)
+    dx_first = crossed(dx_send, SQUARE, 0)
     keep_outer, pass_outer = grad_call(
-        "outer", "second", info, tied(outer_args, dq1), got_outer, after(came_outer, dq1)
+        "outer", "second", info, tied(outer_args, dx_keep), got_outer, after(came_outer, dx_keep)
     )
     keep_inner, pass_inner = grad_call(
         "inner", "second", info, tied(inner_args, keep_outer), got_inner, after(came_inner, keep_outer)
     )
-    dq2, own2, send2 = head_back(2, keep_inner)
-    if two:
-        plane_inner = add_parts([keep_inner, after(crossed(pass_inner, PLANE, 1), dq2)]).astype(bf16)
-        pass_on_inner = crossed(plane_inner[2:], ROW, 0)
-        own2 = after(own2, plane_inner)
-    gots = [core_swap(send) for send in (send0, send1, send2)]
-    dx_keep, dx_send, proj = finish_dx(info, (dq0, dq1, dq2), (own0, own1, own2), gots, mine, theirs, cosine, sine)
-    dx_first = crossed(dx_send, SQUARE, 0)
-    if two:
-        pair_inner = (plane_inner[:2].astype(f32) + after(pass_on_inner, dx_keep).astype(f32)).astype(bf16)
-        last_inner = crossed(pair_inner[1], ROW, 1)
-        proj = after(proj, pair_inner)
-    keep, give = finish_dw(info, after(proj, dx_keep), xs)
-    got = core_swap(give)
-    dx_first = after(dx_first, give)
+    dx_first = after(dx_first, keep_inner)
     dx_pass = (dx_keep[1] + dx_first[1].astype(f32)).astype(bf16)
     dx_second = crossed(dx_pass, SQUARE, 1)
-    row_outer = add_parts([keep_outer, after(crossed(pass_outer, ROW, 1), dx_pass)]).astype(bf16)
+    keep, give = finish_dw(info, after(proj, dx_pass), xs)
+    got = core_swap(give)
+    dx_second = after(dx_second, give)
+    d_x = add_parts([grad_one, dx_keep[0], dx_first[0], dx_second]).astype(bf16)
+    d_x_first = crossed(d_x[2:], ROW, 0)
+    by_row_step = keep + after(got, d_x).astype(f32)
+    passed_m = swap2(by_row_step[2:].astype(bf16), "rm")
+    if two:
+        plane_inner = add_parts([keep_inner, after(crossed(pass_inner, PLANE, 1), by_row_step)]).astype(bf16)
+        pass_on_inner = crossed(plane_inner[2:], ROW, 0)
+    row_outer = add_parts([keep_outer, after(crossed(pass_outer, ROW, 1), by_row_step)]).astype(bf16)
     if two:
         pass_on_outer = crossed(row_outer[2:], PLANE, 0)
-    by_row_step = keep + after(got, row_outer).astype(f32)
-    passed_m = swap2(by_row_step[2:].astype(bf16), "rm")
-    dx_second = after(dx_second, by_row_step)
-    d_x = add_parts([grad_one, dx_keep[0], dx_first[0], dx_second]).astype(bf16)
-    d_x_first = crossed(d_x[2:], ROW, 0)
-    if two:
-        pair_outer = (row_outer[:2].astype(f32) + after(pass_on_outer, d_x).astype(f32)).astype(bf16)
-        last_outer = crossed(pair_outer[1], PLANE, 1)
-        passed_m = after(passed_m, pair_outer)
-    near_far = by_row_step[:2] + passed_m.astype(f32)
+        d_x_first = after(d_x_first, plane_inner, row_outer)
+    d_x_pass = jnp.stack([d_x[1], d_x_first[1]])
+    d_x_second = crossed(d_x_pass, ROW, 1)
+    near_far = by_row_step[:2] + after(passed_m, d_x_pass).astype(f32)
     near_sum = near_far[0]
     far_low = swap2(near_far[1].astype(bf16), "rz")
-    d_x_first = after(d_x_first, near_far)
-    d_x_second = crossed(jnp.stack([d_x[1], d_x_first[1]]), ROW, 1)
-    far_sum = after(far_low, d_x_first).astype(f32)
+    if two:
+        pair_inner = (plane_inner[:2].astype(f32) + after(pass_on_inner, near_far).astype(f32)).astype(bf16)
+        last_inner = crossed(pair_inner[1], ROW, 1)
+        pair_outer = (row_outer[:2].astype(f32) + after(pass_on_outer, near_far).astype(f32)).astype(bf16)
+        last_outer = crossed(pair_outer[1], PLANE, 1)
+        far_low = after(far_low, pair_inner, pair_outer)
+    far_sum = far_low.astype(f32)
+    kept = jnp.where(z == c, near_sum, far_sum)
+    passed = core_swap(jnp.where(z == c, far_sum, near_sum).astype(bf16)).astype(f32)
+    d_x_second = after(d_x_second, kept)
     d_input = from_slots(by_slot((d_x[:2], d_x_first, d_x_second))).astype(f32)
+    g_qkv = dp_sum(kept, passed, c)
     if two:
-        inner_sums = [pair_inner[0].astype(f32) + after(last_inner, far_sum).astype(f32)]
-        outer_sums = [pair_outer[0].astype(f32) + after(last_outer, far_sum).astype(f32)]
+        inner_sums = [pair_inner[0].astype(f32) + after(last_inner, passed).astype(f32)]
+        outer_sums = [pair_outer[0].astype(f32) + after(last_outer, passed).astype(f32)]
     else:
         outer_sums = generic_outer(row_outer, c)
         inner_sums = generic_inner(first_inner, keep_inner, pass_inner, c)
-    mixed_three = scatter_steps(after(mixed_keep, give_outer), after(mixed_send, give_outer), ROW, dq0)
-    mixed_out = from_slots(by_slot([after(part, give) for part in mixed_three]))
-    kept = jnp.where(z == c, near_sum, far_sum)
-    passed = core_swap(jnp.where(z == c, far_sum, near_sum).astype(bf16)).astype(f32)
-    g_qkv = dp_sum(kept, passed, c)
+    mixed_out = from_slots(by_slot((mixed_keep, mixed_first, mixed_second)))
 
     half_rows = feat // 2
     third = half_rows // 3

time: 295 us -> 282 us (0.956)
  waiting for transfers between devices: 95.3 us -> 85.2 us
  Pallas kernels: 100 us -> 95.9 us
    ppermute x36, waiting for transfers between devices: 81.3 us -> 71.1 us  [crossed(): return lax.ppermute(value, axes + ('cc',), pairs)]
    ppermute x18 -> x16, starting transfers between devices: 5.07 us -> 14 us  [core_swap(): return lax.ppermute(value, 'cc', [(0, 1), (1, 0)])]
    ppermute x36, starting transfers between devices: 50.4 us -> 45.1 us  [crossed(): return lax.ppermute(value, axes + ('cc',), pairs)]
    pallas_call x4 -> x2, Pallas kernels: 29.7 us -> 25.3 us  [the longest x1 20.2 us: attend_back(): pl.pallas_call(attend_back_kernel, grid=(count, 4 // QB), in_specs=[pl.Bl...]
    ppermute x4, starting transfers between devices: 6.36 us -> 3.15 us  [swap2(): return lax.ppermute(value, axis, [(0, 1), (1, 0)])]
    ppermute x18 -> x16, waiting for transfers between devices: 6.1 us -> 4.8 us  [core_swap(): return lax.ppermute(value, 'cc', [(0, 1), (1, 0)])]
    unnamed x76 -> x86, local copies, waits for them, and re-layouts: 6.82 us -> 5.74 us
  transfers between devices with their start and end apart: 58 -> 56, of which waited for: 22 -> 23; matrix products, arithmetic and copies ran while one was open for 8% -> 9% of each run, Pallas kernels for 25% -> 25%
where the time goes in v6:
time: 282 us; the launch traced here: 281 us
  Pallas kernels  95.9 us (34%)
  waiting for transfers between devices  85.2 us (30%)
  starting transfers between devices  62.2 us (22%)
  local copies, waits for them, and re-layouts  21 us (7%)
  other arithmetic  14 us (5%)
    ppermute x36, waiting for transfers between devices, crossed(): return lax.ppermute(value, axes + ('cc',), pairs)  71.1 us
    ppermute x36, starting transfers between devices, crossed(): return lax.ppermute(value, axes + ('cc',), pairs)  45.1 us
    pallas_call x1, Pallas kernels, middle(): pl.pallas_call(middle_kernel, in_specs=[SM] + [VM] * 7 + [HB] * 16, out_s...  21.5 us
    pallas_call x1, Pallas kernels, attend_back(): pl.pallas_call(attend_back_kernel, grid=(count, 4 // QB), in_specs=[pl.Bl...  20.2 us
    ppermute x16, starting transfers between devices, core_swap(): return lax.ppermute(value, 'cc', [(0, 1), (1, 0)])  14 us
    pallas_call x2, Pallas kernels, attend(): pl.pallas_call(attend_kernel, grid=(heads,), in_specs=[pl.BlockSpec((HD,...  13.3 us
    pallas_call x2, Pallas kernels, grad_call(): pl.pallas_call(functools.partial(give_kernel, blocks), grid_spec=pltpu.Pr...  10.3 us
    ppermute x4, waiting for transfers between devices, swap2(): return lax.ppermute(value, axis, [(0, 1), (1, 0)])  9.32 us
  transfers between devices with their start and end apart: 56, of which 23 were waited for; matrix products, arithmetic and copies ran while one was open for 9% of the time, Pallas kernels for 25%

profile of v6, /device:TPU:0, one launch (start us, length us, event | category | flops | bytes accessed | tf_op | source)
XLA Modules:
  0.0 280.7 jit_solution(11339817031686829352)
XLA Ops:
  1.6 3.0 %collective-permute-start.6 = (bf16[96,576]{1,0:T(8,128)(2,1)S(1)}, bf16[96,576]{1,0:T(8,128)(2,1)S(1)}, u32[]{:S(2)}, u32[]{:S(2)}) collective-permute-start(bf16[96,576]{1,0:T(8,128)(2,1)S(1)} %pad_maximum_fusion.20), channel_id=1, source_target_pairs={{0,16},{16,0},{1,17},{17,1},{2,18},{18,2},{3,19},{19,3},{4,20},{20... | collective-permute-start | bytes 331784 | tf_op jit(solution)/shard_map/ppermute | solution.py:513
  7.5 1.6 collective-permute-start.15
  9.2 2.7 collective-permute-start
  16.4 5.5 %collective-permute-done = bf16[2,192,256]{2,1,0:T(8,128)(2,1)S(1)} collective-permute-done((bf16[2,192,256]{2,1,0:T(8,128)(2,1)S(1)}, bf16[2,192,256]{2,1,0:T(8,128)(2,1)S(1)}, u32[]{:S(2)}, u32[]{:S(2)}) %collective-permute-start) | collective-permute-done | bytes 196640 | tf_op jit(solution)/shard_map/ppermute | solution.py:523
  22.3 3.4 %collective-permute-start.8 = (bf16[2,96,576]{2,1,0:T(8,128)(2,1)S(1)}, bf16[2,96,576]{2,1,0:T(8,128)(2,1)S(1)}, u32[]{:S(2)}, u32[]{:S(2)}) collective-permute-start(bf16[2,96,576]{2,1,0:T(8,128)(2,1)S(1)} %pad_maximum_fusion.10), channel_id=1, source_target_pairs={{0,8},{1,5},{4,12},{5,1},{8,0},{9,13},{12,4},{13,9},{2,10},{3,7},{... | collective-permute-start | bytes 663560 | tf_op jit(solution)/shard_map/ppermute | solution.py:523
  26.0 11.8 %collective-permute-done.1 = bf16[2,192,256]{2,1,0:T(8,128)(2,1)S(1)} collective-permute-done((bf16[2,192,256]{2,1,0:T(8,128)(2,1)S(1)}, bf16[2,192,256]{2,1,0:T(8,128)(2,1)S(1)}, u32[]{:S(2)}, u32[]{:S(2)}) %collective-permute-start.1) | collective-permute-done | bytes 196640 | tf_op jit(solution)/shard_map/ppermute | solution.py:523
  37.9 1.6 collective-permute-start.4
  39.7 2.5 collective-permute-done.3
  42.3 1.6 collective-permute-start.20
  43.9 1.9 collective-permute-done.4.xb
  45.9 2.0 collective-permute-start.5
  49.4 6.1 %collective-permute-start.10 = (bf16[4,96,576]{2,1,0:T(8,128)(2,1)S(1)}, bf16[4,96,576]{2,1,0:T(8,128)(2,1)S(1)}, u32[]{:S(2)}, u32[]{:S(2)}) collective-permute-start(bf16[4,96,576]{2,1,0:T(8,128)(2,1)S(1)} %pad_maximum_fusion.3.mine_ref.refs_3_), channel_id=1, source_target_pairs={{0,1},{1,0},{2,3},{3,2},{4,5},{5,4},{6,7},{7,6},{8,9},{9,8},{10,11... | collective-permute-start | bytes 1327112 | tf_op jit(solution)/shard_map/ppermute | solution.py:447
  60.2 4.0 %qkv.1 = (bf16[192,1024]{1,0:T(8,128)(2,1)}, bf16[384,1024]{1,0:T(8,128)(2,1)}) custom-call(s32[8]{0:T(128)} %stack.141.info, bf16[4,192,256]{2,1,0:T(8,128)(2,1)} %copy-done.2, bf16[4,192,256]{2,1,0:T(8,128)(2,1)} %copy-done.5, bf16[2,4,192,256]{3,2,1,0:T(8,128)(2,1)} %collective-permute-done.5.xc, bf16[4,96,576]{2,1,0:T(8,128)(2,1)} %copy-done.1, ...), custom_call_target="tpu_custom_call" | custom-call | tf_op jit(solution)/shard_map/qkv/pallas_call | solution.py:182
  64.2 5.2 %collective-permute-start.11 = (bf16[384,1024]{1,0:T(8,128)(2,1)}, bf16[384,1024]{1,0:T(8,128)(2,1)}, u32[]{:S(2)}, u32[]{:S(2)}) collective-permute-start(bf16[384,1024]{1,0:T(8,128)(2,1)} %get-tuple-element.99.ko_ref.vo_ref), channel_id=1, source_target_pairs={{0,1},{1,0},{2,3},{3,2},{4,5},{5,4},{6,7},{7,6},{8,9},{9,8},{10,11... | collective-permute-start | bytes 2359304 | tf_op jit(solution)/shard_map/ppermute | solution.py:447
  69.4 2.2 collective-permute-start.16
  74.1 6.7 %attend.2 = (f32[192,512]{1,0:T(8,128)}, f32[3,1,512]{2,1,0:T(1,128)}, bf16[2,192,256]{2,1,0:T(8,128)(2,1)}) custom-call(bf16[192,1024]{1,0:T(8,128)(2,1)} %get-tuple-element.139.q_ref, bf16[384,1024]{1,0:T(8,128)(2,1)} %get-tuple-element.99.ko_ref.vo_ref, bf16[384,1024]{1,0:T(8,128)(2,1)} %get-tuple-element.99.ko_ref.vo_ref, ...), custom_call_target="tpu_custom_call" | custom-call | flops 19327352832 | bytes 25165824 | tf_op jit(solution)/shard_map/attend/pallas_call | solution.py:66
  80.7 1.9 collective-permute-done.12.c1
  82.7 3.5 %collective-permute-start.19 = (bf16[2,192,256]{2,1,0:T(8,128)(2,1)S(1)}, bf16[2,192,256]{2,1,0:T(8,128)(2,1)S(1)}, u32[]{:S(2)}, u32[]{:S(2)}) collective-permute-start(bf16[2,192,256]{2,1,0:T(8,128)(2,1)S(1)} %pad_maximum_fusion.14), channel_id=1, source_target_pairs={{0,4},{1,9},{4,0},{5,13},{8,12},{9,1},{12,8},{13,5},{2,6},{3,11},{... | collective-permute-start | bytes 589832 | tf_op jit(solution)/shard_map/ppermute | solution.py:523
  87.0 1.5 collective-permute-start.25
  88.5 6.6 %attend.3 = (f32[192,512]{1,0:T(8,128)}, f32[3,1,512]{2,1,0:T(1,128)}, bf16[2,192,256]{2,1,0:T(8,128)(2,1)}) custom-call(bf16[192,1024]{1,0:T(8,128)(2,1)} %get-tuple-element.139.q_ref, bf16[384,1024]{1,0:T(8,128)(2,1)} %get-tuple-element.99.ko_ref.vo_ref, bf16[384,1024]{1,0:T(8,128)(2,1)} %get-tuple-element.99.ko_ref.vo_ref, ...), custom_call_target="tpu_custom_call" | custom-call | flops 19327352832 | bytes 25165824 | tf_op jit(solution)/shard_map/attend/pallas_call | solution.py:66
  96.8 8.5 %collective-permute-done.18.a2 = bf16[2,192,256]{2,1,0:T(8,128)(2,1)S(1)} collective-permute-done((bf16[2,192,256]{2,1,0:T(8,128)(2,1)S(1)}, bf16[2,192,256]{2,1,0:T(8,128)(2,1)S(1)}, u32[]{:S(2)}, u32[]{:S(2)}) %collective-permute-start.18) | collective-permute-done | bytes 196640 | tf_op jit(solution)/shard_map/ppermute | solution.py:523
  106.2 9.1 %collective-permute-done.27.refs_11_ = bf16[4,96,768]{2,1,0:T(8,128)(2,1)S(1)} collective-permute-done((bf16[4,96,768]{2,1,0:T(8,128)(2,1)S(1)}, bf16[4,96,768]{2,1,0:T(8,128)(2,1)S(1)}, u32[]{:S(2)}, u32[]{:S(2)}) %collective-permute-start.27) | collective-permute-done | bytes 589856 | tf_op jit(solution)/shard_map/ppermute | solution.py:523
  117.3 1.9 collective-permute-done.30.refs_14_
  120.2 21.5 %middle.1 = (bf16[2,192,256]{2,1,0:T(8,128)(2,1)}, bf16[2,192,256]{2,1,0:T(8,128)(2,1)}, bf16[2,192,256]{2,1,0:T(8,128)(2,1)}, bf16[2,192,256]{2,1,0:T(8,128)(2,...) custom-call(s32[8]{0:T(128)} %stack.141.info, ...), custom_call_target="tpu_custom_call" | custom-call | flops 86973087744 | bytes 339738624 | tf_op jit(solution)/shard_map/middle/pallas_call | solution.py:347
  144.0 4.7 %outer_give.1 = bf16[2,2,4,96,768]{4,3,2,1,0:T(8,128)(2,1)} custom-call(s32[8]{0:T(128)} %stack.141.info, bf16[768,256]{1,0:T(8,128)(2,1)} %get-tuple-element.151.refs_0_, bf16[256,3072]{1,0:T(8,128)(2,1)} %get-tuple-element.126.refs_1_.refs_2_, bf16[256,3072]{1,0:T(8,128)(2,1)} %get-tuple-element.126.refs_1_.refs_2_), custom_call_target="tpu_custom_call" | custom-call | flops 3623878656 | bytes 7077889 | tf_op jit(solution)/shard_map/outer_give/pallas_call | solution.py:433
  149.5 5.6 %inner_give.1 = bf16[2,2,4,144,768]{4,3,2,1,0:T(8,128)(2,1)} custom-call(s32[8]{0:T(128)} %stack.141.info, bf16[768,256]{1,0:T(8,128)(2,1)} %get-tuple-element.154.refs_0_, bf16[256,3072]{1,0:T(8,128)(2,1)} %get-tuple-element.131.refs_1_, bf16[768,256]{1,0:T(8,128)(2,1)} %get-tuple-element.132.refs_2_, bf16[4,256,256]{2,1,0:T(8,128)(2,1)} %get-tuple-element.133.refs_3_, ...), custom_call_target="tpu_custom_call" | custom-call | flops 3623878656 | bytes 10616833 | tf_op jit(solution)/shard_map/inner_give/pallas_call | solution.py:433
  157.2 1.6 fusion.24
  158.8 1.9 collective-permute-start.35
  160.7 3.5 %collective-permute-done.32 = bf16[2,192,256]{2,1,0:T(8,128)(2,1)S(1)} collective-permute-done((bf16[2,192,256]{2,1,0:T(8,128)(2,1)}, bf16[2,192,256]{2,1,0:T(8,128)(2,1)S(1)}, u32[]{:S(2)}, u32[]{:S(2)}) %collective-permute-start.32) | collective-permute-done | bytes 196640 | tf_op jit(solution)/shard_map/ppermute | solution.py:523
  166.8 3.6 %outer_first.1 = bf16[2,4,96,768]{3,2,1,0:T(8,128)(2,1)} custom-call(s32[8]{0:T(128)} %stack.141.info, bf16[768,256]{1,0:T(8,128)(2,1)} %get-tuple-element.151.refs_0_, bf16[256,3072]{1,0:T(8,128)(2,1)} %get-tuple-element.126.refs_1_.refs_2_, bf16[256,3072]{1,0:T(8,128)(2,1)} %get-tuple-element.126.refs_1_.refs_2_, ...), custom_call_target="tpu_custom_call" | custom-call | flops 1811939328 | bytes 3538945 | tf_op jit(solution)/shard_map/outer_first/pallas_call | solution.py:438
  170.4 2.0 collective-permute-start.38
  172.4 1.8 copy-done
  174.2 4.2 %inner_first.1 = bf16[2,4,144,768]{3,2,1,0:T(8,128)(2,1)} custom-call(s32[8]{0:T(128)} %stack.141.info, bf16[768,256]{1,0:T(8,128)(2,1)} %get-tuple-element.154.refs_0_, bf16[256,3072]{1,0:T(8,128)(2,1)} %get-tuple-element.131.refs_1_, bf16[768,256]{1,0:T(8,128)(2,1)} %get-tuple-element.132.refs_2_, bf16[4,256,256]{2,1,0:T(8,128)(2,1)} %get-tuple-element.133.refs_3_, ...), custom_call_target="tpu_custom_call" | custom-call | flops 1811939328 | bytes 5308417 | tf_op jit(solution)/shard_map/inner_first/pallas_call | solution.py:438
  178.4 20.2 %attend_back.1 = (bf16[192,1024]{1,0:T(8,128)(2,1)}, f32[3,1024,128]{2,1,0:T(8,128)}, bf16[3,1024,128]{2,1,0:T(8,128)(2,1)}) custom-call(bf16[192,1024]{1,0:T(8,128)(2,1)} %get-tuple-element.139.q_ref, bf16[384,1024]{1,0:T(8,128)(2,1)} %get-tuple-element.99.ko_ref.vo_ref, bf16[384,1024]{1,0:T(8,128)(2,1)} %get-tuple-element.99.ko_ref.vo_ref, ...), custom_call_target="tpu_custom_call" | custom-call | flops 96636764160 | bytes 150994944 | tf_op jit(solution)/shard_map/attend_back/pallas_call | solution.py:119
  198.6 1.9 collective-permute-done.38.refs_4_
  202.0 5.1 %finish_dx.1 = (f32[2,4,192,256]{3,2,1,0:T(8,128)}, bf16[2,4,192,256]{3,2,1,0:T(8,128)(2,1)}, bf16[576,1024]{1,0:T(8,128)(2,1)}) custom-call(s32[8]{0:T(128)} %stack.141.info, bf16[192,1024]{1,0:T(8,128)(2,1)} %get-tuple-element.144.refs_0_, f32[3,1024,128]{2,1,0:T(8,128)} %get-tuple-element.147.refs_1_, bf16[3,1024,128]{2,1,0:T(8,128)(2,1)} %copy-done.11, ...), custom_call_target="tpu_custom_call" | custom-call | flops 1 | bytes 1 | tf_op jit(solution)/shard_map/finish_dx/pallas_call | solution.py:205
  210.2 4.1 %outer_second.1 = (bf16[4,96,768]{2,1,0:T(8,128)(2,1)}, bf16[4,96,768]{2,1,0:T(8,128)(2,1)}) custom-call(s32[8]{0:T(128)} %stack.141.info, bf16[768,256]{1,0:T(8,128)(2,1)} %get-tuple-element.151.refs_0_, bf16[256,3072]{1,0:T(8,128)(2,1)} %get-tuple-element.126.refs_1_.refs_2_, bf16[256,3072]{1,0:T(8,128)(2,1)} %get-tuple-element.126.refs_1_.refs_2_, ...), custom_call_target="tpu_custom_call" | custom-call | flops 1 | bytes 1 | tf_op jit(solution)/shard_map/outer_second/pallas_call | solution.py:442
  216.4 5.1 %inner_second.1 = (bf16[4,144,768]{2,1,0:T(8,128)(2,1)}, bf16[4,144,768]{2,1,0:T(8,128)(2,1)}) custom-call(s32[8]{0:T(128)} %stack.141.info, bf16[768,256]{1,0:T(8,128)(2,1)} %get-tuple-element.154.refs_0_, bf16[256,3072]{1,0:T(8,128)(2,1)} %get-tuple-element.131.refs_1_, bf16[768,256]{1,0:T(8,128)(2,1)} %get-tuple-element.132.refs_2_, ...), custom_call_target="tpu_custom_call" | custom-call | flops 1 | bytes 1 | tf_op jit(solution)/shard_map/inner_second/pallas_call | solution.py:442
  222.6 2.9 %collective-permute-start.42 = (bf16[4,192,256]{2,1,0:T(8,128)(2,1)S(1)}, bf16[4,192,256]{2,1,0:T(8,128)(2,1)S(1)}, u32[]{:S(2)}, u32[]{:S(2)}) collective-permute-start(bf16[4,192,256]{2,1,0:T(8,128)(2,1)S(1)} %fusion.3), channel_id=1, source_target_pairs={{0,2},{1,5},{2,0},{3,7},{4,6},{5,1},{6,4},{7,3},{8,10},{9,13},{10,... | collective-permute-start | bytes 1179656 | tf_op jit(solution)/shard_map/ppermute | solution.py:523
  225.4 4.5 %finish_dw.1 = (f32[4,96,576]{2,1,0:T(8,128)}, bf16[4,96,576]{2,1,0:T(8,128)(2,1)}) custom-call(s32[8]{0:T(128)} %stack.141.info, bf16[576,1024]{1,0:T(8,128)(2,1)} %get-tuple-element.159.p_ref, bf16[4,192,256]{2,1,0:T(8,128)(2,1)} %copy-done.2, bf16[4,192,256]{2,1,0:T(8,128)(2,1)} %copy-done.5, bf16[2,4,192,256]{3,2,1,0:T(8,128)(2,1)} %collective-permute-done.5.xc), custom_call_target="tpu_custom_call" | custom-call | flops 5435817984 | bytes 18874368 | tf_op jit(solution)/shard_map/finish_dw/pallas_call | solution.py:224
  233.5 2.4 collective-permute-done.46
  237.1 2.4 collective-permute-start.51
  239.5 3.6 %collective-permute-done.44 = bf16[4,144,768]{2,1,0:T(8,128)(2,1)S(1)} collective-permute-done((bf16[4,144,768]{2,1,0:T(8,128)(2,1)}, bf16[4,144,768]{2,1,0:T(8,128)(2,1)S(1)}, u32[]{:S(2)}, u32[]{:S(2)}) %collective-permute-start.44) | collective-permute-done | bytes 884768 | tf_op jit(solution)/shard_map/ppermute | solution.py:523
  243.4 4.1 %collective-permute-done.43 = bf16[2,192,256]{2,1,0:T(8,128)(2,1)S(1)} collective-permute-done((bf16[2,192,256]{2,1,0:T(8,128)(2,1)S(1)}, bf16[2,192,256]{2,1,0:T(8,128)(2,1)S(1)}, u32[]{:S(2)}, u32[]{:S(2)}) %collective-permute-start.43) | collective-permute-done | bytes 196640 | tf_op jit(solution)/shard_map/ppermute | solution.py:523
  247.6 7.3 %collective-permute-done.48 = bf16[2,96,576]{2,1,0:T(8,128)(2,1)S(1)} collective-permute-done((bf16[2,96,576]{2,1,0:T(8,128)(2,1)S(1)}, bf16[2,96,576]{2,1,0:T(8,128)(2,1)S(1)}, u32[]{:S(2)}, u32[]{:S(2)}) %collective-permute-start.48) | collective-permute-done | bytes 221216 | tf_op jit(solution)/shard_map/ppermute | solution.py:513
  255.1 2.7 collective-permute-start.50
  259.4 9.9 %collective-permute-done.50 = bf16[2,144,768]{2,1,0:T(8,128)(2,1)S(1)} collective-permute-done((bf16[2,144,768]{2,1,0:T(8,128)(2,1)S(1)}, bf16[2,144,768]{2,1,0:T(8,128)(2,1)S(1)}, u32[]{:S(2)}, u32[]{:S(2)}) %collective-permute-start.50) | collective-permute-done | bytes 442400 | tf_op jit(solution)/shard_map/ppermute | solution.py:523
  275.1 2.0 collective-permute-done.53
  (271 shorter events, 55.0 us)
Async XLA Ops:
  1.6 14.6 %collective-permute-start.6 = (bf16[96,576]{1,0:T(8,128)(2,1)S(1)}, bf16[96,576]{1,0:T(8,128)(2,1)S(1)}, u32[]{:S(2)}, u32[]{:S(2)}) collective-permute-start(bf16[96,576]{1,0:T(8,128)(2,1)S(1)} %pad_maximum_fusion.20), channel_id=1, source_target_pairs={{0,16},{16,0},{1,17},{17,1},{2,18},{18,2},{3,19},{19,3},{4,20},{20... | collective-permute-start | bytes 331784 | tf_op jit(solution)/shard_map/ppermute | solution.py:513
  7.5 61.9 %collective-permute-start.15 = (bf16[96,768]{1,0:T(8,128)(2,1)}, bf16[96,768]{1,0:T(8,128)(2,1)S(1)}, u32[]{:S(2)}, u32[]{:S(2)}) collective-permute-start(bf16[96,768]{1,0:T(8,128)(2,1)} %get-tuple-element.106), channel_id=1, source_target_pairs={{0,4},{1,9},{4,0},{5,13},{8,12},{9,1},{12,8},{13,5},{2,6},{3,11},{... | collective-permute-start | bytes 442376 | tf_op jit(solution)/shard_map/ppermute | solution.py:523
  9.2 12.8 %collective-permute-start = (bf16[2,192,256]{2,1,0:T(8,128)(2,1)S(1)}, bf16[2,192,256]{2,1,0:T(8,128)(2,1)S(1)}, u32[]{:S(2)}, u32[]{:S(2)}) collective-permute-start(bf16[2,192,256]{2,1,0:T(8,128)(2,1)S(1)} %slice_bitcast_fusion.5), channel_id=1, source_target_pairs={{0,8},{1,5},{4,12},{5,1},{8,0},{9,13},{12,4},{13,9},{2,10},{3,7},{... | collective-permute-start | bytes 589832 | tf_op jit(solution)/shard_map/ppermute | solution.py:523
  12.1 13.7 %collective-permute-start.2 = (bf16[144,768]{1,0:T(8,128)(2,1)S(1)}, bf16[144,768]{1,0:T(8,128)(2,1)S(1)}, u32[]{:S(2)}, u32[]{:S(2)}) collective-permute-start(bf16[144,768]{1,0:T(8,128)(2,1)S(1)} %pad_maximum_fusion.12), channel_id=1, source_target_pairs={{0,4},{1,9},{4,0},{5,13},{8,12},{9,1},{12,8},{13,5},{2,6},{3,11},{... | collective-permute-start | bytes 663560 | tf_op jit(solution)/shard_map/ppermute | solution.py:523
  22.0 15.8 %collective-permute-start.1 = (bf16[2,192,256]{2,1,0:T(8,128)(2,1)S(1)}, bf16[2,192,256]{2,1,0:T(8,128)(2,1)S(1)}, u32[]{:S(2)}, u32[]{:S(2)}) collective-permute-start(bf16[2,192,256]{2,1,0:T(8,128)(2,1)S(1)} %pad_maximum_fusion.13), channel_id=1, source_target_pairs={{0,4},{1,9},{4,0},{5,13},{8,12},{9,1},{12,8},{13,5},{2,6},{3,11},{... | collective-permute-start | bytes 589832 | tf_op jit(solution)/shard_map/ppermute | solution.py:523
  22.3 17.2 %collective-permute-start.8 = (bf16[2,96,576]{2,1,0:T(8,128)(2,1)S(1)}, bf16[2,96,576]{2,1,0:T(8,128)(2,1)S(1)}, u32[]{:S(2)}, u32[]{:S(2)}) collective-permute-start(bf16[2,96,576]{2,1,0:T(8,128)(2,1)S(1)} %pad_maximum_fusion.10), channel_id=1, source_target_pairs={{0,8},{1,5},{4,12},{5,1},{8,0},{9,13},{12,4},{13,9},{2,10},{3,7},{... | collective-permute-start | bytes 663560 | tf_op jit(solution)/shard_map/ppermute | solution.py:523
  25.8 16.4 %collective-permute-start.3 = (bf16[2,144,768]{2,1,0:T(8,128)(2,1)S(1)}, bf16[2,144,768]{2,1,0:T(8,128)(2,1)S(1)}, u32[]{:S(2)}, u32[]{:S(2)}) collective-permute-start(bf16[2,144,768]{2,1,0:T(8,128)(2,1)S(1)} %pad_maximum_fusion.4), channel_id=1, source_target_pairs={{0,8},{1,5},{4,12},{5,1},{8,0},{9,13},{12,4},{13,9},{2,10},{3,7},{... | collective-permute-start | bytes 1327112 | tf_op jit(solution)/shard_map/ppermute | solution.py:523
  37.9 7.8 %collective-permute-start.4 = (bf16[4,192,256]{2,1,0:T(8,128)(2,1)S(1)}, bf16[4,192,256]{2,1,0:T(8,128)(2,1)S(1)}, u32[]{:S(2)}, u32[]{:S(2)}) collective-permute-start(bf16[4,192,256]{2,1,0:T(8,128)(2,1)S(1)} %pad_maximum_fusion.5.xa.x_ref), channel_id=1, source_target_pairs={{0,2},{1,5},{2,0},{3,7},{4,6},{5,1},{6,4},{7,3},{8,10},{9,13},{10,... | collective-permute-start | bytes 1179656 | tf_op jit(solution)/shard_map/ppermute | solution.py:523
  39.6 9.7 %collective-permute-start.9 = (bf16[2,96,576]{2,1,0:T(8,128)(2,1)S(1)}, bf16[2,96,576]{2,1,0:T(8,128)(2,1)S(1)}, u32[]{:S(2)}, u32[]{:S(2)}) collective-permute-start(bf16[2,96,576]{2,1,0:T(8,128)(2,1)S(1)} %pad_maximum_fusion.11), channel_id=1, source_target_pairs={{0,4},{1,9},{4,0},{5,13},{8,12},{9,1},{12,8},{13,5},{2,6},{3,11},{... | collective-permute-start | bytes 663560 | tf_op jit(solution)/shard_map/ppermute | solution.py:523
  42.3 27.1 %collective-permute-start.20 = (bf16[4,144,768]{2,1,0:T(8,128)(2,1)S(1)}, bf16[4,144,768]{2,1,0:T(8,128)(2,1)}, u32[]{:S(2)}, u32[]{:S(2)}) collective-permute-start(bf16[4,144,768]{2,1,0:T(8,128)(2,1)S(1)} %pad_maximum_fusion.refs_0_), channel_id=1, source_target_pairs={{0,2},{1,17},{2,0},{3,19},{16,18},{17,1},{18,16},{19,3},{4,6},{5,2... | collective-permute-start | bytes 2654216 | tf_op jit(solution)/shard_map/ppermute | solution.py:523
  45.9 14.3 %collective-permute-start.5 = (bf16[2,4,192,256]{3,2,1,0:T(8,128)(2,1)S(1)}, bf16[2,4,192,256]{3,2,1,0:T(8,128)(2,1)}, u32[]{:S(2)}, u32[]{:S(2)}) collective-permute-start(bf16[2,4,192,256]{3,2,1,0:T(8,128)(2,1)S(1)} %pad_maximum_fusion.1), channel_id=1, source_target_pairs={{0,4},{1,3},{2,6},{3,1},{4,0},{5,7},{6,2},{7,5},{8,12},{9,11},{10,... | collective-permute-start | bytes 2359304 | tf_op jit(solution)/shard_map/ppermute | solution.py:523
  49.4 9.8 %collective-permute-start.10 = (bf16[4,96,576]{2,1,0:T(8,128)(2,1)S(1)}, bf16[4,96,576]{2,1,0:T(8,128)(2,1)S(1)}, u32[]{:S(2)}, u32[]{:S(2)}) collective-permute-start(bf16[4,96,576]{2,1,0:T(8,128)(2,1)S(1)} %pad_maximum_fusion.3.mine_ref.refs_3_), channel_id=1, source_target_pairs={{0,1},{1,0},{2,3},{3,2},{4,5},{5,4},{6,7},{7,6},{8,9},{9,8},{10,11... | collective-permute-start | bytes 1327112 | tf_op jit(solution)/shard_map/ppermute | solution.py:447
  58.7 27.7 %collective-permute-start.14 = (bf16[4,144,768]{2,1,0:T(8,128)(2,1)S(1)}, bf16[4,144,768]{2,1,0:T(8,128)(2,1)}, u32[]{:S(2)}, u32[]{:S(2)}) collective-permute-start(bf16[4,144,768]{2,1,0:T(8,128)(2,1)S(1)} %pad_maximum_fusion.refs_0_), channel_id=1, source_target_pairs={{0,16},{1,3},{2,18},{3,1},{16,0},{17,19},{18,2},{19,17},{4,20},{5,... | collective-permute-start | bytes 2654216 | tf_op jit(solution)/shard_map/ppermute | solution.py:523
  64.2 9.2 %collective-permute-start.11 = (bf16[384,1024]{1,0:T(8,128)(2,1)}, bf16[384,1024]{1,0:T(8,128)(2,1)}, u32[]{:S(2)}, u32[]{:S(2)}) collective-permute-start(bf16[384,1024]{1,0:T(8,128)(2,1)} %get-tuple-element.99.ko_ref.vo_ref), channel_id=1, source_target_pairs={{0,1},{1,0},{2,3},{3,2},{4,5},{5,4},{6,7},{7,6},{8,9},{9,8},{10,11... | collective-permute-start | bytes 2359304 | tf_op jit(solution)/shard_map/ppermute | solution.py:447
  69.4 16.8 %collective-permute-start.16 = (bf16[2,96,768]{2,1,0:T(8,128)(2,1)S(1)}, bf16[2,96,768]{2,1,0:T(8,128)(2,1)S(1)}, u32[]{:S(2)}, u32[]{:S(2)}) collective-permute-start(bf16[2,96,768]{2,1,0:T(8,128)(2,1)S(1)} %pad_maximum_fusion.8), channel_id=1, source_target_pairs={{0,8},{1,5},{4,12},{5,1},{8,0},{9,13},{12,4},{13,9},{2,10},{3,7},{... | collective-permute-start | bytes 884744 | tf_op jit(solution)/shard_map/ppermute | solution.py:523
  72.6 10.1 %collective-permute-start.12 = (bf16[2,192,256]{2,1,0:T(8,128)(2,1)S(1)}, bf16[2,192,256]{2,1,0:T(8,128)(2,1)S(1)}, u32[]{:S(2)}, u32[]{:S(2)}) collective-permute-start(bf16[2,192,256]{2,1,0:T(8,128)(2,1)S(1)} %get-tuple-element.192), channel_id=1, source_target_pairs={{0,8},{1,5},{4,12},{5,1},{8,0},{9,13},{12,4},{13,9},{2,10},{3,7},{... | collective-permute-start | bytes 589832 | tf_op jit(solution)/shard_map/ppermute | solution.py:523
  73.4 13.6 %collective-permute-start.13 = (bf16[4,144,768]{2,1,0:T(8,128)(2,1)S(1)}, bf16[4,144,768]{2,1,0:T(8,128)(2,1)}, u32[]{:S(2)}, u32[]{:S(2)}) collective-permute-start(bf16[4,144,768]{2,1,0:T(8,128)(2,1)S(1)} %pad_maximum_fusion.refs_0_), channel_id=1, source_target_pairs={{0,1},{1,0},{2,3},{3,2},{4,5},{5,4},{6,7},{7,6},{8,9},{9,8},{10,11... | collective-permute-start | bytes 2654216 | tf_op jit(solution)/shard_map/ppermute | solution.py:447
  73.4 32.2 %collective-permute-start.21 = (bf16[4,144,768]{2,1,0:T(8,128)(2,1)}, bf16[4,144,768]{2,1,0:T(8,128)(2,1)}, u32[]{:S(2)}, u32[]{:S(2)}) collective-permute-start(bf16[4,144,768]{2,1,0:T(8,128)(2,1)} %collective-permute-done.20.refs_1_), channel_id=1, source_target_pairs={{0,16},{1,3},{2,18},{3,1},{16,0},{17,19},{18,2},{19,17},{4,20},{5,... | collective-permute-start | bytes 2654216 | tf_op jit(solution)/shard_map/ppermute | solution.py:523
  82.7 13.5 %collective-permute-start.19 = (bf16[2,192,256]{2,1,0:T(8,128)(2,1)S(1)}, bf16[2,192,256]{2,1,0:T(8,128)(2,1)S(1)}, u32[]{:S(2)}, u32[]{:S(2)}) collective-permute-start(bf16[2,192,256]{2,1,0:T(8,128)(2,1)S(1)} %pad_maximum_fusion.14), channel_id=1, source_target_pairs={{0,4},{1,9},{4,0},{5,13},{8,12},{9,1},{12,8},{13,5},{2,6},{3,11},{... | collective-permute-start | bytes 589832 | tf_op jit(solution)/shard_map/ppermute | solution.py:523
  86.3 9.8 %collective-permute-start.17 = (bf16[2,192,256]{2,1,0:T(8,128)(2,1)}, bf16[2,192,256]{2,1,0:T(8,128)(2,1)S(1)}, u32[]{:S(2)}, u32[]{:S(2)}) collective-permute-start(bf16[2,192,256]{2,1,0:T(8,128)(2,1)} %get-tuple-element.100), channel_id=1, source_target_pairs={{0,4},{1,3},{2,6},{3,1},{4,0},{5,7},{6,2},{7,5},{8,12},{9,11},{10,... | collective-permute-start | bytes 589832 | tf_op jit(solution)/shard_map/ppermute | solution.py:523
  86.4 19.7 %collective-permute-start.26 = (bf16[4,96,768]{2,1,0:T(8,128)(2,1)S(1)}, bf16[4,96,768]{2,1,0:T(8,128)(2,1)}, u32[]{:S(2)}, u32[]{:S(2)}) collective-permute-start(bf16[4,96,768]{2,1,0:T(8,128)(2,1)S(1)} %pad_maximum_fusion.2.refs_8_), channel_id=1, source_target_pairs={{0,16},{1,3},{2,18},{3,1},{16,0},{17,19},{18,2},{19,17},{4,20},{5,... | collective-permute-start | bytes 1769480 | tf_op jit(solution)/shard_map/ppermute | solution.py:523
  87.0 18.3 %collective-permute-start.25 = (bf16[4,96,768]{2,1,0:T(8,128)(2,1)S(1)}, bf16[4,96,768]{2,1,0:T(8,128)(2,1)S(1)}, u32[]{:S(2)}, u32[]{:S(2)}) collective-permute-start(bf16[4,96,768]{2,1,0:T(8,128)(2,1)S(1)} %pad_maximum_fusion.2.refs_8_), channel_id=1, source_target_pairs={{0,2},{1,17},{2,0},{3,19},{16,18},{17,1},{18,16},{19,3},{4,6},{5,2... | collective-permute-start | bytes 1769480 | tf_op jit(solution)/shard_map/ppermute | solution.py:523
  96.1 19.7 %collective-permute-start.22 = (bf16[4,144,768]{2,1,0:T(8,128)(2,1)}, bf16[4,144,768]{2,1,0:T(8,128)(2,1)S(1)}, u32[]{:S(2)}, u32[]{:S(2)}) collective-permute-start(bf16[4,144,768]{2,1,0:T(8,128)(2,1)} %collective-permute-done.20.refs_1_), channel_id=1, source_target_pairs={{0,1},{1,0},{2,3},{3,2},{4,5},{5,4},{6,7},{7,6},{8,9},{9,8},{10,11... | collective-permute-start | bytes 2654216 | tf_op jit(solution)/shard_map/ppermute | solution.py:447
  96.3 9.1 %collective-permute-start.18 = (bf16[2,192,256]{2,1,0:T(8,128)(2,1)S(1)}, bf16[2,192,256]{2,1,0:T(8,128)(2,1)S(1)}, u32[]{:S(2)}, u32[]{:S(2)}) collective-permute-start(bf16[2,192,256]{2,1,0:T(8,128)(2,1)S(1)} %pad_maximum_fusion.15), channel_id=1, source_target_pairs={{0,2},{1,5},{2,0},{3,7},{4,6},{5,1},{6,4},{7,3},{8,10},{9,13},{10,... | collective-permute-start | bytes 589832 | tf_op jit(solution)/shard_map/ppermute | solution.py:523
  105.4 9.9 %collective-permute-start.27 = (bf16[4,96,768]{2,1,0:T(8,128)(2,1)S(1)}, bf16[4,96,768]{2,1,0:T(8,128)(2,1)S(1)}, u32[]{:S(2)}, u32[]{:S(2)}) collective-permute-start(bf16[4,96,768]{2,1,0:T(8,128)(2,1)S(1)} %collective-permute-done.25.refs_9_), channel_id=1, source_target_pairs={{0,16},{1,3},{2,18},{3,1},{16,0},{17,19},{18,2},{19,17},{4,20},{5,... | collective-permute-start | bytes 1769480 | tf_op jit(solution)/shard_map/ppermute | solution.py:523
  105.6 9.7 %collective-permute-start.28 = (bf16[4,96,768]{2,1,0:T(8,128)(2,1)S(1)}, bf16[4,96,768]{2,1,0:T(8,128)(2,1)S(1)}, u32[]{:S(2)}, u32[]{:S(2)}) collective-permute-start(bf16[4,96,768]{2,1,0:T(8,128)(2,1)S(1)} %pad_maximum_fusion.2.refs_8_), channel_id=1, source_target_pairs={{0,1},{1,0},{2,3},{3,2},{4,5},{5,4},{6,7},{7,6},{8,9},{9,8},{10,11... | collective-permute-start | bytes 1769480 | tf_op jit(solution)/shard_map/ppermute | solution.py:447
  105.6 10.3 %collective-permute-start.23 = (bf16[4,144,768]{2,1,0:T(8,128)(2,1)}, bf16[4,144,768]{2,1,0:T(8,128)(2,1)S(1)}, u32[]{:S(2)}, u32[]{:S(2)}) collective-permute-start(bf16[4,144,768]{2,1,0:T(8,128)(2,1)} %collective-permute-done.14.refs_2_), channel_id=1, source_target_pairs={{0,1},{1,0},{2,3},{3,2},{4,5},{5,4},{6,7},{7,6},{8,9},{9,8},{10,11... | collective-permute-start | bytes 2654216 | tf_op jit(solution)/shard_map/ppermute | solution.py:447
  106.1 9.8 %collective-permute-start.24 = (bf16[4,144,768]{2,1,0:T(8,128)(2,1)}, bf16[4,144,768]{2,1,0:T(8,128)(2,1)S(1)}, u32[]{:S(2)}, u32[]{:S(2)}) collective-permute-start(bf16[4,144,768]{2,1,0:T(8,128)(2,1)} %collective-permute-done.21.refs_3_), channel_id=1, source_target_pairs={{0,1},{1,0},{2,3},{3,2},{4,5},{5,4},{6,7},{7,6},{8,9},{9,8},{10,11... | collective-permute-start | bytes 2654216 | tf_op jit(solution)/shard_map/ppermute | solution.py:447
  142.6 6.1 %collective-permute-start.33 = (bf16[2,192,256]{2,1,0:T(8,128)(2,1)}, bf16[2,192,256]{2,1,0:T(8,128)(2,1)S(1)}, u32[]{:S(2)}, u32[]{:S(2)}) collective-permute-start(bf16[2,192,256]{2,1,0:T(8,128)(2,1)} %get-tuple-element.128), channel_id=1, source_target_pairs={{0,4},{1,3},{2,6},{3,1},{4,0},{5,7},{6,2},{7,5},{8,12},{9,11},{10,... | collective-permute-start | bytes 589832 | tf_op jit(solution)/shard_map/ppermute | solution.py:523
  155.1 17.3 %collective-permute-start.37 = (bf16[2,2,4,144,768]{4,3,2,1,0:T(8,128)(2,1)}, bf16[2,2,4,144,768]{4,3,2,1,0:T(8,128)(2,1)S(1)}, u32[]{:S(2)}, u32[]{:S(2)}) collective-permute-start(bf16[2,2,4,144,768]{4,3,2,1,0:T(8,128)(2,1)} %inner_give.1), channel_id=1, source_target_pairs={{0,1},{1,0},{2,3},{3,2},{4,5},{5,4},{6,7},{7,6},{8,9},{9,8},{10,11... | collective-permute-start | bytes 10616840 | tf_op jit(solution)/shard_map/ppermute | solution.py:447
  155.2 11.6 %collective-permute-start.36 = (bf16[2,2,4,96,768]{4,3,2,1,0:T(8,128)(2,1)}, bf16[2,2,4,96,768]{4,3,2,1,0:T(8,128)(2,1)}, u32[]{:S(2)}, u32[]{:S(2)}) collective-permute-start(bf16[2,2,4,96,768]{4,3,2,1,0:T(8,128)(2,1)} %outer_give.1), channel_id=1, source_target_pairs={{0,1},{1,0},{2,3},{3,2},{4,5},{5,4},{6,7},{7,6},{8,9},{9,8},{10,11... | collective-permute-start | bytes 7077896 | tf_op jit(solution)/shard_map/ppermute | solution.py:447
  155.7 8.5 %collective-permute-start.32 = (bf16[2,192,256]{2,1,0:T(8,128)(2,1)}, bf16[2,192,256]{2,1,0:T(8,128)(2,1)S(1)}, u32[]{:S(2)}, u32[]{:S(2)}) collective-permute-start(bf16[2,192,256]{2,1,0:T(8,128)(2,1)} %get-tuple-element.123), channel_id=1, source_target_pairs={{0,8},{1,5},{4,12},{5,1},{8,0},{9,13},{12,4},{13,9},{2,10},{3,7},{... | collective-permute-start | bytes 589832 | tf_op jit(solution)/shard_map/ppermute | solution.py:523
  158.8 8.1 %collective-permute-start.35 = (bf16[2,192,256]{2,1,0:T(8,128)(2,1)}, bf16[2,192,256]{2,1,0:T(8,128)(2,1)}, u32[]{:S(2)}, u32[]{:S(2)}) collective-permute-start(bf16[2,192,256]{2,1,0:T(8,128)(2,1)} %pad_maximum_fusion.16), channel_id=1, source_target_pairs={{0,2},{1,5},{2,0},{3,7},{4,6},{5,1},{6,4},{7,3},{8,10},{9,13},{10,... | collective-permute-start | bytes 589832 | tf_op jit(solution)/shard_map/ppermute | solution.py:523
  165.5 12.9 %collective-permute-start.34 = (bf16[2,192,256]{2,1,0:T(8,128)(2,1)}, bf16[2,192,256]{2,1,0:T(8,128)(2,1)}, u32[]{:S(2)}, u32[]{:S(2)}) collective-permute-start(bf16[2,192,256]{2,1,0:T(8,128)(2,1)} %pad_maximum_fusion.17), channel_id=1, source_target_pairs={{0,4},{1,9},{4,0},{5,13},{8,12},{9,1},{12,8},{13,5},{2,6},{3,11},{... | collective-permute-start | bytes 589832 | tf_op jit(solution)/shard_map/ppermute | solution.py:523
  170.4 30.1 %collective-permute-start.38 = (bf16[2,4,96,768]{3,2,1,0:T(8,128)(2,1)}, bf16[2,4,96,768]{3,2,1,0:T(8,128)(2,1)}, u32[]{:S(2)}, u32[]{:S(2)}) collective-permute-start(bf16[2,4,96,768]{3,2,1,0:T(8,128)(2,1)} %outer_first.1), channel_id=1, source_target_pairs={{0,8},{1,5},{4,12},{5,1},{8,0},{9,13},{12,4},{13,9},{2,10},{3,7},{... | collective-permute-start | bytes 3538952 | tf_op jit(solution)/shard_map/ppermute | solution.py:523
  178.4 36.7 %collective-permute-start.41 = (bf16[2,4,144,768]{3,2,1,0:T(8,128)(2,1)}, bf16[2,4,144,768]{3,2,1,0:T(8,128)(2,1)S(1)}, u32[]{:S(2)}, u32[]{:S(2)}) collective-permute-start(bf16[2,4,144,768]{3,2,1,0:T(8,128)(2,1)} %inner_first.1), channel_id=1, source_target_pairs={{0,16},{1,3},{2,18},{3,1},{16,0},{17,19},{18,2},{19,17},{4,20},{5,... | collective-permute-start | bytes 5308424 | tf_op jit(solution)/shard_map/ppermute | solution.py:523
  207.1 14.4 %collective-permute-start.40 = (bf16[2,4,192,256]{3,2,1,0:T(8,128)(2,1)}, bf16[2,4,192,256]{3,2,1,0:T(8,128)(2,1)}, u32[]{:S(2)}, u32[]{:S(2)}) collective-permute-start(bf16[2,4,192,256]{3,2,1,0:T(8,128)(2,1)} %get-tuple-element.150), channel_id=1, source_target_pairs={{0,4},{1,3},{2,6},{3,1},{4,0},{5,7},{6,2},{7,5},{8,12},{9,11},{10,... | collective-permute-start | bytes 2359304 | tf_op jit(solution)/shard_map/ppermute | solution.py:523
  214.3 21.5 %collective-permute-start.46 = (bf16[4,96,768]{2,1,0:T(8,128)(2,1)}, bf16[4,96,768]{2,1,0:T(8,128)(2,1)}, u32[]{:S(2)}, u32[]{:S(2)}) collective-permute-start(bf16[4,96,768]{2,1,0:T(8,128)(2,1)} %get-tuple-element.166), channel_id=1, source_target_pairs={{0,4},{1,9},{4,0},{5,13},{8,12},{9,1},{12,8},{13,5},{2,6},{3,11},{... | collective-permute-start | bytes 1769480 | tf_op jit(solution)/shard_map/ppermute | solution.py:523
  222.6 8.6 %collective-permute-start.42 = (bf16[4,192,256]{2,1,0:T(8,128)(2,1)S(1)}, bf16[4,192,256]{2,1,0:T(8,128)(2,1)S(1)}, u32[]{:S(2)}, u32[]{:S(2)}) collective-permute-start(bf16[4,192,256]{2,1,0:T(8,128)(2,1)S(1)} %fusion.3), channel_id=1, source_target_pairs={{0,2},{1,5},{2,0},{3,7},{4,6},{5,1},{6,4},{7,3},{8,10},{9,13},{10,... | collective-permute-start | bytes 1179656 | tf_op jit(solution)/shard_map/ppermute | solution.py:523
  229.9 13.3 %collective-permute-start.44 = (bf16[4,144,768]{2,1,0:T(8,128)(2,1)}, bf16[4,144,768]{2,1,0:T(8,128)(2,1)S(1)}, u32[]{:S(2)}, u32[]{:S(2)}) collective-permute-start(bf16[4,144,768]{2,1,0:T(8,128)(2,1)} %get-tuple-element.162), channel_id=1, source_target_pairs={{0,2},{1,17},{2,0},{3,19},{16,18},{17,1},{18,16},{19,3},{4,6},{5,2... | collective-permute-start | bytes 2654216 | tf_op jit(solution)/shard_map/ppermute | solution.py:523
  232.5 15.0 %collective-permute-start.43 = (bf16[2,192,256]{2,1,0:T(8,128)(2,1)S(1)}, bf16[2,192,256]{2,1,0:T(8,128)(2,1)S(1)}, u32[]{:S(2)}, u32[]{:S(2)}) collective-permute-start(bf16[2,192,256]{2,1,0:T(8,128)(2,1)S(1)} %slice.331), channel_id=1, source_target_pairs={{0,8},{1,5},{4,12},{5,1},{8,0},{9,13},{12,4},{13,9},{2,10},{3,7},{... | collective-permute-start | bytes 589832 | tf_op jit(solution)/shard_map/ppermute | solution.py:523
  235.9 19.0 %collective-permute-start.48 = (bf16[2,96,576]{2,1,0:T(8,128)(2,1)S(1)}, bf16[2,96,576]{2,1,0:T(8,128)(2,1)S(1)}, u32[]{:S(2)}, u32[]{:S(2)}) collective-permute-start(bf16[2,96,576]{2,1,0:T(8,128)(2,1)S(1)} %slice.394), channel_id=1, source_target_pairs={{0,8},{8,0},{1,9},{9,1},{2,10},{10,2},{3,11},{11,3},{4,12},{12,4},... | collective-permute-start | bytes 663560 | tf_op jit(solution)/shard_map/ppermute | solution.py:513
  237.1 17.9 %collective-permute-start.51 = (bf16[2,96,768]{2,1,0:T(8,128)(2,1)S(1)}, bf16[2,96,768]{2,1,0:T(8,128)(2,1)S(1)}, u32[]{:S(2)}, u32[]{:S(2)}) collective-permute-start(bf16[2,96,768]{2,1,0:T(8,128)(2,1)S(1)} %slice.339), channel_id=1, source_target_pairs={{0,16},{1,3},{2,18},{3,1},{16,0},{17,19},{18,2},{19,17},{4,20},{5,... | collective-permute-start | bytes 884744 | tf_op jit(solution)/shard_map/ppermute | solution.py:523
  247.5 23.8 %collective-permute-start.47 = (bf16[2,192,256]{2,1,0:T(8,128)(2,1)S(1)}, bf16[2,192,256]{2,1,0:T(8,128)(2,1)S(1)}, u32[]{:S(2)}, u32[]{:S(2)}) collective-permute-start(bf16[2,192,256]{2,1,0:T(8,128)(2,1)S(1)} %pad_maximum_fusion.18), channel_id=1, source_target_pairs={{0,4},{1,9},{4,0},{5,13},{8,12},{9,1},{12,8},{13,5},{2,6},{3,11},{... | collective-permute-start | bytes 589832 | tf_op jit(solution)/shard_map/ppermute | solution.py:523
  255.0 14.4 %collective-permute-start.49 = (bf16[96,576]{1,0:T(8,128)(2,1)S(1)}, bf16[96,576]{1,0:T(8,128)(2,1)S(1)}, u32[]{:S(2)}, u32[]{:S(2)}) collective-permute-start(bf16[96,576]{1,0:T(8,128)(2,1)S(1)} %fusion.5), channel_id=1, source_target_pairs={{0,4},{4,0},{1,5},{5,1},{2,6},{6,2},{3,7},{7,3},{8,12},{12,8},{9,1... | collective-permute-start | bytes 331784 | tf_op jit(solution)/shard_map/ppermute | solution.py:513
  255.1 14.2 %collective-permute-start.50 = (bf16[2,144,768]{2,1,0:T(8,128)(2,1)S(1)}, bf16[2,144,768]{2,1,0:T(8,128)(2,1)S(1)}, u32[]{:S(2)}, u32[]{:S(2)}) collective-permute-start(bf16[2,144,768]{2,1,0:T(8,128)(2,1)S(1)} %slice.337), channel_id=1, source_target_pairs={{0,8},{1,5},{4,12},{5,1},{8,0},{9,13},{12,4},{13,9},{2,10},{3,7},{... | collective-permute-start | bytes 1327112 | tf_op jit(solution)/shard_map/ppermute | solution.py:523
  257.9 13.4 %collective-permute-start.55 = (bf16[96,768]{1,0:T(8,128)(2,1)S(1)}, bf16[96,768]{1,0:T(8,128)(2,1)S(1)}, u32[]{:S(2)}, u32[]{:S(2)}) collective-permute-start(bf16[96,768]{1,0:T(8,128)(2,1)S(1)} %slice_bitcast_fusion.6), channel_id=1, source_target_pairs={{0,2},{1,17},{2,0},{3,19},{16,18},{17,1},{18,16},{19,3},{4,6},{5,2... | collective-permute-start | bytes 442376 | tf_op jit(solution)/shard_map/ppermute | solution.py:523
  270.3 8.3 %collective-permute-start.54 = (bf16[144,768]{1,0:T(8,128)(2,1)S(1)}, bf16[144,768]{1,0:T(8,128)(2,1)S(1)}, u32[]{:S(2)}, u32[]{:S(2)}) collective-permute-start(bf16[144,768]{1,0:T(8,128)(2,1)S(1)} %slice_bitcast_fusion.1), channel_id=1, source_target_pairs={{0,4},{1,9},{4,0},{5,13},{8,12},{9,1},{12,8},{13,5},{2,6},{3,11},{... | collective-permute-start | bytes 663560 | tf_op jit(solution)/shard_map/ppermute | solution.py:523
  (50 other events, 341.9 us)

commit v7 on v6

--- a/solution.py
+++ b/solution.py
@@ -230,7 +230,7 @@
 def middle_kernel(info, a0,a1,a2, x_ref, c0,c1,c2, *refs):
     chunk_a=refs[:8]; chunk_b=refs[8:16]
     (mixk_ref, mixs_ref, ek_ref, es_ref, g1_ref, attnT_ref, hidT_ref, outT_ref, bl_ref, act_ref, il_ref, norm_ref,
-                  win, woT, wo, ns, gp_s, t_s, f_s, sems)=refs[16:]
+                  win, woT, wo, wpk, gp_s, t_s, f_s, sems)=refs[16:]
     row=info[0]; z=info[1]; y=info[2]; c=info[3]; group=info[5]
     feat=a0.shape[1]; n=a0.shape[2]; width=4*feat; ffc=chunk_a[0].shape[2]; half=feat//2; fh=ffc//2; third=half//3
     def go(src,dst,s): pltpu.make_async_copy(src,dst,sems.at[s]).start()
@@ -245,16 +245,11 @@
                     step=row_step(core,i)
                     yield ref.at[i],xor(row,step),g,col,kc+spot
     for ref,r,g,col,_ in each(chunk_a):
-        for j in range(3):
-            go(ref.at[half:half+third,j*256:(j+1)*256],wo.at[r,pl.ds(pl.multiple_of((col*2+g)*half+j*third,16),third),:],0)
-    for ref,r,g,col,where in each(chunk_a):
-        if where==0:
-            go(ref.at[half+third:half+third+16,:],ns.at[r],3)
+        go(ref.at[half:half+third,:],wpk.at[r,col*2+g],0)
     for ref,r,g,col,_ in each(chunk_a):
         go(ref.at[0:half,:],win.at[pl.ds(pl.multiple_of(r*feat+g*half,16),half),pl.ds(pl.multiple_of(col*ffc,128),ffc)],1)
     for ref,r,g,col,_ in each(chunk_b):
-        for t in range(2):
-            go(ref.at[:,t*fh:(t+1)*fh],woT.at[pl.ds(pl.multiple_of(r*feat+t*half,16),half),pl.ds(pl.multiple_of((col*2+g)*fh,128),fh)],2)
+        go(ref,woT.at[pl.ds(pl.multiple_of(r*feat,64),feat),pl.ds(pl.multiple_of((col*2+g)*fh,128),fh)],2)
     def group_of(s):
         return xor(y,y_step(c,s))*2+xor(z,z_step(c,s))
     def row_of(s):
@@ -265,14 +260,15 @@
         t_s[rows_at(row_of(s),feat,64),:]=x_ref[s]
     attn=attnT_ref[...].T
     x=t_s[...].T.astype(f32)
-    pltpu.make_async_copy(wo,wo,sems.at[0]).wait()
-    pltpu.make_async_copy(ns,ns,sems.at[3]).wait()
+    pltpu.make_async_copy(wpk,wpk,sems.at[0]).wait()
+    for r in range(4):
+        for q in range(8):
+            for j in range(3):
+                wo[r,q*half+j*third:q*half+(j+1)*third,:]=wpk[r,q,:,j*256:(j+1)*256]
+    wide=256-feat; pieces=feat//wide
+    addends=[sum(wpk[r,0,0:16,j*256+feat:(j+1)*256].astype(f32) for j in range(3)) for r in range(4)]
     def vector(which):
-        out=[]
-        for r in range(4):
-            v=ns[r].astype(f32)[0:3,which*feat:(which+1)*feat]
-            out.append(jnp.sum(v,axis=0,keepdims=True))
-        return jnp.concatenate(out,axis=1)
+        return jnp.concatenate([addends[r][which*pieces+t:which*pieces+t+1] for r in range(4) for t in range(pieces)],axis=1)
     gain1=vector(0); shift1=vector(1); gain2=vector(2); shift2=vector(3)
     branch=jnp.concatenate([mm(attn,wo[r])[:,:feat] for r in range(4)],axis=1)
     def stats(v):
@@ -325,13 +321,14 @@
     gh=f_s[...]
     sums=jnp.concatenate((jnp.sum(gh*cent1,axis=0,keepdims=True),jnp.sum(gh,axis=0,keepdims=True))+sums2+(jnp.zeros((4,width),f32),),axis=0)
     for r in range(4):
-        norm_ref[r]=sums[:,r*feat:(r+1)*feat]
+        lines=[sums[i:i+1,r*feat+t*wide:r*feat+(t+1)*wide] for i in range(4) for t in range(pieces)]
+        lines=jnp.concatenate(lines+[jnp.zeros((third-4*pieces,wide),f32)],axis=0)
+        norm_ref[r]=jnp.concatenate([jnp.zeros((third,feat),f32),lines],axis=1)
     grad1=back(gh*gain1,cent1,inv1)
     bl=grad1.astype(bf16)
-    padded=jnp.concatenate([bl,jnp.zeros((n,256-feat),bf16)],axis=1)
     da=jnp.zeros((width,n),f32)
     for r in range(4):
-        piece=padded[:,r*feat:r*feat+256]
+        piece=jnp.concatenate([bl[:,r*feat:(r+1)*feat],jnp.zeros((n,wide),bf16)],axis=1)
         bl_ref[r]=piece
         da=da+mm(wo[r],piece,NT)
     t_s[...]=da.astype(bf16)
@@ -346,8 +343,8 @@
     S=jax.ShapeDtypeStruct
     return pl.pallas_call(middle_kernel,in_specs=[SM]+[VM]*7+[HB]*16,out_specs=[VM]*12,
         out_shape=[S((2,feat,n),bf16)]*4+[S((4,feat,n),f32),S((width,n),bf16),S((width,n),bf16),S((width,n),bf16),
-                   S((4,n,256),bf16),S((n,ff),bf16),S((n,ff),bf16),S((4,8,feat),f32)],
-        scratch_shapes=[pltpu.VMEM((width,ff),bf16),pltpu.VMEM((width,ff),bf16),pltpu.VMEM((4,width,256),bf16),pltpu.VMEM((4,16,width),bf16),
+                   S((4,n,256),bf16),S((n,ff),bf16),S((n,ff),bf16),S((4,feat//6,256),f32)],
+        scratch_shapes=[pltpu.VMEM((width,ff),bf16),pltpu.VMEM((width,ff),bf16),pltpu.VMEM((4,width,256),bf16),pltpu.VMEM((4,8,feat//6,width),bf16),
                         pltpu.VMEM((n,ff),f32),pltpu.VMEM((width,n),bf16),pltpu.VMEM((n,width),f32),pltpu.SemaphoreType.DMA((4,))],
         compiler_params=pltpu.CompilerParams(vmem_limit_bytes=56*1024*1024),
         cost_estimate=pl.CostEstimate(flops=int(6.0*(12*n*width*ff*2))+1,bytes_accessed=int(6.0*(24*width*ff))+1,transcendentals=int(6.0*(2*n*ff))+1),
@@ -371,8 +368,7 @@
         for g in range(2):
             kx=xor(g,info[5])
             slot=jnp.where(core==0,2*kx+ky,2*ky+kx)
-            for t in range(2):
-                put(slot,slice(0,half),slice(t*fh,(t+1)*fh),value[t*half:(t+1)*half,g*fh:(g+1)*fh])
+            put(slot,slice(0,2*half),slice(0,fh),value[:,g*fh:(g+1)*fh])
 
 def inner_blocks(info,which,a,b,refs,put):
     hidT_ref,il_ref,attnT_ref,bl_ref,norm_ref=refs
@@ -386,9 +382,9 @@
         put(s,slice(0,half),slice(None),value[s*half:(s+1)*half])
         outs=mm(heads,bl_ref[r])
         for j in range(3):
-            put(s,slice(half,half+third),slice(j*256,(j+1)*256),outs[j*third:(j+1)*third])
-        line=jnp.concatenate([norm_ref[r][i:i+1] for i in range(4)],axis=1)
-        put(s,slice(half+third,half+third+16),slice(None),jnp.concatenate([line,jnp.zeros((15,line.shape[1]),f32)],axis=0))
+            piece=outs[j*third:(j+1)*third]
+            if j==0: piece=piece+norm_ref[r]
+            put(s,slice(half,half+third),slice(j*256,(j+1)*256),piece)
 
 def give_kernel(blocks,info,*refs):
     out=refs[-1]
@@ -417,31 +413,31 @@
         return lambda j,s:index(a,j,s)
     whole=pl.BlockSpec((width,n),at(lambda i,j,s:(0,0)))
     if kind=="inner":
-        blocks,rows=inner_blocks,half+half//3+16
+        blocks,rows,lanes=inner_blocks,half+half//3,ffc
         specs=[whole,pl.BlockSpec((n,ffc),at(lambda i,j,s:(0,target(s,which,i,j)[2]))),whole,
-               pl.BlockSpec((4,n,256),at(lambda i,j,s:(0,0,0))),pl.BlockSpec((4,8,width//4),at(lambda i,j,s:(0,0,0)))]
+               pl.BlockSpec((4,n,256),at(lambda i,j,s:(0,0,0))),pl.BlockSpec((4,half//3,256),at(lambda i,j,s:(0,0,0)))]
     else:
-        blocks,rows=outer_blocks,half
+        blocks,rows,lanes=outer_blocks,2*half,ffc//2
         args=(args[0],args[1],args[1])
         def column(ky): return at(lambda i,j,s:(0,xor(s[2],ky)*2+xor(s[3],which)))
         specs=[whole,pl.BlockSpec((n,ffc),column(0)),pl.BlockSpec((n,ffc),column(1))]
     weight={"give":4,"first":2,"second":0}[stage]
     cost=pl.CostEstimate(flops=int(6.0*(weight*width*n*ffc))+1,bytes_accessed=int(6.0*(4*weight*rows*ffc))+1,transcendentals=int(6.0*(0))+1)
     name=kind+"_"+stage
-    five=(1,1,4,rows,ffc)
+    five=(1,1,4,rows,lanes)
     if stage=="give":
         return pl.pallas_call(functools.partial(give_kernel,blocks),
             grid_spec=pltpu.PrefetchScalarGridSpec(num_scalar_prefetch=1,grid=(2,2),in_specs=specs,out_specs=pl.BlockSpec(five,lambda i,j,s:(i,j,0,0,0))),
-            out_shape=S((2,2,4,rows,ffc),bf16),cost_estimate=cost,name=name)(info,*args)
-    got_spec=pl.BlockSpec(five,lambda j,s:(a,j,0,0,0)); one=pl.BlockSpec((1,4,rows,ffc),lambda j,s:(j,0,0,0))
+            out_shape=S((2,2,4,rows,lanes),bf16),cost_estimate=cost,name=name)(info,*args)
+    got_spec=pl.BlockSpec(five,lambda j,s:(a,j,0,0,0)); one=pl.BlockSpec((1,4,rows,lanes),lambda j,s:(j,0,0,0))
     if stage=="first":
         return pl.pallas_call(functools.partial(first_kernel,blocks),
             grid_spec=pltpu.PrefetchScalarGridSpec(num_scalar_prefetch=1,grid=(2,),in_specs=specs+[got_spec],out_specs=one),
-            out_shape=S((2,4,rows,ffc),bf16),cost_estimate=cost,name=name)(info,*args,got)
-    full=pl.BlockSpec((4,rows,ffc),lambda j,s:(0,0,0))
+            out_shape=S((2,4,rows,lanes),bf16),cost_estimate=cost,name=name)(info,*args,got)
+    full=pl.BlockSpec((4,rows,lanes),lambda j,s:(0,0,0))
     return pl.pallas_call(functools.partial(second_kernel,blocks),
         grid_spec=pltpu.PrefetchScalarGridSpec(num_scalar_prefetch=1,grid=(2,),in_specs=specs+[got_spec,one],out_specs=[full,full]),
-        out_shape=[S((4,rows,ffc),bf16)]*2,cost_estimate=cost,name=name)(info,*args,got,came)
+        out_shape=[S((4,rows,lanes),bf16)]*2,cost_estimate=cost,name=name)(info,*args,got,came)
 
 def core_swap(value):
     return lax.ppermute(value, "cc", [(0, 1), (1, 0)])
@@ -465,31 +461,20 @@
 
 
 def dp_sum(this_half, other_half, c):
-    if lax.axis_size("dp") != 2:
-        whole = jnp.concatenate(
-            [jnp.where(c == 0, this_half, other_half), jnp.where(c == 0, other_half, this_half)], axis=0
-        )
-        return lax.psum_scatter(whole.astype(bf16), "dp", scatter_dimension=0, tiled=True).astype(f32)
-    same = lax.axis_index("dp") == c
-    keep = jnp.where(same, this_half, other_half)
-    return keep + swap2(jnp.where(same, other_half, this_half).astype(bf16), "dp").astype(f32)
-
-
-def pack_outer(part):
-    turned = part.T
-    half = turned.shape[0] // 2
-    return jnp.concatenate([turned[:half], turned[half:]], axis=1)
-
-
-def unpack_outer(packed):
-    wide = packed.shape[1] // 2
-    return jnp.concatenate([packed[:, :wide], packed[:, wide:]], axis=0).T
-
-
-def pack_output(part):
+    whole = jnp.concatenate(
+        [jnp.where(c == 0, this_half, other_half), jnp.where(c == 0, other_half, this_half)], axis=0
+    )
+    return lax.psum_scatter(whole.astype(bf16), "dp", scatter_dimension=0, tiled=True).astype(f32)
+
+
+def pack_output(part, norms):
     third = part.shape[0] // 3
-    padded = jnp.pad(part, ((0, 0), (0, 256 - part.shape[1])))
-    return jnp.concatenate([padded[j * third : (j + 1) * third] for j in range(3)], axis=1)
+    wide = 256 - part.shape[1]
+    addends = jnp.pad(norms.reshape(3, -1, wide), ((0, 0), (0, third - norms.shape[1] // wide), (0, 0)))
+    pieces = []
+    for j in range(3):
+        pieces += [part[j * third : (j + 1) * third], addends[j]]
+    return jnp.concatenate(pieces, axis=1)
 
 
 def unpack_output(packed, feat):
@@ -500,9 +485,7 @@
     line = jnp.concatenate([first_gain, first_shift, second_gain, second_shift])
     high = lax.reduce_precision(line, 8, 7)
     middle_part = lax.reduce_precision(line - high, 8, 7)
-    rest = line - high - middle_part
-    rows = jnp.stack([high, middle_part, rest]).astype(bf16)
-    return jnp.pad(rows, ((0, 13), (0, 0)))
+    return jnp.stack([high, middle_part, line - high - middle_part]).astype(bf16)
 
 
 def after(value, *earlier):
@@ -557,9 +540,9 @@
         for g in range(2):
             parts = [w.reshape((2, w.shape[0] // 2) + w.shape[1:])[g] for w in (inner, outer, output)]
             if which == 0:
-                halves.append(jnp.concatenate([parts[0], pack_output(parts[2]), norms], axis=0))
+                halves.append(jnp.concatenate([parts[0], pack_output(parts[2], norms)], axis=0))
             else:
-                halves.append(pack_outer(parts[1]))
+                halves.append(parts[1].T)
         whole = lax.all_gather(jnp.stack(halves), GROUP)
         flat = whole.reshape((-1,) + whole.shape[2:])
         arrays = []
@@ -641,16 +624,16 @@
         back = swap_by(turn(jnp.stack(parts)), row)
         return back.reshape(2, 2, feat, half).transpose(0, 2, 1, 3).reshape(2, feat, cols)
 
-    this_half, other_half = dp_halves(jnp.concatenate([w_query, w_key, w_value], axis=1), c)
     token_blocks = to_slots(tokens)
+    this_half, other_half = dp_halves(jnp.concatenate([after(w_query, token_blocks), w_key, w_value], axis=1), c)
     token_three = scatter_steps(token_blocks[:2], token_blocks[2:], ROW)
     x_own = jnp.stack(by_slot(token_three))
     other_columns = core_swap(other_half)
     norms = pack_norms(first_gain, first_shift, second_gain, second_shift)
     if two:
-        block_a = jnp.concatenate([after(w_inner, token_blocks), pack_output(w_output), norms], axis=0)
+        block_a = jnp.concatenate([after(w_inner, token_blocks), pack_output(w_output, norms)], axis=0)
         pair_a = row_pair(block_a)
-        block_b = pack_outer(w_outer)
+        block_b = w_outer.T
         near_b = crossed(after(block_b, token_blocks), ROW, 1)
     pieces = []
     for s in range(4):
@@ -696,10 +679,10 @@
     if two:
         near_a, far_a = crossed(row_a, PLANE, 1), crossed(row_a, PLANE, 0)
         both_a = crossed(after(near_a, kv_own), PLANE, 0)
-        row_a_swapped = core_swap(after(row_a, kv_own))
+        row_a_swapped = core_swap(row_a)
         far_a = after(far_a, low_b)
         both_a = after(both_a, low_b)
-        pair_b = jnp.stack([block_b, after(near_b, kv_own)])
+        pair_b = jnp.stack([block_b, after(near_b, xs[1])])
         row_b = row_rest(pair_b, low_b)
         q_second = after(q_second, row_a_swapped, far_a, row_b)
         near_b, far_b = crossed(row_b, PLANE, 1), crossed(row_b, PLANE, 0)
@@ -738,7 +721,7 @@
     mixed_pass = jnp.stack([mixed_keep[1], mixed_first[1]])
     first_outer = grad_call("outer", "first", info, tied(outer_args, mixed_pass, grads[2]), got_outer)
     came_outer = crossed(first_outer, ROW, 0)
-    first_inner = grad_call("inner", "first", info, tied(inner_args, first_outer), got_inner)
+    first_inner = grad_call("inner", "first", info, tied(inner_args, first_outer, mixed_pass), got_inner)
     came_inner = crossed(first_inner, PLANE, 0) if two else jnp.zeros_like(first_inner)
     mixed_second = crossed(mixed_pass, ROW, 1)
     dq, own, send = head_back(0, heads, first_inner, mixed_second)
@@ -762,9 +745,14 @@
     d_x = add_parts([grad_one, dx_keep[0], dx_first[0], dx_second]).astype(bf16)
     d_x_first = crossed(d_x[2:], ROW, 0)
     by_row_step = keep + after(got, d_x).astype(f32)
-    passed_m = swap2(by_row_step[2:].astype(bf16), "rm")
     if two:
-        plane_inner = add_parts([keep_inner, after(crossed(pass_inner, PLANE, 1), by_row_step)]).astype(bf16)
+        here = group == c
+        across = lax.ppermute(
+            by_row_step.astype(bf16), ("dp", "cc"), [(2, 0), (1, 3)]
+        )
+    plane_parts = (keep_inner, after(crossed(pass_inner, PLANE, 1), by_row_step)) if two else None
+    if two:
+        plane_inner = add_parts(plane_parts).astype(bf16)
         pass_on_inner = crossed(plane_inner[2:], ROW, 0)
     row_outer = add_parts([keep_outer, after(crossed(pass_outer, ROW, 1), by_row_step)]).astype(bf16)
     if two:
@@ -772,37 +760,45 @@
         d_x_first = after(d_x_first, plane_inner, row_outer)
     d_x_pass = jnp.stack([d_x[1], d_x_first[1]])
     d_x_second = crossed(d_x_pass, ROW, 1)
-    near_far = by_row_step[:2] + after(passed_m, d_x_pass).astype(f32)
-    near_sum = near_far[0]
-    far_low = swap2(near_far[1].astype(bf16), "rz")
     if two:
-        pair_inner = (plane_inner[:2].astype(f32) + after(pass_on_inner, near_far).astype(f32)).astype(bf16)
+        summed = by_row_step + after(across, d_x_pass).astype(f32)
+        active = [(g * 5 + 2 * side, g * 5 + 2 * (1 - side)) for g in range(2) for side in range(2)]
+        passed_m = lax.ppermute(summed[2:].astype(bf16), ("dp", "rm", "cc"), active)
+        pair_inner = (plane_inner[:2].astype(f32) + after(pass_on_inner, summed).astype(f32)).astype(bf16)
         last_inner = crossed(pair_inner[1], ROW, 1)
-        pair_outer = (row_outer[:2].astype(f32) + after(pass_on_outer, near_far).astype(f32)).astype(bf16)
+        pair_outer = (row_outer[:2].astype(f32) + after(pass_on_outer, pair_inner).astype(f32)).astype(bf16)
         last_outer = crossed(pair_outer[1], PLANE, 1)
-        far_low = after(far_low, pair_inner, pair_outer)
-    far_sum = far_low.astype(f32)
-    kept = jnp.where(z == c, near_sum, far_sum)
-    passed = core_swap(jnp.where(z == c, far_sum, near_sum).astype(bf16)).astype(f32)
-    d_x_second = after(d_x_second, kept)
-    d_input = from_slots(by_slot((d_x[:2], d_x_first, d_x_second))).astype(f32)
-    g_qkv = dp_sum(kept, passed, c)
-    if two:
-        inner_sums = [pair_inner[0].astype(f32) + after(last_inner, passed).astype(f32)]
-        outer_sums = [pair_outer[0].astype(f32) + after(last_outer, passed).astype(f32)]
+        near_far = summed[:2] + after(passed_m, pair_outer).astype(f32)
+        far_low = lax.ppermute(near_far[1].astype(bf16), ("dp", "rz", "cc"), active)
+        d_x_second = after(d_x_second, near_far)
+        d_input = from_slots(by_slot((d_x[:2], d_x_first, d_x_second))).astype(f32)
+        near_sum = near_far[0]
+        far_sum = after(far_low, d_x_second).astype(f32)
+        kept = jnp.where(z == c, near_sum, far_sum)
+        passed = core_swap(jnp.where(z == c, far_sum, near_sum).astype(bf16)).astype(f32)
+        g_qkv = jnp.where(here, kept, passed)
+        inner_sums = [pair_inner[0].astype(f32) + after(last_inner, far_sum).astype(f32)]
+        outer_sums = [pair_outer[0].astype(f32) + after(last_outer, far_sum).astype(f32)]
     else:
+        near_far = by_row_step[:2] + swap2(by_row_step[2:].astype(bf16), "rm").astype(f32)
+        near_sum = near_far[0]
+        far_sum = swap2(near_far[1].astype(bf16), "rz").astype(f32)
+        kept = jnp.where(z == c, near_sum, far_sum)
+        passed = core_swap(jnp.where(z == c, far_sum, near_sum).astype(bf16)).astype(f32)
+        d_input = from_slots(by_slot((d_x[:2], d_x_first, d_x_second))).astype(f32)
+        g_qkv = dp_sum(kept, passed, c)
         outer_sums = generic_outer(row_outer, c)
         inner_sums = generic_inner(first_inner, keep_inner, pass_inner, c)
     mixed_out = from_slots(by_slot((mixed_keep, mixed_first, mixed_second)))
 
     half_rows = feat // 2
     third = half_rows // 3
-    g_outer = jnp.concatenate([unpack_outer(part) for part in outer_sums], axis=0)
+    g_outer = jnp.concatenate([part.T for part in outer_sums], axis=0)
     g_inner = jnp.concatenate([part[:half_rows] for part in inner_sums], axis=0)
     g_output = jnp.concatenate(
         [unpack_output(part[half_rows : half_rows + third], feat) for part in inner_sums], axis=0
     )
-    g_norms = inner_sums[0][half_rows + third].reshape(4, feat)
+    g_norms = inner_sums[0][half_rows : half_rows + 4 * feat // (256 - feat), feat:256].reshape(4, feat)
     if not two:
         g_outer, g_inner, g_output = (
             lax.psum_scatter(g.astype(bf16), "dp", scatter_dimension=0, tiled=True).astype(f32)

time: 282 us -> 273 us (0.968)
  waiting for transfers between devices: 85.2 us -> 78.4 us
    ppermute x4 -> x1, waiting for transfers between devices: 9.32 us -> 0.01 us  [swap2(): return lax.ppermute(value, axis, [(0, 1), (1, 0)])]
    ppermute x16, starting transfers between devices: 14 us -> 6.34 us  [core_swap(): return lax.ppermute(value, 'cc', [(0, 1), (1, 0)])]
    ppermute x0 -> x3, waiting for transfers between devices: none -> 7.63 us  [the longest x1 4.69 us: local(): lax.ppermute(by_row_step.astype(bf16), ('dp', 'cc'), [(2, 0), (1, 3)])]
    ppermute x0 -> x3, starting transfers between devices: none -> 6.1 us  [the longest x1 2.9 us: local(): passed_m = lax.ppermute(summed[2:].astype(bf16), ('dp', 'rm', 'cc'), active)]
    ppermute x36, waiting for transfers between devices: 71.1 us -> 65.5 us  [crossed(): return lax.ppermute(value, axes + ('cc',), pairs)]
    ppermute x36, starting transfers between devices: 45.1 us -> 48.7 us  [crossed(): return lax.ppermute(value, axes + ('cc',), pairs)]
    slice x11, local copies, waits for them, and re-layouts: 3.33 us -> 0.17 us  [by_slot(): return [keep[0], second[0], first[0], second[1]]]
    unnamed x86 -> x84, local copies, waits for them, and re-layouts: 5.74 us -> 5.55 us
  transfers between devices with their start and end apart: 56 -> 56, of which waited for: 23 -> 25; matrix products, arithmetic and copies ran while one was open for 9% -> 8% of each run, Pallas kernels for 25% -> 25%
where the time goes in v7:
time: 273 us
  Pallas kernels  95.4 us (35%)
  waiting for transfers between devices  78.4 us (29%)
  starting transfers between devices  64.1 us (23%)
  local copies, waits for them, and re-layouts  19.2 us (7%)
  other arithmetic  13.1 us (5%)
    ppermute x36, waiting for transfers between devices, crossed(): return lax.ppermute(value, axes + ('cc',), pairs)  65.5 us
    ppermute x36, starting transfers between devices, crossed(): return lax.ppermute(value, axes + ('cc',), pairs)  48.7 us
    pallas_call x1, Pallas kernels, middle(): pl.pallas_call(middle_kernel, in_specs=[SM] + [VM] * 7 + [HB] * 16, out_s...  21.4 us
    pallas_call x1, Pallas kernels, attend_back(): pl.pallas_call(attend_back_kernel, grid=(count, 4 // QB), in_specs=[pl.Bl...  20.2 us
    pallas_call x2, Pallas kernels, attend(): pl.pallas_call(attend_kernel, grid=(heads,), in_specs=[pl.BlockSpec((HD,...  13.3 us
    pallas_call x2, Pallas kernels, grad_call(): pl.pallas_call(functools.partial(give_kernel, blocks), grid_spec=pltpu.Pr...  10.3 us
    pallas_call x2, Pallas kernels, grad_call(): pl.pallas_call(functools.partial(second_kernel, blocks), grid_spec=pltpu....  9.03 us
    pallas_call x2, Pallas kernels, grad_call(): pl.pallas_call(functools.partial(first_kernel, blocks), grid_spec=pltpu.P...  7.78 us
  transfers between devices with their start and end apart: 56, of which 25 were waited for; matrix products, arithmetic and copies ran while one was open for 8% of the time, Pallas kernels for 25%

profile of v7, /device:TPU:0, one launch (start us, length us, event | category | flops | bytes accessed | tf_op | source)
XLA Modules:
  0.0 272.6 jit_solution(14800423437597026236)
XLA Ops:
  2.2 3.0 %collective-permute-start.6 = (bf16[96,576]{1,0:T(8,128)(2,1)S(1)}, bf16[96,576]{1,0:T(8,128)(2,1)S(1)}, u32[]{:S(2)}, u32[]{:S(2)}) collective-permute-start(bf16[96,576]{1,0:T(8,128)(2,1)S(1)} %pad_maximum_fusion.19), channel_id=1, source_target_pairs={{0,16},{16,0},{1,17},{17,1},{2,18},{18,2},{3,19},{19,3},{4,20},{20... | collective-permute-start | bytes 331784 | tf_op jit(solution)/shard_map/ppermute | solution.py:496
  5.2 1.6 collective-permute-start.15
  6.8 2.7 collective-permute-start
  15.2 4.0 %collective-permute-start.1 = (bf16[2,192,256]{2,1,0:T(8,128)(2,1)S(1)}, bf16[2,192,256]{2,1,0:T(8,128)(2,1)S(1)}, u32[]{:S(2)}, u32[]{:S(2)}) collective-permute-start(bf16[2,192,256]{2,1,0:T(8,128)(2,1)S(1)} %pad_maximum_fusion.12), channel_id=1, source_target_pairs={{0,4},{1,9},{4,0},{5,13},{8,12},{9,1},{12,8},{13,5},{2,6},{3,11},{... | collective-permute-start | bytes 589832 | tf_op jit(solution)/shard_map/ppermute | solution.py:506
  19.4 3.7 %collective-permute-start.3 = (bf16[2,128,768]{2,1,0:T(8,128)(2,1)S(1)}, bf16[2,128,768]{2,1,0:T(8,128)(2,1)S(1)}, u32[]{:S(2)}, u32[]{:S(2)}) collective-permute-start(bf16[2,128,768]{2,1,0:T(8,128)(2,1)S(1)} %pad_maximum_fusion.5), channel_id=1, source_target_pairs={{0,8},{1,5},{4,12},{5,1},{8,0},{9,13},{12,4},{13,9},{2,10},{3,7},{... | collective-permute-start | bytes 1179656 | tf_op jit(solution)/shard_map/ppermute | solution.py:506
  24.0 4.4 %collective-permute-done.1 = bf16[2,192,256]{2,1,0:T(8,128)(2,1)S(1)} collective-permute-done((bf16[2,192,256]{2,1,0:T(8,128)(2,1)S(1)}, bf16[2,192,256]{2,1,0:T(8,128)(2,1)S(1)}, u32[]{:S(2)}, u32[]{:S(2)}) %collective-permute-start.1) | collective-permute-done | bytes 196640 | tf_op jit(solution)/shard_map/ppermute | solution.py:506
  28.5 1.6 collective-permute-start.4
  30.1 8.2 %collective-permute-done.8 = bf16[2,96,576]{2,1,0:T(8,128)(2,1)S(1)} collective-permute-done((bf16[2,96,576]{2,1,0:T(8,128)(2,1)S(1)}, bf16[2,96,576]{2,1,0:T(8,128)(2,1)S(1)}, u32[]{:S(2)}, u32[]{:S(2)}) %collective-permute-start.8) | collective-permute-done | bytes 221216 | tf_op jit(solution)/shard_map/ppermute | solution.py:506
  38.3 4.0 %collective-permute-start.9 = (bf16[2,96,576]{2,1,0:T(8,128)(2,1)S(1)}, bf16[2,96,576]{2,1,0:T(8,128)(2,1)S(1)}, u32[]{:S(2)}, u32[]{:S(2)}) collective-permute-start(bf16[2,96,576]{2,1,0:T(8,128)(2,1)S(1)} %pad_maximum_fusion.11), channel_id=1, source_target_pairs={{0,4},{1,9},{4,0},{5,13},{8,12},{9,1},{12,8},{13,5},{2,6},{3,11},{... | collective-permute-start | bytes 663560 | tf_op jit(solution)/shard_map/ppermute | solution.py:506
  42.4 1.6 collective-permute-start.20
  44.1 3.9 %collective-permute-done.9 = bf16[2,96,576]{2,1,0:T(8,128)(2,1)S(1)} collective-permute-done((bf16[2,96,576]{2,1,0:T(8,128)(2,1)S(1)}, bf16[2,96,576]{2,1,0:T(8,128)(2,1)S(1)}, u32[]{:S(2)}, u32[]{:S(2)}) %collective-permute-start.9) | collective-permute-done | bytes 221216 | tf_op jit(solution)/shard_map/ppermute | solution.py:506
  52.7 3.0 %collective-permute-start.16 = (bf16[2,192,384]{2,1,0:T(8,128)(2,1)S(1)}, bf16[2,192,384]{2,1,0:T(8,128)(2,1)S(1)}, u32[]{:S(2)}, u32[]{:S(2)}) collective-permute-start(bf16[2,192,384]{2,1,0:T(8,128)(2,1)S(1)} %pad_maximum_fusion.8), channel_id=1, source_target_pairs={{0,8},{1,5},{4,12},{5,1},{8,0},{9,13},{12,4},{13,9},{2,10},{3,7},{... | collective-permute-start | bytes 884744 | tf_op jit(solution)/shard_map/ppermute | solution.py:506
  55.7 4.1 %collective-permute-done.5.xc = bf16[2,4,192,256]{3,2,1,0:T(8,128)(2,1)} collective-permute-done((bf16[2,4,192,256]{3,2,1,0:T(8,128)(2,1)S(1)}, bf16[2,4,192,256]{3,2,1,0:T(8,128)(2,1)}, u32[]{:S(2)}, u32[]{:S(2)}) %collective-permute-start.5) | collective-permute-done | bytes 786464 | tf_op jit(solution)/shard_map/ppermute | solution.py:506
  59.8 4.0 %qkv.1 = (bf16[192,1024]{1,0:T(8,128)(2,1)}, bf16[384,1024]{1,0:T(8,128)(2,1)}) custom-call(s32[8]{0:T(128)} %stack.140.info, bf16[4,192,256]{2,1,0:T(8,128)(2,1)} %copy-done.2, bf16[4,192,256]{2,1,0:T(8,128)(2,1)} %copy-done.4, bf16[2,4,192,256]{3,2,1,0:T(8,128)(2,1)} %collective-permute-done.5.xc, bf16[4,96,576]{2,1,0:T(8,128)(2,1)} %copy-done.1, ...), custom_call_target="tpu_custom_call" | custom-call | tf_op jit(solution)/shard_map/qkv/pallas_call | solution.py:182
  63.8 3.2 %collective-permute-start.11 = (bf16[384,1024]{1,0:T(8,128)(2,1)}, bf16[384,1024]{1,0:T(8,128)(2,1)}, u32[]{:S(2)}, u32[]{:S(2)}) collective-permute-start(bf16[384,1024]{1,0:T(8,128)(2,1)} %get-tuple-element.101.ko_ref.vo_ref), channel_id=1, source_target_pairs={{0,1},{1,0},{2,3},{3,2},{4,5},{5,4},{6,7},{7,6},{8,9},{9,8},{10,11... | collective-permute-start | bytes 2359304 | tf_op jit(solution)/shard_map/ppermute | solution.py:443
  69.9 6.6 %attend.2 = (f32[192,512]{1,0:T(8,128)}, f32[3,1,512]{2,1,0:T(1,128)}, bf16[2,192,256]{2,1,0:T(8,128)(2,1)}) custom-call(bf16[192,1024]{1,0:T(8,128)(2,1)} %get-tuple-element.140.q_ref, bf16[384,1024]{1,0:T(8,128)(2,1)} %get-tuple-element.101.ko_ref.vo_ref, bf16[384,1024]{1,0:T(8,128)(2,1)} %get-tuple-element.101.ko_ref.vo_ref, ...), custom_call_target="tpu_custom_call" | custom-call | flops 19327352832 | bytes 25165824 | tf_op jit(solution)/shard_map/attend/pallas_call | solution.py:66
  77.1 1.6 collective-permute-start.17
  78.7 1.6 collective-permute-start.25
  80.3 6.6 %attend.3 = (f32[192,512]{1,0:T(8,128)}, f32[3,1,512]{2,1,0:T(1,128)}, bf16[2,192,256]{2,1,0:T(8,128)(2,1)}) custom-call(bf16[192,1024]{1,0:T(8,128)(2,1)} %get-tuple-element.140.q_ref, bf16[384,1024]{1,0:T(8,128)(2,1)} %get-tuple-element.101.ko_ref.vo_ref, bf16[384,1024]{1,0:T(8,128)(2,1)} %get-tuple-element.101.ko_ref.vo_ref, ...), custom_call_target="tpu_custom_call" | custom-call | flops 19327352832 | bytes 25165824 | tf_op jit(solution)/shard_map/attend/pallas_call | solution.py:66
  90.0 5.8 %collective-permute-done.18.a2 = bf16[2,192,256]{2,1,0:T(8,128)(2,1)S(1)} collective-permute-done((bf16[2,192,256]{2,1,0:T(8,128)(2,1)S(1)}, bf16[2,192,256]{2,1,0:T(8,128)(2,1)S(1)}, u32[]{:S(2)}, u32[]{:S(2)}) %collective-permute-start.18) | collective-permute-done | bytes 196640 | tf_op jit(solution)/shard_map/ppermute | solution.py:506
  95.8 1.5 collective-permute-start.27
  98.4 7.4 %collective-permute-done.27.refs_11_ = bf16[4,192,384]{2,1,0:T(8,128)(2,1)S(1)} collective-permute-done((bf16[4,192,384]{2,1,0:T(8,128)(2,1)S(1)}, bf16[4,192,384]{2,1,0:T(8,128)(2,1)S(1)}, u32[]{:S(2)}, u32[]{:S(2)}) %collective-permute-start.27) | collective-permute-done | bytes 589856 | tf_op jit(solution)/shard_map/ppermute | solution.py:506
  110.3 21.4 %middle.1 = (bf16[2,192,256]{2,1,0:T(8,128)(2,1)}, bf16[2,192,256]{2,1,0:T(8,128)(2,1)}, bf16[2,192,256]{2,1,0:T(8,128)(2,1)}, bf16[2,192,256]{2,1,0:T(8,128)(2,...) custom-call(s32[8]{0:T(128)} %stack.140.info, ...), custom_call_target="tpu_custom_call" | custom-call | flops 86973087744 | bytes 339738624 | tf_op jit(solution)/shard_map/middle/pallas_call | solution.py:344
  133.1 4.7 %outer_give.1 = bf16[2,2,4,192,384]{4,3,2,1,0:T(8,128)(2,1)} custom-call(s32[8]{0:T(128)} %stack.140.info, bf16[768,256]{1,0:T(8,128)(2,1)} %get-tuple-element.152.refs_0_, bf16[256,3072]{1,0:T(8,128)(2,1)} %get-tuple-element.127.refs_1_.refs_2_, bf16[256,3072]{1,0:T(8,128)(2,1)} %get-tuple-element.127.refs_1_.refs_2_), custom_call_target="tpu_custom_call" | custom-call | flops 3623878656 | bytes 14155777 | tf_op jit(solution)/shard_map/outer_give/pallas_call | solution.py:429
  139.3 5.7 %inner_give.1 = bf16[2,2,4,128,768]{4,3,2,1,0:T(8,128)(2,1)} custom-call(s32[8]{0:T(128)} %stack.140.info, bf16[768,256]{1,0:T(8,128)(2,1)} %get-tuple-element.155.refs_0_, bf16[256,3072]{1,0:T(8,128)(2,1)} %get-tuple-element.132.refs_1_, bf16[768,256]{1,0:T(8,128)(2,1)} %get-tuple-element.133.refs_2_, bf16[4,256,256]{2,1,0:T(8,128)(2,1)} %get-tuple-element.134.refs_3_, ...), custom_call_target="tpu_custom_call" | custom-call | flops 3623878656 | bytes 9437185 | tf_op jit(solution)/shard_map/inner_give/pallas_call | solution.py:429
  145.5 1.6 collective-permute-start.32
  147.6 6.4 %collective-permute-done.32 = bf16[2,192,256]{2,1,0:T(8,128)(2,1)S(1)} collective-permute-done((bf16[2,192,256]{2,1,0:T(8,128)(2,1)}, bf16[2,192,256]{2,1,0:T(8,128)(2,1)S(1)}, u32[]{:S(2)}, u32[]{:S(2)}) %collective-permute-start.32) | collective-permute-done | bytes 196640 | tf_op jit(solution)/shard_map/ppermute | solution.py:506
  155.9 3.6 %outer_first.1 = bf16[2,4,192,384]{3,2,1,0:T(8,128)(2,1)} custom-call(s32[8]{0:T(128)} %stack.140.info, bf16[768,256]{1,0:T(8,128)(2,1)} %get-tuple-element.152.refs_0_, bf16[256,3072]{1,0:T(8,128)(2,1)} %get-tuple-element.127.refs_1_.refs_2_, bf16[256,3072]{1,0:T(8,128)(2,1)} %get-tuple-element.127.refs_1_.refs_2_, ...), custom_call_target="tpu_custom_call" | custom-call | flops 1811939328 | bytes 7077889 | tf_op jit(solution)/shard_map/outer_first/pallas_call | solution.py:434
  160.5 1.7 copy-done
  162.2 4.1 %inner_first.1 = bf16[2,4,128,768]{3,2,1,0:T(8,128)(2,1)} custom-call(s32[8]{0:T(128)} %stack.140.info, bf16[768,256]{1,0:T(8,128)(2,1)} %get-tuple-element.155.refs_0_, bf16[256,3072]{1,0:T(8,128)(2,1)} %get-tuple-element.132.refs_1_, bf16[768,256]{1,0:T(8,128)(2,1)} %get-tuple-element.133.refs_2_, bf16[4,256,256]{2,1,0:T(8,128)(2,1)} %get-tuple-element.134.refs_3_, ...), custom_call_target="tpu_custom_call" | custom-call | flops 1811939328 | bytes 4718593 | tf_op jit(solution)/shard_map/inner_first/pallas_call | solution.py:434
  167.8 20.2 %attend_back.1 = (bf16[192,1024]{1,0:T(8,128)(2,1)}, f32[3,1024,128]{2,1,0:T(8,128)}, bf16[3,1024,128]{2,1,0:T(8,128)(2,1)}) custom-call(bf16[192,1024]{1,0:T(8,128)(2,1)} %get-tuple-element.140.q_ref, bf16[384,1024]{1,0:T(8,128)(2,1)} %get-tuple-element.101.ko_ref.vo_ref, bf16[384,1024]{1,0:T(8,128)(2,1)} %get-tuple-element.101.ko_ref.vo_ref, ...), custom_call_target="tpu_custom_call" | custom-call | flops 96636764160 | bytes 150994944 | tf_op jit(solution)/shard_map/attend_back/pallas_call | solution.py:119
  191.4 5.1 %finish_dx.1 = (f32[2,4,192,256]{3,2,1,0:T(8,128)}, bf16[2,4,192,256]{3,2,1,0:T(8,128)(2,1)}, bf16[576,1024]{1,0:T(8,128)(2,1)}) custom-call(s32[8]{0:T(128)} %stack.140.info, bf16[192,1024]{1,0:T(8,128)(2,1)} %get-tuple-element.145.refs_0_, f32[3,1024,128]{2,1,0:T(8,128)} %get-tuple-element.148.refs_1_, bf16[3,1024,128]{2,1,0:T(8,128)(2,1)} %copy-done.8, ...), custom_call_target="tpu_custom_call" | custom-call | flops 1 | bytes 1 | tf_op jit(solution)/shard_map/finish_dx/pallas_call | solution.py:205
  196.5 2.0 collective-permute-start.40
  198.6 4.2 %outer_second.1 = (bf16[4,192,384]{2,1,0:T(8,128)(2,1)}, bf16[4,192,384]{2,1,0:T(8,128)(2,1)}) custom-call(s32[8]{0:T(128)} %stack.140.info, bf16[768,256]{1,0:T(8,128)(2,1)} %get-tuple-element.152.refs_0_, bf16[256,3072]{1,0:T(8,128)(2,1)} %get-tuple-element.127.refs_1_.refs_2_, bf16[256,3072]{1,0:T(8,128)(2,1)} %get-tuple-element.127.refs_1_.refs_2_, ...), custom_call_target="tpu_custom_call" | custom-call | flops 1 | bytes 1 | tf_op jit(solution)/shard_map/outer_second/pallas_call | solution.py:438
  204.0 4.9 %inner_second.1 = (bf16[4,128,768]{2,1,0:T(8,128)(2,1)}, bf16[4,128,768]{2,1,0:T(8,128)(2,1)}) custom-call(s32[8]{0:T(128)} %stack.140.info, bf16[768,256]{1,0:T(8,128)(2,1)} %get-tuple-element.155.refs_0_, bf16[256,3072]{1,0:T(8,128)(2,1)} %get-tuple-element.132.refs_1_, bf16[768,256]{1,0:T(8,128)(2,1)} %get-tuple-element.133.refs_2_, ...), custom_call_target="tpu_custom_call" | custom-call | flops 1 | bytes 1 | tf_op jit(solution)/shard_map/inner_second/pallas_call | solution.py:438
  209.3 5.9 %collective-permute-done.40 = bf16[2,4,192,256]{3,2,1,0:T(8,128)(2,1)} collective-permute-done((bf16[2,4,192,256]{3,2,1,0:T(8,128)(2,1)}, bf16[2,4,192,256]{3,2,1,0:T(8,128)(2,1)}, u32[]{:S(2)}, u32[]{:S(2)}) %collective-permute-start.40) | collective-permute-done | bytes 786464 | tf_op jit(solution)/shard_map/ppermute | solution.py:506
  216.3 4.4 %finish_dw.1 = (f32[4,96,576]{2,1,0:T(8,128)}, bf16[4,96,576]{2,1,0:T(8,128)(2,1)}) custom-call(s32[8]{0:T(128)} %stack.140.info, bf16[576,1024]{1,0:T(8,128)(2,1)} %get-tuple-element.160.p_ref, bf16[4,192,256]{2,1,0:T(8,128)(2,1)} %copy-done.2, bf16[4,192,256]{2,1,0:T(8,128)(2,1)} %copy-done.4, bf16[2,4,192,256]{3,2,1,0:T(8,128)(2,1)} %collective-permute-done.5.xc), custom_call_target="tpu_custom_call" | custom-call | flops 5435817984 | bytes 18874368 | tf_op jit(solution)/shard_map/finish_dw/pallas_call | solution.py:224
  220.7 4.7 %collective-permute-done.42 = bf16[4,192,256]{2,1,0:T(8,128)(2,1)} collective-permute-done((bf16[4,192,256]{2,1,0:T(8,128)(2,1)S(1)}, bf16[4,192,256]{2,1,0:T(8,128)(2,1)}, u32[]{:S(2)}, u32[]{:S(2)}) %collective-permute-start.42) | collective-permute-done | bytes 393248 | tf_op jit(solution)/shard_map/ppermute | solution.py:506
  225.4 1.6 fusion.1
  227.0 2.0 collective-permute-start.43
  236.7 2.1 collective-permute-start.47
  238.7 4.7 %collective-permute-done.48 = bf16[4,96,576]{2,1,0:T(8,128)(2,1)S(1)} collective-permute-done((bf16[4,96,576]{2,1,0:T(8,128)(2,1)S(1)}, bf16[4,96,576]{2,1,0:T(8,128)(2,1)S(1)}, u32[]{:S(2)}, u32[]{:S(2)}) %collective-permute-start.48) | collective-permute-done | bytes 442400 | tf_op jit(solution)/shard_map/ppermute | solution.py:750
  243.6 2.9 %collective-permute-start.49 = (bf16[2,96,576]{2,1,0:T(8,128)(2,1)S(1)}, bf16[2,96,576]{2,1,0:T(8,128)(2,1)S(1)}, u32[]{:S(2)}, u32[]{:S(2)}) collective-permute-start(bf16[2,96,576]{2,1,0:T(8,128)(2,1)S(1)} %slice.389), channel_id=1, source_target_pairs={{0,8},{8,0},{17,25},{25,17},{2,10},{10,2},{19,27},{27,19},{4,12},{... | collective-permute-start | bytes 663560 | tf_op jit(solution)/shard_map/ppermute | solution.py:766
  246.5 7.5 %collective-permute-done.51 = bf16[2,128,768]{2,1,0:T(8,128)(2,1)S(1)} collective-permute-done((bf16[2,128,768]{2,1,0:T(8,128)(2,1)S(1)}, bf16[2,128,768]{2,1,0:T(8,128)(2,1)S(1)}, u32[]{:S(2)}, u32[]{:S(2)}) %collective-permute-start.51) | collective-permute-done | bytes 393248 | tf_op jit(solution)/shard_map/ppermute | solution.py:506
  254.2 2.4 collective-permute-done.49
  256.7 1.9 collective-permute-start.52
  260.0 2.1 collective-permute-start.54
  265.6 2.1 collective-permute-done.54
  (273 shorter events, 56.4 us)
Async XLA Ops:
  2.2 12.0 %collective-permute-start.6 = (bf16[96,576]{1,0:T(8,128)(2,1)S(1)}, bf16[96,576]{1,0:T(8,128)(2,1)S(1)}, u32[]{:S(2)}, u32[]{:S(2)}) collective-permute-start(bf16[96,576]{1,0:T(8,128)(2,1)S(1)} %pad_maximum_fusion.19), channel_id=1, source_target_pairs={{0,16},{16,0},{1,17},{17,1},{2,18},{18,2},{3,19},{19,3},{4,20},{20... | collective-permute-start | bytes 331784 | tf_op jit(solution)/shard_map/ppermute | solution.py:496
  5.2 46.2 %collective-permute-start.15 = (bf16[192,384]{1,0:T(8,128)(2,1)S(1)}, bf16[192,384]{1,0:T(8,128)(2,1)S(1)}, u32[]{:S(2)}, u32[]{:S(2)}) collective-permute-start(bf16[192,384]{1,0:T(8,128)(2,1)S(1)} %bitcast.133), channel_id=1, source_target_pairs={{0,4},{1,9},{4,0},{5,13},{8,12},{9,1},{12,8},{13,5},{2,6},{3,11},{... | collective-permute-start | bytes 442376 | tf_op jit(solution)/shard_map/ppermute | solution.py:506
  6.8 8.3 %collective-permute-start = (bf16[2,192,256]{2,1,0:T(8,128)(2,1)S(1)}, bf16[2,192,256]{2,1,0:T(8,128)(2,1)S(1)}, u32[]{:S(2)}, u32[]{:S(2)}) collective-permute-start(bf16[2,192,256]{2,1,0:T(8,128)(2,1)S(1)} %slice_bitcast_fusion.5), channel_id=1, source_target_pairs={{0,8},{1,5},{4,12},{5,1},{8,0},{9,13},{12,4},{13,9},{2,10},{3,7},{... | collective-permute-start | bytes 589832 | tf_op jit(solution)/shard_map/ppermute | solution.py:506
  10.0 9.4 %collective-permute-start.2 = (bf16[128,768]{1,0:T(8,128)(2,1)S(1)}, bf16[128,768]{1,0:T(8,128)(2,1)S(1)}, u32[]{:S(2)}, u32[]{:S(2)}) collective-permute-start(bf16[128,768]{1,0:T(8,128)(2,1)S(1)} %get-tuple-element.216), channel_id=1, source_target_pairs={{0,4},{1,9},{4,0},{5,13},{8,12},{9,1},{12,8},{13,5},{2,6},{3,11},{... | collective-permute-start | bytes 589832 | tf_op jit(solution)/shard_map/ppermute | solution.py:506
  14.3 9.4 %collective-permute-start.7 = (bf16[96,576]{1,0:T(8,128)(2,1)S(1)}, bf16[96,576]{1,0:T(8,128)(2,1)S(1)}, u32[]{:S(2)}, u32[]{:S(2)}) collective-permute-start(bf16[96,576]{1,0:T(8,128)(2,1)S(1)} %broadcast_select_fusion), channel_id=1, source_target_pairs={{0,1},{1,0},{2,3},{3,2},{4,5},{5,4},{6,7},{7,6},{8,9},{9,8},{10,11... | collective-permute-start | bytes 331784 | tf_op jit(solution)/shard_map/ppermute | solution.py:443
  15.2 13.2 %collective-permute-start.1 = (bf16[2,192,256]{2,1,0:T(8,128)(2,1)S(1)}, bf16[2,192,256]{2,1,0:T(8,128)(2,1)S(1)}, u32[]{:S(2)}, u32[]{:S(2)}) collective-permute-start(bf16[2,192,256]{2,1,0:T(8,128)(2,1)S(1)} %pad_maximum_fusion.12), channel_id=1, source_target_pairs={{0,4},{1,9},{4,0},{5,13},{8,12},{9,1},{12,8},{13,5},{2,6},{3,11},{... | collective-permute-start | bytes 589832 | tf_op jit(solution)/shard_map/ppermute | solution.py:506
  19.4 22.9 %collective-permute-start.3 = (bf16[2,128,768]{2,1,0:T(8,128)(2,1)S(1)}, bf16[2,128,768]{2,1,0:T(8,128)(2,1)S(1)}, u32[]{:S(2)}, u32[]{:S(2)}) collective-permute-start(bf16[2,128,768]{2,1,0:T(8,128)(2,1)S(1)} %pad_maximum_fusion.5), channel_id=1, source_target_pairs={{0,8},{1,5},{4,12},{5,1},{8,0},{9,13},{12,4},{13,9},{2,10},{3,7},{... | collective-permute-start | bytes 1179656 | tf_op jit(solution)/shard_map/ppermute | solution.py:506
  23.9 14.3 %collective-permute-start.8 = (bf16[2,96,576]{2,1,0:T(8,128)(2,1)S(1)}, bf16[2,96,576]{2,1,0:T(8,128)(2,1)S(1)}, u32[]{:S(2)}, u32[]{:S(2)}) collective-permute-start(bf16[2,96,576]{2,1,0:T(8,128)(2,1)S(1)} %pad_maximum_fusion.10), channel_id=1, source_target_pairs={{0,8},{1,5},{4,12},{5,1},{8,0},{9,13},{12,4},{13,9},{2,10},{3,7},{... | collective-permute-start | bytes 663560 | tf_op jit(solution)/shard_map/ppermute | solution.py:506
  28.5 15.5 %collective-permute-start.4 = (bf16[4,192,256]{2,1,0:T(8,128)(2,1)S(1)}, bf16[4,192,256]{2,1,0:T(8,128)(2,1)S(1)}, u32[]{:S(2)}, u32[]{:S(2)}) collective-permute-start(bf16[4,192,256]{2,1,0:T(8,128)(2,1)S(1)} %pad_maximum_fusion.4.xa.x_ref), channel_id=1, source_target_pairs={{0,2},{1,5},{2,0},{3,7},{4,6},{5,1},{6,4},{7,3},{8,10},{9,13},{10,... | collective-permute-start | bytes 1179656 | tf_op jit(solution)/shard_map/ppermute | solution.py:506
  38.3 9.8 %collective-permute-start.9 = (bf16[2,96,576]{2,1,0:T(8,128)(2,1)S(1)}, bf16[2,96,576]{2,1,0:T(8,128)(2,1)S(1)}, u32[]{:S(2)}, u32[]{:S(2)}) collective-permute-start(bf16[2,96,576]{2,1,0:T(8,128)(2,1)S(1)} %pad_maximum_fusion.11), channel_id=1, source_target_pairs={{0,4},{1,9},{4,0},{5,13},{8,12},{9,1},{12,8},{13,5},{2,6},{3,11},{... | collective-permute-start | bytes 663560 | tf_op jit(solution)/shard_map/ppermute | solution.py:506
  42.4 24.8 %collective-permute-start.20 = (bf16[4,128,768]{2,1,0:T(8,128)(2,1)S(1)}, bf16[4,128,768]{2,1,0:T(8,128)(2,1)}, u32[]{:S(2)}, u32[]{:S(2)}) collective-permute-start(bf16[4,128,768]{2,1,0:T(8,128)(2,1)S(1)} %pad_maximum_fusion.refs_0_), channel_id=1, source_target_pairs={{0,2},{1,17},{2,0},{3,19},{16,18},{17,1},{18,16},{19,3},{4,6},{5,2... | collective-permute-start | bytes 2359304 | tf_op jit(solution)/shard_map/ppermute | solution.py:506
  44.1 15.8 %collective-permute-start.5 = (bf16[2,4,192,256]{3,2,1,0:T(8,128)(2,1)S(1)}, bf16[2,4,192,256]{3,2,1,0:T(8,128)(2,1)}, u32[]{:S(2)}, u32[]{:S(2)}) collective-permute-start(bf16[2,4,192,256]{3,2,1,0:T(8,128)(2,1)S(1)} %pad_maximum_fusion.1), channel_id=1, source_target_pairs={{0,4},{1,3},{2,6},{3,1},{4,0},{5,7},{6,2},{7,5},{8,12},{9,11},{10,... | collective-permute-start | bytes 2359304 | tf_op jit(solution)/shard_map/ppermute | solution.py:506
  50.9 27.7 %collective-permute-start.14 = (bf16[4,128,768]{2,1,0:T(8,128)(2,1)S(1)}, bf16[4,128,768]{2,1,0:T(8,128)(2,1)}, u32[]{:S(2)}, u32[]{:S(2)}) collective-permute-start(bf16[4,128,768]{2,1,0:T(8,128)(2,1)S(1)} %pad_maximum_fusion.refs_0_), channel_id=1, source_target_pairs={{0,16},{1,3},{2,18},{3,1},{16,0},{17,19},{18,2},{19,17},{4,20},{5,... | collective-permute-start | bytes 2359304 | tf_op jit(solution)/shard_map/ppermute | solution.py:506
  51.5 28.9 %collective-permute-start.13 = (bf16[4,128,768]{2,1,0:T(8,128)(2,1)S(1)}, bf16[4,128,768]{2,1,0:T(8,128)(2,1)}, u32[]{:S(2)}, u32[]{:S(2)}) collective-permute-start(bf16[4,128,768]{2,1,0:T(8,128)(2,1)S(1)} %pad_maximum_fusion.refs_0_), channel_id=1, source_target_pairs={{0,1},{1,0},{2,3},{3,2},{4,5},{5,4},{6,7},{7,6},{8,9},{9,8},{10,11... | collective-permute-start | bytes 2359304 | tf_op jit(solution)/shard_map/ppermute | solution.py:443
  52.7 24.3 %collective-permute-start.16 = (bf16[2,192,384]{2,1,0:T(8,128)(2,1)S(1)}, bf16[2,192,384]{2,1,0:T(8,128)(2,1)S(1)}, u32[]{:S(2)}, u32[]{:S(2)}) collective-permute-start(bf16[2,192,384]{2,1,0:T(8,128)(2,1)S(1)} %pad_maximum_fusion.8), channel_id=1, source_target_pairs={{0,8},{1,5},{4,12},{5,1},{8,0},{9,13},{12,4},{13,9},{2,10},{3,7},{... | collective-permute-start | bytes 884744 | tf_op jit(solution)/shard_map/ppermute | solution.py:506
  68.1 8.4 %collective-permute-start.12 = (bf16[2,192,256]{2,1,0:T(8,128)(2,1)S(1)}, bf16[2,192,256]{2,1,0:T(8,128)(2,1)S(1)}, u32[]{:S(2)}, u32[]{:S(2)}) collective-permute-start(bf16[2,192,256]{2,1,0:T(8,128)(2,1)S(1)} %get-tuple-element.192), channel_id=1, source_target_pairs={{0,8},{1,5},{4,12},{5,1},{8,0},{9,13},{12,4},{13,9},{2,10},{3,7},{... | collective-permute-start | bytes 589832 | tf_op jit(solution)/shard_map/ppermute | solution.py:506
  69.3 28.1 %collective-permute-start.21 = (bf16[4,128,768]{2,1,0:T(8,128)(2,1)}, bf16[4,128,768]{2,1,0:T(8,128)(2,1)}, u32[]{:S(2)}, u32[]{:S(2)}) collective-permute-start(bf16[4,128,768]{2,1,0:T(8,128)(2,1)} %collective-permute-done.20.refs_1_), channel_id=1, source_target_pairs={{0,16},{1,3},{2,18},{3,1},{16,0},{17,19},{18,2},{19,17},{4,20},{5,... | collective-permute-start | bytes 2359304 | tf_op jit(solution)/shard_map/ppermute | solution.py:506
  76.6 13.4 %collective-permute-start.19 = (bf16[2,192,256]{2,1,0:T(8,128)(2,1)S(1)}, bf16[2,192,256]{2,1,0:T(8,128)(2,1)S(1)}, u32[]{:S(2)}, u32[]{:S(2)}) collective-permute-start(bf16[2,192,256]{2,1,0:T(8,128)(2,1)S(1)} %pad_maximum_fusion.14), channel_id=1, source_target_pairs={{0,4},{1,9},{4,0},{5,13},{8,12},{9,1},{12,8},{13,5},{2,6},{3,11},{... | collective-permute-start | bytes 589832 | tf_op jit(solution)/shard_map/ppermute | solution.py:506
  77.1 10.8 %collective-permute-start.17 = (bf16[2,192,256]{2,1,0:T(8,128)(2,1)}, bf16[2,192,256]{2,1,0:T(8,128)(2,1)S(1)}, u32[]{:S(2)}, u32[]{:S(2)}) collective-permute-start(bf16[2,192,256]{2,1,0:T(8,128)(2,1)} %get-tuple-element.102), channel_id=1, source_target_pairs={{0,4},{1,3},{2,6},{3,1},{4,0},{5,7},{6,2},{7,5},{8,12},{9,11},{10,... | collective-permute-start | bytes 589832 | tf_op jit(solution)/shard_map/ppermute | solution.py:506
  78.7 17.1 %collective-permute-start.25 = (bf16[4,192,384]{2,1,0:T(8,128)(2,1)S(1)}, bf16[4,192,384]{2,1,0:T(8,128)(2,1)S(1)}, u32[]{:S(2)}, u32[]{:S(2)}) collective-permute-start(bf16[4,192,384]{2,1,0:T(8,128)(2,1)S(1)} %pad_maximum_fusion.2.refs_8_), channel_id=1, source_target_pairs={{0,2},{1,17},{2,0},{3,19},{16,18},{17,1},{18,16},{19,3},{4,6},{5,2... | collective-permute-start | bytes 1769480 | tf_op jit(solution)/shard_map/ppermute | solution.py:506
  87.9 7.9 %collective-permute-start.18 = (bf16[2,192,256]{2,1,0:T(8,128)(2,1)S(1)}, bf16[2,192,256]{2,1,0:T(8,128)(2,1)S(1)}, u32[]{:S(2)}, u32[]{:S(2)}) collective-permute-start(bf16[2,192,256]{2,1,0:T(8,128)(2,1)S(1)} %pad_maximum_fusion.15), channel_id=1, source_target_pairs={{0,2},{1,5},{2,0},{3,7},{4,6},{5,1},{6,4},{7,3},{8,10},{9,13},{10,... | collective-permute-start | bytes 589832 | tf_op jit(solution)/shard_map/ppermute | solution.py:506
  88.5 9.9 %collective-permute-start.26 = (bf16[4,192,384]{2,1,0:T(8,128)(2,1)S(1)}, bf16[4,192,384]{2,1,0:T(8,128)(2,1)S(1)}, u32[]{:S(2)}, u32[]{:S(2)}) collective-permute-start(bf16[4,192,384]{2,1,0:T(8,128)(2,1)S(1)} %pad_maximum_fusion.2.refs_8_), channel_id=1, source_target_pairs={{0,16},{1,3},{2,18},{3,1},{16,0},{17,19},{18,2},{19,17},{4,20},{5,... | collective-permute-start | bytes 1769480 | tf_op jit(solution)/shard_map/ppermute | solution.py:506
  90.0 16.3 %collective-permute-start.22 = (bf16[4,128,768]{2,1,0:T(8,128)(2,1)}, bf16[4,128,768]{2,1,0:T(8,128)(2,1)S(1)}, u32[]{:S(2)}, u32[]{:S(2)}) collective-permute-start(bf16[4,128,768]{2,1,0:T(8,128)(2,1)} %collective-permute-done.20.refs_1_), channel_id=1, source_target_pairs={{0,1},{1,0},{2,3},{3,2},{4,5},{5,4},{6,7},{7,6},{8,9},{9,8},{10,11... | collective-permute-start | bytes 2359304 | tf_op jit(solution)/shard_map/ppermute | solution.py:443
  95.8 9.9 %collective-permute-start.27 = (bf16[4,192,384]{2,1,0:T(8,128)(2,1)S(1)}, bf16[4,192,384]{2,1,0:T(8,128)(2,1)S(1)}, u32[]{:S(2)}, u32[]{:S(2)}) collective-permute-start(bf16[4,192,384]{2,1,0:T(8,128)(2,1)S(1)} %collective-permute-done.25.refs_9_), channel_id=1, source_target_pairs={{0,16},{1,3},{2,18},{3,1},{16,0},{17,19},{18,2},{19,17},{4,20},{5,... | collective-permute-start | bytes 1769480 | tf_op jit(solution)/shard_map/ppermute | solution.py:506
  97.4 8.4 %collective-permute-start.28 = (bf16[4,192,384]{2,1,0:T(8,128)(2,1)S(1)}, bf16[4,192,384]{2,1,0:T(8,128)(2,1)S(1)}, u32[]{:S(2)}, u32[]{:S(2)}) collective-permute-start(bf16[4,192,384]{2,1,0:T(8,128)(2,1)S(1)} %pad_maximum_fusion.2.refs_8_), channel_id=1, source_target_pairs={{0,1},{1,0},{2,3},{3,2},{4,5},{5,4},{6,7},{7,6},{8,9},{9,8},{10,11... | collective-permute-start | bytes 1769480 | tf_op jit(solution)/shard_map/ppermute | solution.py:443
  97.4 9.0 %collective-permute-start.23 = (bf16[4,128,768]{2,1,0:T(8,128)(2,1)}, bf16[4,128,768]{2,1,0:T(8,128)(2,1)S(1)}, u32[]{:S(2)}, u32[]{:S(2)}) collective-permute-start(bf16[4,128,768]{2,1,0:T(8,128)(2,1)} %collective-permute-done.14.refs_2_), channel_id=1, source_target_pairs={{0,1},{1,0},{2,3},{3,2},{4,5},{5,4},{6,7},{7,6},{8,9},{9,8},{10,11... | collective-permute-start | bytes 2359304 | tf_op jit(solution)/shard_map/ppermute | solution.py:443
  98.4 8.0 %collective-permute-start.24 = (bf16[4,128,768]{2,1,0:T(8,128)(2,1)}, bf16[4,128,768]{2,1,0:T(8,128)(2,1)S(1)}, u32[]{:S(2)}, u32[]{:S(2)}) collective-permute-start(bf16[4,128,768]{2,1,0:T(8,128)(2,1)} %collective-permute-done.21.refs_3_), channel_id=1, source_target_pairs={{0,1},{1,0},{2,3},{3,2},{4,5},{5,4},{6,7},{7,6},{8,9},{9,8},{10,11... | collective-permute-start | bytes 2359304 | tf_op jit(solution)/shard_map/ppermute | solution.py:443
  145.0 15.5 %collective-permute-start.37 = (bf16[2,2,4,128,768]{4,3,2,1,0:T(8,128)(2,1)}, bf16[2,2,4,128,768]{4,3,2,1,0:T(8,128)(2,1)S(1)}, u32[]{:S(2)}, u32[]{:S(2)}) collective-permute-start(bf16[2,2,4,128,768]{4,3,2,1,0:T(8,128)(2,1)} %inner_give.1), channel_id=1, source_target_pairs={{0,1},{1,0},{2,3},{3,2},{4,5},{5,4},{6,7},{7,6},{8,9},{9,8},{10,11... | collective-permute-start | bytes 9437192 | tf_op jit(solution)/shard_map/ppermute | solution.py:443
  145.0 10.9 %collective-permute-start.36 = (bf16[2,2,4,192,384]{4,3,2,1,0:T(8,128)(2,1)}, bf16[2,2,4,192,384]{4,3,2,1,0:T(8,128)(2,1)}, u32[]{:S(2)}, u32[]{:S(2)}) collective-permute-start(bf16[2,2,4,192,384]{4,3,2,1,0:T(8,128)(2,1)} %outer_give.1), channel_id=1, source_target_pairs={{0,1},{1,0},{2,3},{3,2},{4,5},{5,4},{6,7},{7,6},{8,9},{9,8},{10,11... | collective-permute-start | bytes 7077896 | tf_op jit(solution)/shard_map/ppermute | solution.py:443
  145.5 8.6 %collective-permute-start.32 = (bf16[2,192,256]{2,1,0:T(8,128)(2,1)}, bf16[2,192,256]{2,1,0:T(8,128)(2,1)S(1)}, u32[]{:S(2)}, u32[]{:S(2)}) collective-permute-start(bf16[2,192,256]{2,1,0:T(8,128)(2,1)} %get-tuple-element.124), channel_id=1, source_target_pairs={{0,8},{1,5},{4,12},{5,1},{8,0},{9,13},{12,4},{13,9},{2,10},{3,7},{... | collective-permute-start | bytes 589832 | tf_op jit(solution)/shard_map/ppermute | solution.py:506
  147.1 8.8 %collective-permute-start.35 = (bf16[2,192,256]{2,1,0:T(8,128)(2,1)}, bf16[2,192,256]{2,1,0:T(8,128)(2,1)}, u32[]{:S(2)}, u32[]{:S(2)}) collective-permute-start(bf16[2,192,256]{2,1,0:T(8,128)(2,1)} %pad_maximum_fusion.16), channel_id=1, source_target_pairs={{0,2},{1,5},{2,0},{3,7},{4,6},{5,1},{6,4},{7,3},{8,10},{9,13},{10,... | collective-permute-start | bytes 589832 | tf_op jit(solution)/shard_map/ppermute | solution.py:506
  154.8 13.1 %collective-permute-start.34 = (bf16[2,192,256]{2,1,0:T(8,128)(2,1)}, bf16[2,192,256]{2,1,0:T(8,128)(2,1)S(1)}, u32[]{:S(2)}, u32[]{:S(2)}) collective-permute-start(bf16[2,192,256]{2,1,0:T(8,128)(2,1)} %pad_maximum_fusion.17), channel_id=1, source_target_pairs={{0,4},{1,9},{4,0},{5,13},{8,12},{9,1},{12,8},{13,5},{2,6},{3,11},{... | collective-permute-start | bytes 589832 | tf_op jit(solution)/shard_map/ppermute | solution.py:506
  159.5 30.1 %collective-permute-start.38 = (bf16[2,4,192,384]{3,2,1,0:T(8,128)(2,1)}, bf16[2,4,192,384]{3,2,1,0:T(8,128)(2,1)}, u32[]{:S(2)}, u32[]{:S(2)}) collective-permute-start(bf16[2,4,192,384]{3,2,1,0:T(8,128)(2,1)} %outer_first.1), channel_id=1, source_target_pairs={{0,8},{1,5},{4,12},{5,1},{8,0},{9,13},{12,4},{13,9},{2,10},{3,7},{... | collective-permute-start | bytes 3538952 | tf_op jit(solution)/shard_map/ppermute | solution.py:506
  166.3 36.5 %collective-permute-start.41 = (bf16[2,4,128,768]{3,2,1,0:T(8,128)(2,1)}, bf16[2,4,128,768]{3,2,1,0:T(8,128)(2,1)S(1)}, u32[]{:S(2)}, u32[]{:S(2)}) collective-permute-start(bf16[2,4,128,768]{3,2,1,0:T(8,128)(2,1)} %inner_first.1), channel_id=1, source_target_pairs={{0,16},{1,3},{2,18},{3,1},{16,0},{17,19},{18,2},{19,17},{4,20},{5,... | collective-permute-start | bytes 4718600 | tf_op jit(solution)/shard_map/ppermute | solution.py:506
  196.5 18.7 %collective-permute-start.40 = (bf16[2,4,192,256]{3,2,1,0:T(8,128)(2,1)}, bf16[2,4,192,256]{3,2,1,0:T(8,128)(2,1)}, u32[]{:S(2)}, u32[]{:S(2)}) collective-permute-start(bf16[2,4,192,256]{3,2,1,0:T(8,128)(2,1)} %get-tuple-element.151), channel_id=1, source_target_pairs={{0,4},{1,3},{2,6},{3,1},{4,0},{5,7},{6,2},{7,5},{8,12},{9,11},{10,... | collective-permute-start | bytes 2359304 | tf_op jit(solution)/shard_map/ppermute | solution.py:506
  202.7 26.5 %collective-permute-start.46 = (bf16[4,192,384]{2,1,0:T(8,128)(2,1)}, bf16[4,192,384]{2,1,0:T(8,128)(2,1)}, u32[]{:S(2)}, u32[]{:S(2)}) collective-permute-start(bf16[4,192,384]{2,1,0:T(8,128)(2,1)} %get-tuple-element.167), channel_id=1, source_target_pairs={{0,4},{1,9},{4,0},{5,13},{8,12},{9,1},{12,8},{13,5},{2,6},{3,11},{... | collective-permute-start | bytes 1769480 | tf_op jit(solution)/shard_map/ppermute | solution.py:506
  208.9 24.4 %collective-permute-start.44 = (bf16[4,128,768]{2,1,0:T(8,128)(2,1)}, bf16[4,128,768]{2,1,0:T(8,128)(2,1)}, u32[]{:S(2)}, u32[]{:S(2)}) collective-permute-start(bf16[4,128,768]{2,1,0:T(8,128)(2,1)} %get-tuple-element.163), channel_id=1, source_target_pairs={{0,2},{1,17},{2,0},{3,19},{16,18},{17,1},{18,16},{19,3},{4,6},{5,2... | collective-permute-start | bytes 2359304 | tf_op jit(solution)/shard_map/ppermute | solution.py:506
  216.3 9.1 %collective-permute-start.42 = (bf16[4,192,256]{2,1,0:T(8,128)(2,1)S(1)}, bf16[4,192,256]{2,1,0:T(8,128)(2,1)}, u32[]{:S(2)}, u32[]{:S(2)}) collective-permute-start(bf16[4,192,256]{2,1,0:T(8,128)(2,1)S(1)} %fusion.3), channel_id=1, source_target_pairs={{0,2},{1,5},{2,0},{3,7},{4,6},{5,1},{6,4},{7,3},{8,10},{9,13},{10,... | collective-permute-start | bytes 1179656 | tf_op jit(solution)/shard_map/ppermute | solution.py:506
  220.7 8.4 %collective-permute-start.45 = (bf16[4,96,576]{2,1,0:T(8,128)(2,1)}, bf16[4,96,576]{2,1,0:T(8,128)(2,1)S(1)}, u32[]{:S(2)}, u32[]{:S(2)}) collective-permute-start(bf16[4,96,576]{2,1,0:T(8,128)(2,1)} %get-tuple-element.161), channel_id=1, source_target_pairs={{0,1},{1,0},{2,3},{3,2},{4,5},{5,4},{6,7},{7,6},{8,9},{9,8},{10,11... | collective-permute-start | bytes 1327112 | tf_op jit(solution)/shard_map/ppermute | solution.py:443
  227.0 8.8 %collective-permute-start.43 = (bf16[2,192,256]{2,1,0:T(8,128)(2,1)S(1)}, bf16[2,192,256]{2,1,0:T(8,128)(2,1)S(1)}, u32[]{:S(2)}, u32[]{:S(2)}) collective-permute-start(bf16[2,192,256]{2,1,0:T(8,128)(2,1)S(1)} %slice.328), channel_id=1, source_target_pairs={{0,8},{1,5},{4,12},{5,1},{8,0},{9,13},{12,4},{13,9},{2,10},{3,7},{... | collective-permute-start | bytes 589832 | tf_op jit(solution)/shard_map/ppermute | solution.py:506
  231.4 22.7 %collective-permute-start.50 = (bf16[2,192,384]{2,1,0:T(8,128)(2,1)S(1)}, bf16[2,192,384]{2,1,0:T(8,128)(2,1)S(1)}, u32[]{:S(2)}, u32[]{:S(2)}) collective-permute-start(bf16[2,192,384]{2,1,0:T(8,128)(2,1)S(1)} %slice.332), channel_id=1, source_target_pairs={{0,16},{1,3},{2,18},{3,1},{16,0},{17,19},{18,2},{19,17},{4,20},{5,... | collective-permute-start | bytes 884744 | tf_op jit(solution)/shard_map/ppermute | solution.py:506
  232.0 11.4 %collective-permute-start.48 = (bf16[4,96,576]{2,1,0:T(8,128)(2,1)S(1)}, bf16[4,96,576]{2,1,0:T(8,128)(2,1)S(1)}, u32[]{:S(2)}, u32[]{:S(2)}) collective-permute-start(bf16[4,96,576]{2,1,0:T(8,128)(2,1)S(1)} %get-tuple-element.178), channel_id=1, source_target_pairs={{16,0},{1,17},{18,2},{3,19},{20,4},{5,21},{22,6},{7,23},{24,8},{9,... | collective-permute-start | bytes 1327112 | tf_op jit(solution)/shard_map/ppermute | solution.py:750
  235.8 18.2 %collective-permute-start.51 = (bf16[2,128,768]{2,1,0:T(8,128)(2,1)S(1)}, bf16[2,128,768]{2,1,0:T(8,128)(2,1)S(1)}, u32[]{:S(2)}, u32[]{:S(2)}) collective-permute-start(bf16[2,128,768]{2,1,0:T(8,128)(2,1)S(1)} %slice.334), channel_id=1, source_target_pairs={{0,8},{1,5},{4,12},{5,1},{8,0},{9,13},{12,4},{13,9},{2,10},{3,7},{... | collective-permute-start | bytes 1179656 | tf_op jit(solution)/shard_map/ppermute | solution.py:506
  236.7 20.0 %collective-permute-start.47 = (bf16[2,192,256]{2,1,0:T(8,128)(2,1)S(1)}, bf16[2,192,256]{2,1,0:T(8,128)(2,1)S(1)}, u32[]{:S(2)}, u32[]{:S(2)}) collective-permute-start(bf16[2,192,256]{2,1,0:T(8,128)(2,1)S(1)} %pad_maximum_fusion.18), channel_id=1, source_target_pairs={{0,4},{1,9},{4,0},{5,13},{8,12},{9,1},{12,8},{13,5},{2,6},{3,11},{... | collective-permute-start | bytes 589832 | tf_op jit(solution)/shard_map/ppermute | solution.py:506
  243.6 13.1 %collective-permute-start.49 = (bf16[2,96,576]{2,1,0:T(8,128)(2,1)S(1)}, bf16[2,96,576]{2,1,0:T(8,128)(2,1)S(1)}, u32[]{:S(2)}, u32[]{:S(2)}) collective-permute-start(bf16[2,96,576]{2,1,0:T(8,128)(2,1)S(1)} %slice.389), channel_id=1, source_target_pairs={{0,8},{8,0},{17,25},{25,17},{2,10},{10,2},{19,27},{27,19},{4,12},{... | collective-permute-start | bytes 663560 | tf_op jit(solution)/shard_map/ppermute | solution.py:766
  256.7 8.0 %collective-permute-start.52 = (bf16[96,576]{1,0:T(8,128)(2,1)S(1)}, bf16[96,576]{1,0:T(8,128)(2,1)S(1)}, u32[]{:S(2)}, u32[]{:S(2)}) collective-permute-start(bf16[96,576]{1,0:T(8,128)(2,1)S(1)} %fusion.5), channel_id=1, source_target_pairs={{0,4},{4,0},{17,21},{21,17},{2,6},{6,2},{19,23},{23,19},{8,12},{12... | collective-permute-start | bytes 331784 | tf_op jit(solution)/shard_map/ppermute | solution.py:772
  260.0 7.7 %collective-permute-start.54 = (bf16[128,768]{1,0:T(8,128)(2,1)S(1)}, bf16[128,768]{1,0:T(8,128)(2,1)S(1)}, u32[]{:S(2)}, u32[]{:S(2)}) collective-permute-start(bf16[128,768]{1,0:T(8,128)(2,1)S(1)} %slice_bitcast_fusion.1), channel_id=1, source_target_pairs={{0,4},{1,9},{4,0},{5,13},{8,12},{9,1},{12,8},{13,5},{2,6},{3,11},{... | collective-permute-start | bytes 589832 | tf_op jit(solution)/shard_map/ppermute | solution.py:506
  264.8 7.0 %collective-permute-start.53 = (bf16[96,576]{1,0:T(8,128)(2,1)S(1)}, bf16[96,576]{1,0:T(8,128)(2,1)S(1)}, u32[]{:S(2)}, u32[]{:S(2)}) collective-permute-start(bf16[96,576]{1,0:T(8,128)(2,1)S(1)} %select_convert_fusion.1), channel_id=1, source_target_pairs={{0,1},{1,0},{2,3},{3,2},{4,5},{5,4},{6,7},{7,6},{8,9},{9,8},{10,11... | collective-permute-start | bytes 331784 | tf_op jit(solution)/shard_map/ppermute | solution.py:443
  (49 other events, 315.4 us)

commit v8 on v7

--- a/solution.py
+++ b/solution.py
@@ -283,7 +283,7 @@
     pltpu.make_async_copy(win,win,sems.at[1]).wait()
     pltpu.make_async_copy(woT,woT,sems.at[2]).wait()
     f_s[...]=jnp.zeros_like(f_s)
-    nb=2; bw=ffc//nb
+    nb=1; bw=ffc//nb
     def forward(j,carry):
         sl=pl.ds(pl.multiple_of(j*bw,128),bw)
         inner=mm(hid,win[:,sl])

time: 273 us -> 270 us (0.989)
  Pallas kernels: 95.4 us -> 92.2 us
    pallas_call x1, Pallas kernels: 21.4 us -> 18.2 us  [middle(): pl.pallas_call(middle_kernel, in_specs=[SM] + [VM] * 7 + [HB] * 16, out_s...]
  transfers between devices with their start and end apart: 56 -> 56, of which waited for: 25 -> 25; matrix products, arithmetic and copies ran while one was open for 8% -> 9% of each run, Pallas kernels for 25% -> 25%
where the time goes in v8:
time: 270 us; the launch traced here: 269 us
  Pallas kernels  92.2 us (34%)
  waiting for transfers between devices  78.4 us (29%)
  starting transfers between devices  64.2 us (24%)
  local copies, waits for them, and re-layouts  19.2 us (7%)
  other arithmetic  13.1 us (5%)
    ppermute x36, waiting for transfers between devices, crossed(): return lax.ppermute(value, axes + ('cc',), pairs)  65.5 us
    ppermute x36, starting transfers between devices, crossed(): return lax.ppermute(value, axes + ('cc',), pairs)  48.7 us
    pallas_call x1, Pallas kernels, attend_back(): pl.pallas_call(attend_back_kernel, grid=(count, 4 // QB), in_specs=[pl.Bl...  20.2 us
    pallas_call x1, Pallas kernels, middle(): pl.pallas_call(middle_kernel, in_specs=[SM] + [VM] * 7 + [HB] * 16, out_s...  18.2 us
    pallas_call x2, Pallas kernels, attend(): pl.pallas_call(attend_kernel, grid=(heads,), in_specs=[pl.BlockSpec((HD,...  13.3 us
    pallas_call x2, Pallas kernels, grad_call(): pl.pallas_call(functools.partial(give_kernel, blocks), grid_spec=pltpu.Pr...  10.3 us
    pallas_call x2, Pallas kernels, grad_call(): pl.pallas_call(functools.partial(second_kernel, blocks), grid_spec=pltpu....  9.03 us
    pallas_call x2, Pallas kernels, grad_call(): pl.pallas_call(functools.partial(first_kernel, blocks), grid_spec=pltpu.P...  7.78 us
  transfers between devices with their start and end apart: 56, of which 25 were waited for; matrix products, arithmetic and copies ran while one was open for 9% of the time, Pallas kernels for 25%

profile of v8, /device:TPU:0, one launch (start us, length us, event | category | flops | bytes accessed | tf_op | source)
XLA Modules:
  0.0 269.4 jit_solution(13744253195784055158)
XLA Ops:
  2.2 3.0 %collective-permute-start.6 = (bf16[96,576]{1,0:T(8,128)(2,1)S(1)}, bf16[96,576]{1,0:T(8,128)(2,1)S(1)}, u32[]{:S(2)}, u32[]{:S(2)}) collective-permute-start(bf16[96,576]{1,0:T(8,128)(2,1)S(1)} %pad_maximum_fusion.19), channel_id=1, source_target_pairs={{0,16},{16,0},{1,17},{17,1},{2,18},{18,2},{3,19},{19,3},{4,20},{20... | collective-permute-start | bytes 331784 | tf_op jit(solution)/shard_map/ppermute | solution.py:496
  5.2 1.6 collective-permute-start.15
  6.8 2.7 collective-permute-start
  15.2 4.0 %collective-permute-start.1 = (bf16[2,192,256]{2,1,0:T(8,128)(2,1)S(1)}, bf16[2,192,256]{2,1,0:T(8,128)(2,1)S(1)}, u32[]{:S(2)}, u32[]{:S(2)}) collective-permute-start(bf16[2,192,256]{2,1,0:T(8,128)(2,1)S(1)} %pad_maximum_fusion.12), channel_id=1, source_target_pairs={{0,4},{1,9},{4,0},{5,13},{8,12},{9,1},{12,8},{13,5},{2,6},{3,11},{... | collective-permute-start | bytes 589832 | tf_op jit(solution)/shard_map/ppermute | solution.py:506
  19.4 3.7 %collective-permute-start.3 = (bf16[2,128,768]{2,1,0:T(8,128)(2,1)S(1)}, bf16[2,128,768]{2,1,0:T(8,128)(2,1)S(1)}, u32[]{:S(2)}, u32[]{:S(2)}) collective-permute-start(bf16[2,128,768]{2,1,0:T(8,128)(2,1)S(1)} %pad_maximum_fusion.5), channel_id=1, source_target_pairs={{0,8},{1,5},{4,12},{5,1},{8,0},{9,13},{12,4},{13,9},{2,10},{3,7},{... | collective-permute-start | bytes 1179656 | tf_op jit(solution)/shard_map/ppermute | solution.py:506
  24.0 4.4 %collective-permute-done.1 = bf16[2,192,256]{2,1,0:T(8,128)(2,1)S(1)} collective-permute-done((bf16[2,192,256]{2,1,0:T(8,128)(2,1)S(1)}, bf16[2,192,256]{2,1,0:T(8,128)(2,1)S(1)}, u32[]{:S(2)}, u32[]{:S(2)}) %collective-permute-start.1) | collective-permute-done | bytes 196640 | tf_op jit(solution)/shard_map/ppermute | solution.py:506
  28.5 1.6 collective-permute-start.4
  30.1 8.2 %collective-permute-done.8 = bf16[2,96,576]{2,1,0:T(8,128)(2,1)S(1)} collective-permute-done((bf16[2,96,576]{2,1,0:T(8,128)(2,1)S(1)}, bf16[2,96,576]{2,1,0:T(8,128)(2,1)S(1)}, u32[]{:S(2)}, u32[]{:S(2)}) %collective-permute-start.8) | collective-permute-done | bytes 221216 | tf_op jit(solution)/shard_map/ppermute | solution.py:506
  38.3 4.0 %collective-permute-start.9 = (bf16[2,96,576]{2,1,0:T(8,128)(2,1)S(1)}, bf16[2,96,576]{2,1,0:T(8,128)(2,1)S(1)}, u32[]{:S(2)}, u32[]{:S(2)}) collective-permute-start(bf16[2,96,576]{2,1,0:T(8,128)(2,1)S(1)} %pad_maximum_fusion.11), channel_id=1, source_target_pairs={{0,4},{1,9},{4,0},{5,13},{8,12},{9,1},{12,8},{13,5},{2,6},{3,11},{... | collective-permute-start | bytes 663560 | tf_op jit(solution)/shard_map/ppermute | solution.py:506
  42.4 1.6 collective-permute-start.20
  44.1 3.9 %collective-permute-done.9 = bf16[2,96,576]{2,1,0:T(8,128)(2,1)S(1)} collective-permute-done((bf16[2,96,576]{2,1,0:T(8,128)(2,1)S(1)}, bf16[2,96,576]{2,1,0:T(8,128)(2,1)S(1)}, u32[]{:S(2)}, u32[]{:S(2)}) %collective-permute-start.9) | collective-permute-done | bytes 221216 | tf_op jit(solution)/shard_map/ppermute | solution.py:506
  52.7 3.0 %collective-permute-start.16 = (bf16[2,192,384]{2,1,0:T(8,128)(2,1)S(1)}, bf16[2,192,384]{2,1,0:T(8,128)(2,1)S(1)}, u32[]{:S(2)}, u32[]{:S(2)}) collective-permute-start(bf16[2,192,384]{2,1,0:T(8,128)(2,1)S(1)} %pad_maximum_fusion.8), channel_id=1, source_target_pairs={{0,8},{1,5},{4,12},{5,1},{8,0},{9,13},{12,4},{13,9},{2,10},{3,7},{... | collective-permute-start | bytes 884744 | tf_op jit(solution)/shard_map/ppermute | solution.py:506
  55.7 4.1 %collective-permute-done.5.xc = bf16[2,4,192,256]{3,2,1,0:T(8,128)(2,1)} collective-permute-done((bf16[2,4,192,256]{3,2,1,0:T(8,128)(2,1)S(1)}, bf16[2,4,192,256]{3,2,1,0:T(8,128)(2,1)}, u32[]{:S(2)}, u32[]{:S(2)}) %collective-permute-start.5) | collective-permute-done | bytes 786464 | tf_op jit(solution)/shard_map/ppermute | solution.py:506
  59.8 4.0 %qkv.1 = (bf16[192,1024]{1,0:T(8,128)(2,1)}, bf16[384,1024]{1,0:T(8,128)(2,1)}) custom-call(s32[8]{0:T(128)} %stack.140.info, bf16[4,192,256]{2,1,0:T(8,128)(2,1)} %copy-done.2, bf16[4,192,256]{2,1,0:T(8,128)(2,1)} %copy-done.4, bf16[2,4,192,256]{3,2,1,0:T(8,128)(2,1)} %collective-permute-done.5.xc, bf16[4,96,576]{2,1,0:T(8,128)(2,1)} %copy-done.1, ...), custom_call_target="tpu_custom_call" | custom-call | tf_op jit(solution)/shard_map/qkv/pallas_call | solution.py:182
  63.8 3.2 %collective-permute-start.11 = (bf16[384,1024]{1,0:T(8,128)(2,1)}, bf16[384,1024]{1,0:T(8,128)(2,1)}, u32[]{:S(2)}, u32[]{:S(2)}) collective-permute-start(bf16[384,1024]{1,0:T(8,128)(2,1)} %get-tuple-element.101.ko_ref.vo_ref), channel_id=1, source_target_pairs={{0,1},{1,0},{2,3},{3,2},{4,5},{5,4},{6,7},{7,6},{8,9},{9,8},{10,11... | collective-permute-start | bytes 2359304 | tf_op jit(solution)/shard_map/ppermute | solution.py:443
  69.9 6.6 %attend.2 = (f32[192,512]{1,0:T(8,128)}, f32[3,1,512]{2,1,0:T(1,128)}, bf16[2,192,256]{2,1,0:T(8,128)(2,1)}) custom-call(bf16[192,1024]{1,0:T(8,128)(2,1)} %get-tuple-element.140.q_ref, bf16[384,1024]{1,0:T(8,128)(2,1)} %get-tuple-element.101.ko_ref.vo_ref, bf16[384,1024]{1,0:T(8,128)(2,1)} %get-tuple-element.101.ko_ref.vo_ref, ...), custom_call_target="tpu_custom_call" | custom-call | flops 19327352832 | bytes 25165824 | tf_op jit(solution)/shard_map/attend/pallas_call | solution.py:66
  77.1 1.6 collective-permute-start.17
  78.7 1.6 collective-permute-start.25
  80.3 6.6 %attend.3 = (f32[192,512]{1,0:T(8,128)}, f32[3,1,512]{2,1,0:T(1,128)}, bf16[2,192,256]{2,1,0:T(8,128)(2,1)}) custom-call(bf16[192,1024]{1,0:T(8,128)(2,1)} %get-tuple-element.140.q_ref, bf16[384,1024]{1,0:T(8,128)(2,1)} %get-tuple-element.101.ko_ref.vo_ref, bf16[384,1024]{1,0:T(8,128)(2,1)} %get-tuple-element.101.ko_ref.vo_ref, ...), custom_call_target="tpu_custom_call" | custom-call | flops 19327352832 | bytes 25165824 | tf_op jit(solution)/shard_map/attend/pallas_call | solution.py:66
  90.0 5.8 %collective-permute-done.18.a2 = bf16[2,192,256]{2,1,0:T(8,128)(2,1)S(1)} collective-permute-done((bf16[2,192,256]{2,1,0:T(8,128)(2,1)S(1)}, bf16[2,192,256]{2,1,0:T(8,128)(2,1)S(1)}, u32[]{:S(2)}, u32[]{:S(2)}) %collective-permute-start.18) | collective-permute-done | bytes 196640 | tf_op jit(solution)/shard_map/ppermute | solution.py:506
  95.8 1.5 collective-permute-start.27
  98.4 7.4 %collective-permute-done.27.refs_11_ = bf16[4,192,384]{2,1,0:T(8,128)(2,1)S(1)} collective-permute-done((bf16[4,192,384]{2,1,0:T(8,128)(2,1)S(1)}, bf16[4,192,384]{2,1,0:T(8,128)(2,1)S(1)}, u32[]{:S(2)}, u32[]{:S(2)}) %collective-permute-start.27) | collective-permute-done | bytes 589856 | tf_op jit(solution)/shard_map/ppermute | solution.py:506
  110.3 18.2 %middle.1 = (bf16[2,192,256]{2,1,0:T(8,128)(2,1)}, bf16[2,192,256]{2,1,0:T(8,128)(2,1)}, bf16[2,192,256]{2,1,0:T(8,128)(2,1)}, bf16[2,192,256]{2,1,0:T(8,128)(2,...) custom-call(s32[8]{0:T(128)} %stack.140.info, ...), custom_call_target="tpu_custom_call" | custom-call | flops 86973087744 | bytes 339738624 | tf_op jit(solution)/shard_map/middle/pallas_call | solution.py:344
  129.9 4.7 %outer_give.1 = bf16[2,2,4,192,384]{4,3,2,1,0:T(8,128)(2,1)} custom-call(s32[8]{0:T(128)} %stack.140.info, bf16[768,256]{1,0:T(8,128)(2,1)} %get-tuple-element.152.refs_0_, bf16[256,3072]{1,0:T(8,128)(2,1)} %get-tuple-element.127.refs_1_.refs_2_, bf16[256,3072]{1,0:T(8,128)(2,1)} %get-tuple-element.127.refs_1_.refs_2_), custom_call_target="tpu_custom_call" | custom-call | flops 3623878656 | bytes 14155777 | tf_op jit(solution)/shard_map/outer_give/pallas_call | solution.py:429
  136.1 5.7 %inner_give.1 = bf16[2,2,4,128,768]{4,3,2,1,0:T(8,128)(2,1)} custom-call(s32[8]{0:T(128)} %stack.140.info, bf16[768,256]{1,0:T(8,128)(2,1)} %get-tuple-element.155.refs_0_, bf16[256,3072]{1,0:T(8,128)(2,1)} %get-tuple-element.132.refs_1_, bf16[768,256]{1,0:T(8,128)(2,1)} %get-tuple-element.133.refs_2_, bf16[4,256,256]{2,1,0:T(8,128)(2,1)} %get-tuple-element.134.refs_3_, ...), custom_call_target="tpu_custom_call" | custom-call | flops 3623878656 | bytes 9437185 | tf_op jit(solution)/shard_map/inner_give/pallas_call | solution.py:429
  142.3 1.7 collective-permute-start.32
  144.5 6.4 %collective-permute-done.32 = bf16[2,192,256]{2,1,0:T(8,128)(2,1)S(1)} collective-permute-done((bf16[2,192,256]{2,1,0:T(8,128)(2,1)}, bf16[2,192,256]{2,1,0:T(8,128)(2,1)S(1)}, u32[]{:S(2)}, u32[]{:S(2)}) %collective-permute-start.32) | collective-permute-done | bytes 196640 | tf_op jit(solution)/shard_map/ppermute | solution.py:506
  152.7 3.6 %outer_first.1 = bf16[2,4,192,384]{3,2,1,0:T(8,128)(2,1)} custom-call(s32[8]{0:T(128)} %stack.140.info, bf16[768,256]{1,0:T(8,128)(2,1)} %get-tuple-element.152.refs_0_, bf16[256,3072]{1,0:T(8,128)(2,1)} %get-tuple-element.127.refs_1_.refs_2_, bf16[256,3072]{1,0:T(8,128)(2,1)} %get-tuple-element.127.refs_1_.refs_2_, ...), custom_call_target="tpu_custom_call" | custom-call | flops 1811939328 | bytes 7077889 | tf_op jit(solution)/shard_map/outer_first/pallas_call | solution.py:434
  157.3 1.7 copy-done
  159.0 4.1 %inner_first.1 = bf16[2,4,128,768]{3,2,1,0:T(8,128)(2,1)} custom-call(s32[8]{0:T(128)} %stack.140.info, bf16[768,256]{1,0:T(8,128)(2,1)} %get-tuple-element.155.refs_0_, bf16[256,3072]{1,0:T(8,128)(2,1)} %get-tuple-element.132.refs_1_, bf16[768,256]{1,0:T(8,128)(2,1)} %get-tuple-element.133.refs_2_, bf16[4,256,256]{2,1,0:T(8,128)(2,1)} %get-tuple-element.134.refs_3_, ...), custom_call_target="tpu_custom_call" | custom-call | flops 1811939328 | bytes 4718593 | tf_op jit(solution)/shard_map/inner_first/pallas_call | solution.py:434
  164.6 20.2 %attend_back.1 = (bf16[192,1024]{1,0:T(8,128)(2,1)}, f32[3,1024,128]{2,1,0:T(8,128)}, bf16[3,1024,128]{2,1,0:T(8,128)(2,1)}) custom-call(bf16[192,1024]{1,0:T(8,128)(2,1)} %get-tuple-element.140.q_ref, bf16[384,1024]{1,0:T(8,128)(2,1)} %get-tuple-element.101.ko_ref.vo_ref, bf16[384,1024]{1,0:T(8,128)(2,1)} %get-tuple-element.101.ko_ref.vo_ref, ...), custom_call_target="tpu_custom_call" | custom-call | flops 96636764160 | bytes 150994944 | tf_op jit(solution)/shard_map/attend_back/pallas_call | solution.py:119
  188.2 5.1 %finish_dx.1 = (f32[2,4,192,256]{3,2,1,0:T(8,128)}, bf16[2,4,192,256]{3,2,1,0:T(8,128)(2,1)}, bf16[576,1024]{1,0:T(8,128)(2,1)}) custom-call(s32[8]{0:T(128)} %stack.140.info, bf16[192,1024]{1,0:T(8,128)(2,1)} %get-tuple-element.145.refs_0_, f32[3,1024,128]{2,1,0:T(8,128)} %get-tuple-element.148.refs_1_, bf16[3,1024,128]{2,1,0:T(8,128)(2,1)} %copy-done.8, ...), custom_call_target="tpu_custom_call" | custom-call | flops 1 | bytes 1 | tf_op jit(solution)/shard_map/finish_dx/pallas_call | solution.py:205
  193.3 2.0 collective-permute-start.40
  195.4 4.2 %outer_second.1 = (bf16[4,192,384]{2,1,0:T(8,128)(2,1)}, bf16[4,192,384]{2,1,0:T(8,128)(2,1)}) custom-call(s32[8]{0:T(128)} %stack.140.info, bf16[768,256]{1,0:T(8,128)(2,1)} %get-tuple-element.152.refs_0_, bf16[256,3072]{1,0:T(8,128)(2,1)} %get-tuple-element.127.refs_1_.refs_2_, bf16[256,3072]{1,0:T(8,128)(2,1)} %get-tuple-element.127.refs_1_.refs_2_, ...), custom_call_target="tpu_custom_call" | custom-call | flops 1 | bytes 1 | tf_op jit(solution)/shard_map/outer_second/pallas_call | solution.py:438
  200.8 4.9 %inner_second.1 = (bf16[4,128,768]{2,1,0:T(8,128)(2,1)}, bf16[4,128,768]{2,1,0:T(8,128)(2,1)}) custom-call(s32[8]{0:T(128)} %stack.140.info, bf16[768,256]{1,0:T(8,128)(2,1)} %get-tuple-element.155.refs_0_, bf16[256,3072]{1,0:T(8,128)(2,1)} %get-tuple-element.132.refs_1_, bf16[768,256]{1,0:T(8,128)(2,1)} %get-tuple-element.133.refs_2_, ...), custom_call_target="tpu_custom_call" | custom-call | flops 1 | bytes 1 | tf_op jit(solution)/shard_map/inner_second/pallas_call | solution.py:438
  206.1 5.7 %collective-permute-done.40 = bf16[2,4,192,256]{3,2,1,0:T(8,128)(2,1)} collective-permute-done((bf16[2,4,192,256]{3,2,1,0:T(8,128)(2,1)}, bf16[2,4,192,256]{3,2,1,0:T(8,128)(2,1)}, u32[]{:S(2)}, u32[]{:S(2)}) %collective-permute-start.40) | collective-permute-done | bytes 786464 | tf_op jit(solution)/shard_map/ppermute | solution.py:506
  213.0 4.4 %finish_dw.1 = (f32[4,96,576]{2,1,0:T(8,128)}, bf16[4,96,576]{2,1,0:T(8,128)(2,1)}) custom-call(s32[8]{0:T(128)} %stack.140.info, bf16[576,1024]{1,0:T(8,128)(2,1)} %get-tuple-element.160.p_ref, bf16[4,192,256]{2,1,0:T(8,128)(2,1)} %copy-done.2, bf16[4,192,256]{2,1,0:T(8,128)(2,1)} %copy-done.4, bf16[2,4,192,256]{3,2,1,0:T(8,128)(2,1)} %collective-permute-done.5.xc), custom_call_target="tpu_custom_call" | custom-call | flops 5435817984 | bytes 18874368 | tf_op jit(solution)/shard_map/finish_dw/pallas_call | solution.py:224
  217.4 4.8 %collective-permute-done.42 = bf16[4,192,256]{2,1,0:T(8,128)(2,1)} collective-permute-done((bf16[4,192,256]{2,1,0:T(8,128)(2,1)S(1)}, bf16[4,192,256]{2,1,0:T(8,128)(2,1)}, u32[]{:S(2)}, u32[]{:S(2)}) %collective-permute-start.42) | collective-permute-done | bytes 393248 | tf_op jit(solution)/shard_map/ppermute | solution.py:506
  222.2 1.6 fusion.1
  223.8 2.0 collective-permute-start.43
  233.5 2.1 collective-permute-start.47
  235.6 4.7 %collective-permute-done.48 = bf16[4,96,576]{2,1,0:T(8,128)(2,1)S(1)} collective-permute-done((bf16[4,96,576]{2,1,0:T(8,128)(2,1)S(1)}, bf16[4,96,576]{2,1,0:T(8,128)(2,1)S(1)}, u32[]{:S(2)}, u32[]{:S(2)}) %collective-permute-start.48) | collective-permute-done | bytes 442400 | tf_op jit(solution)/shard_map/ppermute | solution.py:750
  240.3 2.9 %collective-permute-start.49 = (bf16[2,96,576]{2,1,0:T(8,128)(2,1)S(1)}, bf16[2,96,576]{2,1,0:T(8,128)(2,1)S(1)}, u32[]{:S(2)}, u32[]{:S(2)}) collective-permute-start(bf16[2,96,576]{2,1,0:T(8,128)(2,1)S(1)} %slice.389), channel_id=1, source_target_pairs={{0,8},{8,0},{17,25},{25,17},{2,10},{10,2},{19,27},{27,19},{4,12},{... | collective-permute-start | bytes 663560 | tf_op jit(solution)/shard_map/ppermute | solution.py:766
  243.2 7.6 %collective-permute-done.51 = bf16[2,128,768]{2,1,0:T(8,128)(2,1)S(1)} collective-permute-done((bf16[2,128,768]{2,1,0:T(8,128)(2,1)S(1)}, bf16[2,128,768]{2,1,0:T(8,128)(2,1)S(1)}, u32[]{:S(2)}, u32[]{:S(2)}) %collective-permute-start.51) | collective-permute-done | bytes 393248 | tf_op jit(solution)/shard_map/ppermute | solution.py:506
  251.0 2.4 collective-permute-done.49
  253.5 1.9 collective-permute-start.52
  256.8 2.1 collective-permute-start.54
  262.4 2.1 collective-permute-done.54
  (273 shorter events, 56.4 us)
Async XLA Ops:
  2.2 12.0 %collective-permute-start.6 = (bf16[96,576]{1,0:T(8,128)(2,1)S(1)}, bf16[96,576]{1,0:T(8,128)(2,1)S(1)}, u32[]{:S(2)}, u32[]{:S(2)}) collective-permute-start(bf16[96,576]{1,0:T(8,128)(2,1)S(1)} %pad_maximum_fusion.19), channel_id=1, source_target_pairs={{0,16},{16,0},{1,17},{17,1},{2,18},{18,2},{3,19},{19,3},{4,20},{20... | collective-permute-start | bytes 331784 | tf_op jit(solution)/shard_map/ppermute | solution.py:496
  5.2 46.2 %collective-permute-start.15 = (bf16[192,384]{1,0:T(8,128)(2,1)S(1)}, bf16[192,384]{1,0:T(8,128)(2,1)S(1)}, u32[]{:S(2)}, u32[]{:S(2)}) collective-permute-start(bf16[192,384]{1,0:T(8,128)(2,1)S(1)} %bitcast.133), channel_id=1, source_target_pairs={{0,4},{1,9},{4,0},{5,13},{8,12},{9,1},{12,8},{13,5},{2,6},{3,11},{... | collective-permute-start | bytes 442376 | tf_op jit(solution)/shard_map/ppermute | solution.py:506
  6.8 8.3 %collective-permute-start = (bf16[2,192,256]{2,1,0:T(8,128)(2,1)S(1)}, bf16[2,192,256]{2,1,0:T(8,128)(2,1)S(1)}, u32[]{:S(2)}, u32[]{:S(2)}) collective-permute-start(bf16[2,192,256]{2,1,0:T(8,128)(2,1)S(1)} %slice_bitcast_fusion.5), channel_id=1, source_target_pairs={{0,8},{1,5},{4,12},{5,1},{8,0},{9,13},{12,4},{13,9},{2,10},{3,7},{... | collective-permute-start | bytes 589832 | tf_op jit(solution)/shard_map/ppermute | solution.py:506
  10.0 9.4 %collective-permute-start.2 = (bf16[128,768]{1,0:T(8,128)(2,1)S(1)}, bf16[128,768]{1,0:T(8,128)(2,1)S(1)}, u32[]{:S(2)}, u32[]{:S(2)}) collective-permute-start(bf16[128,768]{1,0:T(8,128)(2,1)S(1)} %get-tuple-element.216), channel_id=1, source_target_pairs={{0,4},{1,9},{4,0},{5,13},{8,12},{9,1},{12,8},{13,5},{2,6},{3,11},{... | collective-permute-start | bytes 589832 | tf_op jit(solution)/shard_map/ppermute | solution.py:506
  14.3 9.4 %collective-permute-start.7 = (bf16[96,576]{1,0:T(8,128)(2,1)S(1)}, bf16[96,576]{1,0:T(8,128)(2,1)S(1)}, u32[]{:S(2)}, u32[]{:S(2)}) collective-permute-start(bf16[96,576]{1,0:T(8,128)(2,1)S(1)} %broadcast_select_fusion), channel_id=1, source_target_pairs={{0,1},{1,0},{2,3},{3,2},{4,5},{5,4},{6,7},{7,6},{8,9},{9,8},{10,11... | collective-permute-start | bytes 331784 | tf_op jit(solution)/shard_map/ppermute | solution.py:443
  15.2 13.2 %collective-permute-start.1 = (bf16[2,192,256]{2,1,0:T(8,128)(2,1)S(1)}, bf16[2,192,256]{2,1,0:T(8,128)(2,1)S(1)}, u32[]{:S(2)}, u32[]{:S(2)}) collective-permute-start(bf16[2,192,256]{2,1,0:T(8,128)(2,1)S(1)} %pad_maximum_fusion.12), channel_id=1, source_target_pairs={{0,4},{1,9},{4,0},{5,13},{8,12},{9,1},{12,8},{13,5},{2,6},{3,11},{... | collective-permute-start | bytes 589832 | tf_op jit(solution)/shard_map/ppermute | solution.py:506
  19.4 22.9 %collective-permute-start.3 = (bf16[2,128,768]{2,1,0:T(8,128)(2,1)S(1)}, bf16[2,128,768]{2,1,0:T(8,128)(2,1)S(1)}, u32[]{:S(2)}, u32[]{:S(2)}) collective-permute-start(bf16[2,128,768]{2,1,0:T(8,128)(2,1)S(1)} %pad_maximum_fusion.5), channel_id=1, source_target_pairs={{0,8},{1,5},{4,12},{5,1},{8,0},{9,13},{12,4},{13,9},{2,10},{3,7},{... | collective-permute-start | bytes 1179656 | tf_op jit(solution)/shard_map/ppermute | solution.py:506
  23.9 14.3 %collective-permute-start.8 = (bf16[2,96,576]{2,1,0:T(8,128)(2,1)S(1)}, bf16[2,96,576]{2,1,0:T(8,128)(2,1)S(1)}, u32[]{:S(2)}, u32[]{:S(2)}) collective-permute-start(bf16[2,96,576]{2,1,0:T(8,128)(2,1)S(1)} %pad_maximum_fusion.10), channel_id=1, source_target_pairs={{0,8},{1,5},{4,12},{5,1},{8,0},{9,13},{12,4},{13,9},{2,10},{3,7},{... | collective-permute-start | bytes 663560 | tf_op jit(solution)/shard_map/ppermute | solution.py:506
  28.5 15.5 %collective-permute-start.4 = (bf16[4,192,256]{2,1,0:T(8,128)(2,1)S(1)}, bf16[4,192,256]{2,1,0:T(8,128)(2,1)S(1)}, u32[]{:S(2)}, u32[]{:S(2)}) collective-permute-start(bf16[4,192,256]{2,1,0:T(8,128)(2,1)S(1)} %pad_maximum_fusion.4.xa.x_ref), channel_id=1, source_target_pairs={{0,2},{1,5},{2,0},{3,7},{4,6},{5,1},{6,4},{7,3},{8,10},{9,13},{10,... | collective-permute-start | bytes 1179656 | tf_op jit(solution)/shard_map/ppermute | solution.py:506
  38.3 9.8 %collective-permute-start.9 = (bf16[2,96,576]{2,1,0:T(8,128)(2,1)S(1)}, bf16[2,96,576]{2,1,0:T(8,128)(2,1)S(1)}, u32[]{:S(2)}, u32[]{:S(2)}) collective-permute-start(bf16[2,96,576]{2,1,0:T(8,128)(2,1)S(1)} %pad_maximum_fusion.11), channel_id=1, source_target_pairs={{0,4},{1,9},{4,0},{5,13},{8,12},{9,1},{12,8},{13,5},{2,6},{3,11},{... | collective-permute-start | bytes 663560 | tf_op jit(solution)/shard_map/ppermute | solution.py:506
  42.4 24.8 %collective-permute-start.20 = (bf16[4,128,768]{2,1,0:T(8,128)(2,1)S(1)}, bf16[4,128,768]{2,1,0:T(8,128)(2,1)}, u32[]{:S(2)}, u32[]{:S(2)}) collective-permute-start(bf16[4,128,768]{2,1,0:T(8,128)(2,1)S(1)} %pad_maximum_fusion.refs_0_), channel_id=1, source_target_pairs={{0,2},{1,17},{2,0},{3,19},{16,18},{17,1},{18,16},{19,3},{4,6},{5,2... | collective-permute-start | bytes 2359304 | tf_op jit(solution)/shard_map/ppermute | solution.py:506
  44.1 15.8 %collective-permute-start.5 = (bf16[2,4,192,256]{3,2,1,0:T(8,128)(2,1)S(1)}, bf16[2,4,192,256]{3,2,1,0:T(8,128)(2,1)}, u32[]{:S(2)}, u32[]{:S(2)}) collective-permute-start(bf16[2,4,192,256]{3,2,1,0:T(8,128)(2,1)S(1)} %pad_maximum_fusion.1), channel_id=1, source_target_pairs={{0,4},{1,3},{2,6},{3,1},{4,0},{5,7},{6,2},{7,5},{8,12},{9,11},{10,... | collective-permute-start | bytes 2359304 | tf_op jit(solution)/shard_map/ppermute | solution.py:506
  50.9 27.7 %collective-permute-start.14 = (bf16[4,128,768]{2,1,0:T(8,128)(2,1)S(1)}, bf16[4,128,768]{2,1,0:T(8,128)(2,1)}, u32[]{:S(2)}, u32[]{:S(2)}) collective-permute-start(bf16[4,128,768]{2,1,0:T(8,128)(2,1)S(1)} %pad_maximum_fusion.refs_0_), channel_id=1, source_target_pairs={{0,16},{1,3},{2,18},{3,1},{16,0},{17,19},{18,2},{19,17},{4,20},{5,... | collective-permute-start | bytes 2359304 | tf_op jit(solution)/shard_map/ppermute | solution.py:506
  51.5 28.9 %collective-permute-start.13 = (bf16[4,128,768]{2,1,0:T(8,128)(2,1)S(1)}, bf16[4,128,768]{2,1,0:T(8,128)(2,1)}, u32[]{:S(2)}, u32[]{:S(2)}) collective-permute-start(bf16[4,128,768]{2,1,0:T(8,128)(2,1)S(1)} %pad_maximum_fusion.refs_0_), channel_id=1, source_target_pairs={{0,1},{1,0},{2,3},{3,2},{4,5},{5,4},{6,7},{7,6},{8,9},{9,8},{10,11... | collective-permute-start | bytes 2359304 | tf_op jit(solution)/shard_map/ppermute | solution.py:443
  52.7 24.3 %collective-permute-start.16 = (bf16[2,192,384]{2,1,0:T(8,128)(2,1)S(1)}, bf16[2,192,384]{2,1,0:T(8,128)(2,1)S(1)}, u32[]{:S(2)}, u32[]{:S(2)}) collective-permute-start(bf16[2,192,384]{2,1,0:T(8,128)(2,1)S(1)} %pad_maximum_fusion.8), channel_id=1, source_target_pairs={{0,8},{1,5},{4,12},{5,1},{8,0},{9,13},{12,4},{13,9},{2,10},{3,7},{... | collective-permute-start | bytes 884744 | tf_op jit(solution)/shard_map/ppermute | solution.py:506
  68.1 8.4 %collective-permute-start.12 = (bf16[2,192,256]{2,1,0:T(8,128)(2,1)S(1)}, bf16[2,192,256]{2,1,0:T(8,128)(2,1)S(1)}, u32[]{:S(2)}, u32[]{:S(2)}) collective-permute-start(bf16[2,192,256]{2,1,0:T(8,128)(2,1)S(1)} %get-tuple-element.192), channel_id=1, source_target_pairs={{0,8},{1,5},{4,12},{5,1},{8,0},{9,13},{12,4},{13,9},{2,10},{3,7},{... | collective-permute-start | bytes 589832 | tf_op jit(solution)/shard_map/ppermute | solution.py:506
  69.3 28.1 %collective-permute-start.21 = (bf16[4,128,768]{2,1,0:T(8,128)(2,1)}, bf16[4,128,768]{2,1,0:T(8,128)(2,1)}, u32[]{:S(2)}, u32[]{:S(2)}) collective-permute-start(bf16[4,128,768]{2,1,0:T(8,128)(2,1)} %collective-permute-done.20.refs_1_), channel_id=1, source_target_pairs={{0,16},{1,3},{2,18},{3,1},{16,0},{17,19},{18,2},{19,17},{4,20},{5,... | collective-permute-start | bytes 2359304 | tf_op jit(solution)/shard_map/ppermute | solution.py:506
  76.6 13.4 %collective-permute-start.19 = (bf16[2,192,256]{2,1,0:T(8,128)(2,1)S(1)}, bf16[2,192,256]{2,1,0:T(8,128)(2,1)S(1)}, u32[]{:S(2)}, u32[]{:S(2)}) collective-permute-start(bf16[2,192,256]{2,1,0:T(8,128)(2,1)S(1)} %pad_maximum_fusion.14), channel_id=1, source_target_pairs={{0,4},{1,9},{4,0},{5,13},{8,12},{9,1},{12,8},{13,5},{2,6},{3,11},{... | collective-permute-start | bytes 589832 | tf_op jit(solution)/shard_map/ppermute | solution.py:506
  77.1 10.8 %collective-permute-start.17 = (bf16[2,192,256]{2,1,0:T(8,128)(2,1)}, bf16[2,192,256]{2,1,0:T(8,128)(2,1)S(1)}, u32[]{:S(2)}, u32[]{:S(2)}) collective-permute-start(bf16[2,192,256]{2,1,0:T(8,128)(2,1)} %get-tuple-element.102), channel_id=1, source_target_pairs={{0,4},{1,3},{2,6},{3,1},{4,0},{5,7},{6,2},{7,5},{8,12},{9,11},{10,... | collective-permute-start | bytes 589832 | tf_op jit(solution)/shard_map/ppermute | solution.py:506
  78.7 17.1 %collective-permute-start.25 = (bf16[4,192,384]{2,1,0:T(8,128)(2,1)S(1)}, bf16[4,192,384]{2,1,0:T(8,128)(2,1)S(1)}, u32[]{:S(2)}, u32[]{:S(2)}) collective-permute-start(bf16[4,192,384]{2,1,0:T(8,128)(2,1)S(1)} %pad_maximum_fusion.2.refs_8_), channel_id=1, source_target_pairs={{0,2},{1,17},{2,0},{3,19},{16,18},{17,1},{18,16},{19,3},{4,6},{5,2... | collective-permute-start | bytes 1769480 | tf_op jit(solution)/shard_map/ppermute | solution.py:506
  87.9 7.9 %collective-permute-start.18 = (bf16[2,192,256]{2,1,0:T(8,128)(2,1)S(1)}, bf16[2,192,256]{2,1,0:T(8,128)(2,1)S(1)}, u32[]{:S(2)}, u32[]{:S(2)}) collective-permute-start(bf16[2,192,256]{2,1,0:T(8,128)(2,1)S(1)} %pad_maximum_fusion.15), channel_id=1, source_target_pairs={{0,2},{1,5},{2,0},{3,7},{4,6},{5,1},{6,4},{7,3},{8,10},{9,13},{10,... | collective-permute-start | bytes 589832 | tf_op jit(solution)/shard_map/ppermute | solution.py:506
  88.5 9.9 %collective-permute-start.26 = (bf16[4,192,384]{2,1,0:T(8,128)(2,1)S(1)}, bf16[4,192,384]{2,1,0:T(8,128)(2,1)S(1)}, u32[]{:S(2)}, u32[]{:S(2)}) collective-permute-start(bf16[4,192,384]{2,1,0:T(8,128)(2,1)S(1)} %pad_maximum_fusion.2.refs_8_), channel_id=1, source_target_pairs={{0,16},{1,3},{2,18},{3,1},{16,0},{17,19},{18,2},{19,17},{4,20},{5,... | collective-permute-start | bytes 1769480 | tf_op jit(solution)/shard_map/ppermute | solution.py:506
  90.0 16.3 %collective-permute-start.22 = (bf16[4,128,768]{2,1,0:T(8,128)(2,1)}, bf16[4,128,768]{2,1,0:T(8,128)(2,1)S(1)}, u32[]{:S(2)}, u32[]{:S(2)}) collective-permute-start(bf16[4,128,768]{2,1,0:T(8,128)(2,1)} %collective-permute-done.20.refs_1_), channel_id=1, source_target_pairs={{0,1},{1,0},{2,3},{3,2},{4,5},{5,4},{6,7},{7,6},{8,9},{9,8},{10,11... | collective-permute-start | bytes 2359304 | tf_op jit(solution)/shard_map/ppermute | solution.py:443
  95.8 9.9 %collective-permute-start.27 = (bf16[4,192,384]{2,1,0:T(8,128)(2,1)S(1)}, bf16[4,192,384]{2,1,0:T(8,128)(2,1)S(1)}, u32[]{:S(2)}, u32[]{:S(2)}) collective-permute-start(bf16[4,192,384]{2,1,0:T(8,128)(2,1)S(1)} %collective-permute-done.25.refs_9_), channel_id=1, source_target_pairs={{0,16},{1,3},{2,18},{3,1},{16,0},{17,19},{18,2},{19,17},{4,20},{5,... | collective-permute-start | bytes 1769480 | tf_op jit(solution)/shard_map/ppermute | solution.py:506
  97.4 8.4 %collective-permute-start.28 = (bf16[4,192,384]{2,1,0:T(8,128)(2,1)S(1)}, bf16[4,192,384]{2,1,0:T(8,128)(2,1)S(1)}, u32[]{:S(2)}, u32[]{:S(2)}) collective-permute-start(bf16[4,192,384]{2,1,0:T(8,128)(2,1)S(1)} %pad_maximum_fusion.2.refs_8_), channel_id=1, source_target_pairs={{0,1},{1,0},{2,3},{3,2},{4,5},{5,4},{6,7},{7,6},{8,9},{9,8},{10,11... | collective-permute-start | bytes 1769480 | tf_op jit(solution)/shard_map/ppermute | solution.py:443
  97.4 9.0 %collective-permute-start.23 = (bf16[4,128,768]{2,1,0:T(8,128)(2,1)}, bf16[4,128,768]{2,1,0:T(8,128)(2,1)S(1)}, u32[]{:S(2)}, u32[]{:S(2)}) collective-permute-start(bf16[4,128,768]{2,1,0:T(8,128)(2,1)} %collective-permute-done.14.refs_2_), channel_id=1, source_target_pairs={{0,1},{1,0},{2,3},{3,2},{4,5},{5,4},{6,7},{7,6},{8,9},{9,8},{10,11... | collective-permute-start | bytes 2359304 | tf_op jit(solution)/shard_map/ppermute | solution.py:443
  98.4 8.0 %collective-permute-start.24 = (bf16[4,128,768]{2,1,0:T(8,128)(2,1)}, bf16[4,128,768]{2,1,0:T(8,128)(2,1)S(1)}, u32[]{:S(2)}, u32[]{:S(2)}) collective-permute-start(bf16[4,128,768]{2,1,0:T(8,128)(2,1)} %collective-permute-done.21.refs_3_), channel_id=1, source_target_pairs={{0,1},{1,0},{2,3},{3,2},{4,5},{5,4},{6,7},{7,6},{8,9},{9,8},{10,11... | collective-permute-start | bytes 2359304 | tf_op jit(solution)/shard_map/ppermute | solution.py:443
  141.7 15.6 %collective-permute-start.37 = (bf16[2,2,4,128,768]{4,3,2,1,0:T(8,128)(2,1)}, bf16[2,2,4,128,768]{4,3,2,1,0:T(8,128)(2,1)S(1)}, u32[]{:S(2)}, u32[]{:S(2)}) collective-permute-start(bf16[2,2,4,128,768]{4,3,2,1,0:T(8,128)(2,1)} %inner_give.1), channel_id=1, source_target_pairs={{0,1},{1,0},{2,3},{3,2},{4,5},{5,4},{6,7},{7,6},{8,9},{9,8},{10,11... | collective-permute-start | bytes 9437192 | tf_op jit(solution)/shard_map/ppermute | solution.py:443
  141.7 10.9 %collective-permute-start.36 = (bf16[2,2,4,192,384]{4,3,2,1,0:T(8,128)(2,1)}, bf16[2,2,4,192,384]{4,3,2,1,0:T(8,128)(2,1)}, u32[]{:S(2)}, u32[]{:S(2)}) collective-permute-start(bf16[2,2,4,192,384]{4,3,2,1,0:T(8,128)(2,1)} %outer_give.1), channel_id=1, source_target_pairs={{0,1},{1,0},{2,3},{3,2},{4,5},{5,4},{6,7},{7,6},{8,9},{9,8},{10,11... | collective-permute-start | bytes 7077896 | tf_op jit(solution)/shard_map/ppermute | solution.py:443
  142.3 8.6 %collective-permute-start.32 = (bf16[2,192,256]{2,1,0:T(8,128)(2,1)}, bf16[2,192,256]{2,1,0:T(8,128)(2,1)S(1)}, u32[]{:S(2)}, u32[]{:S(2)}) collective-permute-start(bf16[2,192,256]{2,1,0:T(8,128)(2,1)} %get-tuple-element.124), channel_id=1, source_target_pairs={{0,8},{1,5},{4,12},{5,1},{8,0},{9,13},{12,4},{13,9},{2,10},{3,7},{... | collective-permute-start | bytes 589832 | tf_op jit(solution)/shard_map/ppermute | solution.py:506
  143.9 8.8 %collective-permute-start.35 = (bf16[2,192,256]{2,1,0:T(8,128)(2,1)}, bf16[2,192,256]{2,1,0:T(8,128)(2,1)}, u32[]{:S(2)}, u32[]{:S(2)}) collective-permute-start(bf16[2,192,256]{2,1,0:T(8,128)(2,1)} %pad_maximum_fusion.16), channel_id=1, source_target_pairs={{0,2},{1,5},{2,0},{3,7},{4,6},{5,1},{6,4},{7,3},{8,10},{9,13},{10,... | collective-permute-start | bytes 589832 | tf_op jit(solution)/shard_map/ppermute | solution.py:506
  151.6 13.0 %collective-permute-start.34 = (bf16[2,192,256]{2,1,0:T(8,128)(2,1)}, bf16[2,192,256]{2,1,0:T(8,128)(2,1)S(1)}, u32[]{:S(2)}, u32[]{:S(2)}) collective-permute-start(bf16[2,192,256]{2,1,0:T(8,128)(2,1)} %pad_maximum_fusion.17), channel_id=1, source_target_pairs={{0,4},{1,9},{4,0},{5,13},{8,12},{9,1},{12,8},{13,5},{2,6},{3,11},{... | collective-permute-start | bytes 589832 | tf_op jit(solution)/shard_map/ppermute | solution.py:506
  156.3 30.1 %collective-permute-start.38 = (bf16[2,4,192,384]{3,2,1,0:T(8,128)(2,1)}, bf16[2,4,192,384]{3,2,1,0:T(8,128)(2,1)}, u32[]{:S(2)}, u32[]{:S(2)}) collective-permute-start(bf16[2,4,192,384]{3,2,1,0:T(8,128)(2,1)} %outer_first.1), channel_id=1, source_target_pairs={{0,8},{1,5},{4,12},{5,1},{8,0},{9,13},{12,4},{13,9},{2,10},{3,7},{... | collective-permute-start | bytes 3538952 | tf_op jit(solution)/shard_map/ppermute | solution.py:506
  163.1 36.5 %collective-permute-start.41 = (bf16[2,4,128,768]{3,2,1,0:T(8,128)(2,1)}, bf16[2,4,128,768]{3,2,1,0:T(8,128)(2,1)S(1)}, u32[]{:S(2)}, u32[]{:S(2)}) collective-permute-start(bf16[2,4,128,768]{3,2,1,0:T(8,128)(2,1)} %inner_first.1), channel_id=1, source_target_pairs={{0,16},{1,3},{2,18},{3,1},{16,0},{17,19},{18,2},{19,17},{4,20},{5,... | collective-permute-start | bytes 4718600 | tf_op jit(solution)/shard_map/ppermute | solution.py:506
  193.3 18.6 %collective-permute-start.40 = (bf16[2,4,192,256]{3,2,1,0:T(8,128)(2,1)}, bf16[2,4,192,256]{3,2,1,0:T(8,128)(2,1)}, u32[]{:S(2)}, u32[]{:S(2)}) collective-permute-start(bf16[2,4,192,256]{3,2,1,0:T(8,128)(2,1)} %get-tuple-element.151), channel_id=1, source_target_pairs={{0,4},{1,3},{2,6},{3,1},{4,0},{5,7},{6,2},{7,5},{8,12},{9,11},{10,... | collective-permute-start | bytes 2359304 | tf_op jit(solution)/shard_map/ppermute | solution.py:506
  199.5 26.5 %collective-permute-start.46 = (bf16[4,192,384]{2,1,0:T(8,128)(2,1)}, bf16[4,192,384]{2,1,0:T(8,128)(2,1)}, u32[]{:S(2)}, u32[]{:S(2)}) collective-permute-start(bf16[4,192,384]{2,1,0:T(8,128)(2,1)} %get-tuple-element.167), channel_id=1, source_target_pairs={{0,4},{1,9},{4,0},{5,13},{8,12},{9,1},{12,8},{13,5},{2,6},{3,11},{... | collective-permute-start | bytes 1769480 | tf_op jit(solution)/shard_map/ppermute | solution.py:506
  205.7 24.4 %collective-permute-start.44 = (bf16[4,128,768]{2,1,0:T(8,128)(2,1)}, bf16[4,128,768]{2,1,0:T(8,128)(2,1)}, u32[]{:S(2)}, u32[]{:S(2)}) collective-permute-start(bf16[4,128,768]{2,1,0:T(8,128)(2,1)} %get-tuple-element.163), channel_id=1, source_target_pairs={{0,2},{1,17},{2,0},{3,19},{16,18},{17,1},{18,16},{19,3},{4,6},{5,2... | collective-permute-start | bytes 2359304 | tf_op jit(solution)/shard_map/ppermute | solution.py:506
  213.0 9.2 %collective-permute-start.42 = (bf16[4,192,256]{2,1,0:T(8,128)(2,1)S(1)}, bf16[4,192,256]{2,1,0:T(8,128)(2,1)}, u32[]{:S(2)}, u32[]{:S(2)}) collective-permute-start(bf16[4,192,256]{2,1,0:T(8,128)(2,1)S(1)} %fusion.3), channel_id=1, source_target_pairs={{0,2},{1,5},{2,0},{3,7},{4,6},{5,1},{6,4},{7,3},{8,10},{9,13},{10,... | collective-permute-start | bytes 1179656 | tf_op jit(solution)/shard_map/ppermute | solution.py:506
  217.4 8.4 %collective-permute-start.45 = (bf16[4,96,576]{2,1,0:T(8,128)(2,1)}, bf16[4,96,576]{2,1,0:T(8,128)(2,1)S(1)}, u32[]{:S(2)}, u32[]{:S(2)}) collective-permute-start(bf16[4,96,576]{2,1,0:T(8,128)(2,1)} %get-tuple-element.161), channel_id=1, source_target_pairs={{0,1},{1,0},{2,3},{3,2},{4,5},{5,4},{6,7},{7,6},{8,9},{9,8},{10,11... | collective-permute-start | bytes 1327112 | tf_op jit(solution)/shard_map/ppermute | solution.py:443
  223.8 8.8 %collective-permute-start.43 = (bf16[2,192,256]{2,1,0:T(8,128)(2,1)S(1)}, bf16[2,192,256]{2,1,0:T(8,128)(2,1)S(1)}, u32[]{:S(2)}, u32[]{:S(2)}) collective-permute-start(bf16[2,192,256]{2,1,0:T(8,128)(2,1)S(1)} %slice.328), channel_id=1, source_target_pairs={{0,8},{1,5},{4,12},{5,1},{8,0},{9,13},{12,4},{13,9},{2,10},{3,7},{... | collective-permute-start | bytes 589832 | tf_op jit(solution)/shard_map/ppermute | solution.py:506
  228.2 22.7 %collective-permute-start.50 = (bf16[2,192,384]{2,1,0:T(8,128)(2,1)S(1)}, bf16[2,192,384]{2,1,0:T(8,128)(2,1)S(1)}, u32[]{:S(2)}, u32[]{:S(2)}) collective-permute-start(bf16[2,192,384]{2,1,0:T(8,128)(2,1)S(1)} %slice.332), channel_id=1, source_target_pairs={{0,16},{1,3},{2,18},{3,1},{16,0},{17,19},{18,2},{19,17},{4,20},{5,... | collective-permute-start | bytes 884744 | tf_op jit(solution)/shard_map/ppermute | solution.py:506
  228.8 11.4 %collective-permute-start.48 = (bf16[4,96,576]{2,1,0:T(8,128)(2,1)S(1)}, bf16[4,96,576]{2,1,0:T(8,128)(2,1)S(1)}, u32[]{:S(2)}, u32[]{:S(2)}) collective-permute-start(bf16[4,96,576]{2,1,0:T(8,128)(2,1)S(1)} %get-tuple-element.178), channel_id=1, source_target_pairs={{16,0},{1,17},{18,2},{3,19},{20,4},{5,21},{22,6},{7,23},{24,8},{9,... | collective-permute-start | bytes 1327112 | tf_op jit(solution)/shard_map/ppermute | solution.py:750
  232.6 18.2 %collective-permute-start.51 = (bf16[2,128,768]{2,1,0:T(8,128)(2,1)S(1)}, bf16[2,128,768]{2,1,0:T(8,128)(2,1)S(1)}, u32[]{:S(2)}, u32[]{:S(2)}) collective-permute-start(bf16[2,128,768]{2,1,0:T(8,128)(2,1)S(1)} %slice.334), channel_id=1, source_target_pairs={{0,8},{1,5},{4,12},{5,1},{8,0},{9,13},{12,4},{13,9},{2,10},{3,7},{... | collective-permute-start | bytes 1179656 | tf_op jit(solution)/shard_map/ppermute | solution.py:506
  233.5 20.1 %collective-permute-start.47 = (bf16[2,192,256]{2,1,0:T(8,128)(2,1)S(1)}, bf16[2,192,256]{2,1,0:T(8,128)(2,1)S(1)}, u32[]{:S(2)}, u32[]{:S(2)}) collective-permute-start(bf16[2,192,256]{2,1,0:T(8,128)(2,1)S(1)} %pad_maximum_fusion.18), channel_id=1, source_target_pairs={{0,4},{1,9},{4,0},{5,13},{8,12},{9,1},{12,8},{13,5},{2,6},{3,11},{... | collective-permute-start | bytes 589832 | tf_op jit(solution)/shard_map/ppermute | solution.py:506
  240.3 13.1 %collective-permute-start.49 = (bf16[2,96,576]{2,1,0:T(8,128)(2,1)S(1)}, bf16[2,96,576]{2,1,0:T(8,128)(2,1)S(1)}, u32[]{:S(2)}, u32[]{:S(2)}) collective-permute-start(bf16[2,96,576]{2,1,0:T(8,128)(2,1)S(1)} %slice.389), channel_id=1, source_target_pairs={{0,8},{8,0},{17,25},{25,17},{2,10},{10,2},{19,27},{27,19},{4,12},{... | collective-permute-start | bytes 663560 | tf_op jit(solution)/shard_map/ppermute | solution.py:766
  253.5 8.0 %collective-permute-start.52 = (bf16[96,576]{1,0:T(8,128)(2,1)S(1)}, bf16[96,576]{1,0:T(8,128)(2,1)S(1)}, u32[]{:S(2)}, u32[]{:S(2)}) collective-permute-start(bf16[96,576]{1,0:T(8,128)(2,1)S(1)} %fusion.5), channel_id=1, source_target_pairs={{0,4},{4,0},{17,21},{21,17},{2,6},{6,2},{19,23},{23,19},{8,12},{12... | collective-permute-start | bytes 331784 | tf_op jit(solution)/shard_map/ppermute | solution.py:772
  256.8 7.8 %collective-permute-start.54 = (bf16[128,768]{1,0:T(8,128)(2,1)S(1)}, bf16[128,768]{1,0:T(8,128)(2,1)S(1)}, u32[]{:S(2)}, u32[]{:S(2)}) collective-permute-start(bf16[128,768]{1,0:T(8,128)(2,1)S(1)} %slice_bitcast_fusion.1), channel_id=1, source_target_pairs={{0,4},{1,9},{4,0},{5,13},{8,12},{9,1},{12,8},{13,5},{2,6},{3,11},{... | collective-permute-start | bytes 589832 | tf_op jit(solution)/shard_map/ppermute | solution.py:506
  261.6 7.0 %collective-permute-start.53 = (bf16[96,576]{1,0:T(8,128)(2,1)S(1)}, bf16[96,576]{1,0:T(8,128)(2,1)S(1)}, u32[]{:S(2)}, u32[]{:S(2)}) collective-permute-start(bf16[96,576]{1,0:T(8,128)(2,1)S(1)} %select_convert_fusion.1), channel_id=1, source_target_pairs={{0,1},{1,0},{2,3},{3,2},{4,5},{5,4},{6,7},{7,6},{8,9},{9,8},{10,11... | collective-permute-start | bytes 331784 | tf_op jit(solution)/shard_map/ppermute | solution.py:443
  (49 other events, 315.3 us)

commit v9 on v8

--- a/solution.py
+++ b/solution.py
@@ -283,7 +283,7 @@
     pltpu.make_async_copy(win,win,sems.at[1]).wait()
     pltpu.make_async_copy(woT,woT,sems.at[2]).wait()
     f_s[...]=jnp.zeros_like(f_s)
-    nb=1; bw=ffc//nb
+    bw=2*ffc
     def forward(j,carry):
         sl=pl.ds(pl.multiple_of(j*bw,128),bw)
         inner=mm(hid,win[:,sl])
@@ -293,7 +293,7 @@
         act_ref[:,sl]=act
         f_s[...]+=mm(act,woT[:,sl],NT)
         return carry
-    lax.fori_loop(0,4*nb,forward,0)
+    lax.fori_loop(0,2,forward,0)
     cent2,inv2=stats(hidden+f_s[...])
     t_s[...]=(cent2*gain2+shift2).astype(bf16).T
     for s in range(4):
@@ -317,7 +317,7 @@
         il_ref[:,sl]=il
         f_s[...]+=mm(il,win[:,sl],NT)
         return carry
-    lax.fori_loop(0,4*nb,backward,0)
+    lax.fori_loop(0,2,backward,0)
     gh=f_s[...]
     sums=jnp.concatenate((jnp.sum(gh*cent1,axis=0,keepdims=True),jnp.sum(gh,axis=0,keepdims=True))+sums2+(jnp.zeros((4,width),f32),),axis=0)
     for r in range(4):

time: 270 us -> 269 us (level)
  no operation moved by 1% of the time
where the time goes in v9:
time: 269 us; the launch traced here: 268 us
  Pallas kernels  90.8 us (34%)
  waiting for transfers between devices  78.4 us (29%)
  starting transfers between devices  64.1 us (24%)
  local copies, waits for them, and re-layouts  19.2 us (7%)
  other arithmetic  13.1 us (5%)
    ppermute x36, waiting for transfers between devices, crossed(): return lax.ppermute(value, axes + ('cc',), pairs)  65.5 us
    ppermute x36, starting transfers between devices, crossed(): return lax.ppermute(value, axes + ('cc',), pairs)  48.7 us
    pallas_call x1, Pallas kernels, attend_back(): pl.pallas_call(attend_back_kernel, grid=(count, 4 // QB), in_specs=[pl.Bl...  19.9 us
    pallas_call x1, Pallas kernels, middle(): pl.pallas_call(middle_kernel, in_specs=[SM] + [VM] * 7 + [HB] * 16, out_s...  16.8 us
    pallas_call x2, Pallas kernels, attend(): pl.pallas_call(attend_kernel, grid=(heads,), in_specs=[pl.BlockSpec((HD,...  13.3 us
    pallas_call x2, Pallas kernels, grad_call(): pl.pallas_call(functools.partial(give_kernel, blocks), grid_spec=pltpu.Pr...  10.3 us
    pallas_call x2, Pallas kernels, grad_call(): pl.pallas_call(functools.partial(second_kernel, blocks), grid_spec=pltpu....  9.03 us
    pallas_call x2, Pallas kernels, grad_call(): pl.pallas_call(functools.partial(first_kernel, blocks), grid_spec=pltpu.P...  8 us
  transfers between devices with their start and end apart: 56, of which 25 were waited for; matrix products, arithmetic and copies ran while one was open for 9% of the time, Pallas kernels for 25%

profile of v9, /device:TPU:0, one launch (start us, length us, event | category | flops | bytes accessed | tf_op | source)
XLA Modules:
  0.0 268.0 jit_solution(17954145751217620713)
XLA Ops:
  2.2 3.0 %collective-permute-start.6 = (bf16[96,576]{1,0:T(8,128)(2,1)S(1)}, bf16[96,576]{1,0:T(8,128)(2,1)S(1)}, u32[]{:S(2)}, u32[]{:S(2)}) collective-permute-start(bf16[96,576]{1,0:T(8,128)(2,1)S(1)} %pad_maximum_fusion.19), channel_id=1, source_target_pairs={{0,16},{16,0},{1,17},{17,1},{2,18},{18,2},{3,19},{19,3},{4,20},{20... | collective-permute-start | bytes 331784 | tf_op jit(solution)/shard_map/ppermute | solution.py:496
  5.2 1.6 collective-permute-start.15
  6.8 2.7 collective-permute-start
  15.2 4.0 %collective-permute-start.1 = (bf16[2,192,256]{2,1,0:T(8,128)(2,1)S(1)}, bf16[2,192,256]{2,1,0:T(8,128)(2,1)S(1)}, u32[]{:S(2)}, u32[]{:S(2)}) collective-permute-start(bf16[2,192,256]{2,1,0:T(8,128)(2,1)S(1)} %pad_maximum_fusion.12), channel_id=1, source_target_pairs={{0,4},{1,9},{4,0},{5,13},{8,12},{9,1},{12,8},{13,5},{2,6},{3,11},{... | collective-permute-start | bytes 589832 | tf_op jit(solution)/shard_map/ppermute | solution.py:506
  19.4 3.7 %collective-permute-start.3 = (bf16[2,128,768]{2,1,0:T(8,128)(2,1)S(1)}, bf16[2,128,768]{2,1,0:T(8,128)(2,1)S(1)}, u32[]{:S(2)}, u32[]{:S(2)}) collective-permute-start(bf16[2,128,768]{2,1,0:T(8,128)(2,1)S(1)} %pad_maximum_fusion.5), channel_id=1, source_target_pairs={{0,8},{1,5},{4,12},{5,1},{8,0},{9,13},{12,4},{13,9},{2,10},{3,7},{... | collective-permute-start | bytes 1179656 | tf_op jit(solution)/shard_map/ppermute | solution.py:506
  24.0 4.4 %collective-permute-done.1 = bf16[2,192,256]{2,1,0:T(8,128)(2,1)S(1)} collective-permute-done((bf16[2,192,256]{2,1,0:T(8,128)(2,1)S(1)}, bf16[2,192,256]{2,1,0:T(8,128)(2,1)S(1)}, u32[]{:S(2)}, u32[]{:S(2)}) %collective-permute-start.1) | collective-permute-done | bytes 196640 | tf_op jit(solution)/shard_map/ppermute | solution.py:506
  28.5 1.6 collective-permute-start.4
  30.1 8.2 %collective-permute-done.8 = bf16[2,96,576]{2,1,0:T(8,128)(2,1)S(1)} collective-permute-done((bf16[2,96,576]{2,1,0:T(8,128)(2,1)S(1)}, bf16[2,96,576]{2,1,0:T(8,128)(2,1)S(1)}, u32[]{:S(2)}, u32[]{:S(2)}) %collective-permute-start.8) | collective-permute-done | bytes 221216 | tf_op jit(solution)/shard_map/ppermute | solution.py:506
  38.3 4.0 %collective-permute-start.9 = (bf16[2,96,576]{2,1,0:T(8,128)(2,1)S(1)}, bf16[2,96,576]{2,1,0:T(8,128)(2,1)S(1)}, u32[]{:S(2)}, u32[]{:S(2)}) collective-permute-start(bf16[2,96,576]{2,1,0:T(8,128)(2,1)S(1)} %pad_maximum_fusion.11), channel_id=1, source_target_pairs={{0,4},{1,9},{4,0},{5,13},{8,12},{9,1},{12,8},{13,5},{2,6},{3,11},{... | collective-permute-start | bytes 663560 | tf_op jit(solution)/shard_map/ppermute | solution.py:506
  42.4 1.6 collective-permute-start.20
  44.1 3.9 %collective-permute-done.9 = bf16[2,96,576]{2,1,0:T(8,128)(2,1)S(1)} collective-permute-done((bf16[2,96,576]{2,1,0:T(8,128)(2,1)S(1)}, bf16[2,96,576]{2,1,0:T(8,128)(2,1)S(1)}, u32[]{:S(2)}, u32[]{:S(2)}) %collective-permute-start.9) | collective-permute-done | bytes 221216 | tf_op jit(solution)/shard_map/ppermute | solution.py:506
  52.7 3.0 %collective-permute-start.16 = (bf16[2,192,384]{2,1,0:T(8,128)(2,1)S(1)}, bf16[2,192,384]{2,1,0:T(8,128)(2,1)S(1)}, u32[]{:S(2)}, u32[]{:S(2)}) collective-permute-start(bf16[2,192,384]{2,1,0:T(8,128)(2,1)S(1)} %pad_maximum_fusion.8), channel_id=1, source_target_pairs={{0,8},{1,5},{4,12},{5,1},{8,0},{9,13},{12,4},{13,9},{2,10},{3,7},{... | collective-permute-start | bytes 884744 | tf_op jit(solution)/shard_map/ppermute | solution.py:506
  55.7 4.1 %collective-permute-done.5.xc = bf16[2,4,192,256]{3,2,1,0:T(8,128)(2,1)} collective-permute-done((bf16[2,4,192,256]{3,2,1,0:T(8,128)(2,1)S(1)}, bf16[2,4,192,256]{3,2,1,0:T(8,128)(2,1)}, u32[]{:S(2)}, u32[]{:S(2)}) %collective-permute-start.5) | collective-permute-done | bytes 786464 | tf_op jit(solution)/shard_map/ppermute | solution.py:506
  59.8 4.0 %qkv.1 = (bf16[192,1024]{1,0:T(8,128)(2,1)}, bf16[384,1024]{1,0:T(8,128)(2,1)}) custom-call(s32[8]{0:T(128)} %stack.140.info, bf16[4,192,256]{2,1,0:T(8,128)(2,1)} %copy-done.2, bf16[4,192,256]{2,1,0:T(8,128)(2,1)} %copy-done.4, bf16[2,4,192,256]{3,2,1,0:T(8,128)(2,1)} %collective-permute-done.5.xc, bf16[4,96,576]{2,1,0:T(8,128)(2,1)} %copy-done.1, ...), custom_call_target="tpu_custom_call" | custom-call | tf_op jit(solution)/shard_map/qkv/pallas_call | solution.py:182
  63.8 3.2 %collective-permute-start.11 = (bf16[384,1024]{1,0:T(8,128)(2,1)}, bf16[384,1024]{1,0:T(8,128)(2,1)}, u32[]{:S(2)}, u32[]{:S(2)}) collective-permute-start(bf16[384,1024]{1,0:T(8,128)(2,1)} %get-tuple-element.101.ko_ref.vo_ref), channel_id=1, source_target_pairs={{0,1},{1,0},{2,3},{3,2},{4,5},{5,4},{6,7},{7,6},{8,9},{9,8},{10,11... | collective-permute-start | bytes 2359304 | tf_op jit(solution)/shard_map/ppermute | solution.py:443
  69.9 6.6 %attend.2 = (f32[192,512]{1,0:T(8,128)}, f32[3,1,512]{2,1,0:T(1,128)}, bf16[2,192,256]{2,1,0:T(8,128)(2,1)}) custom-call(bf16[192,1024]{1,0:T(8,128)(2,1)} %get-tuple-element.140.q_ref, bf16[384,1024]{1,0:T(8,128)(2,1)} %get-tuple-element.101.ko_ref.vo_ref, bf16[384,1024]{1,0:T(8,128)(2,1)} %get-tuple-element.101.ko_ref.vo_ref, ...), custom_call_target="tpu_custom_call" | custom-call | flops 19327352832 | bytes 25165824 | tf_op jit(solution)/shard_map/attend/pallas_call | solution.py:66
  77.1 1.6 collective-permute-start.17
  78.7 1.6 collective-permute-start.25
  80.3 6.6 %attend.3 = (f32[192,512]{1,0:T(8,128)}, f32[3,1,512]{2,1,0:T(1,128)}, bf16[2,192,256]{2,1,0:T(8,128)(2,1)}) custom-call(bf16[192,1024]{1,0:T(8,128)(2,1)} %get-tuple-element.140.q_ref, bf16[384,1024]{1,0:T(8,128)(2,1)} %get-tuple-element.101.ko_ref.vo_ref, bf16[384,1024]{1,0:T(8,128)(2,1)} %get-tuple-element.101.ko_ref.vo_ref, ...), custom_call_target="tpu_custom_call" | custom-call | flops 19327352832 | bytes 25165824 | tf_op jit(solution)/shard_map/attend/pallas_call | solution.py:66
  90.0 5.8 %collective-permute-done.18.a2 = bf16[2,192,256]{2,1,0:T(8,128)(2,1)S(1)} collective-permute-done((bf16[2,192,256]{2,1,0:T(8,128)(2,1)S(1)}, bf16[2,192,256]{2,1,0:T(8,128)(2,1)S(1)}, u32[]{:S(2)}, u32[]{:S(2)}) %collective-permute-start.18) | collective-permute-done | bytes 196640 | tf_op jit(solution)/shard_map/ppermute | solution.py:506
  95.8 1.5 collective-permute-start.27
  98.4 7.4 %collective-permute-done.27.refs_11_ = bf16[4,192,384]{2,1,0:T(8,128)(2,1)S(1)} collective-permute-done((bf16[4,192,384]{2,1,0:T(8,128)(2,1)S(1)}, bf16[4,192,384]{2,1,0:T(8,128)(2,1)S(1)}, u32[]{:S(2)}, u32[]{:S(2)}) %collective-permute-start.27) | collective-permute-done | bytes 589856 | tf_op jit(solution)/shard_map/ppermute | solution.py:506
  110.3 16.8 %middle.1 = (bf16[2,192,256]{2,1,0:T(8,128)(2,1)}, bf16[2,192,256]{2,1,0:T(8,128)(2,1)}, bf16[2,192,256]{2,1,0:T(8,128)(2,1)}, bf16[2,192,256]{2,1,0:T(8,128)(2,...) custom-call(s32[8]{0:T(128)} %stack.140.info, ...), custom_call_target="tpu_custom_call" | custom-call | flops 86973087744 | bytes 339738624 | tf_op jit(solution)/shard_map/middle/pallas_call | solution.py:344
  128.5 4.7 %outer_give.1 = bf16[2,2,4,192,384]{4,3,2,1,0:T(8,128)(2,1)} custom-call(s32[8]{0:T(128)} %stack.140.info, bf16[768,256]{1,0:T(8,128)(2,1)} %get-tuple-element.152.refs_0_, bf16[256,3072]{1,0:T(8,128)(2,1)} %get-tuple-element.127.refs_1_.refs_2_, bf16[256,3072]{1,0:T(8,128)(2,1)} %get-tuple-element.127.refs_1_.refs_2_), custom_call_target="tpu_custom_call" | custom-call | flops 3623878656 | bytes 14155777 | tf_op jit(solution)/shard_map/outer_give/pallas_call | solution.py:429
  134.7 5.7 %inner_give.1 = bf16[2,2,4,128,768]{4,3,2,1,0:T(8,128)(2,1)} custom-call(s32[8]{0:T(128)} %stack.140.info, bf16[768,256]{1,0:T(8,128)(2,1)} %get-tuple-element.155.refs_0_, bf16[256,3072]{1,0:T(8,128)(2,1)} %get-tuple-element.132.refs_1_, bf16[768,256]{1,0:T(8,128)(2,1)} %get-tuple-element.133.refs_2_, bf16[4,256,256]{2,1,0:T(8,128)(2,1)} %get-tuple-element.134.refs_3_, ...), custom_call_target="tpu_custom_call" | custom-call | flops 3623878656 | bytes 9437185 | tf_op jit(solution)/shard_map/inner_give/pallas_call | solution.py:429
  140.9 1.7 collective-permute-start.32
  143.1 6.4 %collective-permute-done.32 = bf16[2,192,256]{2,1,0:T(8,128)(2,1)S(1)} collective-permute-done((bf16[2,192,256]{2,1,0:T(8,128)(2,1)}, bf16[2,192,256]{2,1,0:T(8,128)(2,1)S(1)}, u32[]{:S(2)}, u32[]{:S(2)}) %collective-permute-start.32) | collective-permute-done | bytes 196640 | tf_op jit(solution)/shard_map/ppermute | solution.py:506
  151.3 3.6 %outer_first.1 = bf16[2,4,192,384]{3,2,1,0:T(8,128)(2,1)} custom-call(s32[8]{0:T(128)} %stack.140.info, bf16[768,256]{1,0:T(8,128)(2,1)} %get-tuple-element.152.refs_0_, bf16[256,3072]{1,0:T(8,128)(2,1)} %get-tuple-element.127.refs_1_.refs_2_, bf16[256,3072]{1,0:T(8,128)(2,1)} %get-tuple-element.127.refs_1_.refs_2_, ...), custom_call_target="tpu_custom_call" | custom-call | flops 1811939328 | bytes 7077889 | tf_op jit(solution)/shard_map/outer_first/pallas_call | solution.py:434
  155.9 1.7 copy-done
  157.6 4.3 %inner_first.1 = bf16[2,4,128,768]{3,2,1,0:T(8,128)(2,1)} custom-call(s32[8]{0:T(128)} %stack.140.info, bf16[768,256]{1,0:T(8,128)(2,1)} %get-tuple-element.155.refs_0_, bf16[256,3072]{1,0:T(8,128)(2,1)} %get-tuple-element.132.refs_1_, bf16[768,256]{1,0:T(8,128)(2,1)} %get-tuple-element.133.refs_2_, bf16[4,256,256]{2,1,0:T(8,128)(2,1)} %get-tuple-element.134.refs_3_, ...), custom_call_target="tpu_custom_call" | custom-call | flops 1811939328 | bytes 4718593 | tf_op jit(solution)/shard_map/inner_first/pallas_call | solution.py:434
  163.5 19.9 %attend_back.1 = (bf16[192,1024]{1,0:T(8,128)(2,1)}, f32[3,1024,128]{2,1,0:T(8,128)}, bf16[3,1024,128]{2,1,0:T(8,128)(2,1)}) custom-call(bf16[192,1024]{1,0:T(8,128)(2,1)} %get-tuple-element.140.q_ref, bf16[384,1024]{1,0:T(8,128)(2,1)} %get-tuple-element.101.ko_ref.vo_ref, bf16[384,1024]{1,0:T(8,128)(2,1)} %get-tuple-element.101.ko_ref.vo_ref, ...), custom_call_target="tpu_custom_call" | custom-call | flops 96636764160 | bytes 150994944 | tf_op jit(solution)/shard_map/attend_back/pallas_call | solution.py:119
  186.8 5.1 %finish_dx.1 = (f32[2,4,192,256]{3,2,1,0:T(8,128)}, bf16[2,4,192,256]{3,2,1,0:T(8,128)(2,1)}, bf16[576,1024]{1,0:T(8,128)(2,1)}) custom-call(s32[8]{0:T(128)} %stack.140.info, bf16[192,1024]{1,0:T(8,128)(2,1)} %get-tuple-element.145.refs_0_, f32[3,1024,128]{2,1,0:T(8,128)} %get-tuple-element.148.refs_1_, bf16[3,1024,128]{2,1,0:T(8,128)(2,1)} %copy-done.8, ...), custom_call_target="tpu_custom_call" | custom-call | flops 1 | bytes 1 | tf_op jit(solution)/shard_map/finish_dx/pallas_call | solution.py:205
  191.9 2.0 collective-permute-start.40
  194.0 4.2 %outer_second.1 = (bf16[4,192,384]{2,1,0:T(8,128)(2,1)}, bf16[4,192,384]{2,1,0:T(8,128)(2,1)}) custom-call(s32[8]{0:T(128)} %stack.140.info, bf16[768,256]{1,0:T(8,128)(2,1)} %get-tuple-element.152.refs_0_, bf16[256,3072]{1,0:T(8,128)(2,1)} %get-tuple-element.127.refs_1_.refs_2_, bf16[256,3072]{1,0:T(8,128)(2,1)} %get-tuple-element.127.refs_1_.refs_2_, ...), custom_call_target="tpu_custom_call" | custom-call | flops 1 | bytes 1 | tf_op jit(solution)/shard_map/outer_second/pallas_call | solution.py:438
  199.4 4.9 %inner_second.1 = (bf16[4,128,768]{2,1,0:T(8,128)(2,1)}, bf16[4,128,768]{2,1,0:T(8,128)(2,1)}) custom-call(s32[8]{0:T(128)} %stack.140.info, bf16[768,256]{1,0:T(8,128)(2,1)} %get-tuple-element.155.refs_0_, bf16[256,3072]{1,0:T(8,128)(2,1)} %get-tuple-element.132.refs_1_, bf16[768,256]{1,0:T(8,128)(2,1)} %get-tuple-element.133.refs_2_, ...), custom_call_target="tpu_custom_call" | custom-call | flops 1 | bytes 1 | tf_op jit(solution)/shard_map/inner_second/pallas_call | solution.py:438
  204.7 5.7 %collective-permute-done.40 = bf16[2,4,192,256]{3,2,1,0:T(8,128)(2,1)} collective-permute-done((bf16[2,4,192,256]{3,2,1,0:T(8,128)(2,1)}, bf16[2,4,192,256]{3,2,1,0:T(8,128)(2,1)}, u32[]{:S(2)}, u32[]{:S(2)}) %collective-permute-start.40) | collective-permute-done | bytes 786464 | tf_op jit(solution)/shard_map/ppermute | solution.py:506
  211.6 4.4 %finish_dw.1 = (f32[4,96,576]{2,1,0:T(8,128)}, bf16[4,96,576]{2,1,0:T(8,128)(2,1)}) custom-call(s32[8]{0:T(128)} %stack.140.info, bf16[576,1024]{1,0:T(8,128)(2,1)} %get-tuple-element.160.p_ref, bf16[4,192,256]{2,1,0:T(8,128)(2,1)} %copy-done.2, bf16[4,192,256]{2,1,0:T(8,128)(2,1)} %copy-done.4, bf16[2,4,192,256]{3,2,1,0:T(8,128)(2,1)} %collective-permute-done.5.xc), custom_call_target="tpu_custom_call" | custom-call | flops 5435817984 | bytes 18874368 | tf_op jit(solution)/shard_map/finish_dw/pallas_call | solution.py:224
  216.0 4.8 %collective-permute-done.42 = bf16[4,192,256]{2,1,0:T(8,128)(2,1)} collective-permute-done((bf16[4,192,256]{2,1,0:T(8,128)(2,1)S(1)}, bf16[4,192,256]{2,1,0:T(8,128)(2,1)}, u32[]{:S(2)}, u32[]{:S(2)}) %collective-permute-start.42) | collective-permute-done | bytes 393248 | tf_op jit(solution)/shard_map/ppermute | solution.py:506
  220.8 1.6 fusion.1
  222.4 2.0 collective-permute-start.43
  232.1 2.1 collective-permute-start.47
  234.2 4.7 %collective-permute-done.48 = bf16[4,96,576]{2,1,0:T(8,128)(2,1)S(1)} collective-permute-done((bf16[4,96,576]{2,1,0:T(8,128)(2,1)S(1)}, bf16[4,96,576]{2,1,0:T(8,128)(2,1)S(1)}, u32[]{:S(2)}, u32[]{:S(2)}) %collective-permute-start.48) | collective-permute-done | bytes 442400 | tf_op jit(solution)/shard_map/ppermute | solution.py:750
  239.0 2.9 %collective-permute-start.49 = (bf16[2,96,576]{2,1,0:T(8,128)(2,1)S(1)}, bf16[2,96,576]{2,1,0:T(8,128)(2,1)S(1)}, u32[]{:S(2)}, u32[]{:S(2)}) collective-permute-start(bf16[2,96,576]{2,1,0:T(8,128)(2,1)S(1)} %slice.389), channel_id=1, source_target_pairs={{0,8},{8,0},{17,25},{25,17},{2,10},{10,2},{19,27},{27,19},{4,12},{... | collective-permute-start | bytes 663560 | tf_op jit(solution)/shard_map/ppermute | solution.py:766
  241.8 7.6 %collective-permute-done.51 = bf16[2,128,768]{2,1,0:T(8,128)(2,1)S(1)} collective-permute-done((bf16[2,128,768]{2,1,0:T(8,128)(2,1)S(1)}, bf16[2,128,768]{2,1,0:T(8,128)(2,1)S(1)}, u32[]{:S(2)}, u32[]{:S(2)}) %collective-permute-start.51) | collective-permute-done | bytes 393248 | tf_op jit(solution)/shard_map/ppermute | solution.py:506
  249.6 2.4 collective-permute-done.49
  252.2 1.9 collective-permute-start.52
  255.4 2.1 collective-permute-start.54
  261.0 2.1 collective-permute-done.54
  (273 shorter events, 56.4 us)
Async XLA Ops:
  2.2 12.0 %collective-permute-start.6 = (bf16[96,576]{1,0:T(8,128)(2,1)S(1)}, bf16[96,576]{1,0:T(8,128)(2,1)S(1)}, u32[]{:S(2)}, u32[]{:S(2)}) collective-permute-start(bf16[96,576]{1,0:T(8,128)(2,1)S(1)} %pad_maximum_fusion.19), channel_id=1, source_target_pairs={{0,16},{16,0},{1,17},{17,1},{2,18},{18,2},{3,19},{19,3},{4,20},{20... | collective-permute-start | bytes 331784 | tf_op jit(solution)/shard_map/ppermute | solution.py:496
  5.2 46.2 %collective-permute-start.15 = (bf16[192,384]{1,0:T(8,128)(2,1)S(1)}, bf16[192,384]{1,0:T(8,128)(2,1)S(1)}, u32[]{:S(2)}, u32[]{:S(2)}) collective-permute-start(bf16[192,384]{1,0:T(8,128)(2,1)S(1)} %bitcast.133), channel_id=1, source_target_pairs={{0,4},{1,9},{4,0},{5,13},{8,12},{9,1},{12,8},{13,5},{2,6},{3,11},{... | collective-permute-start | bytes 442376 | tf_op jit(solution)/shard_map/ppermute | solution.py:506
  6.8 8.3 %collective-permute-start = (bf16[2,192,256]{2,1,0:T(8,128)(2,1)S(1)}, bf16[2,192,256]{2,1,0:T(8,128)(2,1)S(1)}, u32[]{:S(2)}, u32[]{:S(2)}) collective-permute-start(bf16[2,192,256]{2,1,0:T(8,128)(2,1)S(1)} %slice_bitcast_fusion.5), channel_id=1, source_target_pairs={{0,8},{1,5},{4,12},{5,1},{8,0},{9,13},{12,4},{13,9},{2,10},{3,7},{... | collective-permute-start | bytes 589832 | tf_op jit(solution)/shard_map/ppermute | solution.py:506
  10.0 9.4 %collective-permute-start.2 = (bf16[128,768]{1,0:T(8,128)(2,1)S(1)}, bf16[128,768]{1,0:T(8,128)(2,1)S(1)}, u32[]{:S(2)}, u32[]{:S(2)}) collective-permute-start(bf16[128,768]{1,0:T(8,128)(2,1)S(1)} %get-tuple-element.216), channel_id=1, source_target_pairs={{0,4},{1,9},{4,0},{5,13},{8,12},{9,1},{12,8},{13,5},{2,6},{3,11},{... | collective-permute-start | bytes 589832 | tf_op jit(solution)/shard_map/ppermute | solution.py:506
  14.3 9.4 %collective-permute-start.7 = (bf16[96,576]{1,0:T(8,128)(2,1)S(1)}, bf16[96,576]{1,0:T(8,128)(2,1)S(1)}, u32[]{:S(2)}, u32[]{:S(2)}) collective-permute-start(bf16[96,576]{1,0:T(8,128)(2,1)S(1)} %broadcast_select_fusion), channel_id=1, source_target_pairs={{0,1},{1,0},{2,3},{3,2},{4,5},{5,4},{6,7},{7,6},{8,9},{9,8},{10,11... | collective-permute-start | bytes 331784 | tf_op jit(solution)/shard_map/ppermute | solution.py:443
  15.2 13.2 %collective-permute-start.1 = (bf16[2,192,256]{2,1,0:T(8,128)(2,1)S(1)}, bf16[2,192,256]{2,1,0:T(8,128)(2,1)S(1)}, u32[]{:S(2)}, u32[]{:S(2)}) collective-permute-start(bf16[2,192,256]{2,1,0:T(8,128)(2,1)S(1)} %pad_maximum_fusion.12), channel_id=1, source_target_pairs={{0,4},{1,9},{4,0},{5,13},{8,12},{9,1},{12,8},{13,5},{2,6},{3,11},{... | collective-permute-start | bytes 589832 | tf_op jit(solution)/shard_map/ppermute | solution.py:506
  19.4 22.9 %collective-permute-start.3 = (bf16[2,128,768]{2,1,0:T(8,128)(2,1)S(1)}, bf16[2,128,768]{2,1,0:T(8,128)(2,1)S(1)}, u32[]{:S(2)}, u32[]{:S(2)}) collective-permute-start(bf16[2,128,768]{2,1,0:T(8,128)(2,1)S(1)} %pad_maximum_fusion.5), channel_id=1, source_target_pairs={{0,8},{1,5},{4,12},{5,1},{8,0},{9,13},{12,4},{13,9},{2,10},{3,7},{... | collective-permute-start | bytes 1179656 | tf_op jit(solution)/shard_map/ppermute | solution.py:506
  23.9 14.3 %collective-permute-start.8 = (bf16[2,96,576]{2,1,0:T(8,128)(2,1)S(1)}, bf16[2,96,576]{2,1,0:T(8,128)(2,1)S(1)}, u32[]{:S(2)}, u32[]{:S(2)}) collective-permute-start(bf16[2,96,576]{2,1,0:T(8,128)(2,1)S(1)} %pad_maximum_fusion.10), channel_id=1, source_target_pairs={{0,8},{1,5},{4,12},{5,1},{8,0},{9,13},{12,4},{13,9},{2,10},{3,7},{... | collective-permute-start | bytes 663560 | tf_op jit(solution)/shard_map/ppermute | solution.py:506
  28.5 15.5 %collective-permute-start.4 = (bf16[4,192,256]{2,1,0:T(8,128)(2,1)S(1)}, bf16[4,192,256]{2,1,0:T(8,128)(2,1)S(1)}, u32[]{:S(2)}, u32[]{:S(2)}) collective-permute-start(bf16[4,192,256]{2,1,0:T(8,128)(2,1)S(1)} %pad_maximum_fusion.4.xa.x_ref), channel_id=1, source_target_pairs={{0,2},{1,5},{2,0},{3,7},{4,6},{5,1},{6,4},{7,3},{8,10},{9,13},{10,... | collective-permute-start | bytes 1179656 | tf_op jit(solution)/shard_map/ppermute | solution.py:506
  38.3 9.8 %collective-permute-start.9 = (bf16[2,96,576]{2,1,0:T(8,128)(2,1)S(1)}, bf16[2,96,576]{2,1,0:T(8,128)(2,1)S(1)}, u32[]{:S(2)}, u32[]{:S(2)}) collective-permute-start(bf16[2,96,576]{2,1,0:T(8,128)(2,1)S(1)} %pad_maximum_fusion.11), channel_id=1, source_target_pairs={{0,4},{1,9},{4,0},{5,13},{8,12},{9,1},{12,8},{13,5},{2,6},{3,11},{... | collective-permute-start | bytes 663560 | tf_op jit(solution)/shard_map/ppermute | solution.py:506
  42.4 24.8 %collective-permute-start.20 = (bf16[4,128,768]{2,1,0:T(8,128)(2,1)S(1)}, bf16[4,128,768]{2,1,0:T(8,128)(2,1)}, u32[]{:S(2)}, u32[]{:S(2)}) collective-permute-start(bf16[4,128,768]{2,1,0:T(8,128)(2,1)S(1)} %pad_maximum_fusion.refs_0_), channel_id=1, source_target_pairs={{0,2},{1,17},{2,0},{3,19},{16,18},{17,1},{18,16},{19,3},{4,6},{5,2... | collective-permute-start | bytes 2359304 | tf_op jit(solution)/shard_map/ppermute | solution.py:506
  44.1 15.8 %collective-permute-start.5 = (bf16[2,4,192,256]{3,2,1,0:T(8,128)(2,1)S(1)}, bf16[2,4,192,256]{3,2,1,0:T(8,128)(2,1)}, u32[]{:S(2)}, u32[]{:S(2)}) collective-permute-start(bf16[2,4,192,256]{3,2,1,0:T(8,128)(2,1)S(1)} %pad_maximum_fusion.1), channel_id=1, source_target_pairs={{0,4},{1,3},{2,6},{3,1},{4,0},{5,7},{6,2},{7,5},{8,12},{9,11},{10,... | collective-permute-start | bytes 2359304 | tf_op jit(solution)/shard_map/ppermute | solution.py:506
  50.9 27.7 %collective-permute-start.14 = (bf16[4,128,768]{2,1,0:T(8,128)(2,1)S(1)}, bf16[4,128,768]{2,1,0:T(8,128)(2,1)}, u32[]{:S(2)}, u32[]{:S(2)}) collective-permute-start(bf16[4,128,768]{2,1,0:T(8,128)(2,1)S(1)} %pad_maximum_fusion.refs_0_), channel_id=1, source_target_pairs={{0,16},{1,3},{2,18},{3,1},{16,0},{17,19},{18,2},{19,17},{4,20},{5,... | collective-permute-start | bytes 2359304 | tf_op jit(solution)/shard_map/ppermute | solution.py:506
  51.5 28.9 %collective-permute-start.13 = (bf16[4,128,768]{2,1,0:T(8,128)(2,1)S(1)}, bf16[4,128,768]{2,1,0:T(8,128)(2,1)}, u32[]{:S(2)}, u32[]{:S(2)}) collective-permute-start(bf16[4,128,768]{2,1,0:T(8,128)(2,1)S(1)} %pad_maximum_fusion.refs_0_), channel_id=1, source_target_pairs={{0,1},{1,0},{2,3},{3,2},{4,5},{5,4},{6,7},{7,6},{8,9},{9,8},{10,11... | collective-permute-start | bytes 2359304 | tf_op jit(solution)/shard_map/ppermute | solution.py:443
  52.7 24.3 %collective-permute-start.16 = (bf16[2,192,384]{2,1,0:T(8,128)(2,1)S(1)}, bf16[2,192,384]{2,1,0:T(8,128)(2,1)S(1)}, u32[]{:S(2)}, u32[]{:S(2)}) collective-permute-start(bf16[2,192,384]{2,1,0:T(8,128)(2,1)S(1)} %pad_maximum_fusion.8), channel_id=1, source_target_pairs={{0,8},{1,5},{4,12},{5,1},{8,0},{9,13},{12,4},{13,9},{2,10},{3,7},{... | collective-permute-start | bytes 884744 | tf_op jit(solution)/shard_map/ppermute | solution.py:506
  68.1 8.4 %collective-permute-start.12 = (bf16[2,192,256]{2,1,0:T(8,128)(2,1)S(1)}, bf16[2,192,256]{2,1,0:T(8,128)(2,1)S(1)}, u32[]{:S(2)}, u32[]{:S(2)}) collective-permute-start(bf16[2,192,256]{2,1,0:T(8,128)(2,1)S(1)} %get-tuple-element.192), channel_id=1, source_target_pairs={{0,8},{1,5},{4,12},{5,1},{8,0},{9,13},{12,4},{13,9},{2,10},{3,7},{... | collective-permute-start | bytes 589832 | tf_op jit(solution)/shard_map/ppermute | solution.py:506
  69.3 28.1 %collective-permute-start.21 = (bf16[4,128,768]{2,1,0:T(8,128)(2,1)}, bf16[4,128,768]{2,1,0:T(8,128)(2,1)}, u32[]{:S(2)}, u32[]{:S(2)}) collective-permute-start(bf16[4,128,768]{2,1,0:T(8,128)(2,1)} %collective-permute-done.20.refs_1_), channel_id=1, source_target_pairs={{0,16},{1,3},{2,18},{3,1},{16,0},{17,19},{18,2},{19,17},{4,20},{5,... | collective-permute-start | bytes 2359304 | tf_op jit(solution)/shard_map/ppermute | solution.py:506
  76.6 13.4 %collective-permute-start.19 = (bf16[2,192,256]{2,1,0:T(8,128)(2,1)S(1)}, bf16[2,192,256]{2,1,0:T(8,128)(2,1)S(1)}, u32[]{:S(2)}, u32[]{:S(2)}) collective-permute-start(bf16[2,192,256]{2,1,0:T(8,128)(2,1)S(1)} %pad_maximum_fusion.14), channel_id=1, source_target_pairs={{0,4},{1,9},{4,0},{5,13},{8,12},{9,1},{12,8},{13,5},{2,6},{3,11},{... | collective-permute-start | bytes 589832 | tf_op jit(solution)/shard_map/ppermute | solution.py:506
  77.1 10.8 %collective-permute-start.17 = (bf16[2,192,256]{2,1,0:T(8,128)(2,1)}, bf16[2,192,256]{2,1,0:T(8,128)(2,1)S(1)}, u32[]{:S(2)}, u32[]{:S(2)}) collective-permute-start(bf16[2,192,256]{2,1,0:T(8,128)(2,1)} %get-tuple-element.102), channel_id=1, source_target_pairs={{0,4},{1,3},{2,6},{3,1},{4,0},{5,7},{6,2},{7,5},{8,12},{9,11},{10,... | collective-permute-start | bytes 589832 | tf_op jit(solution)/shard_map/ppermute | solution.py:506
  78.7 17.1 %collective-permute-start.25 = (bf16[4,192,384]{2,1,0:T(8,128)(2,1)S(1)}, bf16[4,192,384]{2,1,0:T(8,128)(2,1)S(1)}, u32[]{:S(2)}, u32[]{:S(2)}) collective-permute-start(bf16[4,192,384]{2,1,0:T(8,128)(2,1)S(1)} %pad_maximum_fusion.2.refs_8_), channel_id=1, source_target_pairs={{0,2},{1,17},{2,0},{3,19},{16,18},{17,1},{18,16},{19,3},{4,6},{5,2... | collective-permute-start | bytes 1769480 | tf_op jit(solution)/shard_map/ppermute | solution.py:506
  87.9 7.9 %collective-permute-start.18 = (bf16[2,192,256]{2,1,0:T(8,128)(2,1)S(1)}, bf16[2,192,256]{2,1,0:T(8,128)(2,1)S(1)}, u32[]{:S(2)}, u32[]{:S(2)}) collective-permute-start(bf16[2,192,256]{2,1,0:T(8,128)(2,1)S(1)} %pad_maximum_fusion.15), channel_id=1, source_target_pairs={{0,2},{1,5},{2,0},{3,7},{4,6},{5,1},{6,4},{7,3},{8,10},{9,13},{10,... | collective-permute-start | bytes 589832 | tf_op jit(solution)/shard_map/ppermute | solution.py:506
  88.5 9.9 %collective-permute-start.26 = (bf16[4,192,384]{2,1,0:T(8,128)(2,1)S(1)}, bf16[4,192,384]{2,1,0:T(8,128)(2,1)S(1)}, u32[]{:S(2)}, u32[]{:S(2)}) collective-permute-start(bf16[4,192,384]{2,1,0:T(8,128)(2,1)S(1)} %pad_maximum_fusion.2.refs_8_), channel_id=1, source_target_pairs={{0,16},{1,3},{2,18},{3,1},{16,0},{17,19},{18,2},{19,17},{4,20},{5,... | collective-permute-start | bytes 1769480 | tf_op jit(solution)/shard_map/ppermute | solution.py:506
  90.0 16.3 %collective-permute-start.22 = (bf16[4,128,768]{2,1,0:T(8,128)(2,1)}, bf16[4,128,768]{2,1,0:T(8,128)(2,1)S(1)}, u32[]{:S(2)}, u32[]{:S(2)}) collective-permute-start(bf16[4,128,768]{2,1,0:T(8,128)(2,1)} %collective-permute-done.20.refs_1_), channel_id=1, source_target_pairs={{0,1},{1,0},{2,3},{3,2},{4,5},{5,4},{6,7},{7,6},{8,9},{9,8},{10,11... | collective-permute-start | bytes 2359304 | tf_op jit(solution)/shard_map/ppermute | solution.py:443
  95.8 9.9 %collective-permute-start.27 = (bf16[4,192,384]{2,1,0:T(8,128)(2,1)S(1)}, bf16[4,192,384]{2,1,0:T(8,128)(2,1)S(1)}, u32[]{:S(2)}, u32[]{:S(2)}) collective-permute-start(bf16[4,192,384]{2,1,0:T(8,128)(2,1)S(1)} %collective-permute-done.25.refs_9_), channel_id=1, source_target_pairs={{0,16},{1,3},{2,18},{3,1},{16,0},{17,19},{18,2},{19,17},{4,20},{5,... | collective-permute-start | bytes 1769480 | tf_op jit(solution)/shard_map/ppermute | solution.py:506
  97.4 8.4 %collective-permute-start.28 = (bf16[4,192,384]{2,1,0:T(8,128)(2,1)S(1)}, bf16[4,192,384]{2,1,0:T(8,128)(2,1)S(1)}, u32[]{:S(2)}, u32[]{:S(2)}) collective-permute-start(bf16[4,192,384]{2,1,0:T(8,128)(2,1)S(1)} %pad_maximum_fusion.2.refs_8_), channel_id=1, source_target_pairs={{0,1},{1,0},{2,3},{3,2},{4,5},{5,4},{6,7},{7,6},{8,9},{9,8},{10,11... | collective-permute-start | bytes 1769480 | tf_op jit(solution)/shard_map/ppermute | solution.py:443
  97.4 9.0 %collective-permute-start.23 = (bf16[4,128,768]{2,1,0:T(8,128)(2,1)}, bf16[4,128,768]{2,1,0:T(8,128)(2,1)S(1)}, u32[]{:S(2)}, u32[]{:S(2)}) collective-permute-start(bf16[4,128,768]{2,1,0:T(8,128)(2,1)} %collective-permute-done.14.refs_2_), channel_id=1, source_target_pairs={{0,1},{1,0},{2,3},{3,2},{4,5},{5,4},{6,7},{7,6},{8,9},{9,8},{10,11... | collective-permute-start | bytes 2359304 | tf_op jit(solution)/shard_map/ppermute | solution.py:443
  98.4 8.0 %collective-permute-start.24 = (bf16[4,128,768]{2,1,0:T(8,128)(2,1)}, bf16[4,128,768]{2,1,0:T(8,128)(2,1)S(1)}, u32[]{:S(2)}, u32[]{:S(2)}) collective-permute-start(bf16[4,128,768]{2,1,0:T(8,128)(2,1)} %collective-permute-done.21.refs_3_), channel_id=1, source_target_pairs={{0,1},{1,0},{2,3},{3,2},{4,5},{5,4},{6,7},{7,6},{8,9},{9,8},{10,11... | collective-permute-start | bytes 2359304 | tf_op jit(solution)/shard_map/ppermute | solution.py:443
  140.4 15.5 %collective-permute-start.37 = (bf16[2,2,4,128,768]{4,3,2,1,0:T(8,128)(2,1)}, bf16[2,2,4,128,768]{4,3,2,1,0:T(8,128)(2,1)S(1)}, u32[]{:S(2)}, u32[]{:S(2)}) collective-permute-start(bf16[2,2,4,128,768]{4,3,2,1,0:T(8,128)(2,1)} %inner_give.1), channel_id=1, source_target_pairs={{0,1},{1,0},{2,3},{3,2},{4,5},{5,4},{6,7},{7,6},{8,9},{9,8},{10,11... | collective-permute-start | bytes 9437192 | tf_op jit(solution)/shard_map/ppermute | solution.py:443
  140.4 10.9 %collective-permute-start.36 = (bf16[2,2,4,192,384]{4,3,2,1,0:T(8,128)(2,1)}, bf16[2,2,4,192,384]{4,3,2,1,0:T(8,128)(2,1)}, u32[]{:S(2)}, u32[]{:S(2)}) collective-permute-start(bf16[2,2,4,192,384]{4,3,2,1,0:T(8,128)(2,1)} %outer_give.1), channel_id=1, source_target_pairs={{0,1},{1,0},{2,3},{3,2},{4,5},{5,4},{6,7},{7,6},{8,9},{9,8},{10,11... | collective-permute-start | bytes 7077896 | tf_op jit(solution)/shard_map/ppermute | solution.py:443
  140.9 8.6 %collective-permute-start.32 = (bf16[2,192,256]{2,1,0:T(8,128)(2,1)}, bf16[2,192,256]{2,1,0:T(8,128)(2,1)S(1)}, u32[]{:S(2)}, u32[]{:S(2)}) collective-permute-start(bf16[2,192,256]{2,1,0:T(8,128)(2,1)} %get-tuple-element.124), channel_id=1, source_target_pairs={{0,8},{1,5},{4,12},{5,1},{8,0},{9,13},{12,4},{13,9},{2,10},{3,7},{... | collective-permute-start | bytes 589832 | tf_op jit(solution)/shard_map/ppermute | solution.py:506
  142.6 8.7 %collective-permute-start.35 = (bf16[2,192,256]{2,1,0:T(8,128)(2,1)}, bf16[2,192,256]{2,1,0:T(8,128)(2,1)}, u32[]{:S(2)}, u32[]{:S(2)}) collective-permute-start(bf16[2,192,256]{2,1,0:T(8,128)(2,1)} %pad_maximum_fusion.16), channel_id=1, source_target_pairs={{0,2},{1,5},{2,0},{3,7},{4,6},{5,1},{6,4},{7,3},{8,10},{9,13},{10,... | collective-permute-start | bytes 589832 | tf_op jit(solution)/shard_map/ppermute | solution.py:506
  150.2 13.3 %collective-permute-start.34 = (bf16[2,192,256]{2,1,0:T(8,128)(2,1)}, bf16[2,192,256]{2,1,0:T(8,128)(2,1)S(1)}, u32[]{:S(2)}, u32[]{:S(2)}) collective-permute-start(bf16[2,192,256]{2,1,0:T(8,128)(2,1)} %pad_maximum_fusion.17), channel_id=1, source_target_pairs={{0,4},{1,9},{4,0},{5,13},{8,12},{9,1},{12,8},{13,5},{2,6},{3,11},{... | collective-permute-start | bytes 589832 | tf_op jit(solution)/shard_map/ppermute | solution.py:506
  154.9 30.1 %collective-permute-start.38 = (bf16[2,4,192,384]{3,2,1,0:T(8,128)(2,1)}, bf16[2,4,192,384]{3,2,1,0:T(8,128)(2,1)}, u32[]{:S(2)}, u32[]{:S(2)}) collective-permute-start(bf16[2,4,192,384]{3,2,1,0:T(8,128)(2,1)} %outer_first.1), channel_id=1, source_target_pairs={{0,8},{1,5},{4,12},{5,1},{8,0},{9,13},{12,4},{13,9},{2,10},{3,7},{... | collective-permute-start | bytes 3538952 | tf_op jit(solution)/shard_map/ppermute | solution.py:506
  161.9 36.3 %collective-permute-start.41 = (bf16[2,4,128,768]{3,2,1,0:T(8,128)(2,1)}, bf16[2,4,128,768]{3,2,1,0:T(8,128)(2,1)S(1)}, u32[]{:S(2)}, u32[]{:S(2)}) collective-permute-start(bf16[2,4,128,768]{3,2,1,0:T(8,128)(2,1)} %inner_first.1), channel_id=1, source_target_pairs={{0,16},{1,3},{2,18},{3,1},{16,0},{17,19},{18,2},{19,17},{4,20},{5,... | collective-permute-start | bytes 4718600 | tf_op jit(solution)/shard_map/ppermute | solution.py:506
  191.9 18.6 %collective-permute-start.40 = (bf16[2,4,192,256]{3,2,1,0:T(8,128)(2,1)}, bf16[2,4,192,256]{3,2,1,0:T(8,128)(2,1)}, u32[]{:S(2)}, u32[]{:S(2)}) collective-permute-start(bf16[2,4,192,256]{3,2,1,0:T(8,128)(2,1)} %get-tuple-element.151), channel_id=1, source_target_pairs={{0,4},{1,3},{2,6},{3,1},{4,0},{5,7},{6,2},{7,5},{8,12},{9,11},{10,... | collective-permute-start | bytes 2359304 | tf_op jit(solution)/shard_map/ppermute | solution.py:506
  198.1 26.5 %collective-permute-start.46 = (bf16[4,192,384]{2,1,0:T(8,128)(2,1)}, bf16[4,192,384]{2,1,0:T(8,128)(2,1)}, u32[]{:S(2)}, u32[]{:S(2)}) collective-permute-start(bf16[4,192,384]{2,1,0:T(8,128)(2,1)} %get-tuple-element.167), channel_id=1, source_target_pairs={{0,4},{1,9},{4,0},{5,13},{8,12},{9,1},{12,8},{13,5},{2,6},{3,11},{... | collective-permute-start | bytes 1769480 | tf_op jit(solution)/shard_map/ppermute | solution.py:506
  204.3 24.4 %collective-permute-start.44 = (bf16[4,128,768]{2,1,0:T(8,128)(2,1)}, bf16[4,128,768]{2,1,0:T(8,128)(2,1)}, u32[]{:S(2)}, u32[]{:S(2)}) collective-permute-start(bf16[4,128,768]{2,1,0:T(8,128)(2,1)} %get-tuple-element.163), channel_id=1, source_target_pairs={{0,2},{1,17},{2,0},{3,19},{16,18},{17,1},{18,16},{19,3},{4,6},{5,2... | collective-permute-start | bytes 2359304 | tf_op jit(solution)/shard_map/ppermute | solution.py:506
  211.5 9.3 %collective-permute-start.42 = (bf16[4,192,256]{2,1,0:T(8,128)(2,1)S(1)}, bf16[4,192,256]{2,1,0:T(8,128)(2,1)}, u32[]{:S(2)}, u32[]{:S(2)}) collective-permute-start(bf16[4,192,256]{2,1,0:T(8,128)(2,1)S(1)} %fusion.3), channel_id=1, source_target_pairs={{0,2},{1,5},{2,0},{3,7},{4,6},{5,1},{6,4},{7,3},{8,10},{9,13},{10,... | collective-permute-start | bytes 1179656 | tf_op jit(solution)/shard_map/ppermute | solution.py:506
  216.0 8.5 %collective-permute-start.45 = (bf16[4,96,576]{2,1,0:T(8,128)(2,1)}, bf16[4,96,576]{2,1,0:T(8,128)(2,1)S(1)}, u32[]{:S(2)}, u32[]{:S(2)}) collective-permute-start(bf16[4,96,576]{2,1,0:T(8,128)(2,1)} %get-tuple-element.161), channel_id=1, source_target_pairs={{0,1},{1,0},{2,3},{3,2},{4,5},{5,4},{6,7},{7,6},{8,9},{9,8},{10,11... | collective-permute-start | bytes 1327112 | tf_op jit(solution)/shard_map/ppermute | solution.py:443
  222.4 8.8 %collective-permute-start.43 = (bf16[2,192,256]{2,1,0:T(8,128)(2,1)S(1)}, bf16[2,192,256]{2,1,0:T(8,128)(2,1)S(1)}, u32[]{:S(2)}, u32[]{:S(2)}) collective-permute-start(bf16[2,192,256]{2,1,0:T(8,128)(2,1)S(1)} %slice.328), channel_id=1, source_target_pairs={{0,8},{1,5},{4,12},{5,1},{8,0},{9,13},{12,4},{13,9},{2,10},{3,7},{... | collective-permute-start | bytes 589832 | tf_op jit(solution)/shard_map/ppermute | solution.py:506
  226.8 22.7 %collective-permute-start.50 = (bf16[2,192,384]{2,1,0:T(8,128)(2,1)S(1)}, bf16[2,192,384]{2,1,0:T(8,128)(2,1)S(1)}, u32[]{:S(2)}, u32[]{:S(2)}) collective-permute-start(bf16[2,192,384]{2,1,0:T(8,128)(2,1)S(1)} %slice.332), channel_id=1, source_target_pairs={{0,16},{1,3},{2,18},{3,1},{16,0},{17,19},{18,2},{19,17},{4,20},{5,... | collective-permute-start | bytes 884744 | tf_op jit(solution)/shard_map/ppermute | solution.py:506
  227.4 11.5 %collective-permute-start.48 = (bf16[4,96,576]{2,1,0:T(8,128)(2,1)S(1)}, bf16[4,96,576]{2,1,0:T(8,128)(2,1)S(1)}, u32[]{:S(2)}, u32[]{:S(2)}) collective-permute-start(bf16[4,96,576]{2,1,0:T(8,128)(2,1)S(1)} %get-tuple-element.178), channel_id=1, source_target_pairs={{16,0},{1,17},{18,2},{3,19},{20,4},{5,21},{22,6},{7,23},{24,8},{9,... | collective-permute-start | bytes 1327112 | tf_op jit(solution)/shard_map/ppermute | solution.py:750
  231.2 18.2 %collective-permute-start.51 = (bf16[2,128,768]{2,1,0:T(8,128)(2,1)S(1)}, bf16[2,128,768]{2,1,0:T(8,128)(2,1)S(1)}, u32[]{:S(2)}, u32[]{:S(2)}) collective-permute-start(bf16[2,128,768]{2,1,0:T(8,128)(2,1)S(1)} %slice.334), channel_id=1, source_target_pairs={{0,8},{1,5},{4,12},{5,1},{8,0},{9,13},{12,4},{13,9},{2,10},{3,7},{... | collective-permute-start | bytes 1179656 | tf_op jit(solution)/shard_map/ppermute | solution.py:506
  232.1 20.1 %collective-permute-start.47 = (bf16[2,192,256]{2,1,0:T(8,128)(2,1)S(1)}, bf16[2,192,256]{2,1,0:T(8,128)(2,1)S(1)}, u32[]{:S(2)}, u32[]{:S(2)}) collective-permute-start(bf16[2,192,256]{2,1,0:T(8,128)(2,1)S(1)} %pad_maximum_fusion.18), channel_id=1, source_target_pairs={{0,4},{1,9},{4,0},{5,13},{8,12},{9,1},{12,8},{13,5},{2,6},{3,11},{... | collective-permute-start | bytes 589832 | tf_op jit(solution)/shard_map/ppermute | solution.py:506
  239.0 13.1 %collective-permute-start.49 = (bf16[2,96,576]{2,1,0:T(8,128)(2,1)S(1)}, bf16[2,96,576]{2,1,0:T(8,128)(2,1)S(1)}, u32[]{:S(2)}, u32[]{:S(2)}) collective-permute-start(bf16[2,96,576]{2,1,0:T(8,128)(2,1)S(1)} %slice.389), channel_id=1, source_target_pairs={{0,8},{8,0},{17,25},{25,17},{2,10},{10,2},{19,27},{27,19},{4,12},{... | collective-permute-start | bytes 663560 | tf_op jit(solution)/shard_map/ppermute | solution.py:766
  252.2 8.0 %collective-permute-start.52 = (bf16[96,576]{1,0:T(8,128)(2,1)S(1)}, bf16[96,576]{1,0:T(8,128)(2,1)S(1)}, u32[]{:S(2)}, u32[]{:S(2)}) collective-permute-start(bf16[96,576]{1,0:T(8,128)(2,1)S(1)} %fusion.5), channel_id=1, source_target_pairs={{0,4},{4,0},{17,21},{21,17},{2,6},{6,2},{19,23},{23,19},{8,12},{12... | collective-permute-start | bytes 331784 | tf_op jit(solution)/shard_map/ppermute | solution.py:772
  255.4 7.8 %collective-permute-start.54 = (bf16[128,768]{1,0:T(8,128)(2,1)S(1)}, bf16[128,768]{1,0:T(8,128)(2,1)S(1)}, u32[]{:S(2)}, u32[]{:S(2)}) collective-permute-start(bf16[128,768]{1,0:T(8,128)(2,1)S(1)} %slice_bitcast_fusion.1), channel_id=1, source_target_pairs={{0,4},{1,9},{4,0},{5,13},{8,12},{9,1},{12,8},{13,5},{2,6},{3,11},{... | collective-permute-start | bytes 589832 | tf_op jit(solution)/shard_map/ppermute | solution.py:506
  260.2 7.0 %collective-permute-start.53 = (bf16[96,576]{1,0:T(8,128)(2,1)S(1)}, bf16[96,576]{1,0:T(8,128)(2,1)S(1)}, u32[]{:S(2)}, u32[]{:S(2)}) collective-permute-start(bf16[96,576]{1,0:T(8,128)(2,1)S(1)} %select_convert_fusion.1), channel_id=1, source_target_pairs={{0,1},{1,0},{2,3},{3,2},{4,5},{5,4},{6,7},{7,6},{8,9},{9,8},{10,11... | collective-permute-start | bytes 331784 | tf_op jit(solution)/shard_map/ppermute | solution.py:443
  (49 other events, 315.3 us)
